TPU v7x, 128 devices: a whole 4x4x4 slice. The times are simulated.
128 devices in a mesh: gx: 16 (over y_hi, x, core), gz: 8 (over z, y_lo).
Axes of the slice: x: 4, y: 4 (y_hi: 2, y_lo: 2; y = y_hi * 2 + y_lo), z: 4, core: 2. Of those that a mesh axis runs over, the one named last changes fastest.
Arguments:
- adjoint: float32 [3, 256, 128, 1024], P(None, 'gx', None, 'gz'), may hold values from -6 to 6
- velocity: float32 [3, 256, 128, 1024], P(None, 'gx', None, 'gz'), may hold values from -0.45 to 0.45
- viscosity: float32 [256, 128, 1024], P('gx', None, 'gz'), may hold values from 0.02 to 0.15
- filters: bfloat16 [512, 512, 512], P(('gx', 'gz')), may hold values from -0.25 to 0.25
- block_tiles: int32 [256, 8], replicated, may hold values from 0 to 511, all different within a row
- tile_place: int32 [512], replicated, may hold values from 0 to 511, each once
Outputs:
- adjoint_out: float32 [3, 256, 128, 1024], P(None, 'gx', None, 'gz')
- generator_tile_gradient: float32 [512, 3, 512], P(('gx', 'gz'))
Inputs may be any that keep to these rules, and one draw needn't show every extreme that they name: `block_tiles`: each row lists 8 different tiles; every tile is listed by some block. `tile_place`: each tile exactly once.
All inputs are finite; a program needn't handle non-finite values.
Results may differ from a plain program's by a relative error of at most 0.0003.
Values sent between devices are 32-bit elements; how exact they have to be, the bound alone decides.
No kernel may reach another device: no remote copies, remote signals or barrier semaphores. Data moves between devices by JAX's collectives and lax.ppermute only.
A program may use at most 192 MiB of HBM per device.

v0:
```python
import jax
import jax.numpy as jnp
from jax import lax
from jax.sharding import PartitionSpec as P

BY = 4
BZ = 128


def with_halo(block, sides, width, periodic):
    for axis, dim in sides:
        count = lax.axis_size(axis)
        forward = [(i, i + 1) for i in range(count - 1)]
        if periodic:
            forward.append((count - 1, 0))
        backward = [(target, source) for source, target in forward]
        low = lax.ppermute(
            lax.slice_in_dim(block, block.shape[dim] - width, None, axis=dim), axis, forward
        )
        high = lax.ppermute(lax.slice_in_dim(block, 0, width, axis=dim), axis, backward)
        block = jnp.concatenate([low, block, high], axis=dim)
    return block


def advance(padded, visc_pad, velocity):
    centre = padded[..., 1:-1, 1:-1, 1:-1]
    east_cell = padded[..., 2:, 1:-1, 1:-1]
    west_cell = padded[..., :-2, 1:-1, 1:-1]
    north_cell = padded[..., 1:-1, 2:, 1:-1]
    south_cell = padded[..., 1:-1, :-2, 1:-1]
    upper_cell = padded[..., 1:-1, 1:-1, 2:]
    lower_cell = padded[..., 1:-1, 1:-1, :-2]
    visc_mid = visc_pad[1:-1, 1:-1, 1:-1]
    east_face = 0.5 * (visc_mid + visc_pad[2:, 1:-1, 1:-1])
    west_face = 0.5 * (visc_mid + visc_pad[:-2, 1:-1, 1:-1])
    north_face = 0.5 * (visc_mid + visc_pad[1:-1, 2:, 1:-1])
    south_face = 0.5 * (visc_mid + visc_pad[1:-1, :-2, 1:-1])
    upper_face = 0.5 * (visc_mid + visc_pad[1:-1, 1:-1, 2:])
    lower_face = 0.5 * (visc_mid + visc_pad[1:-1, 1:-1, :-2])
    transport = 0.5 * (
        velocity[0] * (east_cell - west_cell)
        + velocity[1] * (north_cell - south_cell)
        + velocity[2] * (upper_cell - lower_cell)
    )
    diffusion = east_face * (east_cell - centre) - west_face * (centre - west_cell)
    diffusion = diffusion + north_face * (north_cell - centre) - south_face * (centre - south_cell)
    diffusion = diffusion + upper_face * (upper_cell - centre) - lower_face * (centre - lower_cell)
    return centre + transport + diffusion


def widened_state(field, width):
    along_x = with_halo(field, (("gx", 1),), width, False)
    return with_halo(along_x, (("gz", 3),), width, True)


def widen_coef(field, width):
    along_x = with_halo(field, (("gx", 1),), width, False)
    return with_halo(along_x, (("gz", 3),), width, True)


def wall_pad(field):
    return jnp.pad(field, ((0, 0),) * (field.ndim - 2) + ((1, 1), (0, 0)))


def cut_blocks(face, group_list):
    comps, rows_all, cols_all = face.shape
    reshaped_array = face.reshape(
        comps, rows_all // BY, BY, group_list, cols_all // (group_list * BZ), BZ
    )
    return reshaped_array.transpose(3, 1, 4, 0, 2, 5).reshape(-1, comps * BY * BZ)


def place_of(lists, tile_place):
    tile_count = tile_place.shape[0]
    matches = lists[:, :, None] == jnp.arange(tile_count, dtype=jnp.int32)[None, None, :]
    return jnp.sum(jnp.where(matches, tile_place[None, None, :], 0), axis=2)


def table_rows(places, blocks, row_count):
    wanted = jnp.arange(row_count, dtype=jnp.int32)
    onehot = jnp.sum((places[None, :, :] == wanted[:, None, None]).astype(jnp.float32), axis=2)
    return jnp.dot(
        onehot, blocks, precision=lax.Precision.HIGHEST, preferred_element_type=jnp.float32
    )


def shards(adjoint, velocity, viscosity, filters, block_tiles, tile_place):
    global_streamwise_index = lax.axis_index("gx")
    gz_index = lax.axis_index("gz")
    visc_pad = wall_pad(widen_coef(viscosity[None], 1)[0])
    state = adjoint
    for step_index in range(2):
        state = advance(wall_pad(widened_state(state, 1)), visc_pad, velocity)
    face = state[:, 0]
    column_blocks = block_tiles.shape[0] // lax.axis_size("gz")
    tile_rows = filters.shape[0]
    blocks = cut_blocks(face, 1) * (global_streamwise_index == 0).astype(jnp.float32)
    lists = lax.dynamic_slice_in_dim(block_tiles, gz_index * column_blocks, column_blocks, 0)
    places = place_of(lists, tile_place)
    sums = lax.psum_scatter(
        table_rows(places, blocks, tile_rows * lax.axis_size(("gx", "gz"))),
        ("gx", "gz"),
        scatter_dimension=0,
        tiled=True,
    )
    tile_view = sums.reshape(tile_rows, 3, -1)
    generator_tile_gradient = jnp.einsum(
        "gvl,gls->gvs",
        tile_view,
        filters.astype(jnp.float32),
        precision=lax.Precision.HIGHEST,
        preferred_element_type=jnp.float32,
    )
    return (state, generator_tile_gradient)


def solution(mesh):
    placed = (
        P(None, "gx", None, "gz"),
        P(None, "gx", None, "gz"),
        P("gx", None, "gz"),
        P(("gx", "gz"), None, None),
        P(),
        P(),
    )
    return jax.shard_map(
        shards,
        mesh=mesh,
        in_specs=placed,
        out_specs=(P(None, "gx", None, "gz"), P(("gx", "gz"), None, None)),
        check_vma=False,
    )
```

profile of v0, /device:TPU:24, one launch (start us, length us, event | category | flops | bytes accessed | tf_op | source)
XLA Modules:
  0.0 347.1 jit_solution(10695477137692074045)
XLA Ops:
  10.9 7.3 %collective-permute-start.5 = (f32[1,1,128,128]{2,3,1,0:T(8,128)S(1)}, f32[1,1,128,128]{2,3,1,0:T(8,128)S(1)}, u32[]{:S(2)}, u32[]{:S(2)}) collective-permute-start(f32[1,1,128,128]{2,3,1,0:T(8,128)S(1)} %get-tuple-element.32), channel_id=1, source_target_pairs={{8,0},{16,8},{24,16},{32,24},{40,32},{48,40},{56,48},{64,56},{72,6... | collective-permute-start | bytes 196616 | tf_op jit(solution)/shard_map/ppermute | solution.py:20
  21.9 7.3 %collective-permute-start = (f32[3,1,128,128]{3,2,0,1:T(8,128)}, f32[3,1,128,128]{3,2,0,1:T(8,128)}, u32[]{:S(2)}, u32[]{:S(2)}) collective-permute-start(f32[3,1,128,128]{3,2,0,1:T(8,128)} %get-tuple-element.21), channel_id=1, source_target_pairs={{8,0},{16,8},{24,16},{32,24},{40,32},{48,40},{56,48},{64,56},{72,6... | collective-permute-start | bytes 589832 | tf_op jit(solution)/shard_map/ppermute | solution.py:20
  31.4 3.7 %slice_bitcast_fusion.2 = (f32[16,128,128]{2,1,0:T(8,128)}, f32[16,128,128]{2,1,0:T(8,128)}, f32[16,128,128]{2,1,0:T(8,128)}) fusion(f32[3,16,128,128]{3,2,1,0:T(8,128)} %param.7), kind=kLoop, calls=%fused_computation.71 | loop fusion | bytes 6291456 | tf_op jit(solution)/shard_map/mul | solution.py:41
  42.1 4.1 %fusion.44 = (f32[3,18,128,1]{3,2,0,1:T(8,128)}, f32[3,18,128,1]{3,2,0,1:T(8,128)}) fusion(f32[3,18,128,128]{3,2,0,1:T(8,128)S(1)} %constant_dynamic-update-slice_fusion), kind=kLoop, calls=%fused_computation.88 | loop fusion | bytes 110592 | tf_op jit(solution)/shard_map/slice | solution.py:18
  46.2 4.1 %copy.82 = f32[3,18,128,1]{2,1,3,0:T(8,128)} copy(f32[3,18,128,1]{3,2,0,1:T(8,128)} %get-tuple-element.14) | data formatting | bytes 55296 | tf_op jit(solution)/shard_map/slice | solution.py:18
  50.3 2.8 collective-permute-start.2
  53.1 4.1 %copy.83 = f32[3,18,128,1]{2,1,3,0:T(8,128)} copy(f32[3,18,128,1]{3,2,0,1:T(8,128)} %get-tuple-element.15) | data formatting | bytes 55296 | tf_op jit(solution)/shard_map/slice | solution.py:20
  57.8 3.5 %fusion.40 = (f32[16,128,128]{1,2,0:T(8,128)}, f32[16,128,128]{1,2,0:T(8,128)}, f32[16,128,128]{1,2,0:T(8,128)}, f32[16,128,128]{1,2,0:T(8,128)}, f32[16,128,128]{1,2,0:T(8,128)}, /*index=5*/f32[16,128,128]{1,2,0:T(8,128)}) fusion(f32[18,128,130]{1,2,0:T(8,128)S(1)} %maximum_bitcast_fusion), kind=kLoop, calls=%fused_computation.68 | loop fusion | flops 3145728 | bytes 12787712 | tf_op jit(solution)/shard_map/mul | solution.py:34
  62.9 2.7 copy.90
  75.7 3.3 copy.84
  79.0 3.2 copy.85
  82.2 8.0 %select_maximum_fusion.4 = f32[3,18,130,130]{3,2,0,1:T(8,128)} fusion(f32[3,18,128,1]{3,2,0,1:T(8,128)} %copy.85, f32[3,18,128,128]{3,2,0,1:T(8,128)} %copy-done.1, f32[3,18,128,1]{3,2,0,1:T(8,128)} %copy.84), kind=kLoop, calls=%fused_computation.6 | loop fusion | flops 7300800 | bytes 7244640 | tf_op jit(solution)/shard_map/concatenate | solution.py:21
  90.2 18.8 %fusion.25 = f32[3,16,128,128]{3,2,0,1:T(8,128)} fusion(f32[3,16,128,128]{3,2,0,1:T(8,128)} %copy.88, f32[3,1,128,128]{3,2,0,1:T(8,128)S(1)} %collective-permute-done.1, f32[3,1,128,128]{3,2,0,1:T(8,128)} %collective-permute-done, f32[3,18,128,1]{3,2,0,1:T(8,128)} %copy.85, f32[3,18,128,128]{3,2,0,1:T(8,128)} %copy-done.1, f32[3,18,128,1]{3,2,0,1:T(8,128)} %copy.84, ...), kind=kLoop, calls=%fused_computation.45 | loop fusion | flops 25165824 | bytes 26007552 | tf_op jit(solution)/shard_map/add | solution.py:48
  117.3 6.2 %collective-permute-done.9 = f32[3,1,128,128]{3,2,0,1:T(8,128)S(1)} collective-permute-done((f32[3,1,128,128]{3,2,0,1:T(8,128)}, f32[3,1,128,128]{3,2,0,1:T(8,128)S(1)}, u32[]{:S(2)}, u32[]{:S(2)}) %collective-permute-start.9) | collective-permute-done | bytes 196640 | tf_op jit(solution)/shard_map/ppermute | solution.py:17
  125.6 4.1 %fusion.43 = (f32[3,18,128,1]{3,2,0,1:T(8,128)}, f32[3,18,128,1]{3,2,0,1:T(8,128)}) fusion(f32[3,18,128,128]{3,2,0,1:T(8,128)S(1)} %pad_maximum_fusion), kind=kLoop, calls=%fused_computation.87 | loop fusion | bytes 110592 | tf_op jit(solution)/shard_map/slice | solution.py:18
  129.7 4.1 %copy.102 = f32[3,18,128,1]{2,1,3,0:T(8,128)} copy(f32[3,18,128,1]{3,2,0,1:T(8,128)} %get-tuple-element.12) | data formatting | bytes 55296 | tf_op jit(solution)/shard_map/slice | solution.py:18
  136.3 4.1 %copy.103 = f32[3,18,128,1]{2,1,3,0:T(8,128)} copy(f32[3,18,128,1]{3,2,0,1:T(8,128)} %get-tuple-element.13) | data formatting | bytes 55296 | tf_op jit(solution)/shard_map/slice | solution.py:20
  143.0 3.3 copy.104
  146.3 3.3 copy.105
  149.7 10.1 %select_maximum_fusion = f32[3,18,130,130]{3,2,0,1:T(8,128)} fusion(f32[3,18,128,1]{3,2,0,1:T(8,128)} %copy.105, f32[3,18,128,1]{3,2,0,1:T(8,128)} %copy.104, f32[3,1,128,128]{3,2,0,1:T(8,128)S(1)} %collective-permute-done.8, f32[3,16,128,128]{3,2,0,1:T(8,128)} %fusion.25, f32[3,1,128,128]{3,2,0,1:T(8,128)S(1)} %collective-permute-done.9), kind=kLoop, calls=%fused_computation.2 | loop fusion | flops 10951200 | bytes 7244640 | tf_op jit(solution)/shard_map/concatenate | solution.py:21
  159.8 19.0 %fusion.9 = f32[3,16,128,128]{3,2,0,1:T(8,128)} fusion(f32[3,16,128,128]{3,2,0,1:T(8,128)} %fusion.25, f32[3,1,128,128]{3,2,0,1:T(8,128)S(1)} %collective-permute-done.9, f32[3,1,128,128]{3,2,0,1:T(8,128)S(1)} %collective-permute-done.8, f32[3,18,128,1]{3,2,0,1:T(8,128)} %copy.105, f32[3,18,128,1]{3,2,0,1:T(8,128)} %copy.104, ...), kind=kLoop, calls=%fused_computation.25 | loop fusion | flops 28311552 | bytes 22468608 | tf_op jit(solution)/shard_map/add | solution.py:48
  179.9 5.2 %fusion.48 = f32[512,1536]{1,0:T(8,128)} fusion(f32[512,32]{0,1:T(8,128)} %convert_reduce_fusion, f32[32,1536]{1,0:T(8,128)S(1)} %mul.223), kind=kOutput, calls=%fused_computation.92 | convolution fusion | flops 301989888 | bytes 3407872 | tf_op jit(solution)/shard_map/dot_general | solution.py:82
  185.1 3.9 %copy.111 = f32[3,16,128,128]{3,2,1,0:T(8,128)} copy(f32[3,16,128,128]{3,2,0,1:T(8,128)} %fusion.9) | data formatting | bytes 6291456
  189.0 148.9 %all-reduce.6.cloned.1.call-done = f32[512,1536]{1,0:T(8,128)} async-done(((f32[512,1536]{1,0:T(8,128)}), f32[512,1536]{1,0:T(8,128)}) %all-reduce.6.cloned.1.call-update) | async-done | bytes 3145744
  (64 shorter events, 47.8 us)
Async XLA Ops:
  7.2 331.6 %copy-start = (bf16[4,512,512]{2,1,0:T(8,128)(2,1)S(1)}, bf16[4,512,512]{2,1,0:T(8,128)(2,1)}, u32[]{:S(2)}) copy-start(bf16[4,512,512]{2,1,0:T(8,128)(2,1)} %param.9) | copy-start | bytes 6291460
  7.2 330.8 %all-reduce.6.cloned.1.call-start = ((), (), s32[]{:S(2)}) async-start(), calls=%async_computation | async-start | bytes 6291456
  8.9 26.2 %copy-start.3 = (f32[16,128,128]{1,2,0:T(8,128)}, f32[16,128,128]{1,2,0:T(8,128)S(1)}, u32[]{:S(2)}) copy-start(f32[16,128,128]{1,2,0:T(8,128)S(1)} %copy.89) | copy-start | bytes 3145732
  9.0 20.2 %collective-permute-start.4 = (f32[1,1,128,128]{2,3,1,0:T(8,128)S(1)}, f32[1,1,128,128]{2,3,1,0:T(8,128)S(1)}, u32[]{:S(2)}, u32[]{:S(2)}) collective-permute-start(f32[1,1,128,128]{2,3,1,0:T(8,128)S(1)} %get-tuple-element.31), channel_id=1, source_target_pairs={{0,8},{8,16},{16,24},{24,32},{32,40},{40,48},{48,56},{56,64},{64,7... | collective-permute-start | bytes 196616 | tf_op jit(solution)/shard_map/ppermute | solution.py:17
  10.9 18.3 %collective-permute-start.5 = (f32[1,1,128,128]{2,3,1,0:T(8,128)S(1)}, f32[1,1,128,128]{2,3,1,0:T(8,128)S(1)}, u32[]{:S(2)}, u32[]{:S(2)}) collective-permute-start(f32[1,1,128,128]{2,3,1,0:T(8,128)S(1)} %get-tuple-element.32), channel_id=1, source_target_pairs={{8,0},{16,8},{24,16},{32,24},{40,32},{48,40},{56,48},{64,56},{72,6... | collective-permute-start | bytes 196616 | tf_op jit(solution)/shard_map/ppermute | solution.py:20
  20.0 19.0 %collective-permute-start.1 = (f32[3,1,128,128]{3,2,0,1:T(8,128)}, f32[3,1,128,128]{3,2,0,1:T(8,128)S(1)}, u32[]{:S(2)}, u32[]{:S(2)}) collective-permute-start(f32[3,1,128,128]{3,2,0,1:T(8,128)} %get-tuple-element.22), channel_id=1, source_target_pairs={{0,8},{8,16},{16,24},{24,32},{32,40},{40,48},{48,56},{56,64},{64,7... | collective-permute-start | bytes 589832 | tf_op jit(solution)/shard_map/ppermute | solution.py:17
  21.9 19.3 %collective-permute-start = (f32[3,1,128,128]{3,2,0,1:T(8,128)}, f32[3,1,128,128]{3,2,0,1:T(8,128)}, u32[]{:S(2)}, u32[]{:S(2)}) collective-permute-start(f32[3,1,128,128]{3,2,0,1:T(8,128)} %get-tuple-element.21), channel_id=1, source_target_pairs={{8,0},{16,8},{24,16},{32,24},{40,32},{48,40},{56,48},{64,56},{72,6... | collective-permute-start | bytes 589832 | tf_op jit(solution)/shard_map/ppermute | solution.py:20
  29.2 6.0 %copy-start.4 = (f32[1,1,128,128]{2,3,1,0:T(8,128)}, f32[1,1,128,128]{2,3,1,0:T(8,128)S(1)}, u32[]{:S(2)}) copy-start(f32[1,1,128,128]{2,3,1,0:T(8,128)S(1)} %collective-permute-done.4) | copy-start | bytes 196612
  29.2 6.0 %copy-start.5 = (f32[1,1,128,128]{2,3,1,0:T(8,128)}, f32[1,1,128,128]{2,3,1,0:T(8,128)S(1)}, u32[]{:S(2)}) copy-start(f32[1,1,128,128]{2,3,1,0:T(8,128)S(1)} %collective-permute-done.5) | copy-start | bytes 196612
  29.2 7.8 %collective-permute-start.6 = (f32[1,18,128,1]{2,3,1,0:T(1,128)S(1)}, f32[1,18,128,1]{2,3,1,0:T(1,128)S(1)}, u32[]{:S(2)}, u32[]{:S(2)}) collective-permute-start(f32[1,18,128,1]{2,3,1,0:T(1,128)S(1)} %get-tuple-element.29), channel_id=1, source_target_pairs={{0,1},{1,2},{2,3},{3,4},{4,5},{5,6},{6,7},{7,0},{8,9},{9,10},{10,1... | collective-permute-start | bytes 27656 | tf_op jit(solution)/shard_map/ppermute | solution.py:17
  31.4 3.8 %copy-start.2 = (f32[3,16,128,128]{3,2,1,0:T(8,128)S(1)}, f32[3,16,128,128]{3,2,1,0:T(8,128)}, u32[]{:S(2)}) copy-start(f32[3,16,128,128]{3,2,1,0:T(8,128)} %param.6) | copy-start | bytes 9437188
  31.4 6.2 %collective-permute-start.7 = (f32[1,18,128,1]{2,3,1,0:T(1,128)S(1)}, f32[1,18,128,1]{2,3,1,0:T(1,128)}, u32[]{:S(2)}, u32[]{:S(2)}) collective-permute-start(f32[1,18,128,1]{2,3,1,0:T(1,128)S(1)} %get-tuple-element.30), channel_id=1, source_target_pairs={{1,0},{2,1},{3,2},{4,3},{5,4},{6,5},{7,6},{0,7},{9,8},{10,9},{11,1... | collective-permute-start | bytes 27656 | tf_op jit(solution)/shard_map/ppermute | solution.py:20
  37.0 0.6 copy-start.6
  42.1 4.1 %copy-start.1 = (f32[3,18,128,128]{3,2,0,1:T(8,128)}, f32[3,18,128,128]{3,2,0,1:T(8,128)S(1)}, u32[]{:S(2)}) copy-start(f32[3,18,128,128]{3,2,0,1:T(8,128)S(1)} %constant_dynamic-update-slice_fusion) | copy-start | bytes 10616836
  50.3 25.4 %collective-permute-start.2 = (f32[3,18,128,1]{2,1,3,0:T(8,128)}, f32[3,18,128,1]{2,1,3,0:T(8,128)}, u32[]{:S(2)}, u32[]{:S(2)}) collective-permute-start(f32[3,18,128,1]{2,1,3,0:T(8,128)} %copy.82), channel_id=1, source_target_pairs={{0,1},{1,2},{2,3},{3,4},{4,5},{5,6},{6,7},{7,0},{8,9},{9,10},{10,1... | collective-permute-start | bytes 82952 | tf_op jit(solution)/shard_map/ppermute | solution.py:17
  57.2 21.8 %collective-permute-start.3 = (f32[3,18,128,1]{2,1,3,0:T(8,128)}, f32[3,18,128,1]{2,1,3,0:T(8,128)}, u32[]{:S(2)}, u32[]{:S(2)}) collective-permute-start(f32[3,18,128,1]{2,1,3,0:T(8,128)} %copy.83), channel_id=1, source_target_pairs={{1,0},{2,1},{3,2},{4,3},{5,4},{6,5},{7,6},{0,7},{9,8},{10,9},{11,1... | collective-permute-start | bytes 82952 | tf_op jit(solution)/shard_map/ppermute | solution.py:20
  90.2 24.9 %copy-start.7 = (s32[256,8]{0,1:T(8,128)S(1)}, s32[256,8]{0,1:T(8,128)}, u32[]{:S(2)}) copy-start(s32[256,8]{0,1:T(8,128)} %param.10) | copy-start | bytes 24580
  110.8 6.5 %collective-permute-start.8 = (f32[3,1,128,128]{3,2,0,1:T(8,128)}, f32[3,1,128,128]{3,2,0,1:T(8,128)S(1)}, u32[]{:S(2)}, u32[]{:S(2)}) collective-permute-start(f32[3,1,128,128]{3,2,0,1:T(8,128)} %get-tuple-element.16), channel_id=1, source_target_pairs={{8,0},{16,8},{24,16},{32,24},{40,32},{48,40},{56,48},{64,56},{72,6... | collective-permute-start | bytes 589832 | tf_op jit(solution)/shard_map/ppermute | solution.py:20
  112.7 10.8 %collective-permute-start.9 = (f32[3,1,128,128]{3,2,0,1:T(8,128)}, f32[3,1,128,128]{3,2,0,1:T(8,128)S(1)}, u32[]{:S(2)}, u32[]{:S(2)}) collective-permute-start(f32[3,1,128,128]{3,2,0,1:T(8,128)} %get-tuple-element.17), channel_id=1, source_target_pairs={{0,8},{8,16},{16,24},{24,32},{32,40},{40,48},{48,56},{56,64},{64,7... | collective-permute-start | bytes 589832 | tf_op jit(solution)/shard_map/ppermute | solution.py:17
  133.8 9.2 %collective-permute-start.10 = (f32[3,18,128,1]{2,1,3,0:T(8,128)}, f32[3,18,128,1]{2,1,3,0:T(8,128)}, u32[]{:S(2)}, u32[]{:S(2)}) collective-permute-start(f32[3,18,128,1]{2,1,3,0:T(8,128)} %copy.102), channel_id=1, source_target_pairs={{0,1},{1,2},{2,3},{3,4},{4,5},{5,6},{6,7},{7,0},{8,9},{9,10},{10,1... | collective-permute-start | bytes 82952 | tf_op jit(solution)/shard_map/ppermute | solution.py:17
  140.4 6.0 %collective-permute-start.11 = (f32[3,18,128,1]{2,1,3,0:T(8,128)}, f32[3,18,128,1]{2,1,3,0:T(8,128)}, u32[]{:S(2)}, u32[]{:S(2)}) collective-permute-start(f32[3,18,128,1]{2,1,3,0:T(8,128)} %copy.103), channel_id=1, source_target_pairs={{1,0},{2,1},{3,2},{4,3},{5,4},{6,5},{7,6},{0,7},{9,8},{10,9},{11,1... | collective-permute-start | bytes 82952 | tf_op jit(solution)/shard_map/ppermute | solution.py:20
Sparse Core Ops, SparseCore 0:
  185.2 152.6 all-reduce.5
where the time goes:
time: 350 us; the launch traced here: 347 us
  waiting for transfers between devices  155 us (44%)
  local copies, waits for them, and re-layouts  73 us (21%)
  other arithmetic  66.2 us (19%)
  starting transfers between devices  32.4 us (9%)
  between operations  14.3 us (4%)
  matrix products  6.08 us (2%)
    unnamed x2, waiting for transfers between devices  149 us
    add x2, other arithmetic, advance(): return centre + transport + diffusion  37.8 us
    concatenate x3, other arithmetic, with_halo(): block = jnp.concatenate([low, block, high], axis=dim)  20.2 us
    ppermute x6, starting transfers between devices, with_halo(): lax.ppermute(lax.slice_in_dim(block, 0, width, axis=dim), axis, backward)  18.8 us
    slice x5, local copies, waits for them, and re-layouts, with_halo(): lax.slice_in_dim(block, block.shape[dim] - width, None, axis=dim)  16.4 us
    ppermute x6, starting transfers between devices, with_halo(): lax.ppermute(lax.slice_in_dim(block, block.shape[dim] - width, None, axis...  13.6 us
    slice x4, local copies, waits for them, and re-layouts, with_halo(): lax.slice_in_dim(block, 0, width, axis=dim)  11.8 us
    unnamed x23, local copies, waits for them, and re-layouts  11.7 us
  transfers between devices with their start and end apart: 13, of which 2 were waited for; matrix products, arithmetic and copies ran while one was open for 15% of the time, Pallas kernels for 0%

commit v1 on v0

v1 whole, which is shorter than its diff:
```python
import functools

import jax
import jax.numpy as jnp
from jax import lax
from jax.experimental import pallas as pl
from jax.experimental.pallas import tpu as pltpu
from jax.sharding import PartitionSpec as P

F32 = jnp.float32
BF16 = jnp.bfloat16
ANY = pl.BlockSpec(memory_space=pl.ANY)
VM = pl.BlockSpec(memory_space=pltpu.VMEM)
SM = pl.BlockSpec(memory_space=pltpu.SMEM)
VLIM = 40 * 1024 * 1024
ROWS = 32


def lanes(shape):
    return lax.broadcasted_iota(jnp.int32, shape, len(shape) - 1)


def roll(x, shift, axis):
    if isinstance(shift, int):
        shift = shift % x.shape[axis]
    return pltpu.roll(x, shift, axis)


def pack_kernel(adj, vel, visc, zl, zr, acc_l, acc_r):
    x = pl.program_id(0)
    lane = lanes((128, 128))
    pair = lane >> 1
    pair_l = ((lane + 2) & 127) >> 1
    planes = [adj[c, 0] for c in range(3)] + [visc[0]] + [vel[c, 0] for c in range(3)]
    for k, plane in enumerate(planes):
        block, m = (0, k * 16 + x) if k < 4 else (1, (k - 4) * 16 + x)
        turned = roll(plane, 2 * m, 1)
        acc_r[block] = jnp.where(pair == m, turned, acc_r[block])
        acc_l[block] = jnp.where(pair_l == m, turned, acc_l[block])

    @pl.when(x == 15)
    def _():
        for block in range(2):
            zr[block] = acc_r[block]
            zl[block] = roll(acc_l[block], 2, 1)


def pack(adj, vel, visc):
    out = jax.ShapeDtypeStruct((2, 128, 128), F32)
    whole = pl.BlockSpec((2, 128, 128), lambda x: (0, 0, 0))
    return pl.pallas_call(
        pack_kernel,
        grid=(16,),
        in_specs=[
            pl.BlockSpec((3, 1, 128, 128), lambda x: (0, x, 0, 0)),
            pl.BlockSpec((3, 1, 128, 128), lambda x: (0, x, 0, 0)),
            pl.BlockSpec((1, 128, 128), lambda x: (x, 0, 0)),
        ],
        out_specs=[whole, whole],
        out_shape=[out, out],
        scratch_shapes=[pltpu.VMEM((2, 128, 128), F32), pltpu.VMEM((2, 128, 128), F32)],
        name="pack",
    )(adj, vel, visc)


def spread(a, group):
    kept = jnp.where((lanes(a.shape) >> 5) == group, a, 0.0)
    kept = kept + roll(kept, 32, 1)
    return kept + roll(kept, 64, 1)


def shift_rows(a, by):
    row = lax.broadcasted_iota(jnp.int32, a.shape, 0)
    moved = roll(a, by, 0)
    edge = 0 if by > 0 else a.shape[0] - 1
    return jnp.where(row == edge, 0.0, moved)


def edge_centre(hl, hr):
    odd = (lanes((128, 128)) & 1) == 1
    return jnp.where(odd, hl[0], hr[0])


def edge_middle(hl, hr, zl, zr, low=None, high=None):
    lane = lanes((128, 128))
    odd = (lane & 1) == 1
    x = (lane >> 1) & 15
    centre = jnp.where(odd, hl[0], hr[0])
    minus = jnp.where(odd, roll(hl[0], 1, 1), roll(zl[0], -1, 1))
    plus = jnp.where(odd, roll(zr[0], 1, 1), roll(hr[0], -1, 1))
    velocity = jnp.where(odd, hl[1], hr[1])
    west = roll(centre, 2, 1)
    east = roll(centre, -2, 1)
    west = jnp.where(x == 0, 0.0 if low is None else roll(low, -30, 1), west)
    east = jnp.where(x == 15, 0.0 if high is None else roll(high, 30, 1), east)
    north = shift_rows(centre, -1)
    south = shift_rows(centre, 1)
    visc = spread(centre, 3)
    total = 0.0
    result = 0.0
    for d, (up, down) in enumerate(((east, west), (north, south), (plus, minus))):
        v = spread(velocity, d)
        a_up = 0.5 * ((visc + spread(up, 3)) + v)
        a_down = 0.5 * ((visc + spread(down, 3)) - v)
        total = total + (a_up + a_down)
        result = result + (a_up * up + a_down * down)
    return result + (1.0 - total) * centre


def coefficients(visc_s, vel_s, edge, coef_s, q):
    lane = lanes((ROWS, 128))
    for r in range(0, 128, ROWS):
        centre = visc_s[q, pl.ds(8 + r, ROWS), :]
        ends = roll(edge[pl.ds(r, ROWS), :], 127 - 2 * (48 + q), 1)
        up = jnp.where(lane == 127, ends, roll(centre, -1, 1))
        down = jnp.where(lane == 0, ends, roll(centre, 1, 1))
        pairs = (
            (visc_s[q + 1, pl.ds(8 + r, ROWS), :], visc_s[q - 1, pl.ds(8 + r, ROWS), :]),
            (visc_s[q, pl.ds(9 + r, ROWS), :], visc_s[q, pl.ds(7 + r, ROWS), :]),
            (up, down),
        )
        total = 0.0
        for d, (plus, minus) in enumerate(pairs):
            v = vel_s[d, q, pl.ds(r, ROWS), :]
            a_plus = 0.5 * ((centre + plus) + v)
            a_minus = 0.5 * ((centre + minus) - v)
            coef_s[2 * d, q, pl.ds(r, ROWS), :] = a_plus
            coef_s[2 * d + 1, q, pl.ds(r, ROWS), :] = a_minus
            total = total + (a_plus + a_minus)
        coef_s[6, q, pl.ds(r, ROWS), :] = 1.0 - total


def apply_step(src, edge, coef_s, q, store):
    lane = lanes((ROWS, 128))
    for r in range(0, 128, ROWS):
        a = [coef_s[k, q, pl.ds(r, ROWS), :] for k in range(7)]
        for c in range(3):
            centre = src[c, q, pl.ds(8 + r, ROWS), :]
            ends = roll(edge[pl.ds(r, ROWS), :], 127 - 2 * (c * 16 + q), 1)
            up = jnp.where(lane == 127, ends, roll(centre, -1, 1))
            down = jnp.where(lane == 0, ends, roll(centre, 1, 1))
            out = a[6] * centre
            out = out + a[0] * src[c, q + 1, pl.ds(8 + r, ROWS), :]
            out = out + a[1] * src[c, q - 1, pl.ds(8 + r, ROWS), :]
            out = out + a[2] * src[c, q, pl.ds(9 + r, ROWS), :]
            out = out + a[3] * src[c, q, pl.ds(7 + r, ROWS), :]
            out = out + a[4] * up
            out = out + a[5] * down
            store(c, r, out)


def clear_walls(ref, lead):
    for index in lead:
        ref[(*index, pl.ds(0, 8), slice(None))] = jnp.zeros((8, 128), F32)
        ref[(*index, pl.ds(136, 8), slice(None))] = jnp.zeros((8, 128), F32)


def scratch(nq):
    return [
        pltpu.VMEM((3, nq, 144, 128), F32),
        pltpu.VMEM((nq, 144, 128), F32),
        pltpu.VMEM((3, nq, 128, 128), F32),
        pltpu.VMEM((3, nq, 144, 128), F32),
        pltpu.VMEM((7, nq, 128, 128), F32),
        pltpu.VMEM((2, 128, 128), F32),
    ]


def begin(copies, sems):
    started = [pltpu.make_async_copy(s, t, sems.at[i]) for i, (s, t) in enumerate(copies)]
    for copy in started:
        copy.start()
    return started


def main_copies(adj, vel, visc, adj_s, visc_s, vel_s, x0, q0, n):
    rows = pl.ds(8, 128)
    pairs = [(adj.at[c, pl.ds(x0, n)], adj_s.at[c, pl.ds(q0, n), rows]) for c in range(3)]
    pairs += [(vel.at[c, pl.ds(x0, n)], vel_s.at[c, pl.ds(q0, n)]) for c in range(3)]
    pairs += [(visc.at[pl.ds(x0, n)], visc_s.at[pl.ds(q0, n), rows])]
    return pairs


def run_steps(adj_s, visc_s, vel_s, mid_s, coef_s, edges, mids, finals, put, after_mid=None):
    for lo, hi in mids:

        def first(q, _):
            coefficients(visc_s, vel_s, edges.at[0], coef_s, q)

            def store(c, r, v):
                mid_s[c, q, pl.ds(8 + r, ROWS), :] = v

            apply_step(adj_s, edges.at[0], coef_s, q, store)
            return 0

        lax.fori_loop(lo, hi, first, 0)
    if after_mid:
        after_mid()
    for lo, hi in finals:

        def second(q, _):
            apply_step(mid_s, edges.at[1], coef_s, q, put(q))
            return 0

        lax.fori_loop(lo, hi, second, 0)


def face_kernel(
    adj, vel, visc, hl, hr, zl, zr,
    face, centre, middle, msg_lo, msg_hi,
    adj_s, visc_s, vel_s, mid_s, coef_s, edges, sems, sems_x, sem_c,
):
    started = begin(main_copies(adj, vel, visc, adj_s, visc_s, vel_s, 0, 1, 3), sems)
    moved = []
    for msg, x, vx in ((msg_lo, 0, 0), (msg_hi, 14, 15)):
        for c in range(3):
            moved.append((adj.at[c, pl.ds(x, 2)], msg.at[pl.ds(2 * c, 2)]))
            moved.append((vel.at[c, pl.ds(vx, 1)], msg.at[pl.ds(6 + c, 1)]))
        moved.append((visc.at[pl.ds(x, 2)], msg.at[pl.ds(9, 2)]))
    moved = begin(moved, sems_x)
    cen = edge_centre(hl, hr)
    centre[0] = cen
    corners = begin([(centre, msg_lo.at[pl.ds(11, 1)]), (centre, msg_hi.at[pl.ds(11, 1)])], sem_c)
    mid = edge_middle(hl, hr, zl, zr)
    middle[...] = mid
    edges[0] = roll(cen, 2, 1)
    edges[1] = roll(mid, 2, 1)
    for c in range(3):
        adj_s[c, 0] = jnp.zeros((144, 128), F32)
        mid_s[c, 0] = jnp.zeros((144, 128), F32)
    visc_s[0] = jnp.zeros((144, 128), F32)
    clear_walls(adj_s, [(c, q) for c in range(3) for q in range(1, 4)])
    clear_walls(mid_s, [(c, q) for c in range(3) for q in range(1, 3)])
    clear_walls(visc_s, [(q,) for q in range(1, 4)])
    for copy in started:
        copy.wait()

    def put(q):
        def store(c, r, v):
            face[c, pl.ds(r, ROWS), :] = v

        return store

    run_steps(adj_s, visc_s, vel_s, mid_s, coef_s, edges, [(1, 3)], [(1, 2)], put)
    for copy in corners + moved:
        copy.wait()


def face_call(adj, vel, visc, hl, hr, zl, zr):
    msg = jax.ShapeDtypeStruct((12, 128, 128), F32)
    return pl.pallas_call(
        face_kernel,
        in_specs=[ANY, ANY, ANY, VM, VM, VM, VM],
        out_specs=[VM, VM, VM, ANY, ANY],
        out_shape=[
            jax.ShapeDtypeStruct((3, 128, 128), F32),
            jax.ShapeDtypeStruct((1, 128, 128), F32),
            jax.ShapeDtypeStruct((128, 128), F32),
            msg,
            msg,
        ],
        scratch_shapes=scratch(4)
        + [
            pltpu.SemaphoreType.DMA((7,)),
            pltpu.SemaphoreType.DMA((14,)),
            pltpu.SemaphoreType.DMA((2,)),
        ],
        compiler_params=pltpu.CompilerParams(vmem_limit_bytes=VLIM),
        name="face",
    )(adj, vel, visc, hl, hr, zl, zr)


def inner_kernel(
    x0, nq, first, adj, vel, visc, centre, middle, *rest
):
    if not first:
        rest = rest[1:]
    out, adj_s, visc_s, vel_s, mid_s, coef_s, edges, out_s, sems, sems_o = rest
    started = begin(main_copies(adj, vel, visc, adj_s, visc_s, vel_s, x0, 0, nq), sems)
    edges[0] = roll(centre[0], -2 * x0, 1)
    edges[1] = roll(middle[...], -2 * x0, 1)
    clear_walls(adj_s, [(c, q) for c in range(3) for q in range(nq)])
    clear_walls(mid_s, [(c, q) for c in range(3) for q in range(nq)])
    clear_walls(visc_s, [(q,) for q in range(nq)])
    for copy in started:
        copy.wait()

    def put(q):
        def store(c, r, v):
            out_s[c, q, pl.ds(r, ROWS), :] = v

        return store

    run_steps(adj_s, visc_s, vel_s, mid_s, coef_s, edges, [(1, nq - 1)], [(2, nq - 2)], put)
    n = nq - 4
    for copy in begin(
        [(out_s.at[c, pl.ds(2, n)], out.at[c, pl.ds(x0 + 2, n)]) for c in range(3)], sems_o
    ):
        copy.wait()


def inner(x0, nq, adj, vel, visc, centre, middle, out=None):
    first = out is None
    args = [adj, vel, visc, centre, middle] + ([] if first else [out])
    return pl.pallas_call(
        functools.partial(inner_kernel, x0, nq, first),
        in_specs=[ANY, ANY, ANY, VM, VM] + ([] if first else [ANY]),
        out_specs=ANY,
        out_shape=jax.ShapeDtypeStruct((3, 16, 128, 128), F32),
        scratch_shapes=scratch(nq)
        + [
            pltpu.VMEM((3, nq, 128, 128), F32),
            pltpu.SemaphoreType.DMA((7,)),
            pltpu.SemaphoreType.DMA((3,)),
        ],
        input_output_aliases={} if first else {5: 0},
        compiler_params=pltpu.CompilerParams(vmem_limit_bytes=VLIM),
        name="inner",
    )(*args)


def outer_kernel(
    place, adj, vel, visc, hl, hr, zl, zr, low, high, _,
    out, adj_s, visc_s, vel_s, mid_s, coef_s, edges, out_s, corner, sems, sems_o, sems_c,
):
    rows = pl.ds(8, 128)
    corners = begin([(low.at[pl.ds(11, 1)], corner.at[pl.ds(0, 1)]), (high.at[pl.ds(11, 1)], corner.at[pl.ds(1, 1)])], sems_c)
    pairs = main_copies(adj, vel, visc, adj_s, visc_s, vel_s, 0, 2, 4)
    pairs += main_copies(adj, vel, visc, adj_s, visc_s, vel_s, 12, 6, 4)
    for msg, q, qv in ((low, 0, 1), (high, 10, 10)):
        for c in range(3):
            pairs.append((msg.at[pl.ds(2 * c, 2)], adj_s.at[c, pl.ds(q, 2), rows]))
            pairs.append((msg.at[pl.ds(6 + c, 1)], vel_s.at[c, pl.ds(qv, 1)]))
        pairs.append((msg.at[pl.ds(9, 2)], visc_s.at[pl.ds(q, 2), rows]))
    started = begin(pairs, sems)
    clear_walls(adj_s, [(c, q) for c in range(3) for q in range(12)])
    clear_walls(mid_s, [(c, q) for c in range(3) for q in range(12)])
    clear_walls(visc_s, [(q,) for q in range(12)])
    for copy in corners:
        copy.wait()
    x = (lanes((128, 128)) >> 1) & 15
    cen = edge_centre(hl, hr)
    mid = edge_middle(hl, hr, zl, zr, corner[0], corner[1])
    turned = jnp.where(x < 6, roll(cen, 4, 1), roll(cen, -12, 1))
    turned = jnp.where(x == 1, roll(corner[0], -28, 1), turned)
    edges[0] = jnp.where(x == 10, roll(corner[1], 20, 1), turned)
    edges[1] = jnp.where(x < 6, roll(mid, 4, 1), roll(mid, -12, 1))
    for copy in started:
        copy.wait()

    def walls():
        @pl.when(place[0] == 0)
        def _():
            for c in range(3):
                mid_s[c, 1] = jnp.zeros((144, 128), F32)

        @pl.when(place[0] == place[1] - 1)
        def _():
            for c in range(3):
                mid_s[c, 10] = jnp.zeros((144, 128), F32)

    def put(q):
        def store(c, r, v):
            out_s[c, q, pl.ds(r, ROWS), :] = v

        return store

    run_steps(
        adj_s, visc_s, vel_s, mid_s, coef_s, edges, [(1, 5), (7, 11)], [(2, 4), (8, 10)], put, walls
    )
    pairs = [(out_s.at[c, pl.ds(2, 2)], out.at[c, pl.ds(0, 2)]) for c in range(3)]
    pairs += [(out_s.at[c, pl.ds(8, 2)], out.at[c, pl.ds(14, 2)]) for c in range(3)]
    for copy in begin(pairs, sems_o):
        copy.wait()


def outer(place, adj, vel, visc, hl, hr, zl, zr, low, high, out):
    return pl.pallas_call(
        outer_kernel,
        in_specs=[SM, ANY, ANY, ANY, VM, VM, VM, VM, ANY, ANY, ANY],
        out_specs=ANY,
        out_shape=jax.ShapeDtypeStruct((3, 16, 128, 128), F32),
        scratch_shapes=scratch(12)
        + [
            pltpu.VMEM((3, 12, 128, 128), F32),
            pltpu.VMEM((2, 128, 128), F32),
            pltpu.SemaphoreType.DMA((28,)),
            pltpu.SemaphoreType.DMA((6,)),
            pltpu.SemaphoreType.DMA((2,)),
        ],
        input_output_aliases={10: 0},
        compiler_params=pltpu.CompilerParams(vmem_limit_bytes=VLIM),
        name="outer",
    )(place, adj, vel, visc, hl, hr, zl, zr, low, high, out)


def pieces(a):
    high = a.astype(BF16)
    rest = a - high.astype(F32)
    mid = rest.astype(BF16)
    low = (rest - mid.astype(F32)).astype(BF16)
    return high, mid, low


def sums_kernel(select, face, out):
    chosen = select[...].astype(BF16)
    for c in range(3):
        total = 0.0
        for piece in pieces(face[c]):
            total = total + jnp.dot(chosen, piece, preferred_element_type=F32)
        for g in range(8):
            out[g, c] = total[g * 16 : g * 16 + 16]


def partial_sums(select, face):
    return pl.pallas_call(
        sums_kernel,
        in_specs=[VM, VM],
        out_specs=VM,
        out_shape=jax.ShapeDtypeStruct((8, 3, 16, 128), F32),
        name="sums",
    )(select, face)


def product_kernel(parts, filters, out, sums):
    total = parts[0]
    for g in range(1, 8):
        total = total + parts[g]
    sums[...] = total
    for p in range(4):
        view = jnp.concatenate([sums[:, p * 4 + i, :] for i in range(4)], axis=1)
        stacked = jnp.concatenate(pieces(view), axis=0)
        wide = jnp.dot(stacked, filters[p], preferred_element_type=F32)
        out[p] = wide[0:3] + (wide[3:6] + wide[6:9])


def product(parts, filters):
    return pl.pallas_call(
        product_kernel,
        in_specs=[VM, VM],
        out_specs=VM,
        out_shape=jax.ShapeDtypeStruct((4, 3, 512), F32),
        scratch_shapes=[pltpu.VMEM((3, 16, 128), F32)],
        compiler_params=pltpu.CompilerParams(vmem_limit_bytes=VLIM),
        name="product",
    )(parts, filters)


def shards(adjoint, velocity, viscosity, filters, block_tiles, tile_place):
    gx = lax.axis_index("gx")
    gz = lax.axis_index("gz")
    nx = lax.axis_size("gx")
    nz = lax.axis_size("gz")
    ring = [(i, (i + 1) % nz) for i in range(nz)]
    back = [(b, a) for a, b in ring]
    along = [(i, i + 1) for i in range(nx - 1)]
    against = [(b, a) for a, b in along]

    lists = lax.dynamic_slice_in_dim(block_tiles, gz * 32, 32, 0)
    tiles = jnp.arange(512, dtype=jnp.int32)
    places = jnp.sum(jnp.where(lists[:, :, None] == tiles, tile_place, 0), axis=2)
    wanted = gx * 32 + jnp.arange(32, dtype=jnp.int32)
    chosen = jnp.sum((places[None] == wanted[:, None, None]).astype(F32), axis=2)
    select = (chosen[:, None, :, None] * jnp.eye(4, dtype=F32)[None, :, None, :]).reshape(128, 128)

    zl, zr = pack(adjoint, velocity, viscosity)
    hl = lax.ppermute(zl, "gz", ring)
    hr = lax.ppermute(zr, "gz", back)
    face, centre, middle, msg_lo, msg_hi = face_call(
        adjoint, velocity, viscosity, hl, hr, zl, zr
    )
    face = jnp.where(gx == 0, face, 0.0)
    got = [lax.ppermute(face, "gx", [(0, k)]) for k in (8, 2, 6)]
    low = lax.ppermute(msg_hi, "gx", along)
    high = lax.ppermute(msg_lo, "gx", against)
    out = inner(0, 10, adjoint, velocity, viscosity, centre, middle)
    face = face + ((got[0] + got[1]) + got[2])
    face = face + lax.ppermute(face, "gx", [(0, 4), (2, 10), (6, 14), (8, 12)])
    out = inner(6, 10, adjoint, velocity, viscosity, centre, middle, out)
    face = face + lax.ppermute(face, "gx", [(i, i + 1) for i in range(0, nx, 2)])
    parts = lax.all_to_all(partial_sums(select, face), "gz", 0, 0)
    gradient = product(parts, filters)
    place = jnp.stack([gx, jnp.int32(nx)]).astype(jnp.int32)
    out = outer(place, adjoint, velocity, viscosity, hl, hr, zl, zr, low, high, out)
    return out, gradient


def solution(mesh):
    placed = (
        P(None, "gx", None, "gz"),
        P(None, "gx", None, "gz"),
        P("gx", None, "gz"),
        P(("gx", "gz"), None, None),
        P(),
        P(),
    )
    return jax.shard_map(
        shards,
        mesh=mesh,
        in_specs=placed,
        out_specs=(P(None, "gx", None, "gz"), P(("gx", "gz"), None, None)),
        check_vma=False,
    )
```

time: 350 us -> 113 us (0.32)
  waiting for transfers between devices: 155 us -> 18 us
  other arithmetic: 66.2 us -> 6.05 us
  local copies, waits for them, and re-layouts: 73 us -> 23.9 us
  Pallas kernels: 0 us -> 37.8 us
  between operations: 14.3 us -> 0.85 us
  starting transfers between devices: 32.4 us -> 24.8 us
  matrix products: 6.08 us -> 0 us
    unnamed x2 -> x0, waiting for transfers between devices: 149 us -> none
    pallas_call x0 -> x7, Pallas kernels: none -> 37.8 us  [the longest x2 11.7 us: inner(): pl.pallas_call(functools.partial(inner_kernel, x0, nq, first), in_specs=[...]
    add x2 -> x4, other arithmetic: 37.8 us -> 2.83 us  [the longest x1 1.63 us: shards(): face + lax.ppermute(face, 'gx', [(i, i + 1) for i in range(0, nx, 2)])]
    slice x9 -> x0, local copies, waits for them, and re-layouts: 28.2 us -> none  [the longest x5 16.4 us: with_halo(): lax.slice_in_dim(block, block.shape[dim] - width, None, axis=dim)]
    concatenate x3 -> x0, other arithmetic: 20.2 us -> none  [with_halo(): block = jnp.concatenate([low, block, high], axis=dim)]
    mul x9 -> x1, local copies, waits for them, and re-layouts: 18.2 us -> 3.83 us  [shards(): chosen[:, None, :, None] * jnp.eye(4, dtype=F32)[None, :, None, :]]
    ppermute x12 -> x9, starting transfers between devices: 32.4 us -> 18.5 us  [the longest x1 7.26 us: shards(): high = lax.ppermute(msg_lo, 'gx', against)]
    ppermute x4 -> x0, local copies, waits for them, and re-layouts: 13.1 us -> none  [the longest x2 6.63 us: with_halo(): lax.ppermute(lax.slice_in_dim(block, block.shape[dim] - width, None, axis...]
  transfers between devices with their start and end apart: 13 -> 10, of which waited for: 2 -> 4; matrix products, arithmetic and copies ran while one was open for 15% -> 10% of each run, Pallas kernels for 0% -> 13%
where the time goes in v1:
time: 113 us; the launch traced here: 111 us
  Pallas kernels  37.8 us (33%)
  starting transfers between devices  24.8 us (22%)
  local copies, waits for them, and re-layouts  23.9 us (21%)
  waiting for transfers between devices  18 us (16%)
  other arithmetic  6.05 us (5%)
    unnamed x51, local copies, waits for them, and re-layouts  19.2 us
    pallas_call x2, Pallas kernels, inner(): pl.pallas_call(functools.partial(inner_kernel, x0, nq, first), in_specs=[...  11.7 us
    pallas_call x1, Pallas kernels, pack(): pl.pallas_call(pack_kernel, grid=(16,), in_specs=[pl.BlockSpec((3, 1, 128...  11.3 us
    ppermute x3, waiting for transfers between devices, shards(): got = [lax.ppermute(face, 'gx', [(0, k)]) for k in (8, 2, 6)]  8.25 us
    ppermute x1, starting transfers between devices, shards(): high = lax.ppermute(msg_lo, 'gx', against)  7.26 us
    pallas_call x1, Pallas kernels, outer(): pl.pallas_call(outer_kernel, in_specs=[SM, ANY, ANY, ANY, VM, VM, VM, VM,...  7.22 us
    all_to_all x1, starting transfers between devices, shards(): parts = lax.all_to_all(partial_sums(select, face), 'gz', 0, 0)  6.32 us
    pallas_call x1, Pallas kernels, face_call(): pl.pallas_call(face_kernel, in_specs=[ANY, ANY, ANY, VM, VM, VM, VM], out...  5.26 us
  transfers between devices with their start and end apart: 10, of which 4 were waited for; matrix products, arithmetic and copies ran while one was open for 10% of the time, Pallas kernels for 13%

profile of v1, /device:TPU:24, one launch (start us, length us, event | category | flops | bytes accessed | tf_op | source)
XLA Modules:
  0.0 111.4 jit_solution(17464551810025007849)
XLA Ops:
  0.7 11.3 %pack.1 = (f32[2,128,128]{2,1,0:T(8,128)}, f32[2,128,128]{2,1,0:T(8,128)}) custom-call(f32[3,16,128,128]{3,2,1,0:T(8,128)} %adj.9, f32[3,16,128,128]{3,2,1,0:T(8,128)} %vel.9, f32[16,128,128]{2,1,0:T(8,128)} %visc.9), custom_call_target="tpu_custom_call" | custom-call | tf_op jit(solution)/shard_map/pack/pallas_call | solution.py:51
  11.9 2.1 %collective-permute-start = (f32[2,128,128]{2,1,0:T(8,128)}, f32[2,128,128]{2,1,0:T(8,128)S(1)}, u32[]{:S(2)}, u32[]{:S(2)}) collective-permute-start(f32[2,128,128]{2,1,0:T(8,128)} %get-tuple-element.9.zl), channel_id=1, source_target_pairs={{0,1},{1,2},{2,3},{3,4},{4,5},{5,6},{6,7},{7,0},{8,9},{9,10},{10,1... | collective-permute-start | bytes 393224 | tf_op jit(solution)/shard_map/ppermute | solution.py:467
  14.8 3.5 %collective-permute-done.hl = f32[2,128,128]{2,1,0:T(8,128)S(1)} collective-permute-done((f32[2,128,128]{2,1,0:T(8,128)}, f32[2,128,128]{2,1,0:T(8,128)S(1)}, u32[]{:S(2)}, u32[]{:S(2)}) %collective-permute-start) | collective-permute-done | bytes 131104 | tf_op jit(solution)/shard_map/ppermute | solution.py:467
  18.3 3.3 %collective-permute-done.1.hr = f32[2,128,128]{2,1,0:T(8,128)S(1)} collective-permute-done((f32[2,128,128]{2,1,0:T(8,128)}, f32[2,128,128]{2,1,0:T(8,128)S(1)}, u32[]{:S(2)}, u32[]{:S(2)}) %collective-permute-start.1) | collective-permute-done | bytes 131104 | tf_op jit(solution)/shard_map/ppermute | solution.py:468
  22.2 1.9 %copy-done.2 = f32[3,16,128,128]{3,2,1,0:T(8,128)S(1)} copy-done((f32[3,16,128,128]{3,2,1,0:T(8,128)S(1)}, f32[3,16,128,128]{3,2,1,0:T(8,128)}, u32[]{:S(2)}) %copy-start.2) | copy-done | bytes 3145752
  28.0 5.3 %face.1 = (f32[3,128,128]{2,1,0:T(8,128)S(1)}, f32[1,128,128]{2,1,0:T(8,128)S(1)}, f32[128,128]{1,0:T(8,128)S(1)}, f32[12,128,128]{2,1,0:T(8,128)S(1)}, f32[12,128,128]{2,1,0:T(8,128)S(1)}) custom-call(f32[3,16,128,128]{3,2,1,0:T(8,128)S(1)} %copy-done.1, f32[3,16,128,128]{3,2,1,0:T(8,128)S(1)} %copy-done.2, f32[16,128,128]{2,1,0:T(8,128)S(1)} %copy-done.5, ...), custom_call_target="tpu_custom_call" | custom-call | tf_op jit(solution)/shard_map/face/pallas_call | solution.py:251
  35.6 1.3 %collective-permute-start.6 = (f32[3,128,128]{2,1,0:T(8,128)}, f32[3,128,128]{2,1,0:T(8,128)}, u32[]{:S(2)}, u32[]{:S(2)}) collective-permute-start(f32[3,128,128]{2,1,0:T(8,128)} %broadcast_select_fusion), channel_id=1, source_target_pairs={{0,48},{1,49},{2,50},{3,51},{4,52},{5,53},{6,54},{7,55}} | collective-permute-start | bytes 589832 | tf_op jit(solution)/shard_map/ppermute | solution.py:473
  36.9 1.3 %collective-permute-start.5 = (f32[3,128,128]{2,1,0:T(8,128)}, f32[3,128,128]{2,1,0:T(8,128)}, u32[]{:S(2)}, u32[]{:S(2)}) collective-permute-start(f32[3,128,128]{2,1,0:T(8,128)} %broadcast_select_fusion), channel_id=1, source_target_pairs={{0,16},{1,17},{2,18},{3,19},{4,20},{5,21},{6,22},{7,23}} | collective-permute-start | bytes 589832 | tf_op jit(solution)/shard_map/ppermute | solution.py:473
  40.3 1.9 %collective-permute-start.2 = (f32[12,128,128]{2,1,0:T(8,128)}, f32[12,128,128]{2,1,0:T(8,128)}, u32[]{:S(2)}, u32[]{:S(2)}) collective-permute-start(f32[12,128,128]{2,1,0:T(8,128)} %copy-done.22), channel_id=1, source_target_pairs={{0,8},{8,16},{16,24},{24,32},{32,40},{40,48},{48,56},{56,64},{64,7... | collective-permute-start | bytes 2359304 | tf_op jit(solution)/shard_map/ppermute | solution.py:474
  42.2 7.3 %collective-permute-start.3 = (f32[12,128,128]{2,1,0:T(8,128)}, f32[12,128,128]{2,1,0:T(8,128)}, u32[]{:S(2)}, u32[]{:S(2)}) collective-permute-start(f32[12,128,128]{2,1,0:T(8,128)} %copy-done.21), channel_id=1, source_target_pairs={{8,0},{16,8},{24,16},{32,24},{40,32},{48,40},{56,48},{64,56},{72,6... | collective-permute-start | bytes 2359304 | tf_op jit(solution)/shard_map/ppermute | solution.py:475
  49.5 8.2 %collective-permute-done.4 = f32[3,128,128]{2,1,0:T(8,128)} collective-permute-done((f32[3,128,128]{2,1,0:T(8,128)}, f32[3,128,128]{2,1,0:T(8,128)}, u32[]{:S(2)}, u32[]{:S(2)}) %collective-permute-start.4) | collective-permute-done | bytes 196640 | tf_op jit(solution)/shard_map/ppermute | solution.py:473
  60.4 3.0 %collective-permute-done.7 = f32[3,128,128]{2,1,0:T(8,128)S(1)} collective-permute-done((f32[3,128,128]{2,1,0:T(8,128)S(1)}, f32[3,128,128]{2,1,0:T(8,128)S(1)}, u32[]{:S(2)}, u32[]{:S(2)}) %collective-permute-start.7) | collective-permute-done | bytes 196640 | tf_op jit(solution)/shard_map/ppermute | solution.py:478
  63.4 2.0 %collective-permute-start.8 = (f32[3,128,128]{2,1,0:T(8,128)S(1)}, f32[3,128,128]{2,1,0:T(8,128)}, u32[]{:S(2)}, u32[]{:S(2)}) collective-permute-start(f32[3,128,128]{2,1,0:T(8,128)S(1)} %add.34), channel_id=1, source_target_pairs={{0,8},{16,24},{32,40},{48,56},{64,72},{80,88},{96,104},{112,120},{... | collective-permute-start | bytes 589832 | tf_op jit(solution)/shard_map/ppermute | solution.py:480
  65.4 1.6 %broadcast_multiply_fusion = f32[32,4,32,4]{3,2,1,0:T(8,128)} fusion(f32[4,4]{1,0:T(4,128)S(1)} %fusion, f32[32,32]{1,0:T(8,128)S(1)} %convert_reduce_fusion), kind=kLoop, calls=%fused_computation | loop fusion | flops 16384 | bytes 69696 | tf_op jit(solution)/shard_map/mul | solution.py:464
  67.1 3.8 %mul.28.select = f32[128,128]{1,0:T(8,128)} reshape(f32[32,4,32,4]{3,2,1,0:T(8,128)} %broadcast_multiply_fusion) | data formatting | bytes 131072 | tf_op jit(solution)/shard_map/mul | solution.py:464
  70.9 1.6 %add.35.face = f32[3,128,128]{2,1,0:T(8,128)} add(f32[3,128,128]{2,1,0:T(8,128)S(1)} %add.34, f32[3,128,128]{2,1,0:T(8,128)} %collective-permute-done.8) | non-fusion elementwise | flops 49152 | bytes 589824 | tf_op jit(solution)/shard_map/add | solution.py:480
  72.5 1.9 %sums.1 = f32[8,3,16,128]{3,2,1,0:T(8,128)} custom-call(f32[128,128]{1,0:T(8,128)} %mul.28.select, f32[3,128,128]{2,1,0:T(8,128)} %add.35.face), custom_call_target="tpu_custom_call" | custom-call | tf_op jit(solution)/shard_map/sums/pallas_call | solution.py:416
  74.4 6.3 %all-to-all-start = ((f32[8,3,16,128]{3,2,1,0:T(8,128)}), f32[8,3,16,128]{3,2,1,0:T(8,128)S(1)}, u32[]{:S(2)}, u32[]{:S(2)}) async-start(f32[8,3,16,128]{3,2,1,0:T(8,128)} %sums.1), calls=%async_computation | async-start | bytes 393216 | tf_op jit(solution)/shard_map/all_to_all | solution.py:481
  80.8 1.9 %copy-done.3 = f32[3,16,128,128]{3,2,1,0:T(8,128)S(1)} copy-done((f32[3,16,128,128]{3,2,1,0:T(8,128)S(1)}, f32[3,16,128,128]{3,2,1,0:T(8,128)}, u32[]{:S(2)}) %copy-start.3) | copy-done | bytes 3145752
  83.9 5.8 %inner.2.rest_0_ = f32[3,16,128,128]{3,2,1,0:T(8,128)} custom-call(f32[3,16,128,128]{3,2,1,0:T(8,128)S(1)} %copy-done.1, f32[3,16,128,128]{3,2,1,0:T(8,128)S(1)} %copy-done.3, f32[16,128,128]{2,1,0:T(8,128)S(1)} %copy-done.6, f32[1,128,128]{2,1,0:T(8,128)S(1)} %get-tuple-element.13.centre, f32[128,128]{1,0:T(8,128)S(1)} %copy-done.19), custom_call_target="tpu_custom_call" | custom-call | tf_op jit(solution)/shard_map/inner/pallas_call | solution.py:305
  89.8 5.9 %inner.3._ = f32[3,16,128,128]{3,2,1,0:T(8,128)} custom-call(f32[3,16,128,128]{3,2,1,0:T(8,128)S(1)} %copy-done.1, f32[3,16,128,128]{3,2,1,0:T(8,128)S(1)} %copy-done.3, f32[16,128,128]{2,1,0:T(8,128)S(1)} %copy-done.6, f32[1,128,128]{2,1,0:T(8,128)S(1)} %get-tuple-element.13.centre, f32[128,128]{1,0:T(8,128)S(1)} %copy-done.20, ...), custom_call_target="tpu_custom_call", output_to_operand_aliasing={{}: (5, {})} | custom-call | tf_op jit(solution)/shard_map/inner/pallas_call | solution.py:305
  95.7 1.6 %copy-done.8 = bf16[4,512,512]{2,1,0:T(8,128)(2,1)S(1)} copy-done((bf16[4,512,512]{2,1,0:T(8,128)(2,1)S(1)}, bf16[4,512,512]{2,1,0:T(8,128)(2,1)}, u32[]{:S(2)}) %copy-start.8) | copy-done | bytes 2097176
  98.3 1.9 %copy-done.4 = f32[3,16,128,128]{3,2,1,0:T(8,128)S(1)} copy-done((f32[3,16,128,128]{3,2,1,0:T(8,128)S(1)}, f32[3,16,128,128]{3,2,1,0:T(8,128)}, u32[]{:S(2)}) %copy-start.4) | copy-done | bytes 3145752
  104.1 7.2 %outer.1 = f32[3,16,128,128]{3,2,1,0:T(8,128)} custom-call(s32[2]{0:T(128)S(1)} %pad_add_fusion.place, f32[3,16,128,128]{3,2,1,0:T(8,128)S(1)} %copy-done.1, f32[3,16,128,128]{3,2,1,0:T(8,128)S(1)} %copy-done.4, f32[16,128,128]{2,1,0:T(8,128)S(1)} %copy-done.7, f32[2,128,128]{2,1,0:T(8,128)S(1)} %copy-done.14, ...), custom_call_target="tpu_custom_call", output_to_operand_aliasing={{}: (10, {})} | custom-call | tf_op jit(solution)/shard_map/outer/pallas_call | solution.py:378
  (68 shorter events, 18.6 us)
Async XLA Ops:
  0.6 13.4 %copy-start = (s32[256,8]{0,1:T(8,128)S(1)}, s32[256,8]{0,1:T(8,128)}, u32[]{:S(2)}) copy-start(s32[256,8]{0,1:T(8,128)} %param.10) | copy-start | bytes 24580
  0.6 21.6 %copy-start.1 = (f32[3,16,128,128]{3,2,1,0:T(8,128)S(1)}, f32[3,16,128,128]{3,2,1,0:T(8,128)}, u32[]{:S(2)}) copy-start(f32[3,16,128,128]{3,2,1,0:T(8,128)} %adj.9) | copy-start | bytes 9437188
  11.9 6.3 %collective-permute-start = (f32[2,128,128]{2,1,0:T(8,128)}, f32[2,128,128]{2,1,0:T(8,128)S(1)}, u32[]{:S(2)}, u32[]{:S(2)}) collective-permute-start(f32[2,128,128]{2,1,0:T(8,128)} %get-tuple-element.9.zl), channel_id=1, source_target_pairs={{0,1},{1,2},{2,3},{3,4},{4,5},{5,6},{6,7},{7,0},{8,9},{9,10},{10,1... | collective-permute-start | bytes 393224 | tf_op jit(solution)/shard_map/ppermute | solution.py:467
  14.0 7.5 %collective-permute-start.1 = (f32[2,128,128]{2,1,0:T(8,128)}, f32[2,128,128]{2,1,0:T(8,128)S(1)}, u32[]{:S(2)}, u32[]{:S(2)}) collective-permute-start(f32[2,128,128]{2,1,0:T(8,128)} %get-tuple-element.10.zr), channel_id=1, source_target_pairs={{1,0},{2,1},{3,2},{4,3},{5,4},{6,5},{7,6},{0,7},{9,8},{10,9},{11,1... | collective-permute-start | bytes 393224 | tf_op jit(solution)/shard_map/ppermute | solution.py:468
  14.1 25.4 %copy-start.24 = (s32[512]{0:T(512)S(1)}, s32[512]{0:T(512)}, u32[]{:S(2)}) copy-start(s32[512]{0:T(512)} %param.11) | copy-start | bytes 6148
  18.3 15.1 %copy-start.13 = (f32[2,128,128]{2,1,0:T(8,128)}, f32[2,128,128]{2,1,0:T(8,128)S(1)}, u32[]{:S(2)}) copy-start(f32[2,128,128]{2,1,0:T(8,128)S(1)} %collective-permute-done.hl) | copy-start | bytes 393220
  22.2 1.9 %copy-start.2 = (f32[3,16,128,128]{3,2,1,0:T(8,128)S(1)}, f32[3,16,128,128]{3,2,1,0:T(8,128)}, u32[]{:S(2)}) copy-start(f32[3,16,128,128]{3,2,1,0:T(8,128)} %vel.9) | copy-start | bytes 9437188
  24.1 1.2 %copy-start.5 = (f32[16,128,128]{2,1,0:T(8,128)S(1)}, f32[16,128,128]{2,1,0:T(8,128)}, u32[]{:S(2)}) copy-start(f32[16,128,128]{2,1,0:T(8,128)} %visc.9) | copy-start | bytes 3145732
  28.0 11.5 %copy-start.23 = (s32[32,8]{1,0:T(8,128)S(1)}, s32[32,8]{1,0:T(8,128)}, u32[]{:S(2)}) copy-start(s32[32,8]{1,0:T(8,128)} %copy.14) | copy-start | bytes 3076
  34.0 1.6 %copy-start.22 = (f32[12,128,128]{2,1,0:T(8,128)}, f32[12,128,128]{2,1,0:T(8,128)S(1)}, u32[]{:S(2)}) copy-start(f32[12,128,128]{2,1,0:T(8,128)S(1)} %get-tuple-element.11) | copy-start | bytes 2359300
  35.6 13.9 %collective-permute-start.6 = (f32[3,128,128]{2,1,0:T(8,128)}, f32[3,128,128]{2,1,0:T(8,128)}, u32[]{:S(2)}, u32[]{:S(2)}) collective-permute-start(f32[3,128,128]{2,1,0:T(8,128)} %broadcast_select_fusion), channel_id=1, source_target_pairs={{0,48},{1,49},{2,50},{3,51},{4,52},{5,53},{6,54},{7,55}} | collective-permute-start | bytes 589832 | tf_op jit(solution)/shard_map/ppermute | solution.py:473
  36.9 12.6 %collective-permute-start.5 = (f32[3,128,128]{2,1,0:T(8,128)}, f32[3,128,128]{2,1,0:T(8,128)}, u32[]{:S(2)}, u32[]{:S(2)}) collective-permute-start(f32[3,128,128]{2,1,0:T(8,128)} %broadcast_select_fusion), channel_id=1, source_target_pairs={{0,16},{1,17},{2,18},{3,19},{4,20},{5,21},{6,22},{7,23}} | collective-permute-start | bytes 589832 | tf_op jit(solution)/shard_map/ppermute | solution.py:473
  38.2 19.5 %collective-permute-start.4 = (f32[3,128,128]{2,1,0:T(8,128)}, f32[3,128,128]{2,1,0:T(8,128)}, u32[]{:S(2)}, u32[]{:S(2)}) collective-permute-start(f32[3,128,128]{2,1,0:T(8,128)} %broadcast_select_fusion), channel_id=1, source_target_pairs={{0,64},{1,65},{2,66},{3,67},{4,68},{5,69},{6,70},{7,71}} | collective-permute-start | bytes 589832 | tf_op jit(solution)/shard_map/ppermute | solution.py:473
  40.3 58.0 %collective-permute-start.2 = (f32[12,128,128]{2,1,0:T(8,128)}, f32[12,128,128]{2,1,0:T(8,128)}, u32[]{:S(2)}, u32[]{:S(2)}) collective-permute-start(f32[12,128,128]{2,1,0:T(8,128)} %copy-done.22), channel_id=1, source_target_pairs={{0,8},{8,16},{16,24},{24,32},{32,40},{40,48},{48,56},{56,64},{64,7... | collective-permute-start | bytes 2359304 | tf_op jit(solution)/shard_map/ppermute | solution.py:474
  42.2 56.1 %collective-permute-start.3 = (f32[12,128,128]{2,1,0:T(8,128)}, f32[12,128,128]{2,1,0:T(8,128)}, u32[]{:S(2)}, u32[]{:S(2)}) collective-permute-start(f32[12,128,128]{2,1,0:T(8,128)} %copy-done.21), channel_id=1, source_target_pairs={{8,0},{16,8},{24,16},{32,24},{40,32},{48,40},{56,48},{64,56},{72,6... | collective-permute-start | bytes 2359304 | tf_op jit(solution)/shard_map/ppermute | solution.py:475
  58.9 4.5 %collective-permute-start.7 = (f32[3,128,128]{2,1,0:T(8,128)S(1)}, f32[3,128,128]{2,1,0:T(8,128)S(1)}, u32[]{:S(2)}, u32[]{:S(2)}) collective-permute-start(f32[3,128,128]{2,1,0:T(8,128)S(1)} %add_add_fusion), channel_id=1, source_target_pairs={{0,32},{16,80},{48,112},{64,96},{1,33},{17,81},{49,113},{65,97},{2... | collective-permute-start | bytes 589832 | tf_op jit(solution)/shard_map/ppermute | solution.py:478
  60.4 20.4 %copy-start.19 = (f32[128,128]{1,0:T(8,128)S(1)}, f32[128,128]{1,0:T(8,128)}, u32[]{:S(2)}) copy-start(f32[128,128]{1,0:T(8,128)} %copy-done.18) | copy-start | bytes 196612
  63.4 7.5 %collective-permute-start.8 = (f32[3,128,128]{2,1,0:T(8,128)S(1)}, f32[3,128,128]{2,1,0:T(8,128)}, u32[]{:S(2)}, u32[]{:S(2)}) collective-permute-start(f32[3,128,128]{2,1,0:T(8,128)S(1)} %add.34), channel_id=1, source_target_pairs={{0,8},{16,24},{32,40},{48,56},{64,72},{80,88},{96,104},{112,120},{... | collective-permute-start | bytes 589832 | tf_op jit(solution)/shard_map/ppermute | solution.py:480
  74.4 21.3 %all-to-all-start = ((f32[8,3,16,128]{3,2,1,0:T(8,128)}), f32[8,3,16,128]{3,2,1,0:T(8,128)S(1)}, u32[]{:S(2)}, u32[]{:S(2)}) async-start(f32[8,3,16,128]{3,2,1,0:T(8,128)} %sums.1), calls=%async_computation | async-start | bytes 393216 | tf_op jit(solution)/shard_map/all_to_all | solution.py:481
  80.8 1.9 %copy-start.3 = (f32[3,16,128,128]{3,2,1,0:T(8,128)S(1)}, f32[3,16,128,128]{3,2,1,0:T(8,128)}, u32[]{:S(2)}) copy-start(f32[3,16,128,128]{3,2,1,0:T(8,128)} %vel.9) | copy-start | bytes 9437188
  83.9 5.8 %copy-start.20 = (f32[128,128]{1,0:T(8,128)S(1)}, f32[128,128]{1,0:T(8,128)}, u32[]{:S(2)}) copy-start(f32[128,128]{1,0:T(8,128)} %copy-done.18) | copy-start | bytes 196612
  89.8 8.6 %copy-start.10 = (f32[2,128,128]{2,1,0:T(8,128)S(1)}, f32[2,128,128]{2,1,0:T(8,128)}, u32[]{:S(2)}) copy-start(f32[2,128,128]{2,1,0:T(8,128)} %get-tuple-element.9.zl) | copy-start | bytes 393220
  95.7 1.6 %copy-start.8 = (bf16[4,512,512]{2,1,0:T(8,128)(2,1)S(1)}, bf16[4,512,512]{2,1,0:T(8,128)(2,1)}, u32[]{:S(2)}) copy-start(bf16[4,512,512]{2,1,0:T(8,128)(2,1)} %filters.1) | copy-start | bytes 6291460
  98.3 1.9 %copy-start.4 = (f32[3,16,128,128]{3,2,1,0:T(8,128)S(1)}, f32[3,16,128,128]{3,2,1,0:T(8,128)}, u32[]{:S(2)}) copy-start(f32[3,16,128,128]{3,2,1,0:T(8,128)} %vel.9) | copy-start | bytes 9437188
  (11 other events, 10.1 us)

commit v2 on v0

v2 whole, which is shorter than its diff:
```python
import functools

import jax
import jax.numpy as jnp
from jax import lax
from jax.experimental import pallas as pl
from jax.experimental.pallas import tpu as pltpu
from jax.sharding import PartitionSpec as P

F32 = jnp.float32
BF16 = jnp.bfloat16
ANY = pl.BlockSpec(memory_space=pl.ANY)
VM = pl.BlockSpec(memory_space=pltpu.VMEM)
SM = pl.BlockSpec(memory_space=pltpu.SMEM)
MIB = 1024 * 1024
ROWS = 32


def lanes(shape):
    return lax.broadcasted_iota(jnp.int32, shape, len(shape) - 1)


def roll(x, shift, axis):
    if isinstance(shift, int):
        shift = shift % x.shape[axis]
    return pltpu.roll(x, shift, axis)


def in_vmem(shape):
    return pltpu.VMEM(shape, F32)


STATE = {
    "adj": (3, 20, 144, 128),
    "visc": (20, 144, 128),
    "vel": (3, 18, 128, 128),
    "mid": (3, 18, 144, 128),
    "coef": (7, 18, 128, 128),
}


def params(mib):
    return pltpu.CompilerParams(vmem_limit_bytes=mib * MIB)


def hbm(x):
    return pltpu.with_memory_space_constraint(x, pltpu.HBM)


def vmem(x):
    return pltpu.with_memory_space_constraint(x, pltpu.VMEM)


def clear_walls(ref, lead):
    for index in lead:
        ref[(*index, pl.ds(0, 8), slice(None))] = jnp.zeros((8, 128), F32)
        ref[(*index, pl.ds(136, 8), slice(None))] = jnp.zeros((8, 128), F32)


def begin(copies, sems):
    started = [pltpu.make_async_copy(s, t, sems.at[i]) for i, (s, t) in enumerate(copies)]
    for copy in started:
        copy.start()
    return started


def pack_kernel(adj, vel, visc, adj_s, visc_s, vel_s, zl, zr, acc_l, acc_r, sems):
    def copies(g):
        rows = pl.ds(g * 32, 32)
        padded = pl.ds(8 + g * 32, 32)
        return (
            (adj.at[:, :, rows], adj_s.at[:, pl.ds(2, 16), padded]),
            (visc.at[:, rows], visc_s.at[pl.ds(2, 16), padded]),
            (vel.at[:, :, rows], vel_s.at[:, pl.ds(1, 16), rows]),
        )

    started = [begin(copies(g), sems.at[g]) for g in range(4)]
    clear_walls(adj_s, [(c, q) for c in range(3) for q in range(1, 20)])
    clear_walls(visc_s, [(q,) for q in range(1, 20)])
    zero = jnp.zeros((144, 128), F32)
    visc_s[1] = zero
    for c in range(3):
        adj_s[c, 1] = zero
    lane = lanes((32, 128))
    pair = lane >> 1
    pair_l = ((lane + 2) & 127) >> 1
    for g in range(4):
        for copy in started[g]:
            copy.wait()
        rows = pl.ds(g * 32, 32)
        padded = pl.ds(8 + g * 32, 32)
        half = g // 2
        left = jnp.zeros((32, 128), F32)
        right = jnp.zeros((32, 128), F32)
        for m in range(64):
            c, x = divmod(m, 16)
            plane = adj_s[c, x + 2, padded] if c < 3 else visc_s[x + 2, padded]
            turned = roll(plane, 2 * m, 1)
            right = jnp.where(pair == m, turned, right)
            left = jnp.where(pair_l == m, turned, left)
        zr[rows] = right
        zl[rows] = roll(left, 2, 1)
        left = jnp.zeros((32, 128), F32)
        right = jnp.zeros((32, 128), F32)
        for m in range(48):
            d, x = divmod(m, 16)
            at = 2 * m + half
            turned = roll(vel_s[d, x + 1, rows], at, 1)
            right = jnp.where(lane == at, turned, right)
            left = jnp.where(lane == (at - 1) % 128, turned, left)
        acc_r[rows] = right
        acc_l[rows] = roll(left, 1, 1)
    even = (lanes((64, 128)) & 1) == 0
    zr[pl.ds(128, 64)] = jnp.where(even, acc_r[pl.ds(0, 64)], acc_r[pl.ds(64, 64)])
    zl[pl.ds(128, 64)] = jnp.where(even, acc_l[pl.ds(0, 64)], acc_l[pl.ds(64, 64)])


def pack(adj, vel, visc):
    return pl.pallas_call(
        pack_kernel,
        in_specs=[ANY, ANY, ANY],
        out_specs=[VM] * 5,
        out_shape=[in_vmem(STATE[k]) for k in ("adj", "visc", "vel")] + [in_vmem((192, 128))] * 2,
        scratch_shapes=[
            pltpu.VMEM((128, 128), F32),
            pltpu.VMEM((128, 128), F32),
            pltpu.SemaphoreType.DMA((4, 3)),
        ],
        compiler_params=params(4),
        name="pack",
    )(hbm(adj), hbm(vel), hbm(visc))


def spread(a, group):
    kept = jnp.where((lanes(a.shape) >> 5) == group, a, 0.0)
    kept = kept + roll(kept, 32, 1)
    return kept + roll(kept, 64, 1)


def shift_rows(a, by):
    row = lax.broadcasted_iota(jnp.int32, a.shape, 0)
    moved = roll(a, by, 0)
    edge = 0 if by > 0 else a.shape[0] - 1
    return jnp.where(row == edge, 0.0, moved)


def edge_centre(hl, hr):
    odd = (lanes((128, 128)) & 1) == 1
    return jnp.where(odd, hl[pl.ds(0, 128)], hr[pl.ds(0, 128)])


def edge_velocity(message):
    both = message[pl.ds(128, 64)]
    odd = (lanes(both.shape) & 1) == 1
    upper = jnp.where(odd, roll(both, 1, 1), both)
    lower = jnp.where(odd, both, roll(both, -1, 1))
    return jnp.concatenate([upper, lower], axis=0)


def edge_middle(hl, hr, zl, zr, low=None, high=None):
    lane = lanes((128, 128))
    odd = (lane & 1) == 1
    x = (lane >> 1) & 15
    first = pl.ds(0, 128)
    left, right = hl[first], hr[first]
    centre = jnp.where(odd, left, right)
    minus = jnp.where(odd, roll(left, 1, 1), roll(zl[first], -1, 1))
    plus = jnp.where(odd, roll(zr[first], 1, 1), roll(right, -1, 1))
    velocity = jnp.where(odd, edge_velocity(hl), edge_velocity(hr))
    west = roll(centre, 2, 1)
    east = roll(centre, -2, 1)
    west = jnp.where(x == 0, 0.0 if low is None else roll(low, -30, 1), west)
    east = jnp.where(x == 15, 0.0 if high is None else roll(high, 30, 1), east)
    north = shift_rows(centre, -1)
    south = shift_rows(centre, 1)
    visc = spread(centre, 3)
    total = 0.0
    result = 0.0
    for d, (up, down) in enumerate(((east, west), (north, south), (plus, minus))):
        v = spread(velocity, d)
        a_up = 0.5 * ((visc + spread(up, 3)) + v)
        a_down = 0.5 * ((visc + spread(down, 3)) - v)
        total = total + (a_up + a_down)
        result = result + (a_up * up + a_down * down)
    return result + (1.0 - total) * centre


def ends(edge, r, m):
    return roll(edge[pl.ds(r, ROWS), :], (127 - 2 * m) % 128 if isinstance(m, int) else 127 - 2 * m, 1)


def first_step(adj_s, visc_s, vel_s, mid_s, coef_s, edge, x, ex):
    lane = lanes((ROWS, 128))
    q, t = x + 2, x + 1
    for r in range(0, 128, ROWS):
        rows, here = pl.ds(r, ROWS), pl.ds(8 + r, ROWS)
        above, below = pl.ds(9 + r, ROWS), pl.ds(7 + r, ROWS)

        def sides(plane, m):
            end = ends(edge, r, m)
            up = jnp.where(lane == 127, end, roll(plane, -1, 1))
            return up, jnp.where(lane == 0, end, roll(plane, 1, 1))

        centre = visc_s[q, here, :]
        pairs = (
            (visc_s[q + 1, here, :], visc_s[q - 1, here, :]),
            (visc_s[q, above, :], visc_s[q, below, :]),
            sides(centre, 48 + ex),
        )
        a = []
        for d, (plus, minus) in enumerate(pairs):
            v = vel_s[d, t, rows, :]
            a.append(0.5 * ((centre + plus) + v))
            a.append(0.5 * ((centre + minus) - v))
        a.append(1.0 - (((a[0] + a[1]) + (a[2] + a[3])) + (a[4] + a[5])))
        for k in range(7):
            coef_s[k, t, rows, :] = a[k]
        for c in range(3):
            centre = adj_s[c, q, here, :]
            up, down = sides(centre, c * 16 + ex)
            out = a[6] * centre
            out = out + a[0] * adj_s[c, q + 1, here, :]
            out = out + a[1] * adj_s[c, q - 1, here, :]
            out = out + a[2] * adj_s[c, q, above, :]
            out = out + a[3] * adj_s[c, q, below, :]
            out = out + a[4] * up
            mid_s[c, t, here, :] = out + a[5] * down
    for c in range(3):
        mid_s[c, t, pl.ds(0, 8), :] = jnp.zeros((8, 128), F32)
        mid_s[c, t, pl.ds(136, 8), :] = jnp.zeros((8, 128), F32)


def second_step(mid_s, coef_s, edge, x, store):
    lane = lanes((ROWS, 128))
    t = x + 1
    for r in range(0, 128, ROWS):
        rows, here = pl.ds(r, ROWS), pl.ds(8 + r, ROWS)
        above, below = pl.ds(9 + r, ROWS), pl.ds(7 + r, ROWS)
        a = [coef_s[k, t, rows, :] for k in range(7)]
        for c in range(3):
            centre = mid_s[c, t, here, :]
            end = ends(edge, r, c * 16 + x)
            out = a[6] * centre
            out = out + a[0] * mid_s[c, t + 1, here, :]
            out = out + a[1] * mid_s[c, t - 1, here, :]
            out = out + a[2] * mid_s[c, t, above, :]
            out = out + a[3] * mid_s[c, t, below, :]
            out = out + a[4] * jnp.where(lane == 127, end, roll(centre, -1, 1))
            store(c, rows, out + a[5] * jnp.where(lane == 0, end, roll(centre, 1, 1)))


def face_kernel(
    place, adj_s, visc_s, vel_s, hl, hr, zl, zr,
    face, mid_s, coef_s, centre, middle, msg_lo, msg_hi, sems,
):
    moved = []
    for msg, q, t in ((msg_lo, 2, 1), (msg_hi, 16, 16)):
        inside = pl.ds(8, 128)
        for c in range(3):
            moved.append((adj_s.at[c, pl.ds(q, 2), inside], msg.at[pl.ds(2 * c, 2)]))
            moved.append((vel_s.at[c, pl.ds(t, 1)], msg.at[pl.ds(6 + c, 1)]))
        moved.append((visc_s.at[pl.ds(q, 2), inside], msg.at[pl.ds(9, 2)]))
    centre[0] = edge_centre(hl, hr)
    moved += [(centre, msg_lo.at[pl.ds(11, 1)]), (centre, msg_hi.at[pl.ds(11, 1)])]
    moved = begin(moved, sems)
    middle[...] = edge_middle(hl, hr, zl, zr)
    for c in range(3):
        mid_s[c, 0] = jnp.zeros((144, 128), F32)
    for x in range(2):
        first_step(adj_s, visc_s, vel_s, mid_s, coef_s, centre.at[0], x, x)
    own = jnp.where(place[0] == 0, 1.0, 0.0)

    def store(c, rows, v):
        face[c, rows, :] = v * own

    second_step(mid_s, coef_s, middle, 0, store)
    for copy in moved:
        copy.wait()


def face_call(place, state, hl, hr, zl, zr):
    msg = pltpu.HBM((12, 128, 128), F32)
    return pl.pallas_call(
        face_kernel,
        in_specs=[SM] + [VM] * 7,
        out_specs=[VM] * 5 + [ANY, ANY],
        out_shape=[
            in_vmem((3, 128, 128)),
            in_vmem(STATE["mid"]),
            in_vmem(STATE["coef"]),
            in_vmem((1, 128, 128)),
            in_vmem((128, 128)),
            msg,
            msg,
        ],
        scratch_shapes=[pltpu.SemaphoreType.DMA((16,))],
        compiler_params=params(4),
        name="face",
    )(place, *[vmem(a) for a in (*state, hl, hr, zl, zr)])


def send(out_s, out, sems, i, x):
    return pltpu.make_async_copy(out_s.at[:, pl.ds(i, 1)], out.at[:, pl.ds(x, 1)], sems.at[i])


def inner_kernel(adj_s, visc_s, vel_s, centre, middle, _, __, mid_s, coef_s, out, out_s, sems):
    def first(x, carry):
        first_step(adj_s, visc_s, vel_s, mid_s, coef_s, centre.at[0], x, x)
        return carry

    lax.fori_loop(2, 9, first, 0)

    def second(x, carry):
        def store(c, rows, v):
            out_s[c, x - 2, rows, :] = v

        second_step(mid_s, coef_s, middle, x, store)
        send(out_s, out, sems, x - 2, x).start()
        return carry

    lax.fori_loop(2, 8, second, 0)
    for i in range(6):
        send(out_s, out, sems, i, i + 2).wait()


def inner(state, centre, middle, mid, coef):
    return pl.pallas_call(
        inner_kernel,
        in_specs=[VM] * 7,
        out_specs=[VM, VM, ANY],
        out_shape=[
            in_vmem(STATE["mid"]),
            in_vmem(STATE["coef"]),
            pltpu.HBM((3, 16, 128, 128), F32),
        ],
        scratch_shapes=[pltpu.VMEM((3, 6, 128, 128), F32), pltpu.SemaphoreType.DMA((6,))],
        input_output_aliases={5: 0, 6: 1},
        compiler_params=params(4),
        name="inner",
    )(*[vmem(a) for a in (*state, centre, middle, mid, coef)])


def outer_kernel(
    place, adj_i, visc_i, vel_i, mid_i, coef_i, centre, middle, hl, hr, zl, zr, low, high, _,
    adj_s, visc_s, vel_s, mid_s, coef_s, out, out_s, corner, edges, sems, sems_o,
):
    inside = pl.ds(8, 128)
    pairs = [(low.at[pl.ds(11, 1)], corner.at[pl.ds(0, 1)])]
    pairs += [(high.at[pl.ds(11, 1)], corner.at[pl.ds(1, 1)])]
    for msg, q, t in ((low, 0, 0), (high, 18, 17)):
        for c in range(3):
            pairs.append((msg.at[pl.ds(2 * c, 2)], adj_s.at[c, pl.ds(q, 2), inside]))
            pairs.append((msg.at[pl.ds(6 + c, 1)], vel_s.at[c, pl.ds(t, 1)]))
        pairs.append((msg.at[pl.ds(9, 2)], visc_s.at[pl.ds(q, 2), inside]))
    started = begin(pairs, sems)

    def first(x, carry):
        first_step(adj_s, visc_s, vel_s, mid_s, coef_s, centre.at[0], x, x)
        return carry

    lax.fori_loop(9, 15, first, 0)

    def second(x, carry):
        def store(c, rows, v):
            out_s[c, x - 8, rows, :] = v

        second_step(mid_s, coef_s, middle, x, store)
        send(out_s, out, sems_o, x - 8, x).start()
        return carry

    lax.fori_loop(8, 14, second, 0)
    for copy in started:
        copy.wait()
    edges[...] = edge_middle(hl, hr, zl, zr, corner[0], corner[1])
    first_step(adj_s, visc_s, vel_s, mid_s, coef_s, corner.at[0], -1, 15)
    first_step(adj_s, visc_s, vel_s, mid_s, coef_s, centre.at[0], 0, 0)
    first_step(adj_s, visc_s, vel_s, mid_s, coef_s, centre.at[0], 15, 15)
    first_step(adj_s, visc_s, vel_s, mid_s, coef_s, corner.at[1], 16, 0)

    @pl.when(place[0] == 0)
    def _():
        for c in range(3):
            mid_s[c, 0] = jnp.zeros((144, 128), F32)

    @pl.when(place[0] == place[1] - 1)
    def _():
        for c in range(3):
            mid_s[c, 17] = jnp.zeros((144, 128), F32)

    for i, x in ((6, 0), (7, 1), (8, 14), (9, 15)):

        def store(c, rows, v, i=i):
            out_s[c, i, rows, :] = v

        second_step(mid_s, coef_s, edges, x, store)
        send(out_s, out, sems_o, i, x).start()
    for i in range(10):
        send(out_s, out, sems_o, i, i + 8 if i < 6 else (0, 1, 14, 15)[i - 6]).wait()


def outer(place, state, mid, coef, centre, middle, hl, hr, zl, zr, low, high, out):
    held = [vmem(a) for a in (*state, mid, coef, centre, middle, hl, hr, zl, zr)]
    return pl.pallas_call(
        outer_kernel,
        in_specs=[SM] + [VM] * 11 + [ANY] * 3,
        out_specs=[VM] * 5 + [ANY],
        out_shape=[in_vmem(STATE[k]) for k in ("adj", "visc", "vel", "mid", "coef")]
        + [pltpu.HBM((3, 16, 128, 128), F32)],
        scratch_shapes=[
            pltpu.VMEM((3, 10, 128, 128), F32),
            pltpu.VMEM((2, 128, 128), F32),
            pltpu.VMEM((128, 128), F32),
            pltpu.SemaphoreType.DMA((16,)),
            pltpu.SemaphoreType.DMA((10,)),
        ],
        input_output_aliases={1: 0, 2: 1, 3: 2, 4: 3, 5: 4, 14: 5},
        compiler_params=params(6),
        name="outer",
    )(place, *held, hbm(low), hbm(high), hbm(out))[-1]


def pieces(a):
    high = a.astype(BF16)
    rest = a - high.astype(F32)
    mid = rest.astype(BF16)
    low = (rest - mid.astype(F32)).astype(BF16)
    return high, mid, low


def sums_kernel(place, places, face, more, out):
    row = lax.broadcasted_iota(jnp.int32, (128, 128), 0)
    column = lanes((128, 128))
    wanted = (row >> 2) + place[0] * 32
    count = jnp.zeros((128, 128), F32)
    for k in range(8):
        count = count + jnp.where(places[pl.ds(k, 1), :] == wanted, 1.0, 0.0)
    chosen = jnp.where((row & 3) == (column & 3), count, 0.0).astype(BF16)
    for c in range(3):
        total = 0.0
        for piece in pieces(face[c] + more[c]):
            total = total + jnp.dot(chosen, piece, preferred_element_type=F32)
        for g in range(8):
            out[g, c] = total[g * 16 : g * 16 + 16]


def partial_sums(place, places, face, more):
    return pl.pallas_call(
        sums_kernel,
        in_specs=[SM, VM, VM, VM],
        out_specs=VM,
        out_shape=jax.ShapeDtypeStruct((8, 3, 16, 128), F32),
        compiler_params=params(4),
        name="sums",
    )(place, places, face, more)


def product_kernel(parts, filters, out, sums):
    total = parts[0]
    for g in range(1, 8):
        total = total + parts[g]
    sums[...] = total
    for p in range(4):
        view = jnp.concatenate([sums[:, p * 4 + i, :] for i in range(4)], axis=1)
        stacked = jnp.concatenate(pieces(view), axis=0)
        wide = jnp.dot(stacked, filters[p], preferred_element_type=F32)
        out[p] = wide[0:3] + (wide[3:6] + wide[6:9])


def product(parts, filters):
    return pl.pallas_call(
        product_kernel,
        in_specs=[VM, VM],
        out_specs=VM,
        out_shape=jax.ShapeDtypeStruct((4, 3, 512), F32),
        scratch_shapes=[pltpu.VMEM((3, 16, 128), F32)],
        compiler_params=params(4),
        name="product",
    )(parts, filters)


def shards(adjoint, velocity, viscosity, filters, block_tiles, tile_place):
    gx = lax.axis_index("gx")
    gz = lax.axis_index("gz")
    nx = lax.axis_size("gx")
    nz = lax.axis_size("gz")
    ring = [(i, (i + 1) % nz) for i in range(nz)]
    back = [(b, a) for a, b in ring]
    along = [(i, i + 1) for i in range(nx - 1)]
    against = [(b, a) for a, b in along]
    place = jnp.stack([gx, jnp.int32(nx)]).astype(jnp.int32)

    *state, zl, zr = pack(adjoint, velocity, viscosity)
    hl = lax.ppermute(zl, "gz", ring)
    hr = lax.ppermute(zr, "gz", back)

    lists = lax.dynamic_slice_in_dim(block_tiles, gz * 32, 32, 0)
    tiles = jnp.arange(512, dtype=jnp.int32)
    places = jnp.sum(jnp.where(lists[:, :, None] == tiles, tile_place, 0), axis=2)
    places = jnp.repeat(places.T, 4, axis=1)

    face, mid, coef, centre, middle, msg_lo, msg_hi = face_call(place, state, hl, hr, zl, zr)
    got = [lax.ppermute(face, "gx", [(0, k)]) for k in (8, 2, 6)]
    low = lax.ppermute(msg_hi, "gx", along)
    high = lax.ppermute(msg_lo, "gx", against)
    face = (face + got[0]) + (got[1] + got[2])
    far = lax.ppermute(face, "gx", [(0, 4), (2, 10), (6, 14), (8, 12)])
    mid, coef, out = inner(state, centre, middle, mid, coef)
    face = face + far
    other = lax.ppermute(face, "gx", [(i, i + 1) for i in range(0, nx, 2)])
    parts = lax.all_to_all(partial_sums(place, places, face, other), "gz", 0, 0)
    out = outer(place, state, mid, coef, centre, middle, hl, hr, zl, zr, low, high, out)
    gradient = product(parts, filters)
    return out, gradient


def solution(mesh):
    placed = (
        P(None, "gx", None, "gz"),
        P(None, "gx", None, "gz"),
        P("gx", None, "gz"),
        P(("gx", "gz"), None, None),
        P(),
        P(),
    )
    return jax.shard_map(
        shards,
        mesh=mesh,
        in_specs=placed,
        out_specs=(P(None, "gx", None, "gz"), P(("gx", "gz"), None, None)),
        check_vma=False,
    )
```

time: 350 us -> 118 us (0.34)
  waiting for transfers between devices: 155 us -> 17.7 us
  other arithmetic: 66.2 us -> 3.93 us
  local copies, waits for them, and re-layouts: 73 us -> 45.1 us
  Pallas kernels: 0 us -> 24.2 us
  between operations: 14.3 us -> 0.8 us
  starting transfers between devices: 32.4 us -> 24.2 us
  matrix products: 6.08 us -> 0 us
    unnamed x2 -> x0, waiting for transfers between devices: 149 us -> none
    add x2, other arithmetic: 37.8 us -> 2.44 us  [the longest x1 1.72 us: shards(): face = face + far]
    unnamed x23 -> x51, local copies, waits for them, and re-layouts: 11.7 us -> 42.8 us
    slice x9 -> x0, local copies, waits for them, and re-layouts: 28.2 us -> none  [the longest x5 16.4 us: with_halo(): lax.slice_in_dim(block, block.shape[dim] - width, None, axis=dim)]
    pallas_call x0 -> x6, Pallas kernels: none -> 24.2 us  [the longest x1 7.96 us: outer(): pl.pallas_call(outer_kernel, in_specs=[SM] + [VM] * 11 + [ANY] * 3, out_s...]
    concatenate x3 -> x0, other arithmetic: 20.2 us -> none  [with_halo(): block = jnp.concatenate([low, block, high], axis=dim)]
    mul x9 -> x0, local copies, waits for them, and re-layouts: 18.2 us -> none  [the longest x1 3.74 us: advance(): velocity[0] * (east_cell - west_cell)]
    ppermute x12 -> x9, starting transfers between devices: 32.4 us -> 17.9 us  [the longest x1 7.26 us: shards(): high = lax.ppermute(msg_lo, 'gx', against)]
  transfers between devices with their start and end apart: 13 -> 10, of which waited for: 2 -> 4; matrix products, arithmetic and copies ran while one was open for 15% -> 6% of each run, Pallas kernels for 0% -> 6%
where the time goes in v2:
time: 118 us; the launch traced here: 116 us
  local copies, waits for them, and re-layouts  45.1 us (38%)
  Pallas kernels  24.2 us (21%)
  starting transfers between devices  24.2 us (21%)
  waiting for transfers between devices  17.7 us (15%)
  other arithmetic  3.93 us (3%)
    unnamed x51, local copies, waits for them, and re-layouts  42.8 us
    ppermute x3, waiting for transfers between devices, shards(): got = [lax.ppermute(face, 'gx', [(0, k)]) for k in (8, 2, 6)]  8.64 us
    pallas_call x1, Pallas kernels, outer(): pl.pallas_call(outer_kernel, in_specs=[SM] + [VM] * 11 + [ANY] * 3, out_s...  7.96 us
    ppermute x1, starting transfers between devices, shards(): high = lax.ppermute(msg_lo, 'gx', against)  7.26 us
    all_to_all x1, starting transfers between devices, shards(): parts = lax.all_to_all(partial_sums(place, places, face, other), 'gz', 0, 0)  6.32 us
    pallas_call x1, Pallas kernels, pack(): pl.pallas_call(pack_kernel, in_specs=[ANY, ANY, ANY], out_specs=[VM] * 5,...  5.41 us
    pallas_call x1, Pallas kernels, inner(): pl.pallas_call(inner_kernel, in_specs=[VM] * 7, out_specs=[VM, VM, ANY],...  4.21 us
    pallas_call x1, Pallas kernels, face_call(): pl.pallas_call(face_kernel, in_specs=[SM] + [VM] * 7, out_specs=[VM] * 5...  3.98 us
  transfers between devices with their start and end apart: 10, of which 4 were waited for; matrix products, arithmetic and copies ran while one was open for 6% of the time, Pallas kernels for 6%

profile of v2, /device:TPU:24, one launch (start us, length us, event | category | flops | bytes accessed | tf_op | source)
XLA Modules:
  0.0 115.8 jit_solution(10718171829801312725)
XLA Ops:
  0.6 5.4 %pack.1 = (f32[3,20,144,128]{3,2,1,0:T(8,128)S(1)}, f32[20,144,128]{2,1,0:T(8,128)S(1)}, f32[3,18,128,128]{3,2,1,0:T(8,128)S(1)}, f32[192,128]{1,0:T(8,128)}, f32[192,128]{1,0:T(8,128)}) custom-call(f32[3,16,128,128]{3,2,1,0:T(8,128)} %adj.1, f32[3,16,128,128]{3,2,1,0:T(8,128)} %vel.1, f32[16,128,128]{2,1,0:T(8,128)} %visc.1), custom_call_target="tpu_custom_call" | custom-call | tf_op jit(solution)/shard_map/pack/pallas_call | solution.py:119
  6.1 2.1 %copy-done.1 = f32[3,20,144,128]{3,2,1,0:T(8,128)} copy-done((f32[3,20,144,128]{3,2,1,0:T(8,128)}, f32[3,20,144,128]{3,2,1,0:T(8,128)S(1)}, u32[]{:S(2)}) %copy-start.1) | copy-done | bytes 4423704
  9.3 2.1 %collective-permute-start = (f32[192,128]{1,0:T(8,128)}, f32[192,128]{1,0:T(8,128)}, u32[]{:S(2)}, u32[]{:S(2)}) collective-permute-start(f32[192,128]{1,0:T(8,128)} %get-tuple-element.21.zl), channel_id=1, source_target_pairs={{0,1},{1,2},{2,3},{3,4},{4,5},{5,6},{6,7},{7,0},{8,9},{9,10},{10,1... | collective-permute-start | bytes 294920 | tf_op jit(solution)/shard_map/ppermute | solution.py:493
  11.5 3.3 %collective-permute-done.hl = f32[192,128]{1,0:T(8,128)} collective-permute-done((f32[192,128]{1,0:T(8,128)}, f32[192,128]{1,0:T(8,128)}, u32[]{:S(2)}, u32[]{:S(2)}) %collective-permute-start) | collective-permute-done | bytes 98336 | tf_op jit(solution)/shard_map/ppermute | solution.py:493
  14.8 2.9 %collective-permute-done.1.hr = f32[192,128]{1,0:T(8,128)} collective-permute-done((f32[192,128]{1,0:T(8,128)}, f32[192,128]{1,0:T(8,128)}, u32[]{:S(2)}, u32[]{:S(2)}) %collective-permute-start.1) | collective-permute-done | bytes 98336 | tf_op jit(solution)/shard_map/ppermute | solution.py:494
  17.7 2.3 %copy-done.2 = f32[3,20,144,128]{3,2,1,0:T(8,128)S(1)} copy-done((f32[3,20,144,128]{3,2,1,0:T(8,128)S(1)}, f32[3,20,144,128]{3,2,1,0:T(8,128)}, u32[]{:S(2)}) %copy-start.2) | copy-done | bytes 4423704
  21.3 4.0 %face.1 = (f32[3,128,128]{2,1,0:T(8,128)S(1)}, f32[3,18,144,128]{3,2,1,0:T(8,128)S(1)}, f32[7,18,128,128]{3,2,1,0:T(8,128)S(1)}, f32[1,128,128]{2,1,0:T(8,128)S(...) custom-call(s32[2]{0:T(128)S(1)} %pad_add_fusion.place, ...), custom_call_target="tpu_custom_call" | custom-call | tf_op jit(solution)/shard_map/face/pallas_call | solution.py:283
  25.3 3.2 %copy-done.5 = f32[7,18,128,128]{3,2,1,0:T(8,128)} copy-done((f32[7,18,128,128]{3,2,1,0:T(8,128)}, f32[7,18,128,128]{3,2,1,0:T(8,128)S(1)}, u32[]{:S(2)}) %copy-start.5) | copy-done | bytes 8257560
  34.3 1.9 %collective-permute-start.2 = (f32[12,128,128]{2,1,0:T(8,128)}, f32[12,128,128]{2,1,0:T(8,128)}, u32[]{:S(2)}, u32[]{:S(2)}) collective-permute-start(f32[12,128,128]{2,1,0:T(8,128)} %get-tuple-element.29), channel_id=1, source_target_pairs={{0,8},{8,16},{16,24},{24,32},{32,40},{40,48},{48,56},{56,64},{64,7... | collective-permute-start | bytes 2359304 | tf_op jit(solution)/shard_map/ppermute | solution.py:503
  36.2 7.3 %collective-permute-start.3 = (f32[12,128,128]{2,1,0:T(8,128)}, f32[12,128,128]{2,1,0:T(8,128)}, u32[]{:S(2)}, u32[]{:S(2)}) collective-permute-start(f32[12,128,128]{2,1,0:T(8,128)} %get-tuple-element.30), channel_id=1, source_target_pairs={{8,0},{16,8},{24,16},{32,24},{40,32},{48,40},{56,48},{64,56},{72,6... | collective-permute-start | bytes 2359304 | tf_op jit(solution)/shard_map/ppermute | solution.py:504
  43.5 8.6 %collective-permute-done.4 = f32[3,128,128]{2,1,0:T(8,128)S(1)} collective-permute-done((f32[3,128,128]{2,1,0:T(8,128)S(1)}, f32[3,128,128]{2,1,0:T(8,128)S(1)}, u32[]{:S(2)}, u32[]{:S(2)}) %collective-permute-start.4) | collective-permute-done | bytes 196640 | tf_op jit(solution)/shard_map/ppermute | solution.py:502
  52.9 2.0 %collective-permute-start.7 = (f32[3,128,128]{2,1,0:T(8,128)}, f32[3,128,128]{2,1,0:T(8,128)}, u32[]{:S(2)}, u32[]{:S(2)}) collective-permute-start(f32[3,128,128]{2,1,0:T(8,128)} %add_add_fusion), channel_id=1, source_target_pairs={{0,32},{16,80},{48,112},{64,96},{1,33},{17,81},{49,113},{65,97},{2... | collective-permute-start | bytes 589832 | tf_op jit(solution)/shard_map/ppermute | solution.py:506
  54.9 2.8 %collective-permute-done.7 = f32[3,128,128]{2,1,0:T(8,128)} collective-permute-done((f32[3,128,128]{2,1,0:T(8,128)}, f32[3,128,128]{2,1,0:T(8,128)}, u32[]{:S(2)}, u32[]{:S(2)}) %collective-permute-start.7) | collective-permute-done | bytes 196640 | tf_op jit(solution)/shard_map/ppermute | solution.py:506
  59.4 2.0 %collective-permute-start.8 = (f32[3,128,128]{2,1,0:T(8,128)}, f32[3,128,128]{2,1,0:T(8,128)}, u32[]{:S(2)}, u32[]{:S(2)}) collective-permute-start(f32[3,128,128]{2,1,0:T(8,128)} %add.19.face), channel_id=1, source_target_pairs={{0,8},{16,24},{32,40},{48,56},{64,72},{80,88},{96,104},{112,120},{... | collective-permute-start | bytes 589832 | tf_op jit(solution)/shard_map/ppermute | solution.py:509
  67.1 6.3 %all-to-all-start = ((f32[8,3,16,128]{3,2,1,0:T(8,128)}), f32[8,3,16,128]{3,2,1,0:T(8,128)}, u32[]{:S(2)}, u32[]{:S(2)}) async-start(f32[8,3,16,128]{3,2,1,0:T(8,128)} %copy-done.18), calls=%async_computation | async-start | bytes 393216 | tf_op jit(solution)/shard_map/all_to_all | solution.py:510
  73.4 2.3 %copy-done.3 = f32[3,20,144,128]{3,2,1,0:T(8,128)S(1)} copy-done((f32[3,20,144,128]{3,2,1,0:T(8,128)S(1)}, f32[3,20,144,128]{3,2,1,0:T(8,128)}, u32[]{:S(2)}) %copy-start.3) | copy-done | bytes 4423704
  75.7 3.3 %copy-done.6 = f32[7,18,128,128]{3,2,1,0:T(8,128)S(1)} copy-done((f32[7,18,128,128]{3,2,1,0:T(8,128)S(1)}, f32[7,18,128,128]{3,2,1,0:T(8,128)}, u32[]{:S(2)}) %copy-start.6) | copy-done | bytes 8257560
  79.0 2.1 %copy-done.10 = f32[3,18,144,128]{3,2,1,0:T(8,128)S(1)} copy-done((f32[3,18,144,128]{3,2,1,0:T(8,128)S(1)}, f32[3,18,144,128]{3,2,1,0:T(8,128)}, u32[]{:S(2)}) %copy-start.10) | copy-done | bytes 3981336
  84.2 4.2 %inner.1 = (f32[3,18,144,128]{3,2,1,0:T(8,128)S(1)}, f32[7,18,128,128]{3,2,1,0:T(8,128)S(1)}, f32[3,16,128,128]{3,2,1,0:T(8,128)}) custom-call(f32[3,20,144,128]{3,2,1,0:T(8,128)S(1)} %copy-done.3, f32[20,144,128]{2,1,0:T(8,128)S(1)} %copy-done.15, ...), custom_call_target="tpu_custom_call", output_to_operand_aliasing={{0}: (5, {}), {1}: (6, {})} | custom-call | tf_op jit(solution)/shard_map/inner/pallas_call | solution.py:327
  88.4 3.2 %copy-done.7 = f32[7,18,128,128]{3,2,1,0:T(8,128)} copy-done((f32[7,18,128,128]{3,2,1,0:T(8,128)}, f32[7,18,128,128]{3,2,1,0:T(8,128)S(1)}, u32[]{:S(2)}) %copy-start.7) | copy-done | bytes 8257560
  97.1 2.3 %copy-done.4 = f32[3,20,144,128]{3,2,1,0:T(8,128)S(1)} copy-done((f32[3,20,144,128]{3,2,1,0:T(8,128)S(1)}, f32[3,20,144,128]{3,2,1,0:T(8,128)}, u32[]{:S(2)}) %copy-start.4) | copy-done | bytes 4423704
  99.4 3.3 %copy-done.8 = f32[7,18,128,128]{3,2,1,0:T(8,128)S(1)} copy-done((f32[7,18,128,128]{3,2,1,0:T(8,128)S(1)}, f32[7,18,128,128]{3,2,1,0:T(8,128)}, u32[]{:S(2)}) %copy-start.8) | copy-done | bytes 8257560
  102.7 2.1 %copy-done.12 = f32[3,18,144,128]{3,2,1,0:T(8,128)S(1)} copy-done((f32[3,18,144,128]{3,2,1,0:T(8,128)S(1)}, f32[3,18,144,128]{3,2,1,0:T(8,128)}, u32[]{:S(2)}) %copy-start.12) | copy-done | bytes 3981336
  107.9 8.0 %outer.1 = (f32[3,20,144,128]{3,2,1,0:T(8,128)S(1)}, f32[20,144,128]{2,1,0:T(8,128)S(1)}, f32[3,18,128,128]{3,2,1,0:T(8,128)S(1)}, f32[3,18,144,128]{3,2,1,0:T(8...) custom-call(s32[2]{0:T(128)S(1)} %pad_add_fusion.place, ...), custom_call_target="tpu_custom_call", output_to_operand_aliasing={{0}: (1, {}), {1}: (2, {}), {2}: (3, {}), {3}: (4, {}), {4}... | custom-call | tf_op jit(solution)/shard_map/outer/pallas_call | solution.py:403
  (61 shorter events, 28.0 us)
Async XLA Ops:
  0.6 60.7 %copy-start = (s32[256,8]{0,1:T(8,128)S(1)}, s32[256,8]{0,1:T(8,128)}, u32[]{:S(2)}) copy-start(s32[256,8]{0,1:T(8,128)} %param.10) | copy-start | bytes 24580
  6.1 2.1 %copy-start.1 = (f32[3,20,144,128]{3,2,1,0:T(8,128)}, f32[3,20,144,128]{3,2,1,0:T(8,128)S(1)}, u32[]{:S(2)}) copy-start(f32[3,20,144,128]{3,2,1,0:T(8,128)S(1)} %get-tuple-element.18.adj_s.adj_i) | copy-start | bytes 13271044
  9.3 5.5 %collective-permute-start = (f32[192,128]{1,0:T(8,128)}, f32[192,128]{1,0:T(8,128)}, u32[]{:S(2)}, u32[]{:S(2)}) collective-permute-start(f32[192,128]{1,0:T(8,128)} %get-tuple-element.21.zl), channel_id=1, source_target_pairs={{0,1},{1,2},{2,3},{3,4},{4,5},{5,6},{6,7},{7,0},{8,9},{9,10},{10,1... | collective-permute-start | bytes 294920 | tf_op jit(solution)/shard_map/ppermute | solution.py:493
  11.4 6.3 %collective-permute-start.1 = (f32[192,128]{1,0:T(8,128)}, f32[192,128]{1,0:T(8,128)}, u32[]{:S(2)}, u32[]{:S(2)}) collective-permute-start(f32[192,128]{1,0:T(8,128)} %get-tuple-element.22.zr), channel_id=1, source_target_pairs={{1,0},{2,1},{3,2},{4,3},{5,4},{6,5},{7,6},{0,7},{9,8},{10,9},{11,1... | collective-permute-start | bytes 294920 | tf_op jit(solution)/shard_map/ppermute | solution.py:494
  17.7 2.3 %copy-start.2 = (f32[3,20,144,128]{3,2,1,0:T(8,128)S(1)}, f32[3,20,144,128]{3,2,1,0:T(8,128)}, u32[]{:S(2)}) copy-start(f32[3,20,144,128]{3,2,1,0:T(8,128)} %copy-done.1) | copy-start | bytes 13271044
  25.3 3.2 %copy-start.5 = (f32[7,18,128,128]{3,2,1,0:T(8,128)}, f32[7,18,128,128]{3,2,1,0:T(8,128)S(1)}, u32[]{:S(2)}) copy-start(f32[7,18,128,128]{3,2,1,0:T(8,128)S(1)} %get-tuple-element.26.__) | copy-start | bytes 24772612
  28.5 1.9 %copy-start.9 = (f32[3,18,144,128]{3,2,1,0:T(8,128)}, f32[3,18,144,128]{3,2,1,0:T(8,128)S(1)}, u32[]{:S(2)}) copy-start(f32[3,18,144,128]{3,2,1,0:T(8,128)S(1)} %get-tuple-element.25._) | copy-start | bytes 11943940
  31.7 11.8 %collective-permute-start.6 = (f32[3,128,128]{2,1,0:T(8,128)S(1)}, f32[3,128,128]{2,1,0:T(8,128)S(1)}, u32[]{:S(2)}, u32[]{:S(2)}) collective-permute-start(f32[3,128,128]{2,1,0:T(8,128)S(1)} %get-tuple-element.33), channel_id=1, source_target_pairs={{0,48},{1,49},{2,50},{3,51},{4,52},{5,53},{6,54},{7,55}} | collective-permute-start | bytes 589832 | tf_op jit(solution)/shard_map/ppermute | solution.py:502
  32.3 11.2 %collective-permute-start.5 = (f32[3,128,128]{2,1,0:T(8,128)S(1)}, f32[3,128,128]{2,1,0:T(8,128)S(1)}, u32[]{:S(2)}, u32[]{:S(2)}) collective-permute-start(f32[3,128,128]{2,1,0:T(8,128)S(1)} %get-tuple-element.33), channel_id=1, source_target_pairs={{0,16},{1,17},{2,18},{3,19},{4,20},{5,21},{6,22},{7,23}} | collective-permute-start | bytes 589832 | tf_op jit(solution)/shard_map/ppermute | solution.py:502
  33.0 19.1 %collective-permute-start.4 = (f32[3,128,128]{2,1,0:T(8,128)S(1)}, f32[3,128,128]{2,1,0:T(8,128)S(1)}, u32[]{:S(2)}, u32[]{:S(2)}) collective-permute-start(f32[3,128,128]{2,1,0:T(8,128)S(1)} %get-tuple-element.33), channel_id=1, source_target_pairs={{0,64},{1,65},{2,66},{3,67},{4,68},{5,69},{6,70},{7,71}} | collective-permute-start | bytes 589832 | tf_op jit(solution)/shard_map/ppermute | solution.py:502
  34.3 62.8 %collective-permute-start.2 = (f32[12,128,128]{2,1,0:T(8,128)}, f32[12,128,128]{2,1,0:T(8,128)}, u32[]{:S(2)}, u32[]{:S(2)}) collective-permute-start(f32[12,128,128]{2,1,0:T(8,128)} %get-tuple-element.29), channel_id=1, source_target_pairs={{0,8},{8,16},{16,24},{24,32},{32,40},{40,48},{48,56},{56,64},{64,7... | collective-permute-start | bytes 2359304 | tf_op jit(solution)/shard_map/ppermute | solution.py:503
  36.2 60.9 %collective-permute-start.3 = (f32[12,128,128]{2,1,0:T(8,128)}, f32[12,128,128]{2,1,0:T(8,128)}, u32[]{:S(2)}, u32[]{:S(2)}) collective-permute-start(f32[12,128,128]{2,1,0:T(8,128)} %get-tuple-element.30), channel_id=1, source_target_pairs={{8,0},{16,8},{24,16},{32,24},{40,32},{48,40},{56,48},{64,56},{72,6... | collective-permute-start | bytes 2359304 | tf_op jit(solution)/shard_map/ppermute | solution.py:504
  52.9 4.8 %collective-permute-start.7 = (f32[3,128,128]{2,1,0:T(8,128)}, f32[3,128,128]{2,1,0:T(8,128)}, u32[]{:S(2)}, u32[]{:S(2)}) collective-permute-start(f32[3,128,128]{2,1,0:T(8,128)} %add_add_fusion), channel_id=1, source_target_pairs={{0,32},{16,80},{48,112},{64,96},{1,33},{17,81},{49,113},{65,97},{2... | collective-permute-start | bytes 589832 | tf_op jit(solution)/shard_map/ppermute | solution.py:506
  59.4 5.7 %collective-permute-start.8 = (f32[3,128,128]{2,1,0:T(8,128)}, f32[3,128,128]{2,1,0:T(8,128)}, u32[]{:S(2)}, u32[]{:S(2)}) collective-permute-start(f32[3,128,128]{2,1,0:T(8,128)} %add.19.face), channel_id=1, source_target_pairs={{0,8},{16,24},{32,40},{48,56},{64,72},{80,88},{96,104},{112,120},{... | collective-permute-start | bytes 589832 | tf_op jit(solution)/shard_map/ppermute | solution.py:509
  67.1 26.4 %all-to-all-start = ((f32[8,3,16,128]{3,2,1,0:T(8,128)}), f32[8,3,16,128]{3,2,1,0:T(8,128)}, u32[]{:S(2)}, u32[]{:S(2)}) async-start(f32[8,3,16,128]{3,2,1,0:T(8,128)} %copy-done.18), calls=%async_computation | async-start | bytes 393216 | tf_op jit(solution)/shard_map/all_to_all | solution.py:510
  73.4 2.3 %copy-start.3 = (f32[3,20,144,128]{3,2,1,0:T(8,128)S(1)}, f32[3,20,144,128]{3,2,1,0:T(8,128)}, u32[]{:S(2)}) copy-start(f32[3,20,144,128]{3,2,1,0:T(8,128)} %copy-done.1) | copy-start | bytes 13271044
  75.7 3.3 %copy-start.6 = (f32[7,18,128,128]{3,2,1,0:T(8,128)S(1)}, f32[7,18,128,128]{3,2,1,0:T(8,128)}, u32[]{:S(2)}) copy-start(f32[7,18,128,128]{3,2,1,0:T(8,128)} %copy-done.5) | copy-start | bytes 24772612
  79.0 2.1 %copy-start.10 = (f32[3,18,144,128]{3,2,1,0:T(8,128)S(1)}, f32[3,18,144,128]{3,2,1,0:T(8,128)}, u32[]{:S(2)}) copy-start(f32[3,18,144,128]{3,2,1,0:T(8,128)} %copy-done.9) | copy-start | bytes 11943940
  88.4 3.2 %copy-start.7 = (f32[7,18,128,128]{3,2,1,0:T(8,128)}, f32[7,18,128,128]{3,2,1,0:T(8,128)S(1)}, u32[]{:S(2)}) copy-start(f32[7,18,128,128]{3,2,1,0:T(8,128)S(1)} %get-tuple-element.28.coef_i) | copy-start | bytes 24772612
  91.6 1.9 %copy-start.11 = (f32[3,18,144,128]{3,2,1,0:T(8,128)}, f32[3,18,144,128]{3,2,1,0:T(8,128)S(1)}, u32[]{:S(2)}) copy-start(f32[3,18,144,128]{3,2,1,0:T(8,128)S(1)} %get-tuple-element.27.mid_i) | copy-start | bytes 11943940
  93.5 1.6 %copy-start.17 = (bf16[4,512,512]{2,1,0:T(8,128)(2,1)S(1)}, bf16[4,512,512]{2,1,0:T(8,128)(2,1)}, u32[]{:S(2)}) copy-start(bf16[4,512,512]{2,1,0:T(8,128)(2,1)} %filters.1) | copy-start | bytes 6291460
  97.1 2.3 %copy-start.4 = (f32[3,20,144,128]{3,2,1,0:T(8,128)S(1)}, f32[3,20,144,128]{3,2,1,0:T(8,128)}, u32[]{:S(2)}) copy-start(f32[3,20,144,128]{3,2,1,0:T(8,128)} %copy-done.1) | copy-start | bytes 13271044
  99.3 3.3 %copy-start.8 = (f32[7,18,128,128]{3,2,1,0:T(8,128)S(1)}, f32[7,18,128,128]{3,2,1,0:T(8,128)}, u32[]{:S(2)}) copy-start(f32[7,18,128,128]{3,2,1,0:T(8,128)} %copy-done.7) | copy-start | bytes 24772612
  102.7 2.1 %copy-start.12 = (f32[3,18,144,128]{3,2,1,0:T(8,128)S(1)}, f32[3,18,144,128]{3,2,1,0:T(8,128)}, u32[]{:S(2)}) copy-start(f32[3,18,144,128]{3,2,1,0:T(8,128)} %copy-done.11) | copy-start | bytes 11943940
  (11 other events, 10.5 us)

commit v3 on v2

--- a/solution.py
+++ b/solution.py
@@ -11,7 +11,6 @@
 BF16 = jnp.bfloat16
 ANY = pl.BlockSpec(memory_space=pl.ANY)
 VM = pl.BlockSpec(memory_space=pltpu.VMEM)
-SM = pl.BlockSpec(memory_space=pltpu.SMEM)
 MIB = 1024 * 1024
 ROWS = 32
 
@@ -250,8 +249,64 @@
 
 
 def face_kernel(
-    place, adj_s, visc_s, vel_s, hl, hr, zl, zr,
-    face, mid_s, coef_s, centre, middle, msg_lo, msg_hi, sems,
+    adj_s, visc_s, vel_s, hl, hr, zl, zr, face, mid_s, coef_s, centre, middle
+):
+    centre[0] = edge_centre(hl, hr)
+    middle[...] = edge_middle(hl, hr, zl, zr)
+    for c in range(3):
+        mid_s[c, 0] = jnp.zeros((144, 128), F32)
+    for x in range(2):
+        first_step(adj_s, visc_s, vel_s, mid_s, coef_s, centre.at[0], x, x)
+    own = jnp.where(lax.axis_index("gx") == 0, 1.0, 0.0)
+
+    def store(c, rows, v):
+        face[c, rows, :] = v * own
+
+    second_step(mid_s, coef_s, middle, 0, store)
+
+
+def face_call(state, hl, hr, zl, zr):
+    return pl.pallas_call(
+        face_kernel,
+        in_specs=[VM] * 7,
+        out_specs=[VM] * 5,
+        out_shape=[
+            in_vmem((3, 128, 128)),
+            in_vmem(STATE["mid"]),
+            in_vmem(STATE["coef"]),
+            in_vmem((1, 128, 128)),
+            in_vmem((128, 128)),
+        ],
+        compiler_params=params(4),
+        name="face",
+    )(*[vmem(a) for a in (*state, hl, hr, zl, zr)])
+
+
+def send(out_s, out, sems, i, x):
+    return pltpu.make_async_copy(out_s.at[:, pl.ds(i, 1)], out.at[:, pl.ds(x, 1)], sems.at[i])
+
+
+def choose(lists, place):
+    gx, gz = lax.axis_index("gx"), lax.axis_index("gz")
+    half = lists[:, pl.ds(pl.multiple_of((gz // 4) * 128, 128), 128)]
+    tile = lax.broadcasted_iota(jnp.int32, (512, 128), 0)
+    listed = jnp.zeros((512, 128), F32)
+    for k in range(8):
+        listed = listed + jnp.where(half[k : k + 1] == tile, 1.0, 0.0)
+    row = lax.broadcasted_iota(jnp.int32, (128, 512), 0)
+    wanted = gx * 32 + ((row >> 4) ^ gz) * 4 + ((row >> 2) & 3)
+    sits = jnp.where(place[...] == wanted, 1.0, 0.0).astype(BF16)
+    count = jnp.dot(sits, listed.astype(BF16), preferred_element_type=F32)
+    row = lax.broadcasted_iota(jnp.int32, (128, 128), 0)
+    column = lanes((128, 128))
+    ours = jnp.where(row == (gz % 4) * 32 + (column >> 2), 1.0, 0.0).astype(BF16)
+    wide = jnp.dot(count.astype(BF16), ours, preferred_element_type=F32)
+    return jnp.where((row & 3) == (column & 3), wide, 0.0)
+
+
+def inner_kernel(
+    adj_s, visc_s, vel_s, centre, middle, lists, place, _, __,
+    mid_s, coef_s, out, chosen, msg_lo, msg_hi, out_s, sems, sems_x,
 ):
     moved = []
     for msg, q, t in ((msg_lo, 2, 1), (msg_hi, 16, 16)):
@@ -260,89 +315,95 @@
             moved.append((adj_s.at[c, pl.ds(q, 2), inside], msg.at[pl.ds(2 * c, 2)]))
             moved.append((vel_s.at[c, pl.ds(t, 1)], msg.at[pl.ds(6 + c, 1)]))
         moved.append((visc_s.at[pl.ds(q, 2), inside], msg.at[pl.ds(9, 2)]))
-    centre[0] = edge_centre(hl, hr)
     moved += [(centre, msg_lo.at[pl.ds(11, 1)]), (centre, msg_hi.at[pl.ds(11, 1)])]
-    moved = begin(moved, sems)
-    middle[...] = edge_middle(hl, hr, zl, zr)
-    for c in range(3):
-        mid_s[c, 0] = jnp.zeros((144, 128), F32)
-    for x in range(2):
+    moved = begin(moved, sems_x)
+
+    def first(x, carry):
         first_step(adj_s, visc_s, vel_s, mid_s, coef_s, centre.at[0], x, x)
-    own = jnp.where(place[0] == 0, 1.0, 0.0)
-
-    def store(c, rows, v):
-        face[c, rows, :] = v * own
-
-    second_step(mid_s, coef_s, middle, 0, store)
+        return carry
+
+    lax.fori_loop(2, 9, first, 0)
+
+    def second(x, carry):
+        def store(c, rows, v):
+            out_s[c, x - 2, rows, :] = v
+
+        second_step(mid_s, coef_s, middle, x, store)
+        send(out_s, out, sems, x - 2, x).start()
+        return carry
+
+    lax.fori_loop(2, 8, second, 0)
+    chosen[...] = choose(lists, place)
     for copy in moved:
         copy.wait()
-
-
-def face_call(place, state, hl, hr, zl, zr):
+    for i in range(6):
+        send(out_s, out, sems, i, i + 2).wait()
+
+
+FIELD = (3, 16, 128, 128)
+
+
+def inner(state, centre, middle, lists, place, mid, coef):
     msg = pltpu.HBM((12, 128, 128), F32)
     return pl.pallas_call(
-        face_kernel,
-        in_specs=[SM] + [VM] * 7,
-        out_specs=[VM] * 5 + [ANY, ANY],
+        inner_kernel,
+        in_specs=[VM] * 9,
+        out_specs=[VM, VM, ANY, VM, ANY, ANY],
         out_shape=[
-            in_vmem((3, 128, 128)),
             in_vmem(STATE["mid"]),
             in_vmem(STATE["coef"]),
-            in_vmem((1, 128, 128)),
+            pltpu.HBM(FIELD, F32),
             in_vmem((128, 128)),
             msg,
             msg,
         ],
-        scratch_shapes=[pltpu.SemaphoreType.DMA((16,))],
-        compiler_params=params(4),
-        name="face",
-    )(place, *[vmem(a) for a in (*state, hl, hr, zl, zr)])
-
-
-def send(out_s, out, sems, i, x):
-    return pltpu.make_async_copy(out_s.at[:, pl.ds(i, 1)], out.at[:, pl.ds(x, 1)], sems.at[i])
-
-
-def inner_kernel(adj_s, visc_s, vel_s, centre, middle, _, __, mid_s, coef_s, out, out_s, sems):
+        scratch_shapes=[
+            pltpu.VMEM((3, 6, 128, 128), F32),
+            pltpu.SemaphoreType.DMA((6,)),
+            pltpu.SemaphoreType.DMA((16,)),
+        ],
+        input_output_aliases={7: 0, 8: 1},
+        compiler_params=params(5),
+        name="inner",
+    )(*[vmem(a) for a in (*state, centre, middle)], lists, place, vmem(mid), vmem(coef))
+
+
+def middle_kernel(adj_s, visc_s, vel_s, centre, middle, _, __, ___, mid_s, coef_s, out, out_s, sems):
     def first(x, carry):
         first_step(adj_s, visc_s, vel_s, mid_s, coef_s, centre.at[0], x, x)
         return carry
 
-    lax.fori_loop(2, 9, first, 0)
+    lax.fori_loop(9, 15, first, 0)
 
     def second(x, carry):
         def store(c, rows, v):
-            out_s[c, x - 2, rows, :] = v
+            out_s[c, x - 8, rows, :] = v
 
         second_step(mid_s, coef_s, middle, x, store)
-        send(out_s, out, sems, x - 2, x).start()
+        send(out_s, out, sems, x - 8, x).start()
         return carry
 
-    lax.fori_loop(2, 8, second, 0)
+    lax.fori_loop(8, 14, second, 0)
     for i in range(6):
-        send(out_s, out, sems, i, i + 2).wait()
-
-
-def inner(state, centre, middle, mid, coef):
-    return pl.pallas_call(
-        inner_kernel,
-        in_specs=[VM] * 7,
+        send(out_s, out, sems, i, i + 8).wait()
+
+
+def middle_call(state, centre, middle, mid, coef, out):
+    return pl.pallas_call(
+        middle_kernel,
+        in_specs=[VM] * 7 + [ANY],
         out_specs=[VM, VM, ANY],
-        out_shape=[
-            in_vmem(STATE["mid"]),
-            in_vmem(STATE["coef"]),
-            pltpu.HBM((3, 16, 128, 128), F32),
-        ],
+        out_shape=[in_vmem(STATE["mid"]), in_vmem(STATE["coef"]), pltpu.HBM(FIELD, F32)],
         scratch_shapes=[pltpu.VMEM((3, 6, 128, 128), F32), pltpu.SemaphoreType.DMA((6,))],
-        input_output_aliases={5: 0, 6: 1},
+        input_output_aliases={5: 0, 6: 1, 7: 2},
         compiler_params=params(4),
-        name="inner",
-    )(*[vmem(a) for a in (*state, centre, middle, mid, coef)])
+        name="middle",
+    )(*[vmem(a) for a in (*state, centre, middle, mid, coef)], hbm(out))
 
 
 def outer_kernel(
-    place, adj_i, visc_i, vel_i, mid_i, coef_i, centre, middle, hl, hr, zl, zr, low, high, _,
-    adj_s, visc_s, vel_s, mid_s, coef_s, out, out_s, corner, edges, sems, sems_o,
+    adj_i, visc_i, vel_i, mid_i, coef_i, centre, hl, hr, zl, zr, low, high, filters, _,
+    adj_s, visc_s, vel_s, mid_s, coef_s, out, kept, out_s, corner, edges, sems, sems_o, sem_f,
 ):
     inside = pl.ds(8, 128)
     pairs = [(low.at[pl.ds(11, 1)], corner.at[pl.ds(0, 1)])]
@@ -353,22 +414,7 @@
             pairs.append((msg.at[pl.ds(6 + c, 1)], vel_s.at[c, pl.ds(t, 1)]))
         pairs.append((msg.at[pl.ds(9, 2)], visc_s.at[pl.ds(q, 2), inside]))
     started = begin(pairs, sems)
-
-    def first(x, carry):
-        first_step(adj_s, visc_s, vel_s, mid_s, coef_s, centre.at[0], x, x)
-        return carry
-
-    lax.fori_loop(9, 15, first, 0)
-
-    def second(x, carry):
-        def store(c, rows, v):
-            out_s[c, x - 8, rows, :] = v
-
-        second_step(mid_s, coef_s, middle, x, store)
-        send(out_s, out, sems_o, x - 8, x).start()
-        return carry
-
-    lax.fori_loop(8, 14, second, 0)
+    fetched = begin([(filters, kept)], sem_f)
     for copy in started:
         copy.wait()
     edges[...] = edge_middle(hl, hr, zl, zr, corner[0], corner[1])
@@ -376,47 +422,70 @@
     first_step(adj_s, visc_s, vel_s, mid_s, coef_s, centre.at[0], 0, 0)
     first_step(adj_s, visc_s, vel_s, mid_s, coef_s, centre.at[0], 15, 15)
     first_step(adj_s, visc_s, vel_s, mid_s, coef_s, corner.at[1], 16, 0)
-
-    @pl.when(place[0] == 0)
+    gx = lax.axis_index("gx")
+
+    @pl.when(gx == 0)
     def _():
         for c in range(3):
             mid_s[c, 0] = jnp.zeros((144, 128), F32)
 
-    @pl.when(place[0] == place[1] - 1)
+    @pl.when(gx == lax.axis_size("gx") - 1)
     def _():
         for c in range(3):
             mid_s[c, 17] = jnp.zeros((144, 128), F32)
 
-    for i, x in ((6, 0), (7, 1), (8, 14), (9, 15)):
+    for i, x in enumerate((0, 1, 14, 15)):
 
         def store(c, rows, v, i=i):
             out_s[c, i, rows, :] = v
 
         second_step(mid_s, coef_s, edges, x, store)
         send(out_s, out, sems_o, i, x).start()
-    for i in range(10):
-        send(out_s, out, sems_o, i, i + 8 if i < 6 else (0, 1, 14, 15)[i - 6]).wait()
-
-
-def outer(place, state, mid, coef, centre, middle, hl, hr, zl, zr, low, high, out):
-    held = [vmem(a) for a in (*state, mid, coef, centre, middle, hl, hr, zl, zr)]
-    return pl.pallas_call(
+    for i, x in enumerate((0, 1, 14, 15)):
+        send(out_s, out, sems_o, i, x).wait()
+    for copy in fetched:
+        copy.wait()
+
+
+def outer(state, mid, coef, centre, hl, hr, zl, zr, low, high, filters, out):
+    held = [vmem(a) for a in (*state, mid, coef, centre, hl, hr, zl, zr)]
+    done = pl.pallas_call(
         outer_kernel,
-        in_specs=[SM] + [VM] * 11 + [ANY] * 3,
-        out_specs=[VM] * 5 + [ANY],
+        in_specs=[VM] * 10 + [ANY] * 4,
+        out_specs=[VM] * 5 + [ANY, VM],
         out_shape=[in_vmem(STATE[k]) for k in ("adj", "visc", "vel", "mid", "coef")]
-        + [pltpu.HBM((3, 16, 128, 128), F32)],
+        + [pltpu.HBM(FIELD, F32), pltpu.VMEM(filters.shape, BF16)],
         scratch_shapes=[
-            pltpu.VMEM((3, 10, 128, 128), F32),
+            pltpu.VMEM((3, 4, 128, 128), F32),
             pltpu.VMEM((2, 128, 128), F32),
             pltpu.VMEM((128, 128), F32),
             pltpu.SemaphoreType.DMA((16,)),
-            pltpu.SemaphoreType.DMA((10,)),
+            pltpu.SemaphoreType.DMA((4,)),
+            pltpu.SemaphoreType.DMA((1,)),
         ],
-        input_output_aliases={1: 0, 2: 1, 3: 2, 4: 3, 5: 4, 14: 5},
-        compiler_params=params(6),
+        input_output_aliases={0: 0, 1: 1, 2: 2, 3: 3, 4: 4, 13: 5},
+        compiler_params=params(4),
         name="outer",
-    )(place, *held, hbm(low), hbm(high), hbm(out))[-1]
+    )(*held, low, high, hbm(filters), hbm(out))
+    return done[5], done[6]
+
+
+def join_kernel(*refs):
+    total = refs[0][...]
+    for ref in refs[1:-1]:
+        total = total + ref[...]
+    refs[-1][...] = total
+
+
+def join(*parts):
+    return pl.pallas_call(
+        join_kernel,
+        in_specs=[VM] * len(parts),
+        out_specs=VM,
+        out_shape=in_vmem(parts[0].shape),
+        compiler_params=params(2),
+        name="join",
+    )(*[vmem(a) for a in parts])
 
 
 def pieces(a):
@@ -427,89 +496,103 @@
     return high, mid, low
 
 
-def sums_kernel(place, places, face, more, out):
-    row = lax.broadcasted_iota(jnp.int32, (128, 128), 0)
-    column = lanes((128, 128))
-    wanted = (row >> 2) + place[0] * 32
-    count = jnp.zeros((128, 128), F32)
-    for k in range(8):
-        count = count + jnp.where(places[pl.ds(k, 1), :] == wanted, 1.0, 0.0)
-    chosen = jnp.where((row & 3) == (column & 3), count, 0.0).astype(BF16)
+PART = (3, 16, 128)
+
+
+def sums_kernel(chosen, face, more, kept, given):
+    matrix = chosen[...].astype(BF16)
     for c in range(3):
         total = 0.0
         for piece in pieces(face[c] + more[c]):
-            total = total + jnp.dot(chosen, piece, preferred_element_type=F32)
-        for g in range(8):
-            out[g, c] = total[g * 16 : g * 16 + 16]
-
-
-def partial_sums(place, places, face, more):
+            total = total + jnp.dot(matrix, piece, preferred_element_type=F32)
+        for k in range(8):
+            (given if k % 2 else kept)[k // 2, c] = total[k * 16 : k * 16 + 16]
+
+
+def partial_sums(chosen, face, more):
     return pl.pallas_call(
         sums_kernel,
-        in_specs=[SM, VM, VM, VM],
-        out_specs=VM,
-        out_shape=jax.ShapeDtypeStruct((8, 3, 16, 128), F32),
-        compiler_params=params(4),
+        in_specs=[VM] * 3,
+        out_specs=[VM, VM],
+        out_shape=[in_vmem((4, *PART))] * 2,
+        compiler_params=params(2),
         name="sums",
-    )(place, places, face, more)
-
-
-def product_kernel(parts, filters, out, sums):
-    total = parts[0]
-    for g in range(1, 8):
-        total = total + parts[g]
-    sums[...] = total
+    )(vmem(chosen), vmem(face), vmem(more))
+
+
+def halve_kernel(kept, came, still, given):
+    for k in range(kept.shape[0]):
+        (given if k % 2 else still)[k // 2] = kept[k] + came[k]
+
+
+def halve(kept, came):
+    return pl.pallas_call(
+        halve_kernel,
+        in_specs=[VM] * 2,
+        out_specs=[VM, VM],
+        out_shape=[in_vmem((kept.shape[0] // 2, *PART))] * 2,
+        compiler_params=params(2),
+        name="halve",
+    )(vmem(kept), vmem(came))
+
+
+def product_kernel(kept, came, filters, out, sums):
+    sums[...] = kept[0] + came[0]
     for p in range(4):
         view = jnp.concatenate([sums[:, p * 4 + i, :] for i in range(4)], axis=1)
         stacked = jnp.concatenate(pieces(view), axis=0)
         wide = jnp.dot(stacked, filters[p], preferred_element_type=F32)
-        out[p] = wide[0:3] + (wide[3:6] + wide[6:9])
-
-
-def product(parts, filters):
+        out[:, p, :] = wide[0:3] + (wide[3:6] + wide[6:9])
+
+
+def product(kept, came, filters):
     return pl.pallas_call(
         product_kernel,
-        in_specs=[VM, VM],
+        in_specs=[VM] * 3,
         out_specs=VM,
-        out_shape=jax.ShapeDtypeStruct((4, 3, 512), F32),
-        scratch_shapes=[pltpu.VMEM((3, 16, 128), F32)],
+        out_shape=jax.ShapeDtypeStruct((3, 4, 512), F32),
+        scratch_shapes=[pltpu.VMEM(PART, F32)],
         compiler_params=params(4),
         name="product",
-    )(parts, filters)
+    )(vmem(kept), vmem(came), vmem(filters))
 
 
 def shards(adjoint, velocity, viscosity, filters, block_tiles, tile_place):
-    gx = lax.axis_index("gx")
-    gz = lax.axis_index("gz")
     nx = lax.axis_size("gx")
     nz = lax.axis_size("gz")
     ring = [(i, (i + 1) % nz) for i in range(nz)]
     back = [(b, a) for a, b in ring]
     along = [(i, i + 1) for i in range(nx - 1)]
     against = [(b, a) for a, b in along]
-    place = jnp.stack([gx, jnp.int32(nx)]).astype(jnp.int32)
 
     *state, zl, zr = pack(adjoint, velocity, viscosity)
     hl = lax.ppermute(zl, "gz", ring)
     hr = lax.ppermute(zr, "gz", back)
-
-    lists = lax.dynamic_slice_in_dim(block_tiles, gz * 32, 32, 0)
-    tiles = jnp.arange(512, dtype=jnp.int32)
-    places = jnp.sum(jnp.where(lists[:, :, None] == tiles, tile_place, 0), axis=2)
-    places = jnp.repeat(places.T, 4, axis=1)
-
-    face, mid, coef, centre, middle, msg_lo, msg_hi = face_call(place, state, hl, hr, zl, zr)
+    face, mid, coef, centre, middle = face_call(state, hl, hr, zl, zr)
+
     got = [lax.ppermute(face, "gx", [(0, k)]) for k in (8, 2, 6)]
+    mid, coef, out, chosen, msg_lo, msg_hi = inner(
+        state, centre, middle, block_tiles.T, tile_place.reshape(1, -1), mid, coef
+    )
+    *got, mid, coef, out, chosen = lax.optimization_barrier((*got, mid, coef, out, chosen))
+    face = join(face, *got)
+    far = lax.ppermute(face, "gx", [(0, 4), (2, 10), (6, 14), (8, 12)])
     low = lax.ppermute(msg_hi, "gx", along)
     high = lax.ppermute(msg_lo, "gx", against)
-    face = (face + got[0]) + (got[1] + got[2])
-    far = lax.ppermute(face, "gx", [(0, 4), (2, 10), (6, 14), (8, 12)])
-    mid, coef, out = inner(state, centre, middle, mid, coef)
-    face = face + far
+    face = join(face, far)
     other = lax.ppermute(face, "gx", [(i, i + 1) for i in range(0, nx, 2)])
-    parts = lax.all_to_all(partial_sums(place, places, face, other), "gz", 0, 0)
-    out = outer(place, state, mid, coef, centre, middle, hl, hr, zl, zr, low, high, out)
-    gradient = product(parts, filters)
+    kept, given = partial_sums(chosen, face, other)
+
+    came = lax.ppermute(given, "gz", [(i, i ^ 1) for i in range(nz)])
+    mid, coef, out = middle_call(state, centre, middle, mid, coef, out)
+    came, mid, coef, out = lax.optimization_barrier((came, mid, coef, out))
+    kept, given = halve(kept, came)
+    came = lax.ppermute(given, "gz", [(i, i ^ 2) for i in range(nz)])
+    out, near = outer(state, mid, coef, centre, hl, hr, zl, zr, low, high, filters, out)
+    came, out = lax.optimization_barrier((came, out))
+    kept, given = halve(kept, came)
+    came = lax.ppermute(given, "gz", [(i, i ^ 4) for i in range(nz)])
+    gradient = product(kept, came, near).transpose(1, 0, 2)
     return out, gradient
 
 

time: 118 us -> 66.2 us (0.56)
  the two profiles are of different devices: /device:TPU:24 before, /device:TPU:20 now
where the time goes in v3:
time: 66.2 us; the launch traced here: 66 us
  waiting for transfers between devices  23.6 us (36%)
  Pallas kernels  20.9 us (32%)
  starting transfers between devices  20.6 us (31%)
  between operations  0.8 us (1%)
    ppermute x1, waiting for transfers between devices, shards(): far = lax.ppermute(face, 'gx', [(0, 4), (2, 10), (6, 14), (8, 12)])  16.1 us
    pallas_call x1, Pallas kernels, outer(): pl.pallas_call(outer_kernel, in_specs=[VM] * 10 + [ANY] * 4, out_specs=[V...  4.9 us
    pallas_call x1, Pallas kernels, pack(): pl.pallas_call(pack_kernel, in_specs=[ANY, ANY, ANY], out_specs=[VM] * 5,...  4.75 us
    pallas_call x1, Pallas kernels, inner(): pl.pallas_call(inner_kernel, in_specs=[VM] * 9, out_specs=[VM, VM, ANY, V...  4.33 us
    pallas_call x1, Pallas kernels, middle_call(): pl.pallas_call(middle_kernel, in_specs=[VM] * 7 + [ANY], out_specs=[VM, V...  3.88 us
    ppermute x1, starting transfers between devices, shards(): high = lax.ppermute(msg_lo, 'gx', against)  3.64 us
    ppermute x1, starting transfers between devices, shards(): hr = lax.ppermute(zr, 'gz', back)  3.55 us
    ppermute x1, waiting for transfers between devices, shards(): hl = lax.ppermute(zl, 'gz', ring)  3.41 us
  transfers between devices with their start and end apart: 12, of which 5 were waited for; matrix products, arithmetic and copies ran while one was open for 0% of the time, Pallas kernels for 14%

profile of v3, /device:TPU:20, one launch (start us, length us, event | category | flops | bytes accessed | tf_op | source)
XLA Modules:
  0.0 66.0 jit_solution(2146543396062965403)
XLA Ops:
  0.6 4.8 %pack.1 = (f32[3,20,144,128]{3,2,1,0:T(8,128)S(1)}, f32[20,144,128]{2,1,0:T(8,128)S(1)}, f32[3,18,128,128]{3,2,1,0:T(8,128)S(1)}, f32[192,128]{1,0:T(8,128)S(1)}, f32[192,128]{1,0:T(8,128)S(1)}) custom-call(f32[3,16,128,128]{3,2,1,0:T(8,128)} %adj.1, f32[3,16,128,128]{3,2,1,0:T(8,128)} %vel.1, f32[16,128,128]{2,1,0:T(8,128)} %visc.1), custom_call_target="tpu_custom_call" | custom-call | tf_op jit(solution)/shard_map/pack/pallas_call | solution.py:118
  5.4 1.4 %collective-permute-start = (f32[192,128]{1,0:T(8,128)S(1)}, f32[192,128]{1,0:T(8,128)S(1)}, u32[]{:S(2)}, u32[]{:S(2)}) collective-permute-start(f32[192,128]{1,0:T(8,128)S(1)} %get-tuple-element.45.zl), channel_id=1, source_target_pairs={{0,1},{1,2},{2,3},{3,4},{4,5},{5,6},{6,7},{7,0},{8,9},{9,10},{10,1... | collective-permute-start | bytes 294920 | tf_op jit(solution)/shard_map/ppermute | solution.py:569
  6.7 3.6 %collective-permute-start.1 = (f32[192,128]{1,0:T(8,128)S(1)}, f32[192,128]{1,0:T(8,128)S(1)}, u32[]{:S(2)}, u32[]{:S(2)}) collective-permute-start(f32[192,128]{1,0:T(8,128)S(1)} %get-tuple-element.46.zr), channel_id=1, source_target_pairs={{1,0},{2,1},{3,2},{4,3},{5,4},{6,5},{7,6},{0,7},{9,8},{10,9},{11,1... | collective-permute-start | bytes 294920 | tf_op jit(solution)/shard_map/ppermute | solution.py:570
  10.3 3.4 %collective-permute-done.hl = f32[192,128]{1,0:T(8,128)S(1)} collective-permute-done((f32[192,128]{1,0:T(8,128)S(1)}, f32[192,128]{1,0:T(8,128)S(1)}, u32[]{:S(2)}, u32[]{:S(2)}) %collective-permute-start) | collective-permute-done | bytes 98336 | tf_op jit(solution)/shard_map/ppermute | solution.py:569
  13.7 1.7 %face.1 = (f32[3,128,128]{2,1,0:T(8,128)S(1)}, f32[3,18,144,128]{3,2,1,0:T(8,128)S(1)}, f32[7,18,128,128]{3,2,1,0:T(8,128)S(1)}, f32[1,128,128]{2,1,0:T(8,128)S(1)}, f32[128,128]{1,0:T(8,128)S(1)}) custom-call(f32[3,20,144,128]{3,2,1,0:T(8,128)S(1)} %get-tuple-element.42.adj_s.adj_i, f32[20,144,128]{2,1,0:T(8,128)S(1)} %get-tuple-element.43.visc_s.visc_i, ...), custom_call_target="tpu_custom_call" | custom-call | tf_op jit(solution)/shard_map/face/pallas_call | solution.py:269
  15.4 4.3 %inner.1 = (f32[3,18,144,128]{3,2,1,0:T(8,128)S(1)}, f32[7,18,128,128]{3,2,1,0:T(8,128)S(1)}, f32[3,16,128,128]{3,2,1,0:T(8,128)}, f32[128,128]{1,0:T(8,128)S(1)...) custom-call(f32[3,20,144,128]{3,2,1,0:T(8,128)S(1)} %get-tuple-element.42.adj_s., ...), custom_call_target="tpu_custom_call", output_to_operand_aliasing={{0}: (7, {}), {1}: (8, {})} | custom-call | tf_op jit(solution)/shard_map/inner/pallas_call | solution.py:348
  19.8 1.9 %collective-permute-start.9 = (f32[12,128,128]{2,1,0:T(8,128)}, f32[12,128,128]{2,1,0:T(8,128)S(1)}, u32[]{:S(2)}, u32[]{:S(2)}) collective-permute-start(f32[12,128,128]{2,1,0:T(8,128)} %get-tuple-element.72), channel_id=1, source_target_pairs={{0,8},{8,16},{16,24},{24,32},{32,40},{40,48},{48,56},{56,64},{64,7... | collective-permute-start | bytes 2359304 | tf_op jit(solution)/shard_map/ppermute | solution.py:580
  21.7 3.6 %collective-permute-start.10 = (f32[12,128,128]{2,1,0:T(8,128)}, f32[12,128,128]{2,1,0:T(8,128)S(1)}, u32[]{:S(2)}, u32[]{:S(2)}) collective-permute-start(f32[12,128,128]{2,1,0:T(8,128)} %get-tuple-element.73), channel_id=1, source_target_pairs={{8,0},{16,8},{24,16},{32,24},{40,32},{48,40},{56,48},{64,56},{72,6... | collective-permute-start | bytes 2359304 | tf_op jit(solution)/shard_map/ppermute | solution.py:581
  25.4 0.7 %collective-permute-start.4 = (f32[3,128,128]{2,1,0:T(8,128)S(1)}, f32[3,128,128]{2,1,0:T(8,128)S(1)}, u32[]{:S(2)}, u32[]{:S(2)}) collective-permute-start(f32[3,128,128]{2,1,0:T(8,128)S(1)} %get-tuple-element.47.refs_0_), channel_id=1, source_target_pairs={{0,48},{1,49},{2,50},{3,51},{4,52},{5,53},{6,54},{7,55}} | collective-permute-start | bytes 589832 | tf_op jit(solution)/shard_map/ppermute | solution.py:573
  26.0 0.7 %collective-permute-start.3 = (f32[3,128,128]{2,1,0:T(8,128)S(1)}, f32[3,128,128]{2,1,0:T(8,128)S(1)}, u32[]{:S(2)}, u32[]{:S(2)}) collective-permute-start(f32[3,128,128]{2,1,0:T(8,128)S(1)} %get-tuple-element.47.refs_0_), channel_id=1, source_target_pairs={{0,16},{1,17},{2,18},{3,19},{4,20},{5,21},{6,22},{7,23}} | collective-permute-start | bytes 589832 | tf_op jit(solution)/shard_map/ppermute | solution.py:573
  26.7 0.7 %collective-permute-start.2 = (f32[3,128,128]{2,1,0:T(8,128)S(1)}, f32[3,128,128]{2,1,0:T(8,128)S(1)}, u32[]{:S(2)}, u32[]{:S(2)}) collective-permute-start(f32[3,128,128]{2,1,0:T(8,128)S(1)} %get-tuple-element.47.refs_0_), channel_id=1, source_target_pairs={{0,64},{1,65},{2,66},{3,67},{4,68},{5,69},{6,70},{7,71}} | collective-permute-start | bytes 589832 | tf_op jit(solution)/shard_map/ppermute | solution.py:573
  27.5 1.3 %collective-permute-start.5 = (f32[3,128,128]{2,1,0:T(8,128)S(1)}, f32[3,128,128]{2,1,0:T(8,128)S(1)}, u32[]{:S(2)}, u32[]{:S(2)}) collective-permute-start(f32[3,128,128]{2,1,0:T(8,128)S(1)} %join.2.refs_0_), channel_id=1, source_target_pairs={{0,32},{16,80},{48,112},{64,96},{1,33},{17,81},{49,113},{65,97},{2... | collective-permute-start | bytes 589832 | tf_op jit(solution)/shard_map/ppermute | solution.py:579
  28.8 16.1 %collective-permute-done.5.refs_1_ = f32[3,128,128]{2,1,0:T(8,128)S(1)} collective-permute-done((f32[3,128,128]{2,1,0:T(8,128)S(1)}, f32[3,128,128]{2,1,0:T(8,128)S(1)}, u32[]{:S(2)}, u32[]{:S(2)}) %collective-permute-start.5) | collective-permute-done | bytes 196640 | tf_op jit(solution)/shard_map/ppermute | solution.py:579
  44.9 1.3 %collective-permute-start.6 = (f32[3,128,128]{2,1,0:T(8,128)S(1)}, f32[3,128,128]{2,1,0:T(8,128)S(1)}, u32[]{:S(2)}, u32[]{:S(2)}) collective-permute-start(f32[3,128,128]{2,1,0:T(8,128)S(1)} %join.3.face), channel_id=1, source_target_pairs={{0,8},{16,24},{32,40},{48,56},{64,72},{80,88},{96,104},{112,120},{... | collective-permute-start | bytes 589832 | tf_op jit(solution)/shard_map/ppermute | solution.py:583
  46.2 1.0 %collective-permute-done.6.more = f32[3,128,128]{2,1,0:T(8,128)S(1)} collective-permute-done((f32[3,128,128]{2,1,0:T(8,128)S(1)}, f32[3,128,128]{2,1,0:T(8,128)S(1)}, u32[]{:S(2)}, u32[]{:S(2)}) %collective-permute-start.6) | collective-permute-done | bytes 196640 | tf_op jit(solution)/shard_map/ppermute | solution.py:583
  47.3 0.2 sums.1
  47.5 1.2 %collective-permute-start.7 = (f32[4,3,16,128]{3,2,1,0:T(8,128)S(1)}, f32[4,3,16,128]{3,2,1,0:T(8,128)S(1)}, u32[]{:S(2)}, u32[]{:S(2)}) collective-permute-start(f32[4,3,16,128]{3,2,1,0:T(8,128)S(1)} %get-tuple-element.61), channel_id=1, source_target_pairs={{0,1},{1,0},{2,3},{3,2},{4,5},{5,4},{6,7},{7,6},{8,9},{9,8},{10,11... | collective-permute-start | bytes 294920 | tf_op jit(solution)/shard_map/ppermute | solution.py:586
  48.7 3.9 %middle.1 = (f32[3,18,144,128]{3,2,1,0:T(8,128)S(1)}, f32[7,18,128,128]{3,2,1,0:T(8,128)S(1)}, f32[3,16,128,128]{3,2,1,0:T(8,128)}) custom-call(f32[3,20,144,128]{3,2,1,0:T(8,128)S(1)} %get-tuple-element.42.adj_s.adj_i, f32[20,144,128]{2,1,0:T(8,128)S(1)} %get-tuple-element.43.visc_s.visc_i, ...), custom_call_target="tpu_custom_call", output_to_operand_aliasing={{0}: (5, {}), {1}: (6, {}), {2}: (7, {})} | custom-call | tf_op jit(solution)/shard_map/middle/pallas_call | solution.py:392
  52.6 0.1 collective-permute-done.7.came
  52.7 1.9 %collective-permute-start.8 = (f32[2,3,16,128]{3,2,1,0:T(8,128)S(1)}, f32[2,3,16,128]{3,2,1,0:T(8,128)S(1)}, u32[]{:S(2)}, u32[]{:S(2)}) collective-permute-start(f32[2,3,16,128]{3,2,1,0:T(8,128)S(1)} %get-tuple-element.69), channel_id=1, source_target_pairs={{0,2},{1,3},{2,0},{3,1},{4,6},{5,7},{6,4},{7,5},{8,10},{9,11},{10,... | collective-permute-start | bytes 147464 | tf_op jit(solution)/shard_map/ppermute | solution.py:590
  54.6 4.9 %outer.1 = (f32[3,20,144,128]{3,2,1,0:T(8,128)S(1)}, f32[20,144,128]{2,1,0:T(8,128)S(1)}, f32[3,18,128,128]{3,2,1,0:T(8,128)S(1)}, f32[3,18,144,128]{3,2,1,0:T(8...) custom-call(f32[3,20,144,128]{3,2,1,0:T(8,128)S(1)} %get-tuple-eleme, ...), custom_call_target="tpu_custom_call", output_to_operand_aliasing={{0}: (0, {}), {1}: (1, {}), {2}: (2, {}), {3}: (3, {}), {4}... | custom-call | tf_op jit(solution)/shard_map/outer/pallas_call | solution.py:452
  59.6 2.4 %collective-permute-start.11 = (f32[1,3,16,128]{3,2,1,0:T(8,128)S(1)}, f32[1,3,16,128]{3,2,1,0:T(8,128)S(1)}, u32[]{:S(2)}, u32[]{:S(2)}) collective-permute-start(f32[1,3,16,128]{3,2,1,0:T(8,128)S(1)} %get-tuple-element.80), channel_id=1, source_target_pairs={{0,4},{1,5},{2,6},{3,7},{4,0},{5,1},{6,2},{7,3},{8,12},{9,13},{10,... | collective-permute-start | bytes 73736 | tf_op jit(solution)/shard_map/ppermute | solution.py:594
  62.0 3.0 %collective-permute-done.11.came = f32[1,3,16,128]{3,2,1,0:T(8,128)S(1)} collective-permute-done((f32[1,3,16,128]{3,2,1,0:T(8,128)S(1)}, f32[1,3,16,128]{3,2,1,0:T(8,128)S(1)}, u32[]{:S(2)}, u32[]{:S(2)}) %collective-permute-start.11) | collective-permute-done | bytes 24608 | tf_op jit(solution)/shard_map/ppermute | solution.py:594
  65.0 1.0 %product.1 = f32[3,4,512]{2,1,0:T(4,128)} custom-call(f32[1,3,16,128]{3,2,1,0:T(8,128)S(1)} %get-tuple-element.79.kept, f32[1,3,16,128]{3,2,1,0:T(8,128)S(1)} %collective-permute-done.11.came, bf16[4,512,512]{2,1,0:T(8,128)(2,1)S(1)} %get-tuple-element.81.filters), custom_call_target="tpu_custom_call" | custom-call | tf_op jit(solution)/shard_map/product/pallas_call | solution.py:549
  (15 shorter events, 0.1 us)
Async XLA Ops:
  5.4 8.3 %collective-permute-start = (f32[192,128]{1,0:T(8,128)S(1)}, f32[192,128]{1,0:T(8,128)S(1)}, u32[]{:S(2)}, u32[]{:S(2)}) collective-permute-start(f32[192,128]{1,0:T(8,128)S(1)} %get-tuple-element.45.zl), channel_id=1, source_target_pairs={{0,1},{1,2},{2,3},{3,4},{4,5},{5,6},{6,7},{7,0},{8,9},{9,10},{10,1... | collective-permute-start | bytes 294920 | tf_op jit(solution)/shard_map/ppermute | solution.py:569
  6.7 7.0 %collective-permute-start.1 = (f32[192,128]{1,0:T(8,128)S(1)}, f32[192,128]{1,0:T(8,128)S(1)}, u32[]{:S(2)}, u32[]{:S(2)}) collective-permute-start(f32[192,128]{1,0:T(8,128)S(1)} %get-tuple-element.46.zr), channel_id=1, source_target_pairs={{1,0},{2,1},{3,2},{4,3},{5,4},{6,5},{7,6},{0,7},{9,8},{10,9},{11,1... | collective-permute-start | bytes 294920 | tf_op jit(solution)/shard_map/ppermute | solution.py:570
  13.7 1.7 %copy-start = (s32[256,8]{0,1:T(8,128)S(1)}, s32[256,8]{0,1:T(8,128)}, u32[]{:S(2)}) copy-start(s32[256,8]{0,1:T(8,128)} %param.10) | copy-start | bytes 24580
  13.7 1.7 %copy-start.1 = (s32[512]{0:T(512)S(1)}, s32[512]{0:T(512)}, u32[]{:S(2)}) copy-start(s32[512]{0:T(512)} %param.11) | copy-start | bytes 6148
  19.8 34.9 %collective-permute-start.9 = (f32[12,128,128]{2,1,0:T(8,128)}, f32[12,128,128]{2,1,0:T(8,128)S(1)}, u32[]{:S(2)}, u32[]{:S(2)}) collective-permute-start(f32[12,128,128]{2,1,0:T(8,128)} %get-tuple-element.72), channel_id=1, source_target_pairs={{0,8},{8,16},{16,24},{24,32},{32,40},{40,48},{48,56},{56,64},{64,7... | collective-permute-start | bytes 2359304 | tf_op jit(solution)/shard_map/ppermute | solution.py:580
  21.7 32.9 %collective-permute-start.10 = (f32[12,128,128]{2,1,0:T(8,128)}, f32[12,128,128]{2,1,0:T(8,128)S(1)}, u32[]{:S(2)}, u32[]{:S(2)}) collective-permute-start(f32[12,128,128]{2,1,0:T(8,128)} %get-tuple-element.73), channel_id=1, source_target_pairs={{8,0},{16,8},{24,16},{32,24},{40,32},{48,40},{56,48},{64,56},{72,6... | collective-permute-start | bytes 2359304 | tf_op jit(solution)/shard_map/ppermute | solution.py:581
  25.4 2.0 %collective-permute-start.4 = (f32[3,128,128]{2,1,0:T(8,128)S(1)}, f32[3,128,128]{2,1,0:T(8,128)S(1)}, u32[]{:S(2)}, u32[]{:S(2)}) collective-permute-start(f32[3,128,128]{2,1,0:T(8,128)S(1)} %get-tuple-element.47.refs_0_), channel_id=1, source_target_pairs={{0,48},{1,49},{2,50},{3,51},{4,52},{5,53},{6,54},{7,55}} | collective-permute-start | bytes 589832 | tf_op jit(solution)/shard_map/ppermute | solution.py:573
  26.0 1.4 %collective-permute-start.3 = (f32[3,128,128]{2,1,0:T(8,128)S(1)}, f32[3,128,128]{2,1,0:T(8,128)S(1)}, u32[]{:S(2)}, u32[]{:S(2)}) collective-permute-start(f32[3,128,128]{2,1,0:T(8,128)S(1)} %get-tuple-element.47.refs_0_), channel_id=1, source_target_pairs={{0,16},{1,17},{2,18},{3,19},{4,20},{5,21},{6,22},{7,23}} | collective-permute-start | bytes 589832 | tf_op jit(solution)/shard_map/ppermute | solution.py:573
  26.7 0.7 %collective-permute-start.2 = (f32[3,128,128]{2,1,0:T(8,128)S(1)}, f32[3,128,128]{2,1,0:T(8,128)S(1)}, u32[]{:S(2)}, u32[]{:S(2)}) collective-permute-start(f32[3,128,128]{2,1,0:T(8,128)S(1)} %get-tuple-element.47.refs_0_), channel_id=1, source_target_pairs={{0,64},{1,65},{2,66},{3,67},{4,68},{5,69},{6,70},{7,71}} | collective-permute-start | bytes 589832 | tf_op jit(solution)/shard_map/ppermute | solution.py:573
  27.5 17.4 %collective-permute-start.5 = (f32[3,128,128]{2,1,0:T(8,128)S(1)}, f32[3,128,128]{2,1,0:T(8,128)S(1)}, u32[]{:S(2)}, u32[]{:S(2)}) collective-permute-start(f32[3,128,128]{2,1,0:T(8,128)S(1)} %join.2.refs_0_), channel_id=1, source_target_pairs={{0,32},{16,80},{48,112},{64,96},{1,33},{17,81},{49,113},{65,97},{2... | collective-permute-start | bytes 589832 | tf_op jit(solution)/shard_map/ppermute | solution.py:579
  44.9 2.4 %collective-permute-start.6 = (f32[3,128,128]{2,1,0:T(8,128)S(1)}, f32[3,128,128]{2,1,0:T(8,128)S(1)}, u32[]{:S(2)}, u32[]{:S(2)}) collective-permute-start(f32[3,128,128]{2,1,0:T(8,128)S(1)} %join.3.face), channel_id=1, source_target_pairs={{0,8},{16,24},{32,40},{48,56},{64,72},{80,88},{96,104},{112,120},{... | collective-permute-start | bytes 589832 | tf_op jit(solution)/shard_map/ppermute | solution.py:583
  47.5 5.2 %collective-permute-start.7 = (f32[4,3,16,128]{3,2,1,0:T(8,128)S(1)}, f32[4,3,16,128]{3,2,1,0:T(8,128)S(1)}, u32[]{:S(2)}, u32[]{:S(2)}) collective-permute-start(f32[4,3,16,128]{3,2,1,0:T(8,128)S(1)} %get-tuple-element.61), channel_id=1, source_target_pairs={{0,1},{1,0},{2,3},{3,2},{4,5},{5,4},{6,7},{7,6},{8,9},{9,8},{10,11... | collective-permute-start | bytes 294920 | tf_op jit(solution)/shard_map/ppermute | solution.py:586
  52.7 6.9 %collective-permute-start.8 = (f32[2,3,16,128]{3,2,1,0:T(8,128)S(1)}, f32[2,3,16,128]{3,2,1,0:T(8,128)S(1)}, u32[]{:S(2)}, u32[]{:S(2)}) collective-permute-start(f32[2,3,16,128]{3,2,1,0:T(8,128)S(1)} %get-tuple-element.69), channel_id=1, source_target_pairs={{0,2},{1,3},{2,0},{3,1},{4,6},{5,7},{6,4},{7,5},{8,10},{9,11},{10,... | collective-permute-start | bytes 147464 | tf_op jit(solution)/shard_map/ppermute | solution.py:590
  59.6 5.4 %collective-permute-start.11 = (f32[1,3,16,128]{3,2,1,0:T(8,128)S(1)}, f32[1,3,16,128]{3,2,1,0:T(8,128)S(1)}, u32[]{:S(2)}, u32[]{:S(2)}) collective-permute-start(f32[1,3,16,128]{3,2,1,0:T(8,128)S(1)} %get-tuple-element.80), channel_id=1, source_target_pairs={{0,4},{1,5},{2,6},{3,7},{4,0},{5,1},{6,2},{7,3},{8,12},{9,13},{10,... | collective-permute-start | bytes 73736 | tf_op jit(solution)/shard_map/ppermute | solution.py:594

commit v4 on v3

--- a/solution.py
+++ b/solution.py
@@ -1,3 +1,5 @@
+import functools
+
 import functools
 
 import jax
@@ -36,6 +38,10 @@
     "mid": (3, 18, 144, 128),
     "coef": (7, 18, 128, 128),
 }
+
+
+def cost(planes):
+    return pl.CostEstimate(flops=planes * 3 * 16384 * 20, transcendentals=0, bytes_accessed=planes * 16384 * 4 * 22)
 
 
 def params(mib):
@@ -278,6 +284,7 @@
             in_vmem((128, 128)),
         ],
         compiler_params=params(4),
+        cost_estimate=cost(3),
         name="face",
     )(*[vmem(a) for a in (*state, hl, hr, zl, zr)])
 
@@ -364,6 +371,7 @@
         ],
         input_output_aliases={7: 0, 8: 1},
         compiler_params=params(5),
+        cost_estimate=cost(13),
         name="inner",
     )(*[vmem(a) for a in (*state, centre, middle)], lists, place, vmem(mid), vmem(coef))
 
@@ -397,77 +405,77 @@
         scratch_shapes=[pltpu.VMEM((3, 6, 128, 128), F32), pltpu.SemaphoreType.DMA((6,))],
         input_output_aliases={5: 0, 6: 1, 7: 2},
         compiler_params=params(4),
+        cost_estimate=cost(12),
         name="middle",
     )(*[vmem(a) for a in (*state, centre, middle, mid, coef)], hbm(out))
 
 
-def outer_kernel(
-    adj_i, visc_i, vel_i, mid_i, coef_i, centre, hl, hr, zl, zr, low, high, filters, _,
+def side_kernel(
+    high, adj_i, visc_i, vel_i, mid_i, coef_i, centre, hl, hr, zl, zr, message, filters, _,
     adj_s, visc_s, vel_s, mid_s, coef_s, out, kept, out_s, corner, edges, sems, sems_o, sem_f,
 ):
     inside = pl.ds(8, 128)
-    pairs = [(low.at[pl.ds(11, 1)], corner.at[pl.ds(0, 1)])]
-    pairs += [(high.at[pl.ds(11, 1)], corner.at[pl.ds(1, 1)])]
-    for msg, q, t in ((low, 0, 0), (high, 18, 17)):
-        for c in range(3):
-            pairs.append((msg.at[pl.ds(2 * c, 2)], adj_s.at[c, pl.ds(q, 2), inside]))
-            pairs.append((msg.at[pl.ds(6 + c, 1)], vel_s.at[c, pl.ds(t, 1)]))
-        pairs.append((msg.at[pl.ds(9, 2)], visc_s.at[pl.ds(q, 2), inside]))
+    q, t = (18, 17) if high else (0, 0)
+    pairs = [(message.at[pl.ds(11, 1)], corner)]
+    for c in range(3):
+        pairs.append((message.at[pl.ds(2 * c, 2)], adj_s.at[c, pl.ds(q, 2), inside]))
+        pairs.append((message.at[pl.ds(6 + c, 1)], vel_s.at[c, pl.ds(t, 1)]))
+    pairs.append((message.at[pl.ds(9, 2)], visc_s.at[pl.ds(q, 2), inside]))
     started = begin(pairs, sems)
-    fetched = begin([(filters, kept)], sem_f)
-    for copy in started:
+    fetched = [] if high else begin([(filters, kept)], sem_f)
+    started[0].wait()
+    beside = (None, corner[0]) if high else (corner[0], None)
+    edges[...] = edge_middle(hl, hr, zl, zr, *beside)
+    for copy in started[1:]:
         copy.wait()
-    edges[...] = edge_middle(hl, hr, zl, zr, corner[0], corner[1])
-    first_step(adj_s, visc_s, vel_s, mid_s, coef_s, corner.at[0], -1, 15)
-    first_step(adj_s, visc_s, vel_s, mid_s, coef_s, centre.at[0], 0, 0)
-    first_step(adj_s, visc_s, vel_s, mid_s, coef_s, centre.at[0], 15, 15)
-    first_step(adj_s, visc_s, vel_s, mid_s, coef_s, corner.at[1], 16, 0)
-    gx = lax.axis_index("gx")
-
-    @pl.when(gx == 0)
+    if high:
+        first_step(adj_s, visc_s, vel_s, mid_s, coef_s, centre.at[0], 15, 15)
+        first_step(adj_s, visc_s, vel_s, mid_s, coef_s, corner.at[0], 16, 0)
+    else:
+        first_step(adj_s, visc_s, vel_s, mid_s, coef_s, centre.at[0], 0, 0)
+        first_step(adj_s, visc_s, vel_s, mid_s, coef_s, corner.at[0], -1, 15)
+
+    @pl.when(lax.axis_index("gx") == (lax.axis_size("gx") - 1 if high else 0))
     def _():
         for c in range(3):
-            mid_s[c, 0] = jnp.zeros((144, 128), F32)
-
-    @pl.when(gx == lax.axis_size("gx") - 1)
-    def _():
-        for c in range(3):
-            mid_s[c, 17] = jnp.zeros((144, 128), F32)
-
-    for i, x in enumerate((0, 1, 14, 15)):
+            mid_s[c, t] = jnp.zeros((144, 128), F32)
+
+    cells = (14, 15) if high else (1, 0)
+    for i, x in enumerate(cells):
 
         def store(c, rows, v, i=i):
             out_s[c, i, rows, :] = v
 
         second_step(mid_s, coef_s, edges, x, store)
         send(out_s, out, sems_o, i, x).start()
-    for i, x in enumerate((0, 1, 14, 15)):
+    for i, x in enumerate(cells):
         send(out_s, out, sems_o, i, x).wait()
     for copy in fetched:
         copy.wait()
 
 
-def outer(state, mid, coef, centre, hl, hr, zl, zr, low, high, filters, out):
+def side_call(high, state, mid, coef, centre, hl, hr, zl, zr, message, filters, out):
     held = [vmem(a) for a in (*state, mid, coef, centre, hl, hr, zl, zr)]
     done = pl.pallas_call(
-        outer_kernel,
-        in_specs=[VM] * 10 + [ANY] * 4,
+        functools.partial(side_kernel, high),
+        in_specs=[VM] * 10 + [ANY] * 3,
         out_specs=[VM] * 5 + [ANY, VM],
         out_shape=[in_vmem(STATE[k]) for k in ("adj", "visc", "vel", "mid", "coef")]
-        + [pltpu.HBM(FIELD, F32), pltpu.VMEM(filters.shape, BF16)],
+        + [pltpu.HBM(FIELD, F32), pltpu.VMEM((8, 128) if high else filters.shape, BF16)],
         scratch_shapes=[
-            pltpu.VMEM((3, 4, 128, 128), F32),
-            pltpu.VMEM((2, 128, 128), F32),
+            pltpu.VMEM((3, 2, 128, 128), F32),
+            pltpu.VMEM((1, 128, 128), F32),
             pltpu.VMEM((128, 128), F32),
-            pltpu.SemaphoreType.DMA((16,)),
-            pltpu.SemaphoreType.DMA((4,)),
+            pltpu.SemaphoreType.DMA((8,)),
+            pltpu.SemaphoreType.DMA((2,)),
             pltpu.SemaphoreType.DMA((1,)),
         ],
-        input_output_aliases={0: 0, 1: 1, 2: 2, 3: 3, 4: 4, 13: 5},
+        input_output_aliases={0: 0, 1: 1, 2: 2, 3: 3, 4: 4, 12: 5},
         compiler_params=params(4),
-        name="outer",
-    )(*held, low, high, hbm(filters), hbm(out))
-    return done[5], done[6]
+        cost_estimate=cost(4),
+        name="side",
+    )(*held, message, hbm(filters), hbm(out))
+    return done[:3], done[3], done[4], done[5], done[6]
 
 
 def join_kernel(*refs):
@@ -574,8 +582,11 @@
     mid, coef, out, chosen, msg_lo, msg_hi = inner(
         state, centre, middle, block_tiles.T, tile_place.reshape(1, -1), mid, coef
     )
-    *got, mid, coef, out, chosen = lax.optimization_barrier((*got, mid, coef, out, chosen))
+    *got, mid, coef, out, msg_lo, msg_hi = lax.optimization_barrier(
+        (*got, mid, coef, out, msg_lo, msg_hi)
+    )
     face = join(face, *got)
+    face, msg_lo, msg_hi = lax.optimization_barrier((face, msg_lo, msg_hi))
     far = lax.ppermute(face, "gx", [(0, 4), (2, 10), (6, 14), (8, 12)])
     low = lax.ppermute(msg_hi, "gx", along)
     high = lax.ppermute(msg_lo, "gx", against)
@@ -588,10 +599,14 @@
     came, mid, coef, out = lax.optimization_barrier((came, mid, coef, out))
     kept, given = halve(kept, came)
     came = lax.ppermute(given, "gz", [(i, i ^ 2) for i in range(nz)])
-    out, near = outer(state, mid, coef, centre, hl, hr, zl, zr, low, high, filters, out)
-    came, out = lax.optimization_barrier((came, out))
+    state, mid, coef, out, near = side_call(
+        False, state, mid, coef, centre, hl, hr, zl, zr, low, filters, out
+    )
+    came, mid, out = lax.optimization_barrier((came, mid, out))
     kept, given = halve(kept, came)
     came = lax.ppermute(given, "gz", [(i, i ^ 4) for i in range(nz)])
+    *_, out, _ = side_call(True, state, mid, coef, centre, hl, hr, zl, zr, high, filters, out)
+    came, out = lax.optimization_barrier((came, out))
     gradient = product(kept, came, near).transpose(1, 0, 2)
     return out, gradient
 

time: 66.2 us -> 63.1 us (0.953)
  the two profiles are of different devices: /device:TPU:20 before, /device:TPU:22 now
where the time goes in v4:
time: 63.1 us; the launch traced here: 62.9 us
  Pallas kernels  23.3 us (37%)
  starting transfers between devices  20.7 us (33%)
  waiting for transfers between devices  18 us (29%)
  between operations  0.82 us (1%)
    ppermute x1, waiting for transfers between devices, shards(): far = lax.ppermute(face, 'gx', [(0, 4), (2, 10), (6, 14), (8, 12)])  7.77 us
    pallas_call x2, Pallas kernels, side_call(): pl.pallas_call(functools.partial(side_kernel, high), in_specs=[VM] * 10 +...  7.27 us
    ppermute x1, waiting for transfers between devices, shards(): came = lax.ppermute(given, 'gz', [(i, i ^ 1) for i in range(nz)])  5.76 us
    pallas_call x1, Pallas kernels, pack(): pl.pallas_call(pack_kernel, in_specs=[ANY, ANY, ANY], out_specs=[VM] * 5,...  4.75 us
    pallas_call x1, Pallas kernels, inner(): pl.pallas_call(inner_kernel, in_specs=[VM] * 9, out_specs=[VM, VM, ANY, V...  4.33 us
    pallas_call x1, Pallas kernels, middle_call(): pl.pallas_call(middle_kernel, in_specs=[VM] * 7 + [ANY], out_specs=[VM, V...  3.88 us
    ppermute x1, starting transfers between devices, shards(): high = lax.ppermute(msg_lo, 'gx', against)  3.64 us
    ppermute x1, starting transfers between devices, shards(): hr = lax.ppermute(zr, 'gz', back)  3.55 us
  transfers between devices with their start and end apart: 12, of which 4 were waited for; matrix products, arithmetic and copies ran while one was open for 0% of the time, Pallas kernels for 25%

profile of v4, /device:TPU:22, one launch (start us, length us, event | category | flops | bytes accessed | tf_op | source)
XLA Modules:
  0.0 62.9 jit_solution(17197830275936999082)
XLA Ops:
  0.6 4.8 %pack.1 = (f32[3,20,144,128]{3,2,1,0:T(8,128)S(1)}, f32[20,144,128]{2,1,0:T(8,128)S(1)}, f32[3,18,128,128]{3,2,1,0:T(8,128)S(1)}, f32[192,128]{1,0:T(8,128)S(1)}, f32[192,128]{1,0:T(8,128)S(1)}) custom-call(f32[3,16,128,128]{3,2,1,0:T(8,128)} %adj.1, f32[3,16,128,128]{3,2,1,0:T(8,128)} %vel.1, f32[16,128,128]{2,1,0:T(8,128)} %visc.1), custom_call_target="tpu_custom_call" | custom-call | tf_op jit(solution)/shard_map/pack/pallas_call | solution.py:124
  5.4 1.4 %collective-permute-start = (f32[192,128]{1,0:T(8,128)S(1)}, f32[192,128]{1,0:T(8,128)S(1)}, u32[]{:S(2)}, u32[]{:S(2)}) collective-permute-start(f32[192,128]{1,0:T(8,128)S(1)} %get-tuple-element.58.zl), channel_id=1, source_target_pairs={{0,1},{1,2},{2,3},{3,4},{4,5},{5,6},{6,7},{7,0},{8,9},{9,10},{10,1... | collective-permute-start | bytes 294920 | tf_op jit(solution)/shard_map/ppermute | solution.py:577
  6.7 3.6 %collective-permute-start.1 = (f32[192,128]{1,0:T(8,128)S(1)}, f32[192,128]{1,0:T(8,128)S(1)}, u32[]{:S(2)}, u32[]{:S(2)}) collective-permute-start(f32[192,128]{1,0:T(8,128)S(1)} %get-tuple-element.59.zr), channel_id=1, source_target_pairs={{1,0},{2,1},{3,2},{4,3},{5,4},{6,5},{7,6},{0,7},{9,8},{10,9},{11,1... | collective-permute-start | bytes 294920 | tf_op jit(solution)/shard_map/ppermute | solution.py:578
  10.3 3.4 %collective-permute-done.hl = f32[192,128]{1,0:T(8,128)S(1)} collective-permute-done((f32[192,128]{1,0:T(8,128)S(1)}, f32[192,128]{1,0:T(8,128)S(1)}, u32[]{:S(2)}, u32[]{:S(2)}) %collective-permute-start) | collective-permute-done | bytes 98336 | tf_op jit(solution)/shard_map/ppermute | solution.py:577
  13.7 1.7 %face.1 = (f32[3,128,128]{2,1,0:T(8,128)S(1)}, f32[3,18,144,128]{3,2,1,0:T(8,128)S(1)}, f32[7,18,128,128]{3,2,1,0:T(8,128)S(1)}, f32[1,128,128]{2,1,0:T(8,128)S(1)}, f32[128,128]{1,0:T(8,128)S(1)}) custom-call(f32[3,20,144,128]{3,2,1,0:T(8,128)S(1)} %get-tuple-element.55.adj_s.adj_i, f32[20,144,128]{2,1,0:T(8,128)S(1)} %get-tuple-element.56.visc_s.visc_i, ...), custom_call_target="tpu_custom_call" | custom-call | flops 2949120 | bytes 4325376 | tf_op jit(solution)/shard_map/face/pallas_call | solution.py:275
  15.4 0.7 %collective-permute-start.4 = (f32[3,128,128]{2,1,0:T(8,128)S(1)}, f32[3,128,128]{2,1,0:T(8,128)S(1)}, u32[]{:S(2)}, u32[]{:S(2)}) collective-permute-start(f32[3,128,128]{2,1,0:T(8,128)S(1)} %get-tuple-element.65.refs_0_), channel_id=1, source_target_pairs={{0,48},{1,49},{2,50},{3,51},{4,52},{5,53},{6,54},{7,55}} | collective-permute-start | bytes 589832 | tf_op jit(solution)/shard_map/ppermute | solution.py:581
  16.1 0.7 %collective-permute-start.3 = (f32[3,128,128]{2,1,0:T(8,128)S(1)}, f32[3,128,128]{2,1,0:T(8,128)S(1)}, u32[]{:S(2)}, u32[]{:S(2)}) collective-permute-start(f32[3,128,128]{2,1,0:T(8,128)S(1)} %get-tuple-element.65.refs_0_), channel_id=1, source_target_pairs={{0,16},{1,17},{2,18},{3,19},{4,20},{5,21},{6,22},{7,23}} | collective-permute-start | bytes 589832 | tf_op jit(solution)/shard_map/ppermute | solution.py:581
  16.8 0.7 %collective-permute-start.2 = (f32[3,128,128]{2,1,0:T(8,128)S(1)}, f32[3,128,128]{2,1,0:T(8,128)S(1)}, u32[]{:S(2)}, u32[]{:S(2)}) collective-permute-start(f32[3,128,128]{2,1,0:T(8,128)S(1)} %get-tuple-element.65.refs_0_), channel_id=1, source_target_pairs={{0,64},{1,65},{2,66},{3,67},{4,68},{5,69},{6,70},{7,71}} | collective-permute-start | bytes 589832 | tf_op jit(solution)/shard_map/ppermute | solution.py:581
  17.5 4.3 %inner.1 = (f32[3,18,144,128]{3,2,1,0:T(8,128)S(1)}, f32[7,18,128,128]{3,2,1,0:T(8,128)S(1)}, f32[3,16,128,128]{3,2,1,0:T(8,128)}, f32[128,128]{1,0:T(8,128)S(1)...) custom-call(f32[3,20,144,128]{3,2,1,0:T(8,128)S(1)} %get-tuple-element.55.adj_s., ...), custom_call_target="tpu_custom_call", output_to_operand_aliasing={{0}: (7, {}), {1}: (8, {})} | custom-call | flops 12779520 | bytes 18743296 | tf_op jit(solution)/shard_map/inner/pallas_call | solution.py:355
  21.9 1.9 %collective-permute-start.9 = (f32[12,128,128]{2,1,0:T(8,128)}, f32[12,128,128]{2,1,0:T(8,128)S(1)}, u32[]{:S(2)}, u32[]{:S(2)}) collective-permute-start(f32[12,128,128]{2,1,0:T(8,128)} %get-tuple-element.90), channel_id=1, source_target_pairs={{0,8},{8,16},{16,24},{24,32},{32,40},{40,48},{48,56},{56,64},{64,7... | collective-permute-start | bytes 2359304 | tf_op jit(solution)/shard_map/ppermute | solution.py:591
  23.9 3.6 %collective-permute-start.11 = (f32[12,128,128]{2,1,0:T(8,128)}, f32[12,128,128]{2,1,0:T(8,128)S(1)}, u32[]{:S(2)}, u32[]{:S(2)}) collective-permute-start(f32[12,128,128]{2,1,0:T(8,128)} %get-tuple-element.101), channel_id=1, source_target_pairs={{8,0},{16,8},{24,16},{32,24},{40,32},{48,40},{56,48},{64,56},{72,6... | collective-permute-start | bytes 2359304 | tf_op jit(solution)/shard_map/ppermute | solution.py:592
  27.5 1.3 %collective-permute-start.5 = (f32[3,128,128]{2,1,0:T(8,128)S(1)}, f32[3,128,128]{2,1,0:T(8,128)S(1)}, u32[]{:S(2)}, u32[]{:S(2)}) collective-permute-start(f32[3,128,128]{2,1,0:T(8,128)S(1)} %join.2.refs_0_), channel_id=1, source_target_pairs={{0,32},{16,80},{48,112},{64,96},{1,33},{17,81},{49,113},{65,97},{2... | collective-permute-start | bytes 589832 | tf_op jit(solution)/shard_map/ppermute | solution.py:590
  28.8 7.8 %collective-permute-done.5.refs_1_ = f32[3,128,128]{2,1,0:T(8,128)S(1)} collective-permute-done((f32[3,128,128]{2,1,0:T(8,128)S(1)}, f32[3,128,128]{2,1,0:T(8,128)S(1)}, u32[]{:S(2)}, u32[]{:S(2)}) %collective-permute-start.5) | collective-permute-done | bytes 196640 | tf_op jit(solution)/shard_map/ppermute | solution.py:590
  36.6 1.3 %collective-permute-start.6 = (f32[3,128,128]{2,1,0:T(8,128)S(1)}, f32[3,128,128]{2,1,0:T(8,128)S(1)}, u32[]{:S(2)}, u32[]{:S(2)}) collective-permute-start(f32[3,128,128]{2,1,0:T(8,128)S(1)} %join.3.face), channel_id=1, source_target_pairs={{0,8},{16,24},{32,40},{48,56},{64,72},{80,88},{96,104},{112,120},{... | collective-permute-start | bytes 589832 | tf_op jit(solution)/shard_map/ppermute | solution.py:594
  37.9 1.0 %collective-permute-done.6.more = f32[3,128,128]{2,1,0:T(8,128)S(1)} collective-permute-done((f32[3,128,128]{2,1,0:T(8,128)S(1)}, f32[3,128,128]{2,1,0:T(8,128)S(1)}, u32[]{:S(2)}, u32[]{:S(2)}) %collective-permute-start.6) | collective-permute-done | bytes 196640 | tf_op jit(solution)/shard_map/ppermute | solution.py:594
  38.9 0.2 sums.1
  39.2 1.2 %collective-permute-start.7 = (f32[4,3,16,128]{3,2,1,0:T(8,128)S(1)}, f32[4,3,16,128]{3,2,1,0:T(8,128)S(1)}, u32[]{:S(2)}, u32[]{:S(2)}) collective-permute-start(f32[4,3,16,128]{3,2,1,0:T(8,128)S(1)} %get-tuple-element.78), channel_id=1, source_target_pairs={{0,1},{1,0},{2,3},{3,2},{4,5},{5,4},{6,7},{7,6},{8,9},{9,8},{10,11... | collective-permute-start | bytes 294920 | tf_op jit(solution)/shard_map/ppermute | solution.py:597
  40.4 3.9 %middle.1 = (f32[3,18,144,128]{3,2,1,0:T(8,128)S(1)}, f32[7,18,128,128]{3,2,1,0:T(8,128)S(1)}, f32[3,16,128,128]{3,2,1,0:T(8,128)}) custom-call(f32[3,20,144,128]{3,2,1,0:T(8,128)S(1)} %get-tuple-element.55.adj_s.adj_i, f32[20,144,128]{2,1,0:T(8,128)S(1)} %get-tuple-element.56.visc_s.visc_i, ...), custom_call_target="tpu_custom_call", output_to_operand_aliasing={{0}: (5, {}), {1}: (6, {}), {2}: (7, {})} | custom-call | flops 11796480 | bytes 17301504 | tf_op jit(solution)/shard_map/middle/pallas_call | solution.py:400
  44.3 5.8 %collective-permute-done.7.came = f32[4,3,16,128]{3,2,1,0:T(8,128)S(1)} collective-permute-done((f32[4,3,16,128]{3,2,1,0:T(8,128)S(1)}, f32[4,3,16,128]{3,2,1,0:T(8,128)S(1)}, u32[]{:S(2)}, u32[]{:S(2)}) %collective-permute-start.7) | collective-permute-done | bytes 98336 | tf_op jit(solution)/shard_map/ppermute | solution.py:597
  50.1 2.0 %collective-permute-start.8 = (f32[2,3,16,128]{3,2,1,0:T(8,128)S(1)}, f32[2,3,16,128]{3,2,1,0:T(8,128)S(1)}, u32[]{:S(2)}, u32[]{:S(2)}) collective-permute-start(f32[2,3,16,128]{3,2,1,0:T(8,128)S(1)} %get-tuple-element.87), channel_id=1, source_target_pairs={{0,2},{1,3},{2,0},{3,1},{4,6},{5,7},{6,4},{7,5},{8,10},{9,11},{10,... | collective-permute-start | bytes 147464 | tf_op jit(solution)/shard_map/ppermute | solution.py:601
  52.1 3.3 %side.2 = (f32[3,20,144,128]{3,2,1,0:T(8,128)S(1)}, f32[20,144,128]{2,1,0:T(8,128)S(1)}, f32[3,18,128,128]{3,2,1,0:T(8,128)S(1)}, f32[3,18,144,128]{3,2,1,0:T(8,...) custom-call(f32[3,20,144,128]{3,2,1,0:T(8,128)S(1)} %get-tuple-eleme, ...), custom_call_target="tpu_custom_call", output_to_operand_aliasing={{0}: (0, {}), {1}: (1, {}), {2}: (2, {}), {3}: (3, {}), {4}... | custom-call | flops 3932160 | bytes 5767168 | tf_op jit(solution)/shard_map/side/pallas_call | solution.py:459
  55.4 2.5 %collective-permute-start.10 = (f32[1,3,16,128]{3,2,1,0:T(8,128)S(1)}, f32[1,3,16,128]{3,2,1,0:T(8,128)S(1)}, u32[]{:S(2)}, u32[]{:S(2)}) collective-permute-start(f32[1,3,16,128]{3,2,1,0:T(8,128)S(1)} %get-tuple-element.95), channel_id=1, source_target_pairs={{0,4},{1,5},{2,6},{3,7},{4,0},{5,1},{6,2},{7,3},{8,12},{9,13},{10,... | collective-permute-start | bytes 73736 | tf_op jit(solution)/shard_map/ppermute | solution.py:607
  57.9 3.9 %side.3 = (f32[3,20,144,128]{3,2,1,0:T(8,128)S(1)}, f32[20,144,128]{2,1,0:T(8,128)S(1)}, f32[3,18,128,128]{3,2,1,0:T(8,128)S(1)}, f32[3,18,144,128]{3,2,1,0:T(8,...) custom-call(f32[3,20,144,128]{3,2,1,0:T(8,128)S(1)} %get-tuple-eleme, ...), custom_call_target="tpu_custom_call", output_to_operand_aliasing={{0}: (0, {}), {1}: (1, {}), {2}: (2, {}), {3}: (3, {}), {4}... | custom-call | flops 3932160 | bytes 5767168 | tf_op jit(solution)/shard_map/side/pallas_call | solution.py:459
  61.9 1.0 %product.1 = f32[3,4,512]{2,1,0:T(4,128)} custom-call(f32[1,3,16,128]{3,2,1,0:T(8,128)S(1)} %get-tuple-element.105.kept, f32[1,3,16,128]{3,2,1,0:T(8,128)S(1)} %collective-permute-done.10.came, bf16[4,512,512]{2,1,0:T(8,128)(2,1)S(1)} %get-tuple-element.107.filters), custom_call_target="tpu_custom_call" | custom-call | tf_op jit(solution)/shard_map/product/pallas_call | solution.py:557
  (16 shorter events, 0.1 us)
Async XLA Ops:
  5.4 8.3 %collective-permute-start = (f32[192,128]{1,0:T(8,128)S(1)}, f32[192,128]{1,0:T(8,128)S(1)}, u32[]{:S(2)}, u32[]{:S(2)}) collective-permute-start(f32[192,128]{1,0:T(8,128)S(1)} %get-tuple-element.58.zl), channel_id=1, source_target_pairs={{0,1},{1,2},{2,3},{3,4},{4,5},{5,6},{6,7},{7,0},{8,9},{9,10},{10,1... | collective-permute-start | bytes 294920 | tf_op jit(solution)/shard_map/ppermute | solution.py:577
  6.7 7.0 %collective-permute-start.1 = (f32[192,128]{1,0:T(8,128)S(1)}, f32[192,128]{1,0:T(8,128)S(1)}, u32[]{:S(2)}, u32[]{:S(2)}) collective-permute-start(f32[192,128]{1,0:T(8,128)S(1)} %get-tuple-element.59.zr), channel_id=1, source_target_pairs={{1,0},{2,1},{3,2},{4,3},{5,4},{6,5},{7,6},{0,7},{9,8},{10,9},{11,1... | collective-permute-start | bytes 294920 | tf_op jit(solution)/shard_map/ppermute | solution.py:578
  13.7 3.8 %copy-start = (s32[256,8]{0,1:T(8,128)S(1)}, s32[256,8]{0,1:T(8,128)}, u32[]{:S(2)}) copy-start(s32[256,8]{0,1:T(8,128)} %param.10) | copy-start | bytes 24580
  13.7 3.8 %copy-start.1 = (s32[512]{0:T(512)S(1)}, s32[512]{0:T(512)}, u32[]{:S(2)}) copy-start(s32[512]{0:T(512)} %param.11) | copy-start | bytes 6148
  15.4 6.4 %collective-permute-start.4 = (f32[3,128,128]{2,1,0:T(8,128)S(1)}, f32[3,128,128]{2,1,0:T(8,128)S(1)}, u32[]{:S(2)}, u32[]{:S(2)}) collective-permute-start(f32[3,128,128]{2,1,0:T(8,128)S(1)} %get-tuple-element.65.refs_0_), channel_id=1, source_target_pairs={{0,48},{1,49},{2,50},{3,51},{4,52},{5,53},{6,54},{7,55}} | collective-permute-start | bytes 589832 | tf_op jit(solution)/shard_map/ppermute | solution.py:581
  16.1 5.7 %collective-permute-start.3 = (f32[3,128,128]{2,1,0:T(8,128)S(1)}, f32[3,128,128]{2,1,0:T(8,128)S(1)}, u32[]{:S(2)}, u32[]{:S(2)}) collective-permute-start(f32[3,128,128]{2,1,0:T(8,128)S(1)} %get-tuple-element.65.refs_0_), channel_id=1, source_target_pairs={{0,16},{1,17},{2,18},{3,19},{4,20},{5,21},{6,22},{7,23}} | collective-permute-start | bytes 589832 | tf_op jit(solution)/shard_map/ppermute | solution.py:581
  16.8 5.1 %collective-permute-start.2 = (f32[3,128,128]{2,1,0:T(8,128)S(1)}, f32[3,128,128]{2,1,0:T(8,128)S(1)}, u32[]{:S(2)}, u32[]{:S(2)}) collective-permute-start(f32[3,128,128]{2,1,0:T(8,128)S(1)} %get-tuple-element.65.refs_0_), channel_id=1, source_target_pairs={{0,64},{1,65},{2,66},{3,67},{4,68},{5,69},{6,70},{7,71}} | collective-permute-start | bytes 589832 | tf_op jit(solution)/shard_map/ppermute | solution.py:581
  21.9 30.1 %collective-permute-start.9 = (f32[12,128,128]{2,1,0:T(8,128)}, f32[12,128,128]{2,1,0:T(8,128)S(1)}, u32[]{:S(2)}, u32[]{:S(2)}) collective-permute-start(f32[12,128,128]{2,1,0:T(8,128)} %get-tuple-element.90), channel_id=1, source_target_pairs={{0,8},{8,16},{16,24},{24,32},{32,40},{40,48},{48,56},{56,64},{64,7... | collective-permute-start | bytes 2359304 | tf_op jit(solution)/shard_map/ppermute | solution.py:591
  23.9 34.1 %collective-permute-start.11 = (f32[12,128,128]{2,1,0:T(8,128)}, f32[12,128,128]{2,1,0:T(8,128)S(1)}, u32[]{:S(2)}, u32[]{:S(2)}) collective-permute-start(f32[12,128,128]{2,1,0:T(8,128)} %get-tuple-element.101), channel_id=1, source_target_pairs={{8,0},{16,8},{24,16},{32,24},{40,32},{48,40},{56,48},{64,56},{72,6... | collective-permute-start | bytes 2359304 | tf_op jit(solution)/shard_map/ppermute | solution.py:592
  27.5 9.1 %collective-permute-start.5 = (f32[3,128,128]{2,1,0:T(8,128)S(1)}, f32[3,128,128]{2,1,0:T(8,128)S(1)}, u32[]{:S(2)}, u32[]{:S(2)}) collective-permute-start(f32[3,128,128]{2,1,0:T(8,128)S(1)} %join.2.refs_0_), channel_id=1, source_target_pairs={{0,32},{16,80},{48,112},{64,96},{1,33},{17,81},{49,113},{65,97},{2... | collective-permute-start | bytes 589832 | tf_op jit(solution)/shard_map/ppermute | solution.py:590
  36.6 2.4 %collective-permute-start.6 = (f32[3,128,128]{2,1,0:T(8,128)S(1)}, f32[3,128,128]{2,1,0:T(8,128)S(1)}, u32[]{:S(2)}, u32[]{:S(2)}) collective-permute-start(f32[3,128,128]{2,1,0:T(8,128)S(1)} %join.3.face), channel_id=1, source_target_pairs={{0,8},{16,24},{32,40},{48,56},{64,72},{80,88},{96,104},{112,120},{... | collective-permute-start | bytes 589832 | tf_op jit(solution)/shard_map/ppermute | solution.py:594
  39.2 10.9 %collective-permute-start.7 = (f32[4,3,16,128]{3,2,1,0:T(8,128)S(1)}, f32[4,3,16,128]{3,2,1,0:T(8,128)S(1)}, u32[]{:S(2)}, u32[]{:S(2)}) collective-permute-start(f32[4,3,16,128]{3,2,1,0:T(8,128)S(1)} %get-tuple-element.78), channel_id=1, source_target_pairs={{0,1},{1,0},{2,3},{3,2},{4,5},{5,4},{6,7},{7,6},{8,9},{9,8},{10,11... | collective-permute-start | bytes 294920 | tf_op jit(solution)/shard_map/ppermute | solution.py:597
  50.1 5.4 %collective-permute-start.8 = (f32[2,3,16,128]{3,2,1,0:T(8,128)S(1)}, f32[2,3,16,128]{3,2,1,0:T(8,128)S(1)}, u32[]{:S(2)}, u32[]{:S(2)}) collective-permute-start(f32[2,3,16,128]{3,2,1,0:T(8,128)S(1)} %get-tuple-element.87), channel_id=1, source_target_pairs={{0,2},{1,3},{2,0},{3,1},{4,6},{5,7},{6,4},{7,5},{8,10},{9,11},{10,... | collective-permute-start | bytes 147464 | tf_op jit(solution)/shard_map/ppermute | solution.py:601
  55.4 6.4 %collective-permute-start.10 = (f32[1,3,16,128]{3,2,1,0:T(8,128)S(1)}, f32[1,3,16,128]{3,2,1,0:T(8,128)S(1)}, u32[]{:S(2)}, u32[]{:S(2)}) collective-permute-start(f32[1,3,16,128]{3,2,1,0:T(8,128)S(1)} %get-tuple-element.95), channel_id=1, source_target_pairs={{0,4},{1,5},{2,6},{3,7},{4,0},{5,1},{6,2},{7,3},{8,12},{9,13},{10,... | collective-permute-start | bytes 73736 | tf_op jit(solution)/shard_map/ppermute | solution.py:607

commit v5 on v3

v5 whole, which is shorter than its diff:
```python
import jax
import jax.numpy as jnp
from jax import lax
from jax.experimental import pallas as pl
from jax.experimental.pallas import tpu as pltpu
from jax.sharding import PartitionSpec as P

F32 = jnp.float32
BF16 = jnp.bfloat16
ANY = pl.BlockSpec(memory_space=pl.ANY)
VM = pl.BlockSpec(memory_space=pltpu.VMEM)
MIB = 1024 * 1024
ROWS = 16
GROUPS = 4


def lanes(shape):
    return lax.broadcasted_iota(jnp.int32, shape, len(shape) - 1)


def roll(x, shift, axis):
    if isinstance(shift, int):
        shift = shift % x.shape[axis]
    return pltpu.roll(x, shift, axis)


def in_vmem(shape):
    return pltpu.VMEM(shape, F32)


STATE = {
    "adj": (3, 20, 144, 128),
    "visc": (20, 144, 128),
    "vel": (3, 18, 128, 128),
    "mid": (3, 18, 144, 128),
    "coef": (7, 18, 128, 128),
}


def cost(planes):
    return pl.CostEstimate(flops=planes * 3 * 16384 * 20, transcendentals=0, bytes_accessed=planes * 16384 * 4 * 22)


def params(mib):
    return pltpu.CompilerParams(vmem_limit_bytes=mib * MIB)


def hbm(x):
    return pltpu.with_memory_space_constraint(x, pltpu.HBM)


def vmem(x):
    return pltpu.with_memory_space_constraint(x, pltpu.VMEM)


def clear_walls(ref, lead):
    for index in lead:
        ref[(*index, pl.ds(0, 8), slice(None))] = jnp.zeros((8, 128), F32)
        ref[(*index, pl.ds(136, 8), slice(None))] = jnp.zeros((8, 128), F32)


def begin(copies, sems):
    started = [pltpu.make_async_copy(s, t, sems.at[i]) for i, (s, t) in enumerate(copies)]
    for copy in started:
        copy.start()
    return started


def pack_kernel(adj, vel, visc, adj_s, visc_s, vel_s, zl, zr, acc_l, acc_r, vel_l, vel_r, sems):
    inside = pl.ds(8, 128)
    n = 16 // GROUPS

    def copies(g):
        xs = pl.ds(g * n, n)
        return (
            (adj.at[:, xs], adj_s.at[:, pl.ds(2 + g * n, n), inside]),
            (visc.at[xs], visc_s.at[pl.ds(2 + g * n, n), inside]),
            (vel.at[:, xs], vel_s.at[:, pl.ds(1 + g * n, n)]),
        )

    started = [begin(copies(g), sems.at[g]) for g in range(GROUPS)]
    clear_walls(adj_s, [(c, q) for c in range(3) for q in range(1, 20)])
    clear_walls(visc_s, [(q,) for q in range(1, 20)])
    zero = jnp.zeros((144, 128), F32)
    visc_s[1] = zero
    for c in range(3):
        adj_s[c, 1] = zero
    lane = lanes((32, 128))
    pair = lane >> 1
    pair_l = ((lane + 2) & 127) >> 1
    for g in range(GROUPS):
        for copy in started[g]:
            copy.wait()
        for r in range(4):
            rows = pl.ds(r * 32, 32)
            padded = pl.ds(8 + r * 32, 32)
            half = r // 2
            if g == 0:
                left = right = vleft = vright = jnp.zeros((32, 128), F32)
            else:
                left, right, vleft, vright = (ref[rows] for ref in (acc_l, acc_r, vel_l, vel_r))
            for c in range(4):
                for x in range(g * n, g * n + n):
                    m = c * 16 + x
                    plane = adj_s[c, x + 2, padded] if c < 3 else visc_s[x + 2, padded]
                    turned = roll(plane, 2 * m, 1)
                    right = jnp.where(pair == m, turned, right)
                    left = jnp.where(pair_l == m, turned, left)
            for d in range(3):
                for x in range(g * n, g * n + n):
                    at = 2 * (d * 16 + x) + half
                    turned = roll(vel_s[d, x + 1, rows], at, 1)
                    vright = jnp.where(lane == at, turned, vright)
                    vleft = jnp.where(lane == (at - 1) % 128, turned, vleft)
            if g < GROUPS - 1:
                acc_l[rows] = left
                acc_r[rows] = right
            else:
                zr[rows] = right
                zl[rows] = roll(left, 2, 1)
                vleft = roll(vleft, 1, 1)
            vel_l[rows] = vleft
            vel_r[rows] = vright
    even = (lanes((64, 128)) & 1) == 0
    zr[pl.ds(128, 64)] = jnp.where(even, vel_r[pl.ds(0, 64)], vel_r[pl.ds(64, 64)])
    zl[pl.ds(128, 64)] = jnp.where(even, vel_l[pl.ds(0, 64)], vel_l[pl.ds(64, 64)])


def pack(adj, vel, visc):
    return pl.pallas_call(
        pack_kernel,
        in_specs=[ANY, ANY, ANY],
        out_specs=[VM] * 5,
        out_shape=[in_vmem(STATE[k]) for k in ("adj", "visc", "vel")] + [in_vmem((192, 128))] * 2,
        scratch_shapes=[
            *[pltpu.VMEM((128, 128), F32)] * 4,
            pltpu.SemaphoreType.DMA((GROUPS, 3)),
        ],
        compiler_params=params(4),
        name="pack",
    )(hbm(adj), hbm(vel), hbm(visc))


def spread(a, group):
    kept = jnp.where((lanes(a.shape) >> 5) == group, a, 0.0)
    kept = kept + roll(kept, 32, 1)
    return kept + roll(kept, 64, 1)


def shift_rows(a, by):
    row = lax.broadcasted_iota(jnp.int32, a.shape, 0)
    moved = roll(a, by, 0)
    edge = 0 if by > 0 else a.shape[0] - 1
    return jnp.where(row == edge, 0.0, moved)


def edge_centre(hl, hr):
    odd = (lanes((128, 128)) & 1) == 1
    return jnp.where(odd, hl[pl.ds(0, 128)], hr[pl.ds(0, 128)])


def edge_velocity(message):
    both = message[pl.ds(128, 64)]
    odd = (lanes(both.shape) & 1) == 1
    upper = jnp.where(odd, roll(both, 1, 1), both)
    lower = jnp.where(odd, both, roll(both, -1, 1))
    return jnp.concatenate([upper, lower], axis=0)


def edge_middle(hl, hr, zl, zr, low=None, high=None):
    lane = lanes((128, 128))
    odd = (lane & 1) == 1
    x = (lane >> 1) & 15
    first = pl.ds(0, 128)
    left, right = hl[first], hr[first]
    centre = jnp.where(odd, left, right)
    minus = jnp.where(odd, roll(left, 1, 1), roll(zl[first], -1, 1))
    plus = jnp.where(odd, roll(zr[first], 1, 1), roll(right, -1, 1))
    velocity = jnp.where(odd, edge_velocity(hl), edge_velocity(hr))
    west = roll(centre, 2, 1)
    east = roll(centre, -2, 1)
    west = jnp.where(x == 0, 0.0 if low is None else roll(low, -30, 1), west)
    east = jnp.where(x == 15, 0.0 if high is None else roll(high, 30, 1), east)
    north = shift_rows(centre, -1)
    south = shift_rows(centre, 1)
    visc = spread(centre, 3)
    total = 0.0
    result = 0.0
    for d, (up, down) in enumerate(((east, west), (north, south), (plus, minus))):
        v = spread(velocity, d)
        a_up = 0.5 * ((visc + spread(up, 3)) + v)
        a_down = 0.5 * ((visc + spread(down, 3)) - v)
        total = total + (a_up + a_down)
        result = result + (a_up * up + a_down * down)
    return result + (1.0 - total) * centre


def ends(edge, r, m):
    return roll(edge[pl.ds(r, ROWS), :], 127 - 2 * m, 1)


def first_step(adj_s, visc_s, vel_s, mid_s, coef_s, edge, x, ex):
    lane = lanes((ROWS, 128))
    q, t = x + 2, x + 1
    for r in range(0, 128, ROWS):
        rows, here = pl.ds(r, ROWS), pl.ds(8 + r, ROWS)
        above, below = pl.ds(9 + r, ROWS), pl.ds(7 + r, ROWS)

        def sides(plane, m):
            end = ends(edge, r, m)
            up = jnp.where(lane == 127, end, roll(plane, -1, 1))
            return up, jnp.where(lane == 0, end, roll(plane, 1, 1))

        centre = visc_s[q, here, :]
        pairs = (
            (visc_s[q + 1, here, :], visc_s[q - 1, here, :]),
            (visc_s[q, above, :], visc_s[q, below, :]),
            sides(centre, 48 + ex),
        )
        a = []
        for d, (plus, minus) in enumerate(pairs):
            v = vel_s[d, t, rows, :]
            a.append(0.5 * ((centre + plus) + v))
            a.append(0.5 * ((centre + minus) - v))
        a.append(1.0 - (((a[0] + a[1]) + (a[2] + a[3])) + (a[4] + a[5])))
        for k in range(7):
            coef_s[k, t, rows, :] = a[k]
        for c in range(3):
            centre = adj_s[c, q, here, :]
            up, down = sides(centre, c * 16 + ex)
            out = a[6] * centre
            out = out + a[0] * adj_s[c, q + 1, here, :]
            out = out + a[1] * adj_s[c, q - 1, here, :]
            out = out + a[2] * adj_s[c, q, above, :]
            out = out + a[3] * adj_s[c, q, below, :]
            out = out + a[4] * up
            mid_s[c, t, here, :] = out + a[5] * down
    for c in range(3):
        mid_s[c, t, pl.ds(0, 8), :] = jnp.zeros((8, 128), F32)
        mid_s[c, t, pl.ds(136, 8), :] = jnp.zeros((8, 128), F32)


def second_step(mid_s, coef_s, edge, x, store):
    lane = lanes((ROWS, 128))
    t = x + 1
    for r in range(0, 128, ROWS):
        rows, here = pl.ds(r, ROWS), pl.ds(8 + r, ROWS)
        above, below = pl.ds(9 + r, ROWS), pl.ds(7 + r, ROWS)
        a = [coef_s[k, t, rows, :] for k in range(7)]
        for c in range(3):
            centre = mid_s[c, t, here, :]
            end = ends(edge, r, c * 16 + x)
            out = a[6] * centre
            out = out + a[0] * mid_s[c, t + 1, here, :]
            out = out + a[1] * mid_s[c, t - 1, here, :]
            out = out + a[2] * mid_s[c, t, above, :]
            out = out + a[3] * mid_s[c, t, below, :]
            out = out + a[4] * jnp.where(lane == 127, end, roll(centre, -1, 1))
            store(c, rows, out + a[5] * jnp.where(lane == 0, end, roll(centre, 1, 1)))


def face_kernel(
    adj_s, visc_s, vel_s, hl, hr, zl, zr, face, mid_s, coef_s, centre, middle
):
    centre[...] = edge_centre(hl, hr)
    middle[...] = edge_middle(hl, hr, zl, zr)
    for c in range(3):
        mid_s[c, 0] = jnp.zeros((144, 128), F32)
    for x in range(2):
        first_step(adj_s, visc_s, vel_s, mid_s, coef_s, centre, x, x)
    own = jnp.where(lax.axis_index("gx") == 0, 1.0, 0.0)

    def store(c, rows, v):
        face[c, rows, :] = v * own

    second_step(mid_s, coef_s, middle, 0, store)


def face_call(state, hl, hr, zl, zr):
    return pl.pallas_call(
        face_kernel,
        in_specs=[VM] * 7,
        out_specs=[VM] * 5,
        out_shape=[
            in_vmem((3, 128, 128)),
            in_vmem(STATE["mid"]),
            in_vmem(STATE["coef"]),
            in_vmem((128, 128)),
            in_vmem((128, 128)),
        ],
        compiler_params=params(4),
        cost_estimate=cost(3),
        name="face",
    )(*[vmem(a) for a in (*state, hl, hr, zl, zr)])


def ship_kernel(adj_s, visc_s, vel_s, _, msg_lo, msg_hi, sems):
    moved = []
    inside = pl.ds(8, 128)
    for msg, q, t in ((msg_lo, 2, 1), (msg_hi, 16, 16)):
        for c in range(3):
            moved.append((adj_s.at[c, pl.ds(q, 2), inside], msg.at[pl.ds(2 * c, 2)]))
            moved.append((vel_s.at[c, pl.ds(t, 1)], msg.at[pl.ds(6 + c, 1)]))
        moved.append((visc_s.at[pl.ds(q, 2), inside], msg.at[pl.ds(9, 2)]))
    for copy in begin(moved, sems):
        copy.wait()


def ship(state, after):
    msg = pltpu.HBM((11, 128, 128), F32)
    return pl.pallas_call(
        ship_kernel,
        in_specs=[VM] * 4,
        out_specs=[ANY, ANY],
        out_shape=[msg, msg],
        scratch_shapes=[pltpu.SemaphoreType.DMA((14,))],
        compiler_params=params(1),
        cost_estimate=pl.CostEstimate(flops=0, transcendentals=0, bytes_accessed=2 * 2 * 11 * 65536),
        name="ship",
    )(*[vmem(a) for a in (*state, after)])


def choose(lists, place):
    gx, gz = lax.axis_index("gx"), lax.axis_index("gz")
    half = lists[:, pl.ds(pl.multiple_of((gz // 4) * 128, 128), 128)]
    tile = lax.broadcasted_iota(jnp.int32, (512, 128), 0)
    listed = jnp.zeros((512, 128), F32)
    for k in range(8):
        listed = listed + jnp.where(half[k : k + 1] == tile, 1.0, 0.0)
    row = lax.broadcasted_iota(jnp.int32, (128, 512), 0)
    wanted = gx * 32 + ((row >> 4) ^ gz) * 4 + ((row >> 2) & 3)
    sits = jnp.where(place[...] == wanted, 1.0, 0.0).astype(BF16)
    count = jnp.dot(sits, listed.astype(BF16), preferred_element_type=F32)
    row = lax.broadcasted_iota(jnp.int32, (128, 128), 0)
    column = lanes((128, 128))
    ours = jnp.where(row == (gz % 4) * 32 + (column >> 2), 1.0, 0.0).astype(BF16)
    wide = jnp.dot(count.astype(BF16), ours, preferred_element_type=F32)
    return jnp.where((row & 3) == (column & 3), wide, 0.0)


FIELD = (3, 16, 128, 128)


def run_first(cells, state, mid_s, coef_s, edge):
    for x in cells:
        first_step(*state, mid_s, coef_s, edge, x, x)


def run_second(cells, mid_s, coef_s, edge, done):
    for x in cells:

        def store(c, rows, v, x=x):
            done[c, x, rows, :] = v

        second_step(mid_s, coef_s, edge, x, store)


def inner_kernel(
    adj_s, visc_s, vel_s, centre, middle, lists, place, _, __, mid_s, coef_s, done, chosen, corner
):
    corner[...] = centre[...]
    chosen[...] = choose(lists, place)
    run_first(range(2, 9), (adj_s, visc_s, vel_s), mid_s, coef_s, centre)
    run_second(range(2, 8), mid_s, coef_s, middle, done)


def inner(state, centre, middle, lists, place, mid, coef):
    return pl.pallas_call(
        inner_kernel,
        in_specs=[VM] * 9,
        out_specs=[VM] * 5,
        out_shape=[
            in_vmem(STATE["mid"]),
            in_vmem(STATE["coef"]),
            in_vmem(FIELD),
            in_vmem((128, 128)),
            in_vmem((128, 128)),
        ],
        input_output_aliases={7: 0, 8: 1},
        compiler_params=params(4),
        cost_estimate=cost(13),
        name="inner",
    )(*[vmem(a) for a in (*state, centre, middle)], lists, place, vmem(mid), vmem(coef))


def middle_kernel(
    adj_i, visc_i, vel_i, centre, middle, _, __, ___, low, high, filters,
    adj_s, visc_s, vel_s, mid_s, coef_s, done, out, kept, sems, sem_o, sem_f,
):
    inside = pl.ds(8, 128)
    pairs = []
    for msg, q, t in ((low, 0, 0), (high, 18, 17)):
        for c in range(3):
            pairs.append((msg.at[pl.ds(2 * c, 2)], adj_s.at[c, pl.ds(q, 2), inside]))
            pairs.append((msg.at[pl.ds(6 + c, 1)], vel_s.at[c, pl.ds(t, 1)]))
        pairs.append((msg.at[pl.ds(9, 2)], visc_s.at[pl.ds(q, 2), inside]))
    started = begin([(done.at[:, pl.ds(2, 6)], out.at[:, pl.ds(2, 6)])], sem_o)
    started += begin(pairs, sems)
    started += begin([(filters, kept)], sem_f)
    run_first(range(9, 15), (adj_s, visc_s, vel_s), mid_s, coef_s, centre)
    run_second(range(8, 14), mid_s, coef_s, middle, done)
    for copy in started:
        copy.wait()


def middle_call(state, centre, middle, mid, coef, done, low, high, filters):
    held = [vmem(a) for a in (*state, centre, middle, mid, coef, done)]
    return pl.pallas_call(
        middle_kernel,
        in_specs=[VM] * 8 + [ANY] * 3,
        out_specs=[VM] * 6 + [ANY, VM],
        out_shape=[in_vmem(STATE[k]) for k in ("adj", "visc", "vel", "mid", "coef")]
        + [in_vmem(FIELD), pltpu.HBM(FIELD, F32), pltpu.VMEM(filters.shape, BF16)],
        scratch_shapes=[
            pltpu.SemaphoreType.DMA((14,)),
            pltpu.SemaphoreType.DMA((1,)),
            pltpu.SemaphoreType.DMA((1,)),
        ],
        input_output_aliases={0: 0, 1: 1, 2: 2, 5: 3, 6: 4, 7: 5},
        compiler_params=params(4),
        cost_estimate=cost(12),
        name="middle",
    )(*held, low, high, hbm(filters))


def sides_kernel(
    adj_s, visc_s, vel_s, centre, hl, hr, zl, zr, low, high, _, __, ___, ____,
    mid_s, coef_s, done, out, edges, sems,
):
    started = begin([(done.at[:, pl.ds(8, 6)], out.at[:, pl.ds(8, 6)])], sems)
    edges[...] = edge_middle(hl, hr, zl, zr, low[...], high[...])
    state = (adj_s, visc_s, vel_s)
    first_step(*state, mid_s, coef_s, low, -1, 15)
    first_step(*state, mid_s, coef_s, high, 16, 0)
    run_first((0, 15), state, mid_s, coef_s, centre)
    gx = lax.axis_index("gx")
    for t, end in ((0, 0), (17, lax.axis_size("gx") - 1)):

        @pl.when(gx == end)
        def _(t=t):
            for c in range(3):
                mid_s[c, t] = jnp.zeros((144, 128), F32)

    for i, x in enumerate((0, 14)):
        run_second((x, x + 1), mid_s, coef_s, edges, done)
        copy = pltpu.make_async_copy(
            done.at[:, pl.ds(x, 2)], out.at[:, pl.ds(x, 2)], sems.at[i + 1]
        )
        copy.start()
        started.append(copy)
    for copy in started:
        copy.wait()


def sides_call(state, centre, hl, hr, zl, zr, low, high, mid, coef, done, out):
    held = [vmem(a) for a in (*state, centre, hl, hr, zl, zr, low, high, mid, coef, done)]
    return pl.pallas_call(
        sides_kernel,
        in_specs=[VM] * 13 + [ANY],
        out_specs=[VM] * 3 + [ANY],
        out_shape=[in_vmem(STATE["mid"]), in_vmem(STATE["coef"]), in_vmem(FIELD)]
        + [pltpu.HBM(FIELD, F32)],
        scratch_shapes=[pltpu.VMEM((128, 128), F32), pltpu.SemaphoreType.DMA((3,))],
        input_output_aliases={10: 0, 11: 1, 12: 2, 13: 3},
        compiler_params=params(4),
        cost_estimate=cost(8),
        name="sides",
    )(*held, hbm(out))[-1]


def join_kernel(*refs):
    total = refs[0][...]
    for ref in refs[1:-1]:
        total = total + ref[...]
    refs[-1][...] = total


def join(*parts):
    return pl.pallas_call(
        join_kernel,
        in_specs=[VM] * len(parts),
        out_specs=VM,
        out_shape=in_vmem(parts[0].shape),
        compiler_params=params(2),
        name="join",
    )(*[vmem(a) for a in parts])


def pieces(a):
    high = a.astype(BF16)
    rest = a - high.astype(F32)
    mid = rest.astype(BF16)
    low = (rest - mid.astype(F32)).astype(BF16)
    return high, mid, low


PART = (3, 16, 128)


def sums_kernel(chosen, face, more, kept, given):
    matrix = chosen[...].astype(BF16)
    for c in range(3):
        total = 0.0
        for piece in pieces(face[c] + more[c]):
            total = total + jnp.dot(matrix, piece, preferred_element_type=F32)
        for k in range(8):
            (given if k % 2 else kept)[k // 2, c] = total[k * 16 : k * 16 + 16]


def partial_sums(chosen, face, more):
    return pl.pallas_call(
        sums_kernel,
        in_specs=[VM] * 3,
        out_specs=[VM, VM],
        out_shape=[in_vmem((4, *PART))] * 2,
        compiler_params=params(2),
        name="sums",
    )(vmem(chosen), vmem(face), vmem(more))


def halve_kernel(kept, came, *parts):
    for k, part in enumerate(parts):
        part[...] = kept[k] + came[k]


def halve(kept, came):
    return pl.pallas_call(
        halve_kernel,
        in_specs=[VM] * 2,
        out_specs=[VM] * 4,
        out_shape=[in_vmem(PART)] * 4,
        compiler_params=params(2),
        name="halve",
    )(vmem(kept), vmem(came))


def product_kernel(a, b, c, d, filters, out, sums):
    sums[...] = (a[...] + b[...]) + (c[...] + d[...])
    for p in range(4):
        view = jnp.concatenate([sums[:, p * 4 + i, :] for i in range(4)], axis=1)
        stacked = jnp.concatenate(pieces(view), axis=0)
        wide = jnp.dot(stacked, filters[p], preferred_element_type=F32)
        out[:, p, :] = wide[0:3] + (wide[3:6] + wide[6:9])


def product(parts, filters):
    return pl.pallas_call(
        product_kernel,
        in_specs=[VM] * 5,
        out_specs=VM,
        out_shape=jax.ShapeDtypeStruct((3, 4, 512), F32),
        scratch_shapes=[pltpu.VMEM(PART, F32)],
        compiler_params=params(4),
        name="product",
    )(*[vmem(a) for a in (*parts, filters)])


def shards(adjoint, velocity, viscosity, filters, block_tiles, tile_place):
    nx = lax.axis_size("gx")
    nz = lax.axis_size("gz")
    ring = [(i, (i + 1) % nz) for i in range(nz)]
    back = [(b, a) for a, b in ring]
    along = [(i, i + 1) for i in range(nx - 1)]
    against = [(b, a) for a, b in along]

    *state, zl, zr = pack(adjoint, velocity, viscosity)
    hl = lax.ppermute(zl, "gz", ring)
    hr = lax.ppermute(zr, "gz", back)
    msg_lo, msg_hi = ship(state, zl)
    low = lax.ppermute(msg_hi, "gx", along)
    high = lax.ppermute(msg_lo, "gx", against)
    hl, hr, *_ = lax.optimization_barrier((hl, hr, msg_lo, msg_hi))
    face, mid, coef, centre, middle = face_call(state, hl, hr, zl, zr)

    got = [lax.ppermute(face, "gx", [(0, k)]) for k in (8, 2, 6)]
    mid, coef, done, chosen, corner = inner(
        state, centre, middle, block_tiles.T, tile_place.reshape(1, -1), mid, coef
    )
    beside = lax.ppermute(corner, "gx", along), lax.ppermute(corner, "gx", against)
    *got, mid, coef, done = lax.optimization_barrier((*got, mid, coef, done))
    face = join(face, *got)
    far = lax.ppermute(face, "gx", [(0, 4), (2, 10), (6, 14), (8, 12)])
    *state, mid, coef, done, out, near = middle_call(
        state, centre, middle, mid, coef, done, low, high, filters
    )
    far, mid, coef, done, *beside = lax.optimization_barrier((far, mid, coef, done, *beside))
    face = join(face, far)
    other = lax.ppermute(face, "gx", [(i, i + 1) for i in range(0, nx, 2)])
    kept, given = partial_sums(chosen, face, other)

    came = lax.ppermute(given, "gz", [(i, i ^ 1) for i in range(nz)])
    out = sides_call(state, centre, hl, hr, zl, zr, *beside, mid, coef, done, out)
    came, out = lax.optimization_barrier((came, out))
    parts = halve(kept, came)
    parts = [parts[0]] + [
        lax.ppermute(parts[k], "gz", [(i, i ^ (2 * k)) for i in range(nz)]) for k in (2, 1, 3)
    ]
    gradient = product(parts, near).transpose(1, 0, 2)
    return out, gradient


def solution(mesh):
    placed = (
        P(None, "gx", None, "gz"),
        P(None, "gx", None, "gz"),
        P("gx", None, "gz"),
        P(("gx", "gz"), None, None),
        P(),
        P(),
    )
    return jax.shard_map(
        shards,
        mesh=mesh,
        in_specs=placed,
        out_specs=(P(None, "gx", None, "gz"), P(("gx", "gz"), None, None)),
        check_vma=False,
    )
```

time: 66.2 us -> 67.5 us (1.020)
  the two profiles are of different devices: /device:TPU:20 before, /device:TPU:24 now
where the time goes in v5:
time: 67.5 us; the launch traced here: 67.2 us
  starting transfers between devices  31.2 us (46%)
  Pallas kernels  19.1 us (28%)
  waiting for transfers between devices  16 us (24%)
  between operations  0.83 us (1%)
    ppermute x1, starting transfers between devices, shards(): lax.ppermute(corner, 'gx', against)  7.26 us
    ppermute x1, starting transfers between devices, shards(): high = lax.ppermute(msg_lo, 'gx', against)  7.26 us
    pallas_call x1, Pallas kernels, middle_call(): pl.pallas_call(middle_kernel, in_specs=[VM] * 8 + [ANY] * 3, out_specs=[V...  4.75 us
    ppermute x3, starting transfers between devices, shards(): lax.ppermute(parts[k], 'gz', [(i, i ^ 2 * k) for i in range(nz)])  4.68 us
    ppermute x3, waiting for transfers between devices, shards(): lax.ppermute(parts[k], 'gz', [(i, i ^ 2 * k) for i in range(nz)])  4.55 us
    pallas_call x1, Pallas kernels, pack(): pl.pallas_call(pack_kernel, in_specs=[ANY, ANY, ANY], out_specs=[VM] * 5,...  4.11 us
    ppermute x3, waiting for transfers between devices, shards(): got = [lax.ppermute(face, 'gx', [(0, k)]) for k in (8, 2, 6)]  3.72 us
    pallas_call x1, Pallas kernels, sides_call(): pl.pallas_call(sides_kernel, in_specs=[VM] * 13 + [ANY], out_specs=[VM] *...  3.39 us
  transfers between devices with their start and end apart: 15, of which 8 were waited for; matrix products, arithmetic and copies ran while one was open for 0% of the time, Pallas kernels for 19%

profile of v5, /device:TPU:24, one launch (start us, length us, event | category | flops | bytes accessed | tf_op | source)
XLA Modules:
  0.0 67.2 jit_solution(16689759247307624377)
XLA Ops:
  0.6 4.1 %pack.1 = (f32[3,20,144,128]{3,2,1,0:T(8,128)S(1)}, f32[20,144,128]{2,1,0:T(8,128)S(1)}, f32[3,18,128,128]{3,2,1,0:T(8,128)S(1)}, f32[192,128]{1,0:T(8,128)S(1)}, f32[192,128]{1,0:T(8,128)S(1)}) custom-call(f32[3,16,128,128]{3,2,1,0:T(8,128)} %adj.1, f32[3,16,128,128]{3,2,1,0:T(8,128)} %vel.1, f32[16,128,128]{2,1,0:T(8,128)} %visc.1), custom_call_target="tpu_custom_call" | custom-call | tf_op jit(solution)/shard_map/pack/pallas_call | solution.py:130
  4.8 1.2 %ship.1 = (f32[11,128,128]{2,1,0:T(8,128)}, f32[11,128,128]{2,1,0:T(8,128)}) custom-call(f32[3,20,144,128]{3,2,1,0:T(8,128)S(1)} %get-tuple-element.50.adj_s.adj_i, f32[20,144,128]{2,1,0:T(8,128)S(1)} %get-tuple-element.51.visc_s.visc_i, f32[3,18,128,128]{3,2,1,0:T(8,128)S(1)} %get-tuple-element.52.vel_s.vel_i, f32[192,128]{1,0:T(8,128)S(1)} %get-tuple-element.53._.zl), custom_call_target="tpu_custom_call" | custom-call | bytes 2883584 | tf_op jit(solution)/shard_map/ship/pallas_call | solution.py:311
  6.0 1.9 %collective-permute-start.6 = (f32[11,128,128]{2,1,0:T(8,128)}, f32[11,128,128]{2,1,0:T(8,128)S(1)}, u32[]{:S(2)}, u32[]{:S(2)}) collective-permute-start(f32[11,128,128]{2,1,0:T(8,128)} %get-tuple-element.56), channel_id=1, source_target_pairs={{0,8},{8,16},{16,24},{24,32},{32,40},{40,48},{48,56},{56,64},{64,7... | collective-permute-start | bytes 2162696 | tf_op jit(solution)/shard_map/ppermute | solution.py:570
  7.9 7.3 %collective-permute-start.7 = (f32[11,128,128]{2,1,0:T(8,128)}, f32[11,128,128]{2,1,0:T(8,128)S(1)}, u32[]{:S(2)}, u32[]{:S(2)}) collective-permute-start(f32[11,128,128]{2,1,0:T(8,128)} %get-tuple-element.55), channel_id=1, source_target_pairs={{8,0},{16,8},{24,16},{32,24},{40,32},{48,40},{56,48},{64,56},{72,6... | collective-permute-start | bytes 2162696 | tf_op jit(solution)/shard_map/ppermute | solution.py:571
  15.2 2.2 %collective-permute-start = (f32[192,128]{1,0:T(8,128)S(1)}, f32[192,128]{1,0:T(8,128)S(1)}, u32[]{:S(2)}, u32[]{:S(2)}) collective-permute-start(f32[192,128]{1,0:T(8,128)S(1)} %get-tuple-element.53._.zl), channel_id=1, source_target_pairs={{0,1},{1,2},{2,3},{3,4},{4,5},{5,6},{6,7},{7,0},{8,9},{9,10},{10,1... | collective-permute-start | bytes 294920 | tf_op jit(solution)/shard_map/ppermute | solution.py:567
  17.3 2.5 %collective-permute-done.hl = f32[192,128]{1,0:T(8,128)S(1)} collective-permute-done((f32[192,128]{1,0:T(8,128)S(1)}, f32[192,128]{1,0:T(8,128)S(1)}, u32[]{:S(2)}, u32[]{:S(2)}) %collective-permute-start) | collective-permute-done | bytes 98336 | tf_op jit(solution)/shard_map/ppermute | solution.py:567
  19.9 3.0 %collective-permute-done.1.hr = f32[192,128]{1,0:T(8,128)S(1)} collective-permute-done((f32[192,128]{1,0:T(8,128)S(1)}, f32[192,128]{1,0:T(8,128)S(1)}, u32[]{:S(2)}, u32[]{:S(2)}) %collective-permute-start.1) | collective-permute-done | bytes 98336 | tf_op jit(solution)/shard_map/ppermute | solution.py:568
  22.9 1.7 %face.1 = (f32[3,128,128]{2,1,0:T(8,128)S(1)}, f32[3,18,144,128]{3,2,1,0:T(8,128)S(1)}, f32[7,18,128,128]{3,2,1,0:T(8,128)S(1)}, f32[128,128]{1,0:T(8,128)S(1)}, f32[128,128]{1,0:T(8,128)S(1)}) custom-call(f32[3,20,144,128]{3,2,1,0:T(8,128)S(1)} %get-tuple-element.50.adj_s.adj_i, f32[20,144,128]{2,1,0:T(8,128)S(1)} %get-tuple-element.51.visc_s.visc_i, ...), custom_call_target="tpu_custom_call" | custom-call | flops 2949120 | bytes 4325376 | tf_op jit(solution)/shard_map/face/pallas_call | solution.py:280
  24.5 1.3 %collective-permute-start.2 = (f32[3,128,128]{2,1,0:T(8,128)S(1)}, f32[3,128,128]{2,1,0:T(8,128)S(1)}, u32[]{:S(2)}, u32[]{:S(2)}) collective-permute-start(f32[3,128,128]{2,1,0:T(8,128)S(1)} %get-tuple-element.64.refs_0_), channel_id=1, source_target_pairs={{0,64},{1,65},{2,66},{3,67},{4,68},{5,69},{6,70},{7,71}} | collective-permute-start | bytes 589832 | tf_op jit(solution)/shard_map/ppermute | solution.py:575
  27.2 2.7 %inner.1 = (f32[3,18,144,128]{3,2,1,0:T(8,128)S(1)}, f32[7,18,128,128]{3,2,1,0:T(8,128)S(1)}, f32[3,16,128,128]{3,2,1,0:T(8,128)S(1)}, f32[128,128]{1,0:T(8,128)S(1)}, f32[128,128]{1,0:T(8,128)S(1)}) custom-call(f32[3,20,144,128]{3,2,1,0:T(8,128)S(1)} %get-tuple-element.50.adj_s.adj_i, ...), custom_call_target="tpu_custom_call", output_to_operand_aliasing={{0}: (7, {}), {1}: (8, {})} | custom-call | flops 12779520 | bytes 18743296 | tf_op jit(solution)/shard_map/inner/pallas_call | solution.py:368
  29.9 3.7 %collective-permute-done.2.refs_1_ = f32[3,128,128]{2,1,0:T(8,128)S(1)} collective-permute-done((f32[3,128,128]{2,1,0:T(8,128)S(1)}, f32[3,128,128]{2,1,0:T(8,128)S(1)}, u32[]{:S(2)}, u32[]{:S(2)}) %collective-permute-start.2) | collective-permute-done | bytes 196640 | tf_op jit(solution)/shard_map/ppermute | solution.py:575
  33.6 1.3 %collective-permute-start.5 = (f32[3,128,128]{2,1,0:T(8,128)S(1)}, f32[3,128,128]{2,1,0:T(8,128)S(1)}, u32[]{:S(2)}, u32[]{:S(2)}) collective-permute-start(f32[3,128,128]{2,1,0:T(8,128)S(1)} %join.2.refs_0_), channel_id=1, source_target_pairs={{0,32},{16,80},{48,112},{64,96},{1,33},{17,81},{49,113},{65,97},{2... | collective-permute-start | bytes 589832 | tf_op jit(solution)/shard_map/ppermute | solution.py:582
  34.9 1.9 %collective-permute-start.8 = (f32[128,128]{1,0:T(8,128)S(1)}, f32[128,128]{1,0:T(8,128)S(1)}, u32[]{:S(2)}, u32[]{:S(2)}) collective-permute-start(f32[128,128]{1,0:T(8,128)S(1)} %get-tuple-element.77), channel_id=1, source_target_pairs={{0,8},{8,16},{16,24},{24,32},{32,40},{40,48},{48,56},{56,64},{64,7... | collective-permute-start | bytes 196616 | tf_op jit(solution)/shard_map/ppermute | solution.py:579
  36.9 7.3 %collective-permute-start.9 = (f32[128,128]{1,0:T(8,128)S(1)}, f32[128,128]{1,0:T(8,128)S(1)}, u32[]{:S(2)}, u32[]{:S(2)}) collective-permute-start(f32[128,128]{1,0:T(8,128)S(1)} %get-tuple-element.77), channel_id=1, source_target_pairs={{8,0},{16,8},{24,16},{32,24},{40,32},{48,40},{56,48},{64,56},{72,6... | collective-permute-start | bytes 196616 | tf_op jit(solution)/shard_map/ppermute | solution.py:579
  44.2 4.8 %middle.1 = (f32[3,20,144,128]{3,2,1,0:T(8,128)S(1)}, f32[20,144,128]{2,1,0:T(8,128)S(1)}, f32[3,18,128,128]{3,2,1,0:T(8,128)S(1)}, f32[3,18,144,128]{3,2,1,0:T(...) custom-call(f32[3,20,144,128]{3,2,1,0:T(8,128)S(1)} %get-tuple-eleme, ...), custom_call_target="tpu_custom_call", output_to_operand_aliasing={{0}: (0, {}), {1}: (1, {}), {2}: (2, {}), {3}: (5, {}), {4}... | custom-call | flops 11796480 | bytes 17301504 | tf_op jit(solution)/shard_map/middle/pallas_call | solution.py:408
  49.0 1.3 %collective-permute-start.10 = (f32[3,128,128]{2,1,0:T(8,128)S(1)}, f32[3,128,128]{2,1,0:T(8,128)S(1)}, u32[]{:S(2)}, u32[]{:S(2)}) collective-permute-start(f32[3,128,128]{2,1,0:T(8,128)S(1)} %join.3.face), channel_id=1, source_target_pairs={{0,8},{16,24},{32,40},{48,56},{64,72},{80,88},{96,104},{112,120},{... | collective-permute-start | bytes 589832 | tf_op jit(solution)/shard_map/ppermute | solution.py:588
  50.3 1.0 %collective-permute-done.10.more = f32[3,128,128]{2,1,0:T(8,128)S(1)} collective-permute-done((f32[3,128,128]{2,1,0:T(8,128)S(1)}, f32[3,128,128]{2,1,0:T(8,128)S(1)}, u32[]{:S(2)}, u32[]{:S(2)}) %collective-permute-start.10) | collective-permute-done | bytes 196640 | tf_op jit(solution)/shard_map/ppermute | solution.py:588
  52.3 3.4 %sides.1 = (f32[3,18,144,128]{3,2,1,0:T(8,128)S(1)}, f32[7,18,128,128]{3,2,1,0:T(8,128)S(1)}, f32[3,16,128,128]{3,2,1,0:T(8,128)S(1)}, f32[3,16,128,128]{3,2,1,0:T(8,128)}) custom-call(f32[3,20,144,128]{3,2,1,0:T(8,128)S(1)} %get-tuple-element.80.adj_s, ...), custom_call_target="tpu_custom_call", output_to_operand_aliasing={{0}: (10, {}), {1}: (11, {}), {2}: (12, {}), {3}: (13, {})} | custom-call | flops 7864320 | bytes 11534336 | tf_op jit(solution)/shard_map/sides/pallas_call | solution.py:457
  55.7 1.2 %collective-permute-done.11.came = f32[4,3,16,128]{3,2,1,0:T(8,128)S(1)} collective-permute-done((f32[4,3,16,128]{3,2,1,0:T(8,128)S(1)}, f32[4,3,16,128]{3,2,1,0:T(8,128)S(1)}, u32[]{:S(2)}, u32[]{:S(2)}) %collective-permute-start.11) | collective-permute-done | bytes 98336 | tf_op jit(solution)/shard_map/ppermute | solution.py:591
  56.9 3.7 %collective-permute-start.12 = (f32[3,16,128]{2,1,0:T(8,128)S(1)}, f32[3,16,128]{2,1,0:T(8,128)S(1)}, u32[]{:S(2)}, u32[]{:S(2)}) collective-permute-start(f32[3,16,128]{2,1,0:T(8,128)S(1)} %get-tuple-element.94), channel_id=1, source_target_pairs={{0,4},{1,5},{2,6},{3,7},{4,0},{5,1},{6,2},{7,3},{8,12},{9,13},{10,... | collective-permute-start | bytes 73736 | tf_op jit(solution)/shard_map/ppermute | solution.py:596
  61.6 0.8 %collective-permute-done.12.b = f32[3,16,128]{2,1,0:T(8,128)S(1)} collective-permute-done((f32[3,16,128]{2,1,0:T(8,128)S(1)}, f32[3,16,128]{2,1,0:T(8,128)S(1)}, u32[]{:S(2)}, u32[]{:S(2)}) %collective-permute-start.12) | collective-permute-done | bytes 24608 | tf_op jit(solution)/shard_map/ppermute | solution.py:596
  62.4 2.0 %collective-permute-done.13.c = f32[3,16,128]{2,1,0:T(8,128)S(1)} collective-permute-done((f32[3,16,128]{2,1,0:T(8,128)S(1)}, f32[3,16,128]{2,1,0:T(8,128)S(1)}, u32[]{:S(2)}, u32[]{:S(2)}) %collective-permute-start.13) | collective-permute-done | bytes 24608 | tf_op jit(solution)/shard_map/ppermute | solution.py:596
  64.4 1.7 %collective-permute-done.14.d = f32[3,16,128]{2,1,0:T(8,128)S(1)} collective-permute-done((f32[3,16,128]{2,1,0:T(8,128)S(1)}, f32[3,16,128]{2,1,0:T(8,128)S(1)}, u32[]{:S(2)}, u32[]{:S(2)}) %collective-permute-start.14) | collective-permute-done | bytes 24608 | tf_op jit(solution)/shard_map/ppermute | solution.py:596
  66.1 1.0 %product.1 = f32[3,4,512]{2,1,0:T(4,128)} custom-call(f32[3,16,128]{2,1,0:T(8,128)S(1)} %get-tuple-element.93.a, f32[3,16,128]{2,1,0:T(8,128)S(1)} %collective-permute-done.12.b, f32[3,16,128]{2,1,0:T(8,128)S(1)} %collective-permute-done.13.c, f32[3,16,128]{2,1,0:T(8,128)S(1)} %collective-permute-done.14.d, bf16[4,512,512]{2,1,0:T(8,128)(2,1)S(1)} %get-tuple-element.97.filters), custom_call_target="tpu_custom_call" | custom-call | tf_op jit(solution)/shard_map/product/pallas_call | solution.py:547
  (21 shorter events, 3.5 us)
Async XLA Ops:
  6.0 38.2 %collective-permute-start.6 = (f32[11,128,128]{2,1,0:T(8,128)}, f32[11,128,128]{2,1,0:T(8,128)S(1)}, u32[]{:S(2)}, u32[]{:S(2)}) collective-permute-start(f32[11,128,128]{2,1,0:T(8,128)} %get-tuple-element.56), channel_id=1, source_target_pairs={{0,8},{8,16},{16,24},{24,32},{32,40},{40,48},{48,56},{56,64},{64,7... | collective-permute-start | bytes 2162696 | tf_op jit(solution)/shard_map/ppermute | solution.py:570
  7.9 36.2 %collective-permute-start.7 = (f32[11,128,128]{2,1,0:T(8,128)}, f32[11,128,128]{2,1,0:T(8,128)S(1)}, u32[]{:S(2)}, u32[]{:S(2)}) collective-permute-start(f32[11,128,128]{2,1,0:T(8,128)} %get-tuple-element.55), channel_id=1, source_target_pairs={{8,0},{16,8},{24,16},{32,24},{40,32},{48,40},{56,48},{64,56},{72,6... | collective-permute-start | bytes 2162696 | tf_op jit(solution)/shard_map/ppermute | solution.py:571
  15.2 4.7 %collective-permute-start = (f32[192,128]{1,0:T(8,128)S(1)}, f32[192,128]{1,0:T(8,128)S(1)}, u32[]{:S(2)}, u32[]{:S(2)}) collective-permute-start(f32[192,128]{1,0:T(8,128)S(1)} %get-tuple-element.53._.zl), channel_id=1, source_target_pairs={{0,1},{1,2},{2,3},{3,4},{4,5},{5,6},{6,7},{7,0},{8,9},{9,10},{10,1... | collective-permute-start | bytes 294920 | tf_op jit(solution)/shard_map/ppermute | solution.py:567
  17.3 9.8 %copy-start = (s32[256,8]{0,1:T(8,128)S(1)}, s32[256,8]{0,1:T(8,128)}, u32[]{:S(2)}) copy-start(s32[256,8]{0,1:T(8,128)} %param.10) | copy-start | bytes 24580
  17.3 9.9 %copy-start.1 = (s32[512]{0:T(512)S(1)}, s32[512]{0:T(512)}, u32[]{:S(2)}) copy-start(s32[512]{0:T(512)} %param.11) | copy-start | bytes 6148
  17.3 5.5 %collective-permute-start.1 = (f32[192,128]{1,0:T(8,128)S(1)}, f32[192,128]{1,0:T(8,128)S(1)}, u32[]{:S(2)}, u32[]{:S(2)}) collective-permute-start(f32[192,128]{1,0:T(8,128)S(1)} %get-tuple-element.54.zr), channel_id=1, source_target_pairs={{1,0},{2,1},{3,2},{4,3},{5,4},{6,5},{7,6},{0,7},{9,8},{10,9},{11,1... | collective-permute-start | bytes 294920 | tf_op jit(solution)/shard_map/ppermute | solution.py:568
  24.5 9.1 %collective-permute-start.2 = (f32[3,128,128]{2,1,0:T(8,128)S(1)}, f32[3,128,128]{2,1,0:T(8,128)S(1)}, u32[]{:S(2)}, u32[]{:S(2)}) collective-permute-start(f32[3,128,128]{2,1,0:T(8,128)S(1)} %get-tuple-element.64.refs_0_), channel_id=1, source_target_pairs={{0,64},{1,65},{2,66},{3,67},{4,68},{5,69},{6,70},{7,71}} | collective-permute-start | bytes 589832 | tf_op jit(solution)/shard_map/ppermute | solution.py:575
  25.8 7.8 %collective-permute-start.3 = (f32[3,128,128]{2,1,0:T(8,128)S(1)}, f32[3,128,128]{2,1,0:T(8,128)S(1)}, u32[]{:S(2)}, u32[]{:S(2)}) collective-permute-start(f32[3,128,128]{2,1,0:T(8,128)S(1)} %get-tuple-element.64.refs_0_), channel_id=1, source_target_pairs={{0,16},{1,17},{2,18},{3,19},{4,20},{5,21},{6,22},{7,23}} | collective-permute-start | bytes 589832 | tf_op jit(solution)/shard_map/ppermute | solution.py:575
  26.5 7.1 %collective-permute-start.4 = (f32[3,128,128]{2,1,0:T(8,128)S(1)}, f32[3,128,128]{2,1,0:T(8,128)S(1)}, u32[]{:S(2)}, u32[]{:S(2)}) collective-permute-start(f32[3,128,128]{2,1,0:T(8,128)S(1)} %get-tuple-element.64.refs_0_), channel_id=1, source_target_pairs={{0,48},{1,49},{2,50},{3,51},{4,52},{5,53},{6,54},{7,55}} | collective-permute-start | bytes 589832 | tf_op jit(solution)/shard_map/ppermute | solution.py:575
  33.6 15.3 %collective-permute-start.5 = (f32[3,128,128]{2,1,0:T(8,128)S(1)}, f32[3,128,128]{2,1,0:T(8,128)S(1)}, u32[]{:S(2)}, u32[]{:S(2)}) collective-permute-start(f32[3,128,128]{2,1,0:T(8,128)S(1)} %join.2.refs_0_), channel_id=1, source_target_pairs={{0,32},{16,80},{48,112},{64,96},{1,33},{17,81},{49,113},{65,97},{2... | collective-permute-start | bytes 589832 | tf_op jit(solution)/shard_map/ppermute | solution.py:582
  34.9 14.0 %collective-permute-start.8 = (f32[128,128]{1,0:T(8,128)S(1)}, f32[128,128]{1,0:T(8,128)S(1)}, u32[]{:S(2)}, u32[]{:S(2)}) collective-permute-start(f32[128,128]{1,0:T(8,128)S(1)} %get-tuple-element.77), channel_id=1, source_target_pairs={{0,8},{8,16},{16,24},{24,32},{32,40},{40,48},{48,56},{56,64},{64,7... | collective-permute-start | bytes 196616 | tf_op jit(solution)/shard_map/ppermute | solution.py:579
  36.9 12.1 %collective-permute-start.9 = (f32[128,128]{1,0:T(8,128)S(1)}, f32[128,128]{1,0:T(8,128)S(1)}, u32[]{:S(2)}, u32[]{:S(2)}) collective-permute-start(f32[128,128]{1,0:T(8,128)S(1)} %get-tuple-element.77), channel_id=1, source_target_pairs={{8,0},{16,8},{24,16},{32,24},{40,32},{48,40},{56,48},{64,56},{72,6... | collective-permute-start | bytes 196616 | tf_op jit(solution)/shard_map/ppermute | solution.py:579
  49.0 2.4 %collective-permute-start.10 = (f32[3,128,128]{2,1,0:T(8,128)S(1)}, f32[3,128,128]{2,1,0:T(8,128)S(1)}, u32[]{:S(2)}, u32[]{:S(2)}) collective-permute-start(f32[3,128,128]{2,1,0:T(8,128)S(1)} %join.3.face), channel_id=1, source_target_pairs={{0,8},{16,24},{32,40},{48,56},{64,72},{80,88},{96,104},{112,120},{... | collective-permute-start | bytes 589832 | tf_op jit(solution)/shard_map/ppermute | solution.py:588
  51.6 5.3 %collective-permute-start.11 = (f32[4,3,16,128]{3,2,1,0:T(8,128)S(1)}, f32[4,3,16,128]{3,2,1,0:T(8,128)S(1)}, u32[]{:S(2)}, u32[]{:S(2)}) collective-permute-start(f32[4,3,16,128]{3,2,1,0:T(8,128)S(1)} %get-tuple-element.79), channel_id=1, source_target_pairs={{0,1},{1,0},{2,3},{3,2},{4,5},{5,4},{6,7},{7,6},{8,9},{9,8},{10,11... | collective-permute-start | bytes 294920 | tf_op jit(solution)/shard_map/ppermute | solution.py:591
  56.9 5.5 %collective-permute-start.12 = (f32[3,16,128]{2,1,0:T(8,128)S(1)}, f32[3,16,128]{2,1,0:T(8,128)S(1)}, u32[]{:S(2)}, u32[]{:S(2)}) collective-permute-start(f32[3,16,128]{2,1,0:T(8,128)S(1)} %get-tuple-element.94), channel_id=1, source_target_pairs={{0,4},{1,5},{2,6},{3,7},{4,0},{5,1},{6,2},{7,3},{8,12},{9,13},{10,... | collective-permute-start | bytes 73736 | tf_op jit(solution)/shard_map/ppermute | solution.py:596
  60.6 3.8 %collective-permute-start.13 = (f32[3,16,128]{2,1,0:T(8,128)S(1)}, f32[3,16,128]{2,1,0:T(8,128)S(1)}, u32[]{:S(2)}, u32[]{:S(2)}) collective-permute-start(f32[3,16,128]{2,1,0:T(8,128)S(1)} %get-tuple-element.95), channel_id=1, source_target_pairs={{0,2},{1,3},{2,0},{3,1},{4,6},{5,7},{6,4},{7,5},{8,10},{9,11},{10,... | collective-permute-start | bytes 73736 | tf_op jit(solution)/shard_map/ppermute | solution.py:596
  61.1 5.0 %collective-permute-start.14 = (f32[3,16,128]{2,1,0:T(8,128)S(1)}, f32[3,16,128]{2,1,0:T(8,128)S(1)}, u32[]{:S(2)}, u32[]{:S(2)}) collective-permute-start(f32[3,16,128]{2,1,0:T(8,128)S(1)} %get-tuple-element.96), channel_id=1, source_target_pairs={{0,6},{1,7},{2,4},{3,5},{4,2},{5,3},{6,0},{7,1},{8,14},{9,15},{10,... | collective-permute-start | bytes 73736 | tf_op jit(solution)/shard_map/ppermute | solution.py:596

commit v6 on v5

--- a/solution.py
+++ b/solution.py
@@ -294,7 +294,7 @@
     )(*[vmem(a) for a in (*state, hl, hr, zl, zr)])
 
 
-def ship_kernel(adj_s, visc_s, vel_s, _, msg_lo, msg_hi, sems):
+def ship_kernel(adj_s, visc_s, vel_s, centre, msg_lo, msg_hi, sems):
     moved = []
     inside = pl.ds(8, 128)
     for msg, q, t in ((msg_lo, 2, 1), (msg_hi, 16, 16)):
@@ -302,22 +302,23 @@
             moved.append((adj_s.at[c, pl.ds(q, 2), inside], msg.at[pl.ds(2 * c, 2)]))
             moved.append((vel_s.at[c, pl.ds(t, 1)], msg.at[pl.ds(6 + c, 1)]))
         moved.append((visc_s.at[pl.ds(q, 2), inside], msg.at[pl.ds(9, 2)]))
+        moved.append((centre, msg.at[11]))
     for copy in begin(moved, sems):
         copy.wait()
 
 
-def ship(state, after):
-    msg = pltpu.HBM((11, 128, 128), F32)
+def ship(state, centre):
+    msg = pltpu.HBM((12, 128, 128), F32)
     return pl.pallas_call(
         ship_kernel,
         in_specs=[VM] * 4,
         out_specs=[ANY, ANY],
         out_shape=[msg, msg],
-        scratch_shapes=[pltpu.SemaphoreType.DMA((14,))],
+        scratch_shapes=[pltpu.SemaphoreType.DMA((16,))],
         compiler_params=params(1),
         cost_estimate=pl.CostEstimate(flops=0, transcendentals=0, bytes_accessed=2 * 2 * 11 * 65536),
         name="ship",
-    )(*[vmem(a) for a in (*state, after)])
+    )(*[vmem(a) for a in (*state, centre)])
 
 
 def choose(lists, place):
@@ -356,9 +357,8 @@
 
 
 def inner_kernel(
-    adj_s, visc_s, vel_s, centre, middle, lists, place, _, __, mid_s, coef_s, done, chosen, corner
+    adj_s, visc_s, vel_s, centre, middle, lists, place, _, __, mid_s, coef_s, done, chosen
 ):
-    corner[...] = centre[...]
     chosen[...] = choose(lists, place)
     run_first(range(2, 9), (adj_s, visc_s, vel_s), mid_s, coef_s, centre)
     run_second(range(2, 8), mid_s, coef_s, middle, done)
@@ -368,12 +368,11 @@
     return pl.pallas_call(
         inner_kernel,
         in_specs=[VM] * 9,
-        out_specs=[VM] * 5,
+        out_specs=[VM] * 4,
         out_shape=[
             in_vmem(STATE["mid"]),
             in_vmem(STATE["coef"]),
             in_vmem(FIELD),
-            in_vmem((128, 128)),
             in_vmem((128, 128)),
         ],
         input_output_aliases={7: 0, 8: 1},
@@ -384,54 +383,47 @@
 
 
 def middle_kernel(
-    adj_i, visc_i, vel_i, centre, middle, _, __, ___, low, high, filters,
-    adj_s, visc_s, vel_s, mid_s, coef_s, done, out, kept, sems, sem_o, sem_f,
+    adj_s, visc_s, vel_s, centre, middle, _, __, ___, filters, mid_s, coef_s, done, out, kept, sems
 ):
-    inside = pl.ds(8, 128)
-    pairs = []
-    for msg, q, t in ((low, 0, 0), (high, 18, 17)):
-        for c in range(3):
-            pairs.append((msg.at[pl.ds(2 * c, 2)], adj_s.at[c, pl.ds(q, 2), inside]))
-            pairs.append((msg.at[pl.ds(6 + c, 1)], vel_s.at[c, pl.ds(t, 1)]))
-        pairs.append((msg.at[pl.ds(9, 2)], visc_s.at[pl.ds(q, 2), inside]))
-    started = begin([(done.at[:, pl.ds(2, 6)], out.at[:, pl.ds(2, 6)])], sem_o)
-    started += begin(pairs, sems)
-    started += begin([(filters, kept)], sem_f)
+    started = begin([(done.at[:, pl.ds(2, 6)], out.at[:, pl.ds(2, 6)]), (filters, kept)], sems)
     run_first(range(9, 15), (adj_s, visc_s, vel_s), mid_s, coef_s, centre)
     run_second(range(8, 14), mid_s, coef_s, middle, done)
     for copy in started:
         copy.wait()
 
 
-def middle_call(state, centre, middle, mid, coef, done, low, high, filters):
+def middle_call(state, centre, middle, mid, coef, done, filters):
     held = [vmem(a) for a in (*state, centre, middle, mid, coef, done)]
     return pl.pallas_call(
         middle_kernel,
-        in_specs=[VM] * 8 + [ANY] * 3,
-        out_specs=[VM] * 6 + [ANY, VM],
-        out_shape=[in_vmem(STATE[k]) for k in ("adj", "visc", "vel", "mid", "coef")]
-        + [in_vmem(FIELD), pltpu.HBM(FIELD, F32), pltpu.VMEM(filters.shape, BF16)],
-        scratch_shapes=[
-            pltpu.SemaphoreType.DMA((14,)),
-            pltpu.SemaphoreType.DMA((1,)),
-            pltpu.SemaphoreType.DMA((1,)),
-        ],
-        input_output_aliases={0: 0, 1: 1, 2: 2, 5: 3, 6: 4, 7: 5},
+        in_specs=[VM] * 8 + [ANY],
+        out_specs=[VM] * 3 + [ANY, VM],
+        out_shape=[in_vmem(STATE["mid"]), in_vmem(STATE["coef"]), in_vmem(FIELD)]
+        + [pltpu.HBM(FIELD, F32), pltpu.VMEM(filters.shape, BF16)],
+        scratch_shapes=[pltpu.SemaphoreType.DMA((2,))],
+        input_output_aliases={5: 0, 6: 1, 7: 2},
         compiler_params=params(4),
         cost_estimate=cost(12),
         name="middle",
-    )(*held, low, high, hbm(filters))
+    )(*held, hbm(filters))
 
 
 def sides_kernel(
-    adj_s, visc_s, vel_s, centre, hl, hr, zl, zr, low, high, _, __, ___, ____,
-    mid_s, coef_s, done, out, edges, sems,
+    adj_i, visc_i, vel_i, centre, hl, hr, zl, zr, low, high, _, __, ___, ____,
+    adj_s, visc_s, vel_s, mid_s, coef_s, done, out, edges, sems,
 ):
     started = begin([(done.at[:, pl.ds(8, 6)], out.at[:, pl.ds(8, 6)])], sems)
-    edges[...] = edge_middle(hl, hr, zl, zr, low[...], high[...])
+    for msg, q, t in ((low, 0, 0), (high, 18, 17)):
+        for i in range(2):
+            for c in range(3):
+                adj_s[c, q + i, pl.ds(8, 128)] = msg[2 * c + i]
+            visc_s[q + i, pl.ds(8, 128)] = msg[9 + i]
+        for d in range(3):
+            vel_s[d, t] = msg[6 + d]
+    edges[...] = edge_middle(hl, hr, zl, zr, low[11], high[11])
     state = (adj_s, visc_s, vel_s)
-    first_step(*state, mid_s, coef_s, low, -1, 15)
-    first_step(*state, mid_s, coef_s, high, 16, 0)
+    first_step(*state, mid_s, coef_s, low.at[11], -1, 15)
+    first_step(*state, mid_s, coef_s, high.at[11], 16, 0)
     run_first((0, 15), state, mid_s, coef_s, centre)
     gx = lax.axis_index("gx")
     for t, end in ((0, 0), (17, lax.axis_size("gx") - 1)):
@@ -457,11 +449,11 @@
     return pl.pallas_call(
         sides_kernel,
         in_specs=[VM] * 13 + [ANY],
-        out_specs=[VM] * 3 + [ANY],
-        out_shape=[in_vmem(STATE["mid"]), in_vmem(STATE["coef"]), in_vmem(FIELD)]
-        + [pltpu.HBM(FIELD, F32)],
+        out_specs=[VM] * 6 + [ANY],
+        out_shape=[in_vmem(STATE[k]) for k in ("adj", "visc", "vel", "mid", "coef")]
+        + [in_vmem(FIELD), pltpu.HBM(FIELD, F32)],
         scratch_shapes=[pltpu.VMEM((128, 128), F32), pltpu.SemaphoreType.DMA((3,))],
-        input_output_aliases={10: 0, 11: 1, 12: 2, 13: 3},
+        input_output_aliases={0: 0, 1: 1, 2: 2, 10: 3, 11: 4, 12: 5, 13: 6},
         compiler_params=params(4),
         cost_estimate=cost(8),
         name="sides",
@@ -497,45 +489,45 @@
 PART = (3, 16, 128)
 
 
-def sums_kernel(chosen, face, more, kept, given):
+def sums_kernel(chosen, face, more, *pairs):
     matrix = chosen[...].astype(BF16)
     for c in range(3):
         total = 0.0
         for piece in pieces(face[c] + more[c]):
             total = total + jnp.dot(matrix, piece, preferred_element_type=F32)
         for k in range(8):
-            (given if k % 2 else kept)[k // 2, c] = total[k * 16 : k * 16 + 16]
+            pairs[k // 2][k % 2, c] = total[k * 16 : k * 16 + 16]
 
 
 def partial_sums(chosen, face, more):
     return pl.pallas_call(
         sums_kernel,
         in_specs=[VM] * 3,
-        out_specs=[VM, VM],
-        out_shape=[in_vmem((4, *PART))] * 2,
+        out_specs=[VM] * 4,
+        out_shape=[in_vmem((2, *PART))] * 4,
         compiler_params=params(2),
         name="sums",
     )(vmem(chosen), vmem(face), vmem(more))
 
 
-def halve_kernel(kept, came, *parts):
-    for k, part in enumerate(parts):
-        part[...] = kept[k] + came[k]
-
-
-def halve(kept, came):
-    return pl.pallas_call(
-        halve_kernel,
-        in_specs=[VM] * 2,
-        out_specs=[VM] * 4,
-        out_shape=[in_vmem(PART)] * 4,
+def gather_kernel(a, b, c, d, kept, given):
+    kept[...] = (a[0] + b[0]) + (c[0] + d[0])
+    given[...] = (a[1] + b[1]) + (c[1] + d[1])
+
+
+def gather(pairs):
+    return pl.pallas_call(
+        gather_kernel,
+        in_specs=[VM] * 4,
+        out_specs=[VM] * 2,
+        out_shape=[in_vmem(PART)] * 2,
         compiler_params=params(2),
-        name="halve",
-    )(vmem(kept), vmem(came))
-
-
-def product_kernel(a, b, c, d, filters, out, sums):
-    sums[...] = (a[...] + b[...]) + (c[...] + d[...])
+        name="gather",
+    )(*[vmem(a) for a in pairs])
+
+
+def product_kernel(kept, came, filters, out, sums):
+    sums[...] = kept[...] + came[...]
     for p in range(4):
         view = jnp.concatenate([sums[:, p * 4 + i, :] for i in range(4)], axis=1)
         stacked = jnp.concatenate(pieces(view), axis=0)
@@ -546,7 +538,7 @@
 def product(parts, filters):
     return pl.pallas_call(
         product_kernel,
-        in_specs=[VM] * 5,
+        in_specs=[VM] * 3,
         out_specs=VM,
         out_shape=jax.ShapeDtypeStruct((3, 4, 512), F32),
         scratch_shapes=[pltpu.VMEM(PART, F32)],
@@ -566,36 +558,34 @@
     *state, zl, zr = pack(adjoint, velocity, viscosity)
     hl = lax.ppermute(zl, "gz", ring)
     hr = lax.ppermute(zr, "gz", back)
-    msg_lo, msg_hi = ship(state, zl)
+    face, mid, coef, centre, middle = face_call(state, hl, hr, zl, zr)
+
+    got = [lax.ppermute(face, "gx", [(0, k)]) for k in (8, 2, 6)]
+    mid, coef, done, chosen = inner(
+        state, centre, middle, block_tiles.T, tile_place.reshape(1, -1), mid, coef
+    )
+    msg_lo, msg_hi = ship(state, centre)
+    *got, mid, coef, done, msg_lo, msg_hi = lax.optimization_barrier(
+        (*got, mid, coef, done, msg_lo, msg_hi)
+    )
+    face = join(face, *got)
+    far = lax.ppermute(face, "gx", [(0, 4), (2, 10), (6, 14), (8, 12)])
+    mid, coef, done, out, near = middle_call(state, centre, middle, mid, coef, done, filters)
+    far, mid, coef, done = lax.optimization_barrier((far, mid, coef, done))
+    face = join(face, far)
+    other = lax.ppermute(face, "gx", [(i, i + 1) for i in range(0, nx, 2)])
+    other, msg_lo, msg_hi = lax.optimization_barrier((other, msg_lo, msg_hi))
     low = lax.ppermute(msg_hi, "gx", along)
     high = lax.ppermute(msg_lo, "gx", against)
-    hl, hr, *_ = lax.optimization_barrier((hl, hr, msg_lo, msg_hi))
-    face, mid, coef, centre, middle = face_call(state, hl, hr, zl, zr)
-
-    got = [lax.ppermute(face, "gx", [(0, k)]) for k in (8, 2, 6)]
-    mid, coef, done, chosen, corner = inner(
-        state, centre, middle, block_tiles.T, tile_place.reshape(1, -1), mid, coef
-    )
-    beside = lax.ppermute(corner, "gx", along), lax.ppermute(corner, "gx", against)
-    *got, mid, coef, done = lax.optimization_barrier((*got, mid, coef, done))
-    face = join(face, *got)
-    far = lax.ppermute(face, "gx", [(0, 4), (2, 10), (6, 14), (8, 12)])
-    *state, mid, coef, done, out, near = middle_call(
-        state, centre, middle, mid, coef, done, low, high, filters
-    )
-    far, mid, coef, done, *beside = lax.optimization_barrier((far, mid, coef, done, *beside))
-    face = join(face, far)
-    other = lax.ppermute(face, "gx", [(i, i + 1) for i in range(0, nx, 2)])
-    kept, given = partial_sums(chosen, face, other)
-
+    own, *pairs = partial_sums(chosen, face, other)
+    pairs = [own] + [
+        lax.ppermute(pairs[k // 2 - 1], "gz", [(i, i ^ k) for i in range(nz)]) for k in (4, 2, 6)
+    ]
+    kept, given = gather(pairs)
     came = lax.ppermute(given, "gz", [(i, i ^ 1) for i in range(nz)])
-    out = sides_call(state, centre, hl, hr, zl, zr, *beside, mid, coef, done, out)
+    out = sides_call(state, centre, hl, hr, zl, zr, low, high, mid, coef, done, out)
     came, out = lax.optimization_barrier((came, out))
-    parts = halve(kept, came)
-    parts = [parts[0]] + [
-        lax.ppermute(parts[k], "gz", [(i, i ^ (2 * k)) for i in range(nz)]) for k in (2, 1, 3)
-    ]
-    gradient = product(parts, near).transpose(1, 0, 2)
+    gradient = product((kept, came), near).transpose(1, 0, 2)
     return out, gradient
 
 

time: 67.5 us -> 60.7 us (0.90)
  the two profiles are of different devices: /device:TPU:24 before, /device:TPU:7 now
where the time goes in v6:
time: 60.7 us; the launch traced here: 60.4 us
  starting transfers between devices  22.4 us (37%)
  waiting for transfers between devices  19.2 us (32%)
  Pallas kernels  17.9 us (29%)
  between operations  0.85 us (1%)
    ppermute x1, waiting for transfers between devices, shards(): other = lax.ppermute(face, 'gx', [(i, i + 1) for i in range(0, nx, 2)])  6.98 us
    ppermute x1, starting transfers between devices, shards(): low = lax.ppermute(msg_hi, 'gx', along)  6.38 us
    ppermute x1, waiting for transfers between devices, shards(): high = lax.ppermute(msg_lo, 'gx', against)  6.19 us
    pallas_call x1, Pallas kernels, pack(): pl.pallas_call(pack_kernel, in_specs=[ANY, ANY, ANY], out_specs=[VM] * 5,...  4.14 us
    ppermute x3, waiting for transfers between devices, shards(): lax.ppermute(pairs[k // 2 - 1], 'gz', [(i, i ^ k) for i in range(nz)])  3.57 us
    ppermute x3, starting transfers between devices, shards(): lax.ppermute(pairs[k // 2 - 1], 'gz', [(i, i ^ k) for i in range(nz)])  3.56 us
    ppermute x1, starting transfers between devices, shards(): hr = lax.ppermute(zr, 'gz', back)  3.55 us
    pallas_call x1, Pallas kernels, middle_call(): pl.pallas_call(middle_kernel, in_specs=[VM] * 8 + [ANY], out_specs=[VM] *...  3.42 us
  transfers between devices with their start and end apart: 13, of which 6 were waited for; matrix products, arithmetic and copies ran while one was open for 0% of the time, Pallas kernels for 18%

profile of v6, /device:TPU:7, one launch (start us, length us, event | category | flops | bytes accessed | tf_op | source)
XLA Modules:
  0.0 60.4 jit_solution(13869685759211650208)
XLA Ops:
  0.6 4.1 %pack.1 = (f32[3,20,144,128]{3,2,1,0:T(8,128)S(1)}, f32[20,144,128]{2,1,0:T(8,128)S(1)}, f32[3,18,128,128]{3,2,1,0:T(8,128)S(1)}, f32[192,128]{1,0:T(8,128)S(1)}, f32[192,128]{1,0:T(8,128)S(1)}) custom-call(f32[3,16,128,128]{3,2,1,0:T(8,128)} %adj.1, f32[3,16,128,128]{3,2,1,0:T(8,128)} %vel.1, f32[16,128,128]{2,1,0:T(8,128)} %visc.1), custom_call_target="tpu_custom_call" | custom-call | tf_op jit(solution)/shard_map/pack/pallas_call | solution.py:130
  4.8 1.4 %collective-permute-start = (f32[192,128]{1,0:T(8,128)S(1)}, f32[192,128]{1,0:T(8,128)S(1)}, u32[]{:S(2)}, u32[]{:S(2)}) collective-permute-start(f32[192,128]{1,0:T(8,128)S(1)} %get-tuple-element.50.zl), channel_id=1, source_target_pairs={{0,1},{1,2},{2,3},{3,4},{4,5},{5,6},{6,7},{7,0},{8,9},{9,10},{10,1... | collective-permute-start | bytes 294920 | tf_op jit(solution)/shard_map/ppermute | solution.py:559
  6.1 3.6 %collective-permute-start.1 = (f32[192,128]{1,0:T(8,128)S(1)}, f32[192,128]{1,0:T(8,128)S(1)}, u32[]{:S(2)}, u32[]{:S(2)}) collective-permute-start(f32[192,128]{1,0:T(8,128)S(1)} %get-tuple-element.51.zr), channel_id=1, source_target_pairs={{1,0},{2,1},{3,2},{4,3},{5,4},{6,5},{7,6},{0,7},{9,8},{10,9},{11,1... | collective-permute-start | bytes 294920 | tf_op jit(solution)/shard_map/ppermute | solution.py:560
  9.7 2.4 %collective-permute-done.hl = f32[192,128]{1,0:T(8,128)S(1)} collective-permute-done((f32[192,128]{1,0:T(8,128)S(1)}, f32[192,128]{1,0:T(8,128)S(1)}, u32[]{:S(2)}, u32[]{:S(2)}) %collective-permute-start) | collective-permute-done | bytes 98336 | tf_op jit(solution)/shard_map/ppermute | solution.py:559
  12.1 1.7 %face.1 = (f32[3,128,128]{2,1,0:T(8,128)S(1)}, f32[3,18,144,128]{3,2,1,0:T(8,128)S(1)}, f32[7,18,128,128]{3,2,1,0:T(8,128)S(1)}, f32[128,128]{1,0:T(8,128)S(1)}, f32[128,128]{1,0:T(8,128)S(1)}) custom-call(f32[3,20,144,128]{3,2,1,0:T(8,128)S(1)} %get-tuple-element.47.adj_s.adj_i, f32[20,144,128]{2,1,0:T(8,128)S(1)} %get-tuple-element.48.visc_s.visc_i, ...), custom_call_target="tpu_custom_call" | custom-call | flops 2949120 | bytes 4325376 | tf_op jit(solution)/shard_map/face/pallas_call | solution.py:280
  13.8 0.7 %collective-permute-start.4 = (f32[3,128,128]{2,1,0:T(8,128)S(1)}, f32[3,128,128]{2,1,0:T(8,128)S(1)}, u32[]{:S(2)}, u32[]{:S(2)}) collective-permute-start(f32[3,128,128]{2,1,0:T(8,128)S(1)} %get-tuple-element.57.refs_0_), channel_id=1, source_target_pairs={{0,48},{1,49},{2,50},{3,51},{4,52},{5,53},{6,54},{7,55}} | collective-permute-start | bytes 589832 | tf_op jit(solution)/shard_map/ppermute | solution.py:563
  14.5 0.7 %collective-permute-start.3 = (f32[3,128,128]{2,1,0:T(8,128)S(1)}, f32[3,128,128]{2,1,0:T(8,128)S(1)}, u32[]{:S(2)}, u32[]{:S(2)}) collective-permute-start(f32[3,128,128]{2,1,0:T(8,128)S(1)} %get-tuple-element.57.refs_0_), channel_id=1, source_target_pairs={{0,16},{1,17},{2,18},{3,19},{4,20},{5,21},{6,22},{7,23}} | collective-permute-start | bytes 589832 | tf_op jit(solution)/shard_map/ppermute | solution.py:563
  15.9 1.3 %ship.1 = (f32[12,128,128]{2,1,0:T(8,128)}, f32[12,128,128]{2,1,0:T(8,128)}) custom-call(f32[3,20,144,128]{3,2,1,0:T(8,128)S(1)} %get-tuple-element.47.adj_s.adj_i, f32[20,144,128]{2,1,0:T(8,128)S(1)} %get-tuple-element.48.visc_s.visc_i, f32[3,18,128,128]{3,2,1,0:T(8,128)S(1)} %get-tuple-element.49.vel_s.vel_i, f32[128,128]{1,0:T(8,128)S(1)} %get-tuple-element.52.centre), custom_call_target="tpu_custom_call" | custom-call | bytes 2883584 | tf_op jit(solution)/shard_map/ship/pallas_call | solution.py:312
  17.2 2.7 %inner.1 = (f32[3,18,144,128]{3,2,1,0:T(8,128)S(1)}, f32[7,18,128,128]{3,2,1,0:T(8,128)S(1)}, f32[3,16,128,128]{3,2,1,0:T(8,128)S(1)}, f32[128,128]{1,0:T(8,128)S(1)}) custom-call(f32[3,20,144,128]{3,2,1,0:T(8,128)S(1)} %get-tuple-element.47.adj_s.adj_i, ...), custom_call_target="tpu_custom_call", output_to_operand_aliasing={{0}: (7, {}), {1}: (8, {})} | custom-call | flops 12779520 | bytes 18743296 | tf_op jit(solution)/shard_map/inner/pallas_call | solution.py:368
  20.0 0.8 %collective-permute-start.5 = (f32[3,128,128]{2,1,0:T(8,128)S(1)}, f32[3,128,128]{2,1,0:T(8,128)S(1)}, u32[]{:S(2)}, u32[]{:S(2)}) collective-permute-start(f32[3,128,128]{2,1,0:T(8,128)S(1)} %join.2.refs_0_), channel_id=1, source_target_pairs={{0,32},{16,80},{48,112},{64,96},{1,33},{17,81},{49,113},{65,97},{2... | collective-permute-start | bytes 589832 | tf_op jit(solution)/shard_map/ppermute | solution.py:572
  20.8 3.4 %middle.1 = (f32[3,18,144,128]{3,2,1,0:T(8,128)S(1)}, f32[7,18,128,128]{3,2,1,0:T(8,128)S(1)}, f32[3,16,128,128]{3,2,1,0:T(8,128)S(1)}, f32[3,16,128,128]{3,2,1,0:T(8,128)}, bf16[4,512,512]{2,1,0:T(8,128)(2,1)S(1)}) custom-call(f32[3,20,144,128]{3,2,1,0:T(8,128)S(1)} %get-tuple-element.47.adj_s.adj_i, ...), custom_call_target="tpu_custom_call", output_to_operand_aliasing={{0}: (5, {}), {1}: (6, {}), {2}: (7, {})} | custom-call | flops 11796480 | bytes 17301504 | tf_op jit(solution)/shard_map/middle/pallas_call | solution.py:397
  24.3 1.3 %collective-permute-start.6 = (f32[3,128,128]{2,1,0:T(8,128)S(1)}, f32[3,128,128]{2,1,0:T(8,128)S(1)}, u32[]{:S(2)}, u32[]{:S(2)}) collective-permute-start(f32[3,128,128]{2,1,0:T(8,128)S(1)} %join.3.face), channel_id=1, source_target_pairs={{0,8},{16,24},{32,40},{48,56},{64,72},{80,88},{96,104},{112,120},{... | collective-permute-start | bytes 589832 | tf_op jit(solution)/shard_map/ppermute | solution.py:576
  25.6 7.0 %collective-permute-done.6.more = f32[3,128,128]{2,1,0:T(8,128)S(1)} collective-permute-done((f32[3,128,128]{2,1,0:T(8,128)S(1)}, f32[3,128,128]{2,1,0:T(8,128)S(1)}, u32[]{:S(2)}, u32[]{:S(2)}) %collective-permute-start.6) | collective-permute-done | bytes 196640 | tf_op jit(solution)/shard_map/ppermute | solution.py:576
  32.5 6.4 %collective-permute-start.11 = (f32[12,128,128]{2,1,0:T(8,128)S(1)}, f32[12,128,128]{2,1,0:T(8,128)S(1)}, u32[]{:S(2)}, u32[]{:S(2)}) collective-permute-start(f32[12,128,128]{2,1,0:T(8,128)S(1)} %copy-done.3), channel_id=1, source_target_pairs={{0,8},{8,16},{16,24},{24,32},{32,40},{40,48},{48,56},{56,64},{64,7... | collective-permute-start | bytes 2359304 | tf_op jit(solution)/shard_map/ppermute | solution.py:578
  38.9 1.9 %collective-permute-start.12 = (f32[12,128,128]{2,1,0:T(8,128)S(1)}, f32[12,128,128]{2,1,0:T(8,128)S(1)}, u32[]{:S(2)}, u32[]{:S(2)}) collective-permute-start(f32[12,128,128]{2,1,0:T(8,128)S(1)} %copy-done.2), channel_id=1, source_target_pairs={{8,0},{16,8},{24,16},{32,24},{40,32},{48,40},{56,48},{64,56},{72,6... | collective-permute-start | bytes 2359304 | tf_op jit(solution)/shard_map/ppermute | solution.py:579
  41.1 2.8 %collective-permute-start.7 = (f32[2,3,16,128]{3,2,1,0:T(8,128)S(1)}, f32[2,3,16,128]{3,2,1,0:T(8,128)S(1)}, u32[]{:S(2)}, u32[]{:S(2)}) collective-permute-start(f32[2,3,16,128]{3,2,1,0:T(8,128)S(1)} %get-tuple-element.77), channel_id=1, source_target_pairs={{0,4},{1,5},{2,6},{3,7},{4,0},{5,1},{6,2},{7,3},{8,12},{9,13},{10,... | collective-permute-start | bytes 147464 | tf_op jit(solution)/shard_map/ppermute | solution.py:582
  44.0 0.7 %collective-permute-start.9 = (f32[2,3,16,128]{3,2,1,0:T(8,128)S(1)}, f32[2,3,16,128]{3,2,1,0:T(8,128)S(1)}, u32[]{:S(2)}, u32[]{:S(2)}) collective-permute-start(f32[2,3,16,128]{3,2,1,0:T(8,128)S(1)} %get-tuple-element.79), channel_id=1, source_target_pairs={{0,6},{1,7},{2,4},{3,5},{4,2},{5,3},{6,0},{7,1},{8,14},{9,15},{10,... | collective-permute-start | bytes 147464 | tf_op jit(solution)/shard_map/ppermute | solution.py:582
  44.7 1.0 %collective-permute-done.7.b = f32[2,3,16,128]{3,2,1,0:T(8,128)S(1)} collective-permute-done((f32[2,3,16,128]{3,2,1,0:T(8,128)S(1)}, f32[2,3,16,128]{3,2,1,0:T(8,128)S(1)}, u32[]{:S(2)}, u32[]{:S(2)}) %collective-permute-start.7) | collective-permute-done | bytes 49184 | tf_op jit(solution)/shard_map/ppermute | solution.py:582
  45.6 1.4 %collective-permute-done.8.c = f32[2,3,16,128]{3,2,1,0:T(8,128)S(1)} collective-permute-done((f32[2,3,16,128]{3,2,1,0:T(8,128)S(1)}, f32[2,3,16,128]{3,2,1,0:T(8,128)S(1)}, u32[]{:S(2)}, u32[]{:S(2)}) %collective-permute-start.8) | collective-permute-done | bytes 49184 | tf_op jit(solution)/shard_map/ppermute | solution.py:582
  47.1 1.2 %collective-permute-done.9.d = f32[2,3,16,128]{3,2,1,0:T(8,128)S(1)} collective-permute-done((f32[2,3,16,128]{3,2,1,0:T(8,128)S(1)}, f32[2,3,16,128]{3,2,1,0:T(8,128)S(1)}, u32[]{:S(2)}, u32[]{:S(2)}) %collective-permute-start.9) | collective-permute-done | bytes 49184 | tf_op jit(solution)/shard_map/ppermute | solution.py:582
  48.3 1.5 %collective-permute-start.10 = (f32[3,16,128]{2,1,0:T(8,128)S(1)}, f32[3,16,128]{2,1,0:T(8,128)S(1)}, u32[]{:S(2)}, u32[]{:S(2)}) collective-permute-start(f32[3,16,128]{2,1,0:T(8,128)S(1)} %get-tuple-element.80), channel_id=1, source_target_pairs={{0,1},{1,0},{2,3},{3,2},{4,5},{5,4},{6,7},{7,6},{8,9},{9,8},{10,11... | collective-permute-start | bytes 73736 | tf_op jit(solution)/shard_map/ppermute | solution.py:585
  49.8 6.2 %collective-permute-done.12.high = f32[12,128,128]{2,1,0:T(8,128)S(1)} collective-permute-done((f32[12,128,128]{2,1,0:T(8,128)S(1)}, f32[12,128,128]{2,1,0:T(8,128)S(1)}, u32[]{:S(2)}, u32[]{:S(2)}) %collective-permute-start.12) | collective-permute-done | bytes 786464 | tf_op jit(solution)/shard_map/ppermute | solution.py:579
  56.0 3.4 %sides.1 = (f32[3,20,144,128]{3,2,1,0:T(8,128)S(1)}, f32[20,144,128]{2,1,0:T(8,128)S(1)}, f32[3,18,128,128]{3,2,1,0:T(8,128)S(1)}, f32[3,18,144,128]{3,2,1,0:T(8...) custom-call(f32[3,20,144,128]{3,2,1,0:T(8,128)S(1)} %get-tuple-eleme, ...), custom_call_target="tpu_custom_call", output_to_operand_aliasing={{0}: (0, {}), {1}: (1, {}), {2}: (2, {}), {3}: (10, {}), {4... | custom-call | flops 7864320 | bytes 11534336 | tf_op jit(solution)/shard_map/sides/pallas_call | solution.py:449
  59.4 1.0 %product.1 = f32[3,4,512]{2,1,0:T(4,128)} custom-call(f32[3,16,128]{2,1,0:T(8,128)S(1)} %get-tuple-element.89.kept, f32[3,16,128]{2,1,0:T(8,128)S(1)} %collective-permute-done.10.came, bf16[4,512,512]{2,1,0:T(8,128)(2,1)S(1)} %get-tuple-element.91.filters), custom_call_target="tpu_custom_call" | custom-call | tf_op jit(solution)/shard_map/product/pallas_call | solution.py:539
  (21 shorter events, 1.0 us)
Async XLA Ops:
  4.8 7.4 %collective-permute-start = (f32[192,128]{1,0:T(8,128)S(1)}, f32[192,128]{1,0:T(8,128)S(1)}, u32[]{:S(2)}, u32[]{:S(2)}) collective-permute-start(f32[192,128]{1,0:T(8,128)S(1)} %get-tuple-element.50.zl), channel_id=1, source_target_pairs={{0,1},{1,2},{2,3},{3,4},{4,5},{5,6},{6,7},{7,0},{8,9},{9,10},{10,1... | collective-permute-start | bytes 294920 | tf_op jit(solution)/shard_map/ppermute | solution.py:559
  6.1 6.0 %collective-permute-start.1 = (f32[192,128]{1,0:T(8,128)S(1)}, f32[192,128]{1,0:T(8,128)S(1)}, u32[]{:S(2)}, u32[]{:S(2)}) collective-permute-start(f32[192,128]{1,0:T(8,128)S(1)} %get-tuple-element.51.zr), channel_id=1, source_target_pairs={{1,0},{2,1},{3,2},{4,3},{5,4},{6,5},{7,6},{0,7},{9,8},{10,9},{11,1... | collective-permute-start | bytes 294920 | tf_op jit(solution)/shard_map/ppermute | solution.py:560
  13.8 6.1 %collective-permute-start.4 = (f32[3,128,128]{2,1,0:T(8,128)S(1)}, f32[3,128,128]{2,1,0:T(8,128)S(1)}, u32[]{:S(2)}, u32[]{:S(2)}) collective-permute-start(f32[3,128,128]{2,1,0:T(8,128)S(1)} %get-tuple-element.57.refs_0_), channel_id=1, source_target_pairs={{0,48},{1,49},{2,50},{3,51},{4,52},{5,53},{6,54},{7,55}} | collective-permute-start | bytes 589832 | tf_op jit(solution)/shard_map/ppermute | solution.py:563
  14.5 5.4 %collective-permute-start.3 = (f32[3,128,128]{2,1,0:T(8,128)S(1)}, f32[3,128,128]{2,1,0:T(8,128)S(1)}, u32[]{:S(2)}, u32[]{:S(2)}) collective-permute-start(f32[3,128,128]{2,1,0:T(8,128)S(1)} %get-tuple-element.57.refs_0_), channel_id=1, source_target_pairs={{0,16},{1,17},{2,18},{3,19},{4,20},{5,21},{6,22},{7,23}} | collective-permute-start | bytes 589832 | tf_op jit(solution)/shard_map/ppermute | solution.py:563
  15.2 4.7 %collective-permute-start.2 = (f32[3,128,128]{2,1,0:T(8,128)S(1)}, f32[3,128,128]{2,1,0:T(8,128)S(1)}, u32[]{:S(2)}, u32[]{:S(2)}) collective-permute-start(f32[3,128,128]{2,1,0:T(8,128)S(1)} %get-tuple-element.57.refs_0_), channel_id=1, source_target_pairs={{0,64},{1,65},{2,66},{3,67},{4,68},{5,69},{6,70},{7,71}} | collective-permute-start | bytes 589832 | tf_op jit(solution)/shard_map/ppermute | solution.py:563
  15.9 1.4 %copy-start = (s32[256,8]{0,1:T(8,128)S(1)}, s32[256,8]{0,1:T(8,128)}, u32[]{:S(2)}) copy-start(s32[256,8]{0,1:T(8,128)} %param.10) | copy-start | bytes 24580
  15.9 1.3 %copy-start.1 = (s32[512]{0:T(512)S(1)}, s32[512]{0:T(512)}, u32[]{:S(2)}) copy-start(s32[512]{0:T(512)} %param.11) | copy-start | bytes 6148
  20.0 12.6 %copy-start.3 = (f32[12,128,128]{2,1,0:T(8,128)S(1)}, f32[12,128,128]{2,1,0:T(8,128)}, u32[]{:S(2)}) copy-start(f32[12,128,128]{2,1,0:T(8,128)} %get-tuple-element.81) | copy-start | bytes 2359300
  20.0 19.0 %copy-start.2 = (f32[12,128,128]{2,1,0:T(8,128)S(1)}, f32[12,128,128]{2,1,0:T(8,128)}, u32[]{:S(2)}) copy-start(f32[12,128,128]{2,1,0:T(8,128)} %get-tuple-element.82) | copy-start | bytes 2359300
  20.0 4.2 %collective-permute-start.5 = (f32[3,128,128]{2,1,0:T(8,128)S(1)}, f32[3,128,128]{2,1,0:T(8,128)S(1)}, u32[]{:S(2)}, u32[]{:S(2)}) collective-permute-start(f32[3,128,128]{2,1,0:T(8,128)S(1)} %join.2.refs_0_), channel_id=1, source_target_pairs={{0,32},{16,80},{48,112},{64,96},{1,33},{17,81},{49,113},{65,97},{2... | collective-permute-start | bytes 589832 | tf_op jit(solution)/shard_map/ppermute | solution.py:572
  24.3 8.3 %collective-permute-start.6 = (f32[3,128,128]{2,1,0:T(8,128)S(1)}, f32[3,128,128]{2,1,0:T(8,128)S(1)}, u32[]{:S(2)}, u32[]{:S(2)}) collective-permute-start(f32[3,128,128]{2,1,0:T(8,128)S(1)} %join.3.face), channel_id=1, source_target_pairs={{0,8},{16,24},{32,40},{48,56},{64,72},{80,88},{96,104},{112,120},{... | collective-permute-start | bytes 589832 | tf_op jit(solution)/shard_map/ppermute | solution.py:576
  32.5 17.2 %collective-permute-start.11 = (f32[12,128,128]{2,1,0:T(8,128)S(1)}, f32[12,128,128]{2,1,0:T(8,128)S(1)}, u32[]{:S(2)}, u32[]{:S(2)}) collective-permute-start(f32[12,128,128]{2,1,0:T(8,128)S(1)} %copy-done.3), channel_id=1, source_target_pairs={{0,8},{8,16},{16,24},{24,32},{32,40},{40,48},{48,56},{56,64},{64,7... | collective-permute-start | bytes 2359304 | tf_op jit(solution)/shard_map/ppermute | solution.py:578
  38.9 17.0 %collective-permute-start.12 = (f32[12,128,128]{2,1,0:T(8,128)S(1)}, f32[12,128,128]{2,1,0:T(8,128)S(1)}, u32[]{:S(2)}, u32[]{:S(2)}) collective-permute-start(f32[12,128,128]{2,1,0:T(8,128)S(1)} %copy-done.2), channel_id=1, source_target_pairs={{8,0},{16,8},{24,16},{32,24},{40,32},{48,40},{56,48},{64,56},{72,6... | collective-permute-start | bytes 2359304 | tf_op jit(solution)/shard_map/ppermute | solution.py:579
  41.1 4.5 %collective-permute-start.7 = (f32[2,3,16,128]{3,2,1,0:T(8,128)S(1)}, f32[2,3,16,128]{3,2,1,0:T(8,128)S(1)}, u32[]{:S(2)}, u32[]{:S(2)}) collective-permute-start(f32[2,3,16,128]{3,2,1,0:T(8,128)S(1)} %get-tuple-element.77), channel_id=1, source_target_pairs={{0,4},{1,5},{2,6},{3,7},{4,0},{5,1},{6,2},{7,3},{8,12},{9,13},{10,... | collective-permute-start | bytes 147464 | tf_op jit(solution)/shard_map/ppermute | solution.py:582
  43.9 3.1 %collective-permute-start.8 = (f32[2,3,16,128]{3,2,1,0:T(8,128)S(1)}, f32[2,3,16,128]{3,2,1,0:T(8,128)S(1)}, u32[]{:S(2)}, u32[]{:S(2)}) collective-permute-start(f32[2,3,16,128]{3,2,1,0:T(8,128)S(1)} %get-tuple-element.78), channel_id=1, source_target_pairs={{0,2},{1,3},{2,0},{3,1},{4,6},{5,7},{6,4},{7,5},{8,10},{9,11},{10,... | collective-permute-start | bytes 147464 | tf_op jit(solution)/shard_map/ppermute | solution.py:582
  44.0 4.3 %collective-permute-start.9 = (f32[2,3,16,128]{3,2,1,0:T(8,128)S(1)}, f32[2,3,16,128]{3,2,1,0:T(8,128)S(1)}, u32[]{:S(2)}, u32[]{:S(2)}) collective-permute-start(f32[2,3,16,128]{3,2,1,0:T(8,128)S(1)} %get-tuple-element.79), channel_id=1, source_target_pairs={{0,6},{1,7},{2,4},{3,5},{4,2},{5,3},{6,0},{7,1},{8,14},{9,15},{10,... | collective-permute-start | bytes 147464 | tf_op jit(solution)/shard_map/ppermute | solution.py:582
  48.3 11.1 %collective-permute-start.10 = (f32[3,16,128]{2,1,0:T(8,128)S(1)}, f32[3,16,128]{2,1,0:T(8,128)S(1)}, u32[]{:S(2)}, u32[]{:S(2)}) collective-permute-start(f32[3,16,128]{2,1,0:T(8,128)S(1)} %get-tuple-element.80), channel_id=1, source_target_pairs={{0,1},{1,0},{2,3},{3,2},{4,5},{5,4},{6,7},{7,6},{8,9},{9,8},{10,11... | collective-permute-start | bytes 73736 | tf_op jit(solution)/shard_map/ppermute | solution.py:585

commit v7 on v6

--- a/solution.py
+++ b/solution.py
@@ -66,7 +66,16 @@
     return started
 
 
-def pack_kernel(adj, vel, visc, adj_s, visc_s, vel_s, zl, zr, acc_l, acc_r, vel_l, vel_r, sems):
+def even(axis):
+    return lax.axis_index(axis) % 2 == 0
+
+
+def in_order(axis, a, b):
+    return jnp.where(even(axis), b, a), jnp.where(even(axis), a, b)
+
+
+def pack_kernel(adj, vel, visc, adj_s, visc_s, vel_s, za, zb, msg_a, msg_b, *rest):
+    acc_l, acc_r, vel_l, vel_r, sems = rest
     inside = pl.ds(8, 128)
     n = 16 // GROUPS
 
@@ -116,22 +125,29 @@
                 acc_l[rows] = left
                 acc_r[rows] = right
             else:
-                zr[rows] = right
-                zl[rows] = roll(left, 2, 1)
+                zb[rows], za[rows] = in_order("gz", roll(left, 2, 1), right)
                 vleft = roll(vleft, 1, 1)
             vel_l[rows] = vleft
             vel_r[rows] = vright
-    even = (lanes((64, 128)) & 1) == 0
-    zr[pl.ds(128, 64)] = jnp.where(even, vel_r[pl.ds(0, 64)], vel_r[pl.ds(64, 64)])
-    zl[pl.ds(128, 64)] = jnp.where(even, vel_l[pl.ds(0, 64)], vel_l[pl.ds(64, 64)])
+    near = jnp.where(even("gx"), 17, 2)
+    for msg, q in ((msg_a, near), (msg_b, 19 - near)):
+        for c in range(3):
+            msg[c] = adj_s[c, q, inside]
+        msg[3] = visc_s[q, inside]
+    first = (lanes((64, 128)) & 1) == 0
+    right = jnp.where(first, vel_r[pl.ds(0, 64)], vel_r[pl.ds(64, 64)])
+    left = jnp.where(first, vel_l[pl.ds(0, 64)], vel_l[pl.ds(64, 64)])
+    zb[pl.ds(128, 64)], za[pl.ds(128, 64)] = in_order("gz", left, right)
 
 
 def pack(adj, vel, visc):
     return pl.pallas_call(
         pack_kernel,
         in_specs=[ANY, ANY, ANY],
-        out_specs=[VM] * 5,
-        out_shape=[in_vmem(STATE[k]) for k in ("adj", "visc", "vel")] + [in_vmem((192, 128))] * 2,
+        out_specs=[VM] * 7,
+        out_shape=[in_vmem(STATE[k]) for k in ("adj", "visc", "vel")]
+        + [in_vmem((192, 128))] * 2
+        + [in_vmem((4, 128, 128))] * 2,
         scratch_shapes=[
             *[pltpu.VMEM((128, 128), F32)] * 4,
             pltpu.SemaphoreType.DMA((GROUPS, 3)),
@@ -156,11 +172,11 @@
 
 def edge_centre(hl, hr):
     odd = (lanes((128, 128)) & 1) == 1
-    return jnp.where(odd, hl[pl.ds(0, 128)], hr[pl.ds(0, 128)])
+    return jnp.where(odd, hl[:128], hr[:128])
 
 
 def edge_velocity(message):
-    both = message[pl.ds(128, 64)]
+    both = message[128:]
     odd = (lanes(both.shape) & 1) == 1
     upper = jnp.where(odd, roll(both, 1, 1), both)
     lower = jnp.where(odd, both, roll(both, -1, 1))
@@ -171,11 +187,10 @@
     lane = lanes((128, 128))
     odd = (lane & 1) == 1
     x = (lane >> 1) & 15
-    first = pl.ds(0, 128)
-    left, right = hl[first], hr[first]
+    left, right = hl[:128], hr[:128]
     centre = jnp.where(odd, left, right)
-    minus = jnp.where(odd, roll(left, 1, 1), roll(zl[first], -1, 1))
-    plus = jnp.where(odd, roll(zr[first], 1, 1), roll(right, -1, 1))
+    minus = jnp.where(odd, roll(left, 1, 1), roll(zl[:128], -1, 1))
+    plus = jnp.where(odd, roll(zr[:128], 1, 1), roll(right, -1, 1))
     velocity = jnp.where(odd, edge_velocity(hl), edge_velocity(hr))
     west = roll(centre, 2, 1)
     east = roll(centre, -2, 1)
@@ -260,8 +275,10 @@
 
 
 def face_kernel(
-    adj_s, visc_s, vel_s, hl, hr, zl, zr, face, mid_s, coef_s, centre, middle
+    adj_s, visc_s, vel_s, ra, rb, za, zb, face, mid_s, coef_s, centre, middle
 ):
+    hl, hr = in_order("gz", ra[...], rb[...])
+    zr, zl = in_order("gz", za[...], zb[...])
     centre[...] = edge_centre(hl, hr)
     middle[...] = edge_middle(hl, hr, zl, zr)
     for c in range(3):
@@ -276,7 +293,7 @@
     second_step(mid_s, coef_s, middle, 0, store)
 
 
-def face_call(state, hl, hr, zl, zr):
+def face_call(state, ha, hb, za, zb):
     return pl.pallas_call(
         face_kernel,
         in_specs=[VM] * 7,
@@ -291,34 +308,7 @@
         compiler_params=params(4),
         cost_estimate=cost(3),
         name="face",
-    )(*[vmem(a) for a in (*state, hl, hr, zl, zr)])
-
-
-def ship_kernel(adj_s, visc_s, vel_s, centre, msg_lo, msg_hi, sems):
-    moved = []
-    inside = pl.ds(8, 128)
-    for msg, q, t in ((msg_lo, 2, 1), (msg_hi, 16, 16)):
-        for c in range(3):
-            moved.append((adj_s.at[c, pl.ds(q, 2), inside], msg.at[pl.ds(2 * c, 2)]))
-            moved.append((vel_s.at[c, pl.ds(t, 1)], msg.at[pl.ds(6 + c, 1)]))
-        moved.append((visc_s.at[pl.ds(q, 2), inside], msg.at[pl.ds(9, 2)]))
-        moved.append((centre, msg.at[11]))
-    for copy in begin(moved, sems):
-        copy.wait()
-
-
-def ship(state, centre):
-    msg = pltpu.HBM((12, 128, 128), F32)
-    return pl.pallas_call(
-        ship_kernel,
-        in_specs=[VM] * 4,
-        out_specs=[ANY, ANY],
-        out_shape=[msg, msg],
-        scratch_shapes=[pltpu.SemaphoreType.DMA((16,))],
-        compiler_params=params(1),
-        cost_estimate=pl.CostEstimate(flops=0, transcendentals=0, bytes_accessed=2 * 2 * 11 * 65536),
-        name="ship",
-    )(*[vmem(a) for a in (*state, centre)])
+    )(*[vmem(a) for a in (*state, ha, hb, za, zb)])
 
 
 def choose(lists, place):
@@ -357,37 +347,47 @@
 
 
 def inner_kernel(
-    adj_s, visc_s, vel_s, centre, middle, lists, place, _, __, mid_s, coef_s, done, chosen
+    adj_i, visc_i, vel_s, centre, middle, lists, place, ra, rb, _, __,
+    adj_s, visc_s, mid_s, coef_s, done, chosen, msg_a, msg_b,
 ):
+    beyond = jnp.where(even("gx"), 18, 1)
+    for msg, q in ((ra, beyond), (rb, 19 - beyond)):
+        for c in range(3):
+            adj_s[c, q, pl.ds(8, 128)] = msg[c]
+        visc_s[q, pl.ds(8, 128)] = msg[3]
+    state = (adj_s, visc_s, vel_s)
+    run_first((0, 15), state, mid_s, coef_s, centre)
+    near = jnp.where(even("gx"), 16, 1)
+    for msg, t in ((msg_a, near), (msg_b, 17 - near)):
+        for c in range(3):
+            msg[c] = mid_s[c, t, pl.ds(8, 128)]
+        msg[3] = centre[...]
     chosen[...] = choose(lists, place)
-    run_first(range(2, 9), (adj_s, visc_s, vel_s), mid_s, coef_s, centre)
-    run_second(range(2, 8), mid_s, coef_s, middle, done)
-
-
-def inner(state, centre, middle, lists, place, mid, coef):
+    run_first(range(2, 9), state, mid_s, coef_s, centre)
+    run_second(range(1, 8), mid_s, coef_s, middle, done)
+
+
+def inner(state, centre, middle, lists, place, ra, rb, mid, coef):
     return pl.pallas_call(
         inner_kernel,
-        in_specs=[VM] * 9,
-        out_specs=[VM] * 4,
-        out_shape=[
-            in_vmem(STATE["mid"]),
-            in_vmem(STATE["coef"]),
-            in_vmem(FIELD),
-            in_vmem((128, 128)),
-        ],
-        input_output_aliases={7: 0, 8: 1},
+        in_specs=[VM] * 11,
+        out_specs=[VM] * 8,
+        out_shape=[in_vmem(STATE[k]) for k in ("adj", "visc", "mid", "coef")]
+        + [in_vmem(FIELD), in_vmem((128, 128))]
+        + [in_vmem((4, 128, 128))] * 2,
+        input_output_aliases={0: 0, 1: 1, 9: 2, 10: 3},
         compiler_params=params(4),
-        cost_estimate=cost(13),
+        cost_estimate=cost(16),
         name="inner",
-    )(*[vmem(a) for a in (*state, centre, middle)], lists, place, vmem(mid), vmem(coef))
+    )(*[vmem(a) for a in (*state, centre, middle)], lists, place, *[vmem(a) for a in (ra, rb, mid, coef)])
 
 
 def middle_kernel(
     adj_s, visc_s, vel_s, centre, middle, _, __, ___, filters, mid_s, coef_s, done, out, kept, sems
 ):
-    started = begin([(done.at[:, pl.ds(2, 6)], out.at[:, pl.ds(2, 6)]), (filters, kept)], sems)
+    started = begin([(done.at[:, pl.ds(1, 7)], out.at[:, pl.ds(1, 7)]), (filters, kept)], sems)
     run_first(range(9, 15), (adj_s, visc_s, vel_s), mid_s, coef_s, centre)
-    run_second(range(8, 14), mid_s, coef_s, middle, done)
+    run_second(range(8, 15), mid_s, coef_s, middle, done)
     for copy in started:
         copy.wait()
 
@@ -408,55 +408,41 @@
     )(*held, hbm(filters))
 
 
-def sides_kernel(
-    adj_i, visc_i, vel_i, centre, hl, hr, zl, zr, low, high, _, __, ___, ____,
-    adj_s, visc_s, vel_s, mid_s, coef_s, done, out, edges, sems,
+def last_kernel(
+    ha, hb, za, zb, ra, rb, _, coef_s, __, ___, mid_s, done, out, edges, sems
 ):
-    started = begin([(done.at[:, pl.ds(8, 6)], out.at[:, pl.ds(8, 6)])], sems)
-    for msg, q, t in ((low, 0, 0), (high, 18, 17)):
-        for i in range(2):
-            for c in range(3):
-                adj_s[c, q + i, pl.ds(8, 128)] = msg[2 * c + i]
-            visc_s[q + i, pl.ds(8, 128)] = msg[9 + i]
-        for d in range(3):
-            vel_s[d, t] = msg[6 + d]
-    edges[...] = edge_middle(hl, hr, zl, zr, low[11], high[11])
-    state = (adj_s, visc_s, vel_s)
-    first_step(*state, mid_s, coef_s, low.at[11], -1, 15)
-    first_step(*state, mid_s, coef_s, high.at[11], 16, 0)
-    run_first((0, 15), state, mid_s, coef_s, centre)
-    gx = lax.axis_index("gx")
-    for t, end in ((0, 0), (17, lax.axis_size("gx") - 1)):
-
-        @pl.when(gx == end)
-        def _(t=t):
-            for c in range(3):
-                mid_s[c, t] = jnp.zeros((144, 128), F32)
-
-    for i, x in enumerate((0, 14)):
-        run_second((x, x + 1), mid_s, coef_s, edges, done)
-        copy = pltpu.make_async_copy(
-            done.at[:, pl.ds(x, 2)], out.at[:, pl.ds(x, 2)], sems.at[i + 1]
-        )
-        copy.start()
-        started.append(copy)
-    for copy in started:
+    copies = [
+        pltpu.make_async_copy(done.at[:, pl.ds(x, n)], out.at[:, pl.ds(x, n)], sems.at[i])
+        for i, (x, n) in enumerate(((8, 7), (0, 1), (15, 1)))
+    ]
+    copies[0].start()
+    hl, hr = in_order("gz", ha[...], hb[...])
+    zr, zl = in_order("gz", za[...], zb[...])
+    low, high = in_order("gx", ra[3], rb[3])
+    edges[...] = edge_middle(hl, hr, zl, zr, low, high)
+    beyond = jnp.where(even("gx"), 17, 0)
+    for msg, t in ((ra, beyond), (rb, 17 - beyond)):
+        for c in range(3):
+            mid_s[c, t, pl.ds(8, 128)] = msg[c]
+    for i, x in ((1, 0), (2, 15)):
+        run_second((x,), mid_s, coef_s, edges, done)
+        copies[i].start()
+    for copy in copies:
         copy.wait()
 
 
-def sides_call(state, centre, hl, hr, zl, zr, low, high, mid, coef, done, out):
-    held = [vmem(a) for a in (*state, centre, hl, hr, zl, zr, low, high, mid, coef, done)]
-    return pl.pallas_call(
-        sides_kernel,
-        in_specs=[VM] * 13 + [ANY],
-        out_specs=[VM] * 6 + [ANY],
-        out_shape=[in_vmem(STATE[k]) for k in ("adj", "visc", "vel", "mid", "coef")]
-        + [in_vmem(FIELD), pltpu.HBM(FIELD, F32)],
+def last_call(ha, hb, za, zb, ra, rb, mid, coef, done, out):
+    held = [vmem(a) for a in (ha, hb, za, zb, ra, rb, mid, coef, done)]
+    return pl.pallas_call(
+        last_kernel,
+        in_specs=[VM] * 9 + [ANY],
+        out_specs=[VM] * 2 + [ANY],
+        out_shape=[in_vmem(STATE["mid"]), in_vmem(FIELD), pltpu.HBM(FIELD, F32)],
         scratch_shapes=[pltpu.VMEM((128, 128), F32), pltpu.SemaphoreType.DMA((3,))],
-        input_output_aliases={0: 0, 1: 1, 2: 2, 10: 3, 11: 4, 12: 5, 13: 6},
+        input_output_aliases={6: 0, 8: 1, 9: 2},
         compiler_params=params(4),
-        cost_estimate=cost(8),
-        name="sides",
+        cost_estimate=cost(4),
+        name="last",
     )(*held, hbm(out))[-1]
 
 
@@ -550,40 +536,42 @@
 def shards(adjoint, velocity, viscosity, filters, block_tiles, tile_place):
     nx = lax.axis_size("gx")
     nz = lax.axis_size("gz")
-    ring = [(i, (i + 1) % nz) for i in range(nz)]
-    back = [(b, a) for a, b in ring]
-    along = [(i, i + 1) for i in range(nx - 1)]
-    against = [(b, a) for a, b in along]
-
-    *state, zl, zr = pack(adjoint, velocity, viscosity)
-    hl = lax.ppermute(zl, "gz", ring)
-    hr = lax.ppermute(zr, "gz", back)
-    face, mid, coef, centre, middle = face_call(state, hl, hr, zl, zr)
+    inside_z = [(i, i ^ 1) for i in range(nz)]
+    across_z = [(i, (i + 1 if i % 2 else i - 1) % nz) for i in range(nz)]
+    inside_x = [(i, i ^ 1) for i in range(nx)]
+    across_x = [(i, i + 1 if i % 2 else i - 1) for i in range(1, nx - 1)]
+
+    *state, za, zb, msg_a, msg_b = pack(adjoint, velocity, viscosity)
+    ha = lax.ppermute(za, "gz", inside_z)
+    hb = lax.ppermute(zb, "gz", across_z)
+    ha, hb, msg_a, msg_b = lax.optimization_barrier((ha, hb, msg_a, msg_b))
+    ra = lax.ppermute(msg_a, "gx", inside_x)
+    rb = lax.ppermute(msg_b, "gx", across_x)
+    face, mid, coef, centre, middle = face_call(state, ha, hb, za, zb)
 
     got = [lax.ppermute(face, "gx", [(0, k)]) for k in (8, 2, 6)]
-    mid, coef, done, chosen = inner(
-        state, centre, middle, block_tiles.T, tile_place.reshape(1, -1), mid, coef
+    adj, visc, mid, coef, done, chosen, msg_a, msg_b = inner(
+        state, centre, middle, block_tiles.T, tile_place.reshape(1, -1), ra, rb, mid, coef
     )
-    msg_lo, msg_hi = ship(state, centre)
-    *got, mid, coef, done, msg_lo, msg_hi = lax.optimization_barrier(
-        (*got, mid, coef, done, msg_lo, msg_hi)
-    )
+    *got, mid, coef, done = lax.optimization_barrier((*got, mid, coef, done))
     face = join(face, *got)
     far = lax.ppermute(face, "gx", [(0, 4), (2, 10), (6, 14), (8, 12)])
-    mid, coef, done, out, near = middle_call(state, centre, middle, mid, coef, done, filters)
+    mid, coef, done, out, near = middle_call(
+        (adj, visc, state[2]), centre, middle, mid, coef, done, filters
+    )
     far, mid, coef, done = lax.optimization_barrier((far, mid, coef, done))
     face = join(face, far)
     other = lax.ppermute(face, "gx", [(i, i + 1) for i in range(0, nx, 2)])
-    other, msg_lo, msg_hi = lax.optimization_barrier((other, msg_lo, msg_hi))
-    low = lax.ppermute(msg_hi, "gx", along)
-    high = lax.ppermute(msg_lo, "gx", against)
+    other, msg_a, msg_b = lax.optimization_barrier((other, msg_a, msg_b))
+    ra = lax.ppermute(msg_a, "gx", inside_x)
+    rb = lax.ppermute(msg_b, "gx", across_x)
     own, *pairs = partial_sums(chosen, face, other)
-    pairs = [own] + [
+    pairs = [
         lax.ppermute(pairs[k // 2 - 1], "gz", [(i, i ^ k) for i in range(nz)]) for k in (4, 2, 6)
     ]
-    kept, given = gather(pairs)
-    came = lax.ppermute(given, "gz", [(i, i ^ 1) for i in range(nz)])
-    out = sides_call(state, centre, hl, hr, zl, zr, low, high, mid, coef, done, out)
+    kept, given = gather((own, *pairs))
+    came = lax.ppermute(given, "gz", inside_z)
+    out = last_call(ha, hb, za, zb, ra, rb, mid, coef, done, out)
     came, out = lax.optimization_barrier((came, out))
     gradient = product((kept, came), near).transpose(1, 0, 2)
     return out, gradient

time: 60.7 us -> 56 us (0.923)
  the two profiles are of different devices: /device:TPU:7 before, /device:TPU:24 now
where the time goes in v7:
time: 56 us; the launch traced here: 55.1 us
  starting transfers between devices  21.9 us (39%)
  waiting for transfers between devices  16.5 us (29%)
  Pallas kernels  15.9 us (28%)
  between operations  0.81 us (1%)
    ppermute x2, starting transfers between devices, shards(): rb = lax.ppermute(msg_b, 'gx', across_x)  8.02 us
    ppermute x3, waiting for transfers between devices, shards(): lax.ppermute(pairs[k // 2 - 1], 'gz', [(i, i ^ k) for i in range(nz)])  4.78 us
    ppermute x3, starting transfers between devices, shards(): lax.ppermute(pairs[k // 2 - 1], 'gz', [(i, i ^ k) for i in range(nz)])  4.67 us
    pallas_call x1, Pallas kernels, pack(): pl.pallas_call(pack_kernel, in_specs=[ANY, ANY, ANY], out_specs=[VM] * 7,...  4.1 us
    ppermute x1, waiting for transfers between devices, shards(): hb = lax.ppermute(zb, 'gz', across_z)  3.38 us
    pallas_call x1, Pallas kernels, middle_call(): pl.pallas_call(middle_kernel, in_specs=[VM] * 8 + [ANY], out_specs=[VM] *...  3.3 us
    pallas_call x1, Pallas kernels, inner(): pl.pallas_call(inner_kernel, in_specs=[VM] * 11, out_specs=[VM] * 8, out_...  3.29 us
    ppermute x3, waiting for transfers between devices, shards(): got = [lax.ppermute(face, 'gx', [(0, k)]) for k in (8, 2, 6)]  2.99 us
  transfers between devices with their start and end apart: 15, of which 9 were waited for; matrix products, arithmetic and copies ran while one was open for 0% of the time, Pallas kernels for 19%

profile of v7, /device:TPU:24, one launch (start us, length us, event | category | flops | bytes accessed | tf_op | source)
XLA Modules:
  0.0 55.1 jit_solution(11495758071457079859)
XLA Ops:
  0.6 4.1 %pack.1 = (f32[3,20,144,128]{3,2,1,0:T(8,128)S(1)}, f32[20,144,128]{2,1,0:T(8,128)S(1)}, f32[3,18,128,128]{3,2,1,0:T(8,128)S(1)}, f32[192,128]{1,0:T(8,128)S(1)}...) custom-call(f32[3,16,128,128]{3,2,1,0:T(8,128)} %adj.1, f32[3,16,128,128]{3,2,1,0:T(8,128)} %vel.1, ...), custom_call_target="tpu_custom_call" | custom-call | tf_op jit(solution)/shard_map/pack/pallas_call | solution.py:144
  4.7 0.8 %collective-permute-start = (f32[192,128]{1,0:T(8,128)S(1)}, f32[192,128]{1,0:T(8,128)S(1)}, u32[]{:S(2)}, u32[]{:S(2)}) collective-permute-start(f32[192,128]{1,0:T(8,128)S(1)} %get-tuple-element.56.za), channel_id=1, source_target_pairs={{0,1},{1,0},{2,3},{3,2},{4,5},{5,4},{6,7},{7,6},{8,9},{9,8},{10,11... | collective-permute-start | bytes 294920 | tf_op jit(solution)/shard_map/ppermute | solution.py:545
  5.6 2.6 %collective-permute-start.1 = (f32[192,128]{1,0:T(8,128)S(1)}, f32[192,128]{1,0:T(8,128)S(1)}, u32[]{:S(2)}, u32[]{:S(2)}) collective-permute-start(f32[192,128]{1,0:T(8,128)S(1)} %get-tuple-element.57.zb), channel_id=1, source_target_pairs={{0,7},{1,2},{2,1},{3,4},{4,3},{5,6},{6,5},{7,0},{8,15},{9,10},{10,... | collective-permute-start | bytes 294920 | tf_op jit(solution)/shard_map/ppermute | solution.py:546
  8.2 1.2 %collective-permute-done.ra.ha = f32[192,128]{1,0:T(8,128)S(1)} collective-permute-done((f32[192,128]{1,0:T(8,128)S(1)}, f32[192,128]{1,0:T(8,128)S(1)}, u32[]{:S(2)}, u32[]{:S(2)}) %collective-permute-start) | collective-permute-done | bytes 98336 | tf_op jit(solution)/shard_map/ppermute | solution.py:545
  9.4 3.4 %collective-permute-done.1.rb.hb = f32[192,128]{1,0:T(8,128)S(1)} collective-permute-done((f32[192,128]{1,0:T(8,128)S(1)}, f32[192,128]{1,0:T(8,128)S(1)}, u32[]{:S(2)}, u32[]{:S(2)}) %collective-permute-start.1) | collective-permute-done | bytes 98336 | tf_op jit(solution)/shard_map/ppermute | solution.py:546
  12.8 5.4 %collective-permute-start.3 = (f32[4,128,128]{2,1,0:T(8,128)S(1)}, f32[4,128,128]{2,1,0:T(8,128)S(1)}, u32[]{:S(2)}, u32[]{:S(2)}) collective-permute-start(f32[4,128,128]{2,1,0:T(8,128)S(1)} %get-tuple-element.65), channel_id=1, source_target_pairs={{8,16},{16,8},{24,32},{32,24},{40,48},{48,40},{56,64},{64,56},{72,... | collective-permute-start | bytes 786440 | tf_op jit(solution)/shard_map/ppermute | solution.py:549
  18.3 1.7 %face.1 = (f32[3,128,128]{2,1,0:T(8,128)S(1)}, f32[3,18,144,128]{3,2,1,0:T(8,128)S(1)}, f32[7,18,128,128]{3,2,1,0:T(8,128)S(1)}, f32[128,128]{1,0:T(8,128)S(1)}, f32[128,128]{1,0:T(8,128)S(1)}) custom-call(f32[3,20,144,128]{3,2,1,0:T(8,128)S(1)} %get-tuple-element.53.adj_s.adj_i, f32[20,144,128]{2,1,0:T(8,128)S(1)} %get-tuple-element.54.visc_s.visc_i, ...), custom_call_target="tpu_custom_call" | custom-call | flops 2949120 | bytes 4325376 | tf_op jit(solution)/shard_map/face/pallas_call | solution.py:297
  20.0 0.7 %collective-permute-start.6 = (f32[3,128,128]{2,1,0:T(8,128)S(1)}, f32[3,128,128]{2,1,0:T(8,128)S(1)}, u32[]{:S(2)}, u32[]{:S(2)}) collective-permute-start(f32[3,128,128]{2,1,0:T(8,128)S(1)} %get-tuple-element.69.refs_0_), channel_id=1, source_target_pairs={{0,48},{1,49},{2,50},{3,51},{4,52},{5,53},{6,54},{7,55}} | collective-permute-start | bytes 589832 | tf_op jit(solution)/shard_map/ppermute | solution.py:552
  21.3 1.3 %collective-permute-start.4 = (f32[3,128,128]{2,1,0:T(8,128)S(1)}, f32[3,128,128]{2,1,0:T(8,128)S(1)}, u32[]{:S(2)}, u32[]{:S(2)}) collective-permute-start(f32[3,128,128]{2,1,0:T(8,128)S(1)} %get-tuple-element.69.refs_0_), channel_id=1, source_target_pairs={{0,64},{1,65},{2,66},{3,67},{4,68},{5,69},{6,70},{7,71}} | collective-permute-start | bytes 589832 | tf_op jit(solution)/shard_map/ppermute | solution.py:552
  22.6 1.5 %collective-permute-done.3.rb = f32[4,128,128]{2,1,0:T(8,128)S(1)} collective-permute-done((f32[4,128,128]{2,1,0:T(8,128)S(1)}, f32[4,128,128]{2,1,0:T(8,128)S(1)}, u32[]{:S(2)}, u32[]{:S(2)}) %collective-permute-start.3) | collective-permute-done | bytes 262176 | tf_op jit(solution)/shard_map/ppermute | solution.py:549
  24.1 3.3 %inner.1 = (f32[3,20,144,128]{3,2,1,0:T(8,128)S(1)}, f32[20,144,128]{2,1,0:T(8,128)S(1)}, f32[3,18,144,128]{3,2,1,0:T(8,128)S(1)}, f32[7,18,128,128]{3,2,1,0:T(8...) custom-call(f32[3,20,144,128]{3,2,1,0:T(8,128)S(1)} %get-tuple-eleme, ...), custom_call_target="tpu_custom_call", output_to_operand_aliasing={{0}: (0, {}), {1}: (1, {}), {2}: (9, {}), {3}: (10, {})} | custom-call | flops 15728640 | bytes 23068672 | tf_op jit(solution)/shard_map/inner/pallas_call | solution.py:371
  27.4 3.0 %collective-permute-done.4.refs_1_ = f32[3,128,128]{2,1,0:T(8,128)S(1)} collective-permute-done((f32[3,128,128]{2,1,0:T(8,128)S(1)}, f32[3,128,128]{2,1,0:T(8,128)S(1)}, u32[]{:S(2)}, u32[]{:S(2)}) %collective-permute-start.4) | collective-permute-done | bytes 196640 | tf_op jit(solution)/shard_map/ppermute | solution.py:552
  30.4 1.3 %collective-permute-start.7 = (f32[3,128,128]{2,1,0:T(8,128)S(1)}, f32[3,128,128]{2,1,0:T(8,128)S(1)}, u32[]{:S(2)}, u32[]{:S(2)}) collective-permute-start(f32[3,128,128]{2,1,0:T(8,128)S(1)} %join.2.refs_0_), channel_id=1, source_target_pairs={{0,32},{16,80},{48,112},{64,96},{1,33},{17,81},{49,113},{65,97},{2... | collective-permute-start | bytes 589832 | tf_op jit(solution)/shard_map/ppermute | solution.py:558
  31.8 3.3 %middle.1 = (f32[3,18,144,128]{3,2,1,0:T(8,128)S(1)}, f32[7,18,128,128]{3,2,1,0:T(8,128)S(1)}, f32[3,16,128,128]{3,2,1,0:T(8,128)S(1)}, f32[3,16,128,128]{3,2,1,0:T(8,128)}, bf16[4,512,512]{2,1,0:T(8,128)(2,1)S(1)}) custom-call(f32[3,20,144,128]{3,2,1,0:T(8,128)S(1)} %get-tuple-element.76.adj_s, ...), custom_call_target="tpu_custom_call", output_to_operand_aliasing={{0}: (5, {}), {1}: (6, {}), {2}: (7, {})} | custom-call | flops 11796480 | bytes 17301504 | tf_op jit(solution)/shard_map/middle/pallas_call | solution.py:397
  35.1 1.3 %collective-permute-start.8 = (f32[3,128,128]{2,1,0:T(8,128)S(1)}, f32[3,128,128]{2,1,0:T(8,128)S(1)}, u32[]{:S(2)}, u32[]{:S(2)}) collective-permute-start(f32[3,128,128]{2,1,0:T(8,128)S(1)} %join.3.face), channel_id=1, source_target_pairs={{0,8},{16,24},{32,40},{48,56},{64,72},{80,88},{96,104},{112,120},{... | collective-permute-start | bytes 589832 | tf_op jit(solution)/shard_map/ppermute | solution.py:564
  36.4 1.0 %collective-permute-done.8.more = f32[3,128,128]{2,1,0:T(8,128)S(1)} collective-permute-done((f32[3,128,128]{2,1,0:T(8,128)S(1)}, f32[3,128,128]{2,1,0:T(8,128)S(1)}, u32[]{:S(2)}, u32[]{:S(2)}) %collective-permute-start.8) | collective-permute-done | bytes 196640 | tf_op jit(solution)/shard_map/ppermute | solution.py:564
  37.8 2.6 %collective-permute-start.14 = (f32[4,128,128]{2,1,0:T(8,128)S(1)}, f32[4,128,128]{2,1,0:T(8,128)S(1)}, u32[]{:S(2)}, u32[]{:S(2)}) collective-permute-start(f32[4,128,128]{2,1,0:T(8,128)S(1)} %get-tuple-element.94), channel_id=1, source_target_pairs={{8,16},{16,8},{24,32},{32,24},{40,48},{48,40},{56,64},{64,56},{72,... | collective-permute-start | bytes 786440 | tf_op jit(solution)/shard_map/ppermute | solution.py:567
  40.7 3.7 %collective-permute-start.9 = (f32[2,3,16,128]{3,2,1,0:T(8,128)S(1)}, f32[2,3,16,128]{3,2,1,0:T(8,128)S(1)}, u32[]{:S(2)}, u32[]{:S(2)}) collective-permute-start(f32[2,3,16,128]{3,2,1,0:T(8,128)S(1)} %get-tuple-element.89), channel_id=1, source_target_pairs={{0,4},{1,5},{2,6},{3,7},{4,0},{5,1},{6,2},{7,3},{8,12},{9,13},{10,... | collective-permute-start | bytes 147464 | tf_op jit(solution)/shard_map/ppermute | solution.py:570
  45.3 1.1 %collective-permute-done.9.b = f32[2,3,16,128]{3,2,1,0:T(8,128)S(1)} collective-permute-done((f32[2,3,16,128]{3,2,1,0:T(8,128)S(1)}, f32[2,3,16,128]{3,2,1,0:T(8,128)S(1)}, u32[]{:S(2)}, u32[]{:S(2)}) %collective-permute-start.9) | collective-permute-done | bytes 49184 | tf_op jit(solution)/shard_map/ppermute | solution.py:570
  46.4 2.0 %collective-permute-done.10.c = f32[2,3,16,128]{3,2,1,0:T(8,128)S(1)} collective-permute-done((f32[2,3,16,128]{3,2,1,0:T(8,128)S(1)}, f32[2,3,16,128]{3,2,1,0:T(8,128)S(1)}, u32[]{:S(2)}, u32[]{:S(2)}) %collective-permute-start.10) | collective-permute-done | bytes 49184 | tf_op jit(solution)/shard_map/ppermute | solution.py:570
  48.4 1.7 %collective-permute-done.11.d = f32[2,3,16,128]{3,2,1,0:T(8,128)S(1)} collective-permute-done((f32[2,3,16,128]{3,2,1,0:T(8,128)S(1)}, f32[2,3,16,128]{3,2,1,0:T(8,128)S(1)}, u32[]{:S(2)}, u32[]{:S(2)}) %collective-permute-start.11) | collective-permute-done | bytes 49184 | tf_op jit(solution)/shard_map/ppermute | solution.py:570
  50.2 2.2 %last.1 = (f32[3,18,144,128]{3,2,1,0:T(8,128)S(1)}, f32[3,16,128,128]{3,2,1,0:T(8,128)S(1)}, f32[3,16,128,128]{3,2,1,0:T(8,128)}) custom-call(f32[192,128]{1,0:T(8,128)S(1)} %collective-permute-done.ra.ha, f32[192,128]{1,0:T(8,128)S(1)} %collective-permute-done.1.rb.hb, ...), custom_call_target="tpu_custom_call", output_to_operand_aliasing={{0}: (6, {}), {1}: (8, {}), {2}: (9, {})} | custom-call | flops 3932160 | bytes 5767168 | tf_op jit(solution)/shard_map/last/pallas_call | solution.py:436
  52.5 1.6 %collective-permute-done.12.came = f32[3,16,128]{2,1,0:T(8,128)S(1)} collective-permute-done((f32[3,16,128]{2,1,0:T(8,128)S(1)}, f32[3,16,128]{2,1,0:T(8,128)S(1)}, u32[]{:S(2)}, u32[]{:S(2)}) %collective-permute-start.12) | collective-permute-done | bytes 24608 | tf_op jit(solution)/shard_map/ppermute | solution.py:573
  54.0 1.0 %product.1 = f32[3,4,512]{2,1,0:T(4,128)} custom-call(f32[3,16,128]{2,1,0:T(8,128)S(1)} %get-tuple-element.101.kept, f32[3,16,128]{2,1,0:T(8,128)S(1)} %collective-permute-done.12.came, bf16[4,512,512]{2,1,0:T(8,128)(2,1)S(1)} %get-tuple-element.103.filters), custom_call_target="tpu_custom_call" | custom-call | tf_op jit(solution)/shard_map/product/pallas_call | solution.py:525
  (20 shorter events, 2.5 us)
Async XLA Ops:
  4.7 4.7 %collective-permute-start = (f32[192,128]{1,0:T(8,128)S(1)}, f32[192,128]{1,0:T(8,128)S(1)}, u32[]{:S(2)}, u32[]{:S(2)}) collective-permute-start(f32[192,128]{1,0:T(8,128)S(1)} %get-tuple-element.56.za), channel_id=1, source_target_pairs={{0,1},{1,0},{2,3},{3,2},{4,5},{5,4},{6,7},{7,6},{8,9},{9,8},{10,11... | collective-permute-start | bytes 294920 | tf_op jit(solution)/shard_map/ppermute | solution.py:545
  5.6 7.3 %collective-permute-start.1 = (f32[192,128]{1,0:T(8,128)S(1)}, f32[192,128]{1,0:T(8,128)S(1)}, u32[]{:S(2)}, u32[]{:S(2)}) collective-permute-start(f32[192,128]{1,0:T(8,128)S(1)} %get-tuple-element.57.zb), channel_id=1, source_target_pairs={{0,7},{1,2},{2,1},{3,4},{4,3},{5,6},{6,5},{7,0},{8,15},{9,10},{10,... | collective-permute-start | bytes 294920 | tf_op jit(solution)/shard_map/ppermute | solution.py:546
  12.8 9.8 %collective-permute-start.2 = (f32[4,128,128]{2,1,0:T(8,128)S(1)}, f32[4,128,128]{2,1,0:T(8,128)S(1)}, u32[]{:S(2)}, u32[]{:S(2)}) collective-permute-start(f32[4,128,128]{2,1,0:T(8,128)S(1)} %get-tuple-element.64), channel_id=1, source_target_pairs={{0,8},{8,0},{16,24},{24,16},{32,40},{40,32},{48,56},{56,48},{64,72... | collective-permute-start | bytes 786440 | tf_op jit(solution)/shard_map/ppermute | solution.py:548
  12.8 11.3 %collective-permute-start.3 = (f32[4,128,128]{2,1,0:T(8,128)S(1)}, f32[4,128,128]{2,1,0:T(8,128)S(1)}, u32[]{:S(2)}, u32[]{:S(2)}) collective-permute-start(f32[4,128,128]{2,1,0:T(8,128)S(1)} %get-tuple-element.65), channel_id=1, source_target_pairs={{8,16},{16,8},{24,32},{32,24},{40,48},{48,40},{56,64},{64,56},{72,... | collective-permute-start | bytes 786440 | tf_op jit(solution)/shard_map/ppermute | solution.py:549
  18.3 5.9 %copy-start = (s32[256,8]{0,1:T(8,128)S(1)}, s32[256,8]{0,1:T(8,128)}, u32[]{:S(2)}) copy-start(s32[256,8]{0,1:T(8,128)} %param.10) | copy-start | bytes 24580
  18.3 5.8 %copy-start.1 = (s32[512]{0:T(512)S(1)}, s32[512]{0:T(512)}, u32[]{:S(2)}) copy-start(s32[512]{0:T(512)} %param.11) | copy-start | bytes 6148
  20.0 7.4 %collective-permute-start.6 = (f32[3,128,128]{2,1,0:T(8,128)S(1)}, f32[3,128,128]{2,1,0:T(8,128)S(1)}, u32[]{:S(2)}, u32[]{:S(2)}) collective-permute-start(f32[3,128,128]{2,1,0:T(8,128)S(1)} %get-tuple-element.69.refs_0_), channel_id=1, source_target_pairs={{0,48},{1,49},{2,50},{3,51},{4,52},{5,53},{6,54},{7,55}} | collective-permute-start | bytes 589832 | tf_op jit(solution)/shard_map/ppermute | solution.py:552
  20.6 6.8 %collective-permute-start.5 = (f32[3,128,128]{2,1,0:T(8,128)S(1)}, f32[3,128,128]{2,1,0:T(8,128)S(1)}, u32[]{:S(2)}, u32[]{:S(2)}) collective-permute-start(f32[3,128,128]{2,1,0:T(8,128)S(1)} %get-tuple-element.69.refs_0_), channel_id=1, source_target_pairs={{0,16},{1,17},{2,18},{3,19},{4,20},{5,21},{6,22},{7,23}} | collective-permute-start | bytes 589832 | tf_op jit(solution)/shard_map/ppermute | solution.py:552
  21.3 9.1 %collective-permute-start.4 = (f32[3,128,128]{2,1,0:T(8,128)S(1)}, f32[3,128,128]{2,1,0:T(8,128)S(1)}, u32[]{:S(2)}, u32[]{:S(2)}) collective-permute-start(f32[3,128,128]{2,1,0:T(8,128)S(1)} %get-tuple-element.69.refs_0_), channel_id=1, source_target_pairs={{0,64},{1,65},{2,66},{3,67},{4,68},{5,69},{6,70},{7,71}} | collective-permute-start | bytes 589832 | tf_op jit(solution)/shard_map/ppermute | solution.py:552
  30.4 4.6 %collective-permute-start.7 = (f32[3,128,128]{2,1,0:T(8,128)S(1)}, f32[3,128,128]{2,1,0:T(8,128)S(1)}, u32[]{:S(2)}, u32[]{:S(2)}) collective-permute-start(f32[3,128,128]{2,1,0:T(8,128)S(1)} %join.2.refs_0_), channel_id=1, source_target_pairs={{0,32},{16,80},{48,112},{64,96},{1,33},{17,81},{49,113},{65,97},{2... | collective-permute-start | bytes 589832 | tf_op jit(solution)/shard_map/ppermute | solution.py:558
  35.1 2.4 %collective-permute-start.8 = (f32[3,128,128]{2,1,0:T(8,128)S(1)}, f32[3,128,128]{2,1,0:T(8,128)S(1)}, u32[]{:S(2)}, u32[]{:S(2)}) collective-permute-start(f32[3,128,128]{2,1,0:T(8,128)S(1)} %join.3.face), channel_id=1, source_target_pairs={{0,8},{16,24},{32,40},{48,56},{64,72},{80,88},{96,104},{112,120},{... | collective-permute-start | bytes 589832 | tf_op jit(solution)/shard_map/ppermute | solution.py:564
  37.5 12.8 %collective-permute-start.13 = (f32[4,128,128]{2,1,0:T(8,128)S(1)}, f32[4,128,128]{2,1,0:T(8,128)S(1)}, u32[]{:S(2)}, u32[]{:S(2)}) collective-permute-start(f32[4,128,128]{2,1,0:T(8,128)S(1)} %get-tuple-element.93), channel_id=1, source_target_pairs={{0,8},{8,0},{16,24},{24,16},{32,40},{40,32},{48,56},{56,48},{64,72... | collective-permute-start | bytes 786440 | tf_op jit(solution)/shard_map/ppermute | solution.py:566
  37.8 12.4 %collective-permute-start.14 = (f32[4,128,128]{2,1,0:T(8,128)S(1)}, f32[4,128,128]{2,1,0:T(8,128)S(1)}, u32[]{:S(2)}, u32[]{:S(2)}) collective-permute-start(f32[4,128,128]{2,1,0:T(8,128)S(1)} %get-tuple-element.94), channel_id=1, source_target_pairs={{8,16},{16,8},{24,32},{32,24},{40,48},{48,40},{56,64},{64,56},{72,... | collective-permute-start | bytes 786440 | tf_op jit(solution)/shard_map/ppermute | solution.py:567
  40.7 5.7 %collective-permute-start.9 = (f32[2,3,16,128]{3,2,1,0:T(8,128)S(1)}, f32[2,3,16,128]{3,2,1,0:T(8,128)S(1)}, u32[]{:S(2)}, u32[]{:S(2)}) collective-permute-start(f32[2,3,16,128]{3,2,1,0:T(8,128)S(1)} %get-tuple-element.89), channel_id=1, source_target_pairs={{0,4},{1,5},{2,6},{3,7},{4,0},{5,1},{6,2},{7,3},{8,12},{9,13},{10,... | collective-permute-start | bytes 147464 | tf_op jit(solution)/shard_map/ppermute | solution.py:570
  44.3 4.1 %collective-permute-start.10 = (f32[2,3,16,128]{3,2,1,0:T(8,128)S(1)}, f32[2,3,16,128]{3,2,1,0:T(8,128)S(1)}, u32[]{:S(2)}, u32[]{:S(2)}) collective-permute-start(f32[2,3,16,128]{3,2,1,0:T(8,128)S(1)} %get-tuple-element.90), channel_id=1, source_target_pairs={{0,2},{1,3},{2,0},{3,1},{4,6},{5,7},{6,4},{7,5},{8,10},{9,11},{10,... | collective-permute-start | bytes 147464 | tf_op jit(solution)/shard_map/ppermute | solution.py:570
  44.8 5.3 %collective-permute-start.11 = (f32[2,3,16,128]{3,2,1,0:T(8,128)S(1)}, f32[2,3,16,128]{3,2,1,0:T(8,128)S(1)}, u32[]{:S(2)}, u32[]{:S(2)}) collective-permute-start(f32[2,3,16,128]{3,2,1,0:T(8,128)S(1)} %get-tuple-element.91), channel_id=1, source_target_pairs={{0,6},{1,7},{2,4},{3,5},{4,2},{5,3},{6,0},{7,1},{8,14},{9,15},{10,... | collective-permute-start | bytes 147464 | tf_op jit(solution)/shard_map/ppermute | solution.py:570
  50.1 3.9 %collective-permute-start.12 = (f32[3,16,128]{2,1,0:T(8,128)S(1)}, f32[3,16,128]{2,1,0:T(8,128)S(1)}, u32[]{:S(2)}, u32[]{:S(2)}) collective-permute-start(f32[3,16,128]{2,1,0:T(8,128)S(1)} %get-tuple-element.92), channel_id=1, source_target_pairs={{0,1},{1,0},{2,3},{3,2},{4,5},{5,4},{6,7},{7,6},{8,9},{9,8},{10,11... | collective-permute-start | bytes 73736 | tf_op jit(solution)/shard_map/ppermute | solution.py:573

commit v8 on v7

--- a/solution.py
+++ b/solution.py
@@ -347,47 +347,70 @@
 
 
 def inner_kernel(
-    adj_i, visc_i, vel_s, centre, middle, lists, place, ra, rb, _, __,
-    adj_s, visc_s, mid_s, coef_s, done, chosen, msg_a, msg_b,
+    adj_s, visc_s, vel_s, centre, middle, lists, place, _, __, mid_s, coef_s, done, chosen
 ):
+    chosen[...] = choose(lists, place)
+    run_first(range(2, 9), (adj_s, visc_s, vel_s), mid_s, coef_s, centre)
+    run_second(range(2, 8), mid_s, coef_s, middle, done)
+
+
+def inner(state, centre, middle, lists, place, mid, coef):
+    return pl.pallas_call(
+        inner_kernel,
+        in_specs=[VM] * 9,
+        out_specs=[VM] * 4,
+        out_shape=[in_vmem(STATE["mid"]), in_vmem(STATE["coef"]), in_vmem(FIELD), in_vmem((128, 128))],
+        input_output_aliases={7: 0, 8: 1},
+        compiler_params=params(4),
+        cost_estimate=cost(13),
+        name="inner",
+    )(*[vmem(a) for a in (*state, centre, middle)], lists, place, *[vmem(a) for a in (mid, coef)])
+
+
+def ends_kernel(
+    adj_i, visc_i, vel_s, centre, middle, ra, rb, _, __, ___, ____,
+    adj_s, visc_s, mid_s, coef_s, done, out, msg_a, msg_b, sems,
+):
+    started = begin([(done.at[:, pl.ds(8, 6)], out.at[:, pl.ds(8, 6)])], sems)
     beyond = jnp.where(even("gx"), 18, 1)
     for msg, q in ((ra, beyond), (rb, 19 - beyond)):
         for c in range(3):
             adj_s[c, q, pl.ds(8, 128)] = msg[c]
         visc_s[q, pl.ds(8, 128)] = msg[3]
-    state = (adj_s, visc_s, vel_s)
-    run_first((0, 15), state, mid_s, coef_s, centre)
+    run_first((0, 15), (adj_s, visc_s, vel_s), mid_s, coef_s, centre)
     near = jnp.where(even("gx"), 16, 1)
     for msg, t in ((msg_a, near), (msg_b, 17 - near)):
         for c in range(3):
             msg[c] = mid_s[c, t, pl.ds(8, 128)]
         msg[3] = centre[...]
-    chosen[...] = choose(lists, place)
-    run_first(range(2, 9), state, mid_s, coef_s, centre)
-    run_second(range(1, 8), mid_s, coef_s, middle, done)
-
-
-def inner(state, centre, middle, lists, place, ra, rb, mid, coef):
-    return pl.pallas_call(
-        inner_kernel,
-        in_specs=[VM] * 11,
-        out_specs=[VM] * 8,
+    run_second((1, 14), mid_s, coef_s, middle, done)
+    for copy in started:
+        copy.wait()
+
+
+def ends_call(state, centre, middle, ra, rb, mid, coef, done, out):
+    held = [vmem(a) for a in (*state, centre, middle, ra, rb, mid, coef, done)]
+    return pl.pallas_call(
+        ends_kernel,
+        in_specs=[VM] * 10 + [ANY],
+        out_specs=[VM] * 5 + [ANY, VM, VM],
         out_shape=[in_vmem(STATE[k]) for k in ("adj", "visc", "mid", "coef")]
-        + [in_vmem(FIELD), in_vmem((128, 128))]
+        + [in_vmem(FIELD), pltpu.HBM(FIELD, F32)]
         + [in_vmem((4, 128, 128))] * 2,
-        input_output_aliases={0: 0, 1: 1, 9: 2, 10: 3},
+        scratch_shapes=[pltpu.SemaphoreType.DMA((1,))],
+        input_output_aliases={0: 0, 1: 1, 7: 2, 8: 3, 9: 4, 10: 5},
         compiler_params=params(4),
-        cost_estimate=cost(16),
-        name="inner",
-    )(*[vmem(a) for a in (*state, centre, middle)], lists, place, *[vmem(a) for a in (ra, rb, mid, coef)])
+        cost_estimate=cost(4),
+        name="ends",
+    )(*held, hbm(out))[2:]
 
 
 def middle_kernel(
     adj_s, visc_s, vel_s, centre, middle, _, __, ___, filters, mid_s, coef_s, done, out, kept, sems
 ):
-    started = begin([(done.at[:, pl.ds(1, 7)], out.at[:, pl.ds(1, 7)]), (filters, kept)], sems)
+    started = begin([(done.at[:, pl.ds(2, 6)], out.at[:, pl.ds(2, 6)]), (filters, kept)], sems)
     run_first(range(9, 15), (adj_s, visc_s, vel_s), mid_s, coef_s, centre)
-    run_second(range(8, 15), mid_s, coef_s, middle, done)
+    run_second(range(8, 14), mid_s, coef_s, middle, done)
     for copy in started:
         copy.wait()
 
@@ -413,9 +436,10 @@
 ):
     copies = [
         pltpu.make_async_copy(done.at[:, pl.ds(x, n)], out.at[:, pl.ds(x, n)], sems.at[i])
-        for i, (x, n) in enumerate(((8, 7), (0, 1), (15, 1)))
+        for i, (x, n) in enumerate(((1, 1), (14, 1), (0, 1), (15, 1)))
     ]
     copies[0].start()
+    copies[1].start()
     hl, hr = in_order("gz", ha[...], hb[...])
     zr, zl = in_order("gz", za[...], zb[...])
     low, high = in_order("gx", ra[3], rb[3])
@@ -424,7 +448,7 @@
     for msg, t in ((ra, beyond), (rb, 17 - beyond)):
         for c in range(3):
             mid_s[c, t, pl.ds(8, 128)] = msg[c]
-    for i, x in ((1, 0), (2, 15)):
+    for i, x in ((2, 0), (3, 15)):
         run_second((x,), mid_s, coef_s, edges, done)
         copies[i].start()
     for copy in copies:
@@ -438,7 +462,7 @@
         in_specs=[VM] * 9 + [ANY],
         out_specs=[VM] * 2 + [ANY],
         out_shape=[in_vmem(STATE["mid"]), in_vmem(FIELD), pltpu.HBM(FIELD, F32)],
-        scratch_shapes=[pltpu.VMEM((128, 128), F32), pltpu.SemaphoreType.DMA((3,))],
+        scratch_shapes=[pltpu.VMEM((128, 128), F32), pltpu.SemaphoreType.DMA((4,))],
         input_output_aliases={6: 0, 8: 1, 9: 2},
         compiler_params=params(4),
         cost_estimate=cost(4),
@@ -544,25 +568,28 @@
     *state, za, zb, msg_a, msg_b = pack(adjoint, velocity, viscosity)
     ha = lax.ppermute(za, "gz", inside_z)
     hb = lax.ppermute(zb, "gz", across_z)
-    ha, hb, msg_a, msg_b = lax.optimization_barrier((ha, hb, msg_a, msg_b))
+    face, mid, coef, centre, middle = face_call(state, ha, hb, za, zb)
+
+    face, msg_a, msg_b = lax.optimization_barrier((face, msg_a, msg_b))
     ra = lax.ppermute(msg_a, "gx", inside_x)
     rb = lax.ppermute(msg_b, "gx", across_x)
-    face, mid, coef, centre, middle = face_call(state, ha, hb, za, zb)
-
     got = [lax.ppermute(face, "gx", [(0, k)]) for k in (8, 2, 6)]
-    adj, visc, mid, coef, done, chosen, msg_a, msg_b = inner(
-        state, centre, middle, block_tiles.T, tile_place.reshape(1, -1), ra, rb, mid, coef
+    mid, coef, done, chosen = inner(
+        state, centre, middle, block_tiles.T, tile_place.reshape(1, -1), mid, coef
     )
     *got, mid, coef, done = lax.optimization_barrier((*got, mid, coef, done))
     face = join(face, *got)
     far = lax.ppermute(face, "gx", [(0, 4), (2, 10), (6, 14), (8, 12)])
-    mid, coef, done, out, near = middle_call(
-        (adj, visc, state[2]), centre, middle, mid, coef, done, filters
-    )
-    far, mid, coef, done = lax.optimization_barrier((far, mid, coef, done))
+    mid, coef, done, out, near = middle_call(state, centre, middle, mid, coef, done, filters)
+    far, mid, coef, done, ra, rb = lax.optimization_barrier((far, mid, coef, done, ra, rb))
     face = join(face, far)
     other = lax.ppermute(face, "gx", [(i, i + 1) for i in range(0, nx, 2)])
-    other, msg_a, msg_b = lax.optimization_barrier((other, msg_a, msg_b))
+    mid, coef, done, out, msg_a, msg_b = ends_call(
+        state, centre, middle, ra, rb, mid, coef, done, out
+    )
+    other, mid, coef, done, msg_a, msg_b = lax.optimization_barrier(
+        (other, mid, coef, done, msg_a, msg_b)
+    )
     ra = lax.ppermute(msg_a, "gx", inside_x)
     rb = lax.ppermute(msg_b, "gx", across_x)
     own, *pairs = partial_sums(chosen, face, other)

time: 56 us -> 55.6 us (level)
  the two profiles are of different devices: /device:TPU:24 before, /device:TPU:30 now
where the time goes in v8:
time: 55.6 us; the launch traced here: 55.3 us
  starting transfers between devices  22.3 us (40%)
  Pallas kernels  16.9 us (30%)
  waiting for transfers between devices  15.3 us (28%)
  between operations  0.85 us (2%)
    ppermute x2, starting transfers between devices, shards(): rb = lax.ppermute(msg_b, 'gx', across_x)  9.29 us
    ppermute x3, waiting for transfers between devices, shards(): lax.ppermute(pairs[k // 2 - 1], 'gz', [(i, i ^ k) for i in range(nz)])  4.78 us
    ppermute x3, starting transfers between devices, shards(): lax.ppermute(pairs[k // 2 - 1], 'gz', [(i, i ^ k) for i in range(nz)])  4.67 us
    ppermute x1, waiting for transfers between devices, shards(): far = lax.ppermute(face, 'gx', [(0, 4), (2, 10), (6, 14), (8, 12)])  4.32 us
    pallas_call x1, Pallas kernels, pack(): pl.pallas_call(pack_kernel, in_specs=[ANY, ANY, ANY], out_specs=[VM] * 7,...  4.1 us
    pallas_call x1, Pallas kernels, middle_call(): pl.pallas_call(middle_kernel, in_specs=[VM] * 8 + [ANY], out_specs=[VM] *...  3.42 us
    ppermute x1, waiting for transfers between devices, shards(): hb = lax.ppermute(zb, 'gz', across_z)  3.38 us
    pallas_call x1, Pallas kernels, inner(): pl.pallas_call(inner_kernel, in_specs=[VM] * 9, out_specs=[VM] * 4, out_s...  2.67 us
  transfers between devices with their start and end apart: 15, of which 7 were waited for; matrix products, arithmetic and copies ran while one was open for 0% of the time, Pallas kernels for 18%

profile of v8, /device:TPU:30, one launch (start us, length us, event | category | flops | bytes accessed | tf_op | source)
XLA Modules:
  0.0 55.3 jit_solution(495163500971195904)
XLA Ops:
  0.6 4.1 %pack.1 = (f32[3,20,144,128]{3,2,1,0:T(8,128)S(1)}, f32[20,144,128]{2,1,0:T(8,128)S(1)}, f32[3,18,128,128]{3,2,1,0:T(8,128)S(1)}, f32[192,128]{1,0:T(8,128)S(1)}...) custom-call(f32[3,16,128,128]{3,2,1,0:T(8,128)} %adj.1, f32[3,16,128,128]{3,2,1,0:T(8,128)} %vel.1, ...), custom_call_target="tpu_custom_call" | custom-call | tf_op jit(solution)/shard_map/pack/pallas_call | solution.py:144
  4.7 0.8 %collective-permute-start = (f32[192,128]{1,0:T(8,128)S(1)}, f32[192,128]{1,0:T(8,128)S(1)}, u32[]{:S(2)}, u32[]{:S(2)}) collective-permute-start(f32[192,128]{1,0:T(8,128)S(1)} %get-tuple-element.62.za), channel_id=1, source_target_pairs={{0,1},{1,0},{2,3},{3,2},{4,5},{5,4},{6,7},{7,6},{8,9},{9,8},{10,11... | collective-permute-start | bytes 294920 | tf_op jit(solution)/shard_map/ppermute | solution.py:569
  5.6 2.6 %collective-permute-start.1 = (f32[192,128]{1,0:T(8,128)S(1)}, f32[192,128]{1,0:T(8,128)S(1)}, u32[]{:S(2)}, u32[]{:S(2)}) collective-permute-start(f32[192,128]{1,0:T(8,128)S(1)} %get-tuple-element.63.zb), channel_id=1, source_target_pairs={{0,7},{1,2},{2,1},{3,4},{4,3},{5,6},{6,5},{7,0},{8,15},{9,10},{10,... | collective-permute-start | bytes 294920 | tf_op jit(solution)/shard_map/ppermute | solution.py:570
  8.2 1.2 %collective-permute-done.ra.ha = f32[192,128]{1,0:T(8,128)S(1)} collective-permute-done((f32[192,128]{1,0:T(8,128)S(1)}, f32[192,128]{1,0:T(8,128)S(1)}, u32[]{:S(2)}, u32[]{:S(2)}) %collective-permute-start) | collective-permute-done | bytes 98336 | tf_op jit(solution)/shard_map/ppermute | solution.py:569
  9.4 3.4 %collective-permute-done.1.rb.hb = f32[192,128]{1,0:T(8,128)S(1)} collective-permute-done((f32[192,128]{1,0:T(8,128)S(1)}, f32[192,128]{1,0:T(8,128)S(1)}, u32[]{:S(2)}, u32[]{:S(2)}) %collective-permute-start.1) | collective-permute-done | bytes 98336 | tf_op jit(solution)/shard_map/ppermute | solution.py:570
  12.8 1.7 %face.1 = (f32[3,128,128]{2,1,0:T(8,128)S(1)}, f32[3,18,144,128]{3,2,1,0:T(8,128)S(1)}, f32[7,18,128,128]{3,2,1,0:T(8,128)S(1)}, f32[128,128]{1,0:T(8,128)S(1)}, f32[128,128]{1,0:T(8,128)S(1)}) custom-call(f32[3,20,144,128]{3,2,1,0:T(8,128)S(1)} %get-tuple-element.59.adj_s.adj_i, f32[20,144,128]{2,1,0:T(8,128)S(1)} %get-tuple-element.60.visc_s.visc_i, ...), custom_call_target="tpu_custom_call" | custom-call | flops 2949120 | bytes 4325376 | tf_op jit(solution)/shard_map/face/pallas_call | solution.py:297
  14.5 0.7 %collective-permute-start.4 = (f32[3,128,128]{2,1,0:T(8,128)S(1)}, f32[3,128,128]{2,1,0:T(8,128)S(1)}, u32[]{:S(2)}, u32[]{:S(2)}) collective-permute-start(f32[3,128,128]{2,1,0:T(8,128)S(1)} %get-tuple-element.72.refs_0_), channel_id=1, source_target_pairs={{0,48},{1,49},{2,50},{3,51},{4,52},{5,53},{6,54},{7,55}} | collective-permute-start | bytes 589832 | tf_op jit(solution)/shard_map/ppermute | solution.py:576
  15.2 0.7 %collective-permute-start.3 = (f32[3,128,128]{2,1,0:T(8,128)S(1)}, f32[3,128,128]{2,1,0:T(8,128)S(1)}, u32[]{:S(2)}, u32[]{:S(2)}) collective-permute-start(f32[3,128,128]{2,1,0:T(8,128)S(1)} %get-tuple-element.72.refs_0_), channel_id=1, source_target_pairs={{0,16},{1,17},{2,18},{3,19},{4,20},{5,21},{6,22},{7,23}} | collective-permute-start | bytes 589832 | tf_op jit(solution)/shard_map/ppermute | solution.py:576
  15.9 0.7 %collective-permute-start.2 = (f32[3,128,128]{2,1,0:T(8,128)S(1)}, f32[3,128,128]{2,1,0:T(8,128)S(1)}, u32[]{:S(2)}, u32[]{:S(2)}) collective-permute-start(f32[3,128,128]{2,1,0:T(8,128)S(1)} %get-tuple-element.72.refs_0_), channel_id=1, source_target_pairs={{0,64},{1,65},{2,66},{3,67},{4,68},{5,69},{6,70},{7,71}} | collective-permute-start | bytes 589832 | tf_op jit(solution)/shard_map/ppermute | solution.py:576
  16.6 2.8 %collective-permute-start.7 = (f32[4,128,128]{2,1,0:T(8,128)S(1)}, f32[4,128,128]{2,1,0:T(8,128)S(1)}, u32[]{:S(2)}, u32[]{:S(2)}) collective-permute-start(f32[4,128,128]{2,1,0:T(8,128)S(1)} %get-tuple-element.86), channel_id=1, source_target_pairs={{8,16},{16,8},{24,32},{32,24},{40,48},{48,40},{56,64},{64,56},{72,... | collective-permute-start | bytes 786440 | tf_op jit(solution)/shard_map/ppermute | solution.py:575
  19.5 2.7 %inner.1 = (f32[3,18,144,128]{3,2,1,0:T(8,128)S(1)}, f32[7,18,128,128]{3,2,1,0:T(8,128)S(1)}, f32[3,16,128,128]{3,2,1,0:T(8,128)S(1)}, f32[128,128]{1,0:T(8,128)S(1)}) custom-call(f32[3,20,144,128]{3,2,1,0:T(8,128)S(1)} %get-tuple-element.59.adj_s.adj_i, ...), custom_call_target="tpu_custom_call", output_to_operand_aliasing={{0}: (7, {}), {1}: (8, {})} | custom-call | flops 12779520 | bytes 18743296 | tf_op jit(solution)/shard_map/inner/pallas_call | solution.py:358
  22.2 1.3 %collective-permute-start.5 = (f32[3,128,128]{2,1,0:T(8,128)S(1)}, f32[3,128,128]{2,1,0:T(8,128)S(1)}, u32[]{:S(2)}, u32[]{:S(2)}) collective-permute-start(f32[3,128,128]{2,1,0:T(8,128)S(1)} %join.2.refs_0_), channel_id=1, source_target_pairs={{0,32},{16,80},{48,112},{64,96},{1,33},{17,81},{49,113},{65,97},{2... | collective-permute-start | bytes 589832 | tf_op jit(solution)/shard_map/ppermute | solution.py:582
  23.5 3.4 %middle.1 = (f32[3,18,144,128]{3,2,1,0:T(8,128)S(1)}, f32[7,18,128,128]{3,2,1,0:T(8,128)S(1)}, f32[3,16,128,128]{3,2,1,0:T(8,128)S(1)}, f32[3,16,128,128]{3,2,1,0:T(8,128)}, bf16[4,512,512]{2,1,0:T(8,128)(2,1)S(1)}) custom-call(f32[3,20,144,128]{3,2,1,0:T(8,128)S(1)} %get-tuple-element.59.adj_s.adj_i, ...), custom_call_target="tpu_custom_call", output_to_operand_aliasing={{0}: (5, {}), {1}: (6, {}), {2}: (7, {})} | custom-call | flops 11796480 | bytes 17301504 | tf_op jit(solution)/shard_map/middle/pallas_call | solution.py:420
  27.0 4.3 %collective-permute-done.5.refs_1_ = f32[3,128,128]{2,1,0:T(8,128)S(1)} collective-permute-done((f32[3,128,128]{2,1,0:T(8,128)S(1)}, f32[3,128,128]{2,1,0:T(8,128)S(1)}, u32[]{:S(2)}, u32[]{:S(2)}) %collective-permute-start.5) | collective-permute-done | bytes 196640 | tf_op jit(solution)/shard_map/ppermute | solution.py:582
  31.3 1.3 %collective-permute-start.8 = (f32[3,128,128]{2,1,0:T(8,128)S(1)}, f32[3,128,128]{2,1,0:T(8,128)S(1)}, u32[]{:S(2)}, u32[]{:S(2)}) collective-permute-start(f32[3,128,128]{2,1,0:T(8,128)S(1)} %join.3.face), channel_id=1, source_target_pairs={{0,8},{16,24},{32,40},{48,56},{64,72},{80,88},{96,104},{112,120},{... | collective-permute-start | bytes 589832 | tf_op jit(solution)/shard_map/ppermute | solution.py:586
  32.6 1.5 %ends.1 = (f32[3,20,144,128]{3,2,1,0:T(8,128)S(1)}, f32[20,144,128]{2,1,0:T(8,128)S(1)}, f32[3,18,144,128]{3,2,1,0:T(8,128)S(1)}, f32[7,18,128,128]{3,2,1,0:T(8,...) custom-call(f32[3,20,144,128]{3,2,1,0:T(8,128)S(1)} %get-tuple-eleme, ...), custom_call_target="tpu_custom_call", output_to_operand_aliasing={{0}: (0, {}), {1}: (1, {}), {2}: (7, {}), {3}: (8, {}), {4}... | custom-call | flops 3932160 | bytes 5767168 | tf_op jit(solution)/shard_map/ends/pallas_call | solution.py:393
  34.2 6.5 %collective-permute-start.14 = (f32[4,128,128]{2,1,0:T(8,128)S(1)}, f32[4,128,128]{2,1,0:T(8,128)S(1)}, u32[]{:S(2)}, u32[]{:S(2)}) collective-permute-start(f32[4,128,128]{2,1,0:T(8,128)S(1)} %get-tuple-element.106), channel_id=1, source_target_pairs={{8,16},{16,8},{24,32},{32,24},{40,48},{48,40},{56,64},{64,56},{72,... | collective-permute-start | bytes 786440 | tf_op jit(solution)/shard_map/ppermute | solution.py:594
  40.9 3.7 %collective-permute-start.9 = (f32[2,3,16,128]{3,2,1,0:T(8,128)S(1)}, f32[2,3,16,128]{3,2,1,0:T(8,128)S(1)}, u32[]{:S(2)}, u32[]{:S(2)}) collective-permute-start(f32[2,3,16,128]{3,2,1,0:T(8,128)S(1)} %get-tuple-element.101), channel_id=1, source_target_pairs={{0,4},{1,5},{2,6},{3,7},{4,0},{5,1},{6,2},{7,3},{8,12},{9,13},{10,... | collective-permute-start | bytes 147464 | tf_op jit(solution)/shard_map/ppermute | solution.py:597
  45.6 1.1 %collective-permute-done.9.b = f32[2,3,16,128]{3,2,1,0:T(8,128)S(1)} collective-permute-done((f32[2,3,16,128]{3,2,1,0:T(8,128)S(1)}, f32[2,3,16,128]{3,2,1,0:T(8,128)S(1)}, u32[]{:S(2)}, u32[]{:S(2)}) %collective-permute-start.9) | collective-permute-done | bytes 49184 | tf_op jit(solution)/shard_map/ppermute | solution.py:597
  46.7 2.0 %collective-permute-done.10.c = f32[2,3,16,128]{3,2,1,0:T(8,128)S(1)} collective-permute-done((f32[2,3,16,128]{3,2,1,0:T(8,128)S(1)}, f32[2,3,16,128]{3,2,1,0:T(8,128)S(1)}, u32[]{:S(2)}, u32[]{:S(2)}) %collective-permute-start.10) | collective-permute-done | bytes 49184 | tf_op jit(solution)/shard_map/ppermute | solution.py:597
  48.7 1.7 %collective-permute-done.11.d = f32[2,3,16,128]{3,2,1,0:T(8,128)S(1)} collective-permute-done((f32[2,3,16,128]{3,2,1,0:T(8,128)S(1)}, f32[2,3,16,128]{3,2,1,0:T(8,128)S(1)}, u32[]{:S(2)}, u32[]{:S(2)}) %collective-permute-start.11) | collective-permute-done | bytes 49184 | tf_op jit(solution)/shard_map/ppermute | solution.py:597
  50.5 2.2 %last.1 = (f32[3,18,144,128]{3,2,1,0:T(8,128)S(1)}, f32[3,16,128,128]{3,2,1,0:T(8,128)S(1)}, f32[3,16,128,128]{3,2,1,0:T(8,128)}) custom-call(f32[192,128]{1,0:T(8,128)S(1)} %collective-permute-done.ra.ha, f32[192,128]{1,0:T(8,128)S(1)} %collective-permute-done.1.rb.hb, ...), custom_call_target="tpu_custom_call", output_to_operand_aliasing={{0}: (6, {}), {1}: (8, {}), {2}: (9, {})} | custom-call | flops 3932160 | bytes 5767168 | tf_op jit(solution)/shard_map/last/pallas_call | solution.py:460
  52.7 1.6 %collective-permute-done.12.came = f32[3,16,128]{2,1,0:T(8,128)S(1)} collective-permute-done((f32[3,16,128]{2,1,0:T(8,128)S(1)}, f32[3,16,128]{2,1,0:T(8,128)S(1)}, u32[]{:S(2)}, u32[]{:S(2)}) %collective-permute-start.12) | collective-permute-done | bytes 24608 | tf_op jit(solution)/shard_map/ppermute | solution.py:600
  54.3 1.0 %product.1 = f32[3,4,512]{2,1,0:T(4,128)} custom-call(f32[3,16,128]{2,1,0:T(8,128)S(1)} %get-tuple-element.113.kept, f32[3,16,128]{2,1,0:T(8,128)S(1)} %collective-permute-done.12.came, bf16[4,512,512]{2,1,0:T(8,128)(2,1)S(1)} %get-tuple-element.115.filters), custom_call_target="tpu_custom_call" | custom-call | tf_op jit(solution)/shard_map/product/pallas_call | solution.py:549
  (21 shorter events, 1.6 us)
Async XLA Ops:
  4.7 4.7 %collective-permute-start = (f32[192,128]{1,0:T(8,128)S(1)}, f32[192,128]{1,0:T(8,128)S(1)}, u32[]{:S(2)}, u32[]{:S(2)}) collective-permute-start(f32[192,128]{1,0:T(8,128)S(1)} %get-tuple-element.62.za), channel_id=1, source_target_pairs={{0,1},{1,0},{2,3},{3,2},{4,5},{5,4},{6,7},{7,6},{8,9},{9,8},{10,11... | collective-permute-start | bytes 294920 | tf_op jit(solution)/shard_map/ppermute | solution.py:569
  5.6 7.3 %collective-permute-start.1 = (f32[192,128]{1,0:T(8,128)S(1)}, f32[192,128]{1,0:T(8,128)S(1)}, u32[]{:S(2)}, u32[]{:S(2)}) collective-permute-start(f32[192,128]{1,0:T(8,128)S(1)} %get-tuple-element.63.zb), channel_id=1, source_target_pairs={{0,7},{1,2},{2,1},{3,4},{4,3},{5,6},{6,5},{7,0},{8,15},{9,10},{10,... | collective-permute-start | bytes 294920 | tf_op jit(solution)/shard_map/ppermute | solution.py:570
  12.8 6.6 %copy-start = (s32[256,8]{0,1:T(8,128)S(1)}, s32[256,8]{0,1:T(8,128)}, u32[]{:S(2)}) copy-start(s32[256,8]{0,1:T(8,128)} %param.10) | copy-start | bytes 24580
  12.8 6.7 %copy-start.1 = (s32[512]{0:T(512)S(1)}, s32[512]{0:T(512)}, u32[]{:S(2)}) copy-start(s32[512]{0:T(512)} %param.11) | copy-start | bytes 6148
  14.5 7.7 %collective-permute-start.4 = (f32[3,128,128]{2,1,0:T(8,128)S(1)}, f32[3,128,128]{2,1,0:T(8,128)S(1)}, u32[]{:S(2)}, u32[]{:S(2)}) collective-permute-start(f32[3,128,128]{2,1,0:T(8,128)S(1)} %get-tuple-element.72.refs_0_), channel_id=1, source_target_pairs={{0,48},{1,49},{2,50},{3,51},{4,52},{5,53},{6,54},{7,55}} | collective-permute-start | bytes 589832 | tf_op jit(solution)/shard_map/ppermute | solution.py:576
  15.2 7.0 %collective-permute-start.3 = (f32[3,128,128]{2,1,0:T(8,128)S(1)}, f32[3,128,128]{2,1,0:T(8,128)S(1)}, u32[]{:S(2)}, u32[]{:S(2)}) collective-permute-start(f32[3,128,128]{2,1,0:T(8,128)S(1)} %get-tuple-element.72.refs_0_), channel_id=1, source_target_pairs={{0,16},{1,17},{2,18},{3,19},{4,20},{5,21},{6,22},{7,23}} | collective-permute-start | bytes 589832 | tf_op jit(solution)/shard_map/ppermute | solution.py:576
  15.9 6.3 %collective-permute-start.2 = (f32[3,128,128]{2,1,0:T(8,128)S(1)}, f32[3,128,128]{2,1,0:T(8,128)S(1)}, u32[]{:S(2)}, u32[]{:S(2)}) collective-permute-start(f32[3,128,128]{2,1,0:T(8,128)S(1)} %get-tuple-element.72.refs_0_), channel_id=1, source_target_pairs={{0,64},{1,65},{2,66},{3,67},{4,68},{5,69},{6,70},{7,71}} | collective-permute-start | bytes 589832 | tf_op jit(solution)/shard_map/ppermute | solution.py:576
  16.5 10.4 %collective-permute-start.6 = (f32[4,128,128]{2,1,0:T(8,128)S(1)}, f32[4,128,128]{2,1,0:T(8,128)S(1)}, u32[]{:S(2)}, u32[]{:S(2)}) collective-permute-start(f32[4,128,128]{2,1,0:T(8,128)S(1)} %get-tuple-element.85), channel_id=1, source_target_pairs={{0,8},{8,0},{16,24},{24,16},{32,40},{40,32},{48,56},{56,48},{64,72... | collective-permute-start | bytes 786440 | tf_op jit(solution)/shard_map/ppermute | solution.py:574
  16.6 10.3 %collective-permute-start.7 = (f32[4,128,128]{2,1,0:T(8,128)S(1)}, f32[4,128,128]{2,1,0:T(8,128)S(1)}, u32[]{:S(2)}, u32[]{:S(2)}) collective-permute-start(f32[4,128,128]{2,1,0:T(8,128)S(1)} %get-tuple-element.86), channel_id=1, source_target_pairs={{8,16},{16,8},{24,32},{32,24},{40,48},{48,40},{56,64},{64,56},{72,... | collective-permute-start | bytes 786440 | tf_op jit(solution)/shard_map/ppermute | solution.py:575
  22.2 9.1 %collective-permute-start.5 = (f32[3,128,128]{2,1,0:T(8,128)S(1)}, f32[3,128,128]{2,1,0:T(8,128)S(1)}, u32[]{:S(2)}, u32[]{:S(2)}) collective-permute-start(f32[3,128,128]{2,1,0:T(8,128)S(1)} %join.2.refs_0_), channel_id=1, source_target_pairs={{0,32},{16,80},{48,112},{64,96},{1,33},{17,81},{49,113},{65,97},{2... | collective-permute-start | bytes 589832 | tf_op jit(solution)/shard_map/ppermute | solution.py:582
  31.3 2.8 %collective-permute-start.8 = (f32[3,128,128]{2,1,0:T(8,128)S(1)}, f32[3,128,128]{2,1,0:T(8,128)S(1)}, u32[]{:S(2)}, u32[]{:S(2)}) collective-permute-start(f32[3,128,128]{2,1,0:T(8,128)S(1)} %join.3.face), channel_id=1, source_target_pairs={{0,8},{16,24},{32,40},{48,56},{64,72},{80,88},{96,104},{112,120},{... | collective-permute-start | bytes 589832 | tf_op jit(solution)/shard_map/ppermute | solution.py:586
  34.1 16.4 %collective-permute-start.13 = (f32[4,128,128]{2,1,0:T(8,128)S(1)}, f32[4,128,128]{2,1,0:T(8,128)S(1)}, u32[]{:S(2)}, u32[]{:S(2)}) collective-permute-start(f32[4,128,128]{2,1,0:T(8,128)S(1)} %get-tuple-element.105), channel_id=1, source_target_pairs={{0,8},{8,0},{16,24},{24,16},{32,40},{40,32},{48,56},{56,48},{64,72... | collective-permute-start | bytes 786440 | tf_op jit(solution)/shard_map/ppermute | solution.py:593
  34.2 16.3 %collective-permute-start.14 = (f32[4,128,128]{2,1,0:T(8,128)S(1)}, f32[4,128,128]{2,1,0:T(8,128)S(1)}, u32[]{:S(2)}, u32[]{:S(2)}) collective-permute-start(f32[4,128,128]{2,1,0:T(8,128)S(1)} %get-tuple-element.106), channel_id=1, source_target_pairs={{8,16},{16,8},{24,32},{32,24},{40,48},{48,40},{56,64},{64,56},{72,... | collective-permute-start | bytes 786440 | tf_op jit(solution)/shard_map/ppermute | solution.py:594
  40.9 5.7 %collective-permute-start.9 = (f32[2,3,16,128]{3,2,1,0:T(8,128)S(1)}, f32[2,3,16,128]{3,2,1,0:T(8,128)S(1)}, u32[]{:S(2)}, u32[]{:S(2)}) collective-permute-start(f32[2,3,16,128]{3,2,1,0:T(8,128)S(1)} %get-tuple-element.101), channel_id=1, source_target_pairs={{0,4},{1,5},{2,6},{3,7},{4,0},{5,1},{6,2},{7,3},{8,12},{9,13},{10,... | collective-permute-start | bytes 147464 | tf_op jit(solution)/shard_map/ppermute | solution.py:597
  44.6 4.1 %collective-permute-start.10 = (f32[2,3,16,128]{3,2,1,0:T(8,128)S(1)}, f32[2,3,16,128]{3,2,1,0:T(8,128)S(1)}, u32[]{:S(2)}, u32[]{:S(2)}) collective-permute-start(f32[2,3,16,128]{3,2,1,0:T(8,128)S(1)} %get-tuple-element.102), channel_id=1, source_target_pairs={{0,2},{1,3},{2,0},{3,1},{4,6},{5,7},{6,4},{7,5},{8,10},{9,11},{10,... | collective-permute-start | bytes 147464 | tf_op jit(solution)/shard_map/ppermute | solution.py:597
  45.1 5.3 %collective-permute-start.11 = (f32[2,3,16,128]{3,2,1,0:T(8,128)S(1)}, f32[2,3,16,128]{3,2,1,0:T(8,128)S(1)}, u32[]{:S(2)}, u32[]{:S(2)}) collective-permute-start(f32[2,3,16,128]{3,2,1,0:T(8,128)S(1)} %get-tuple-element.103), channel_id=1, source_target_pairs={{0,6},{1,7},{2,4},{3,5},{4,2},{5,3},{6,0},{7,1},{8,14},{9,15},{10,... | collective-permute-start | bytes 147464 | tf_op jit(solution)/shard_map/ppermute | solution.py:597
  50.4 3.9 %collective-permute-start.12 = (f32[3,16,128]{2,1,0:T(8,128)S(1)}, f32[3,16,128]{2,1,0:T(8,128)S(1)}, u32[]{:S(2)}, u32[]{:S(2)}) collective-permute-start(f32[3,16,128]{2,1,0:T(8,128)S(1)} %get-tuple-element.104), channel_id=1, source_target_pairs={{0,1},{1,0},{2,3},{3,2},{4,5},{5,4},{6,7},{7,6},{8,9},{9,8},{10,11... | collective-permute-start | bytes 73736 | tf_op jit(solution)/shard_map/ppermute | solution.py:600

commit v9 on v8

--- a/solution.py
+++ b/solution.py
@@ -581,17 +581,14 @@
     face = join(face, *got)
     far = lax.ppermute(face, "gx", [(0, 4), (2, 10), (6, 14), (8, 12)])
     mid, coef, done, out, near = middle_call(state, centre, middle, mid, coef, done, filters)
-    far, mid, coef, done, ra, rb = lax.optimization_barrier((far, mid, coef, done, ra, rb))
-    face = join(face, far)
-    other = lax.ppermute(face, "gx", [(i, i + 1) for i in range(0, nx, 2)])
     mid, coef, done, out, msg_a, msg_b = ends_call(
         state, centre, middle, ra, rb, mid, coef, done, out
     )
-    other, mid, coef, done, msg_a, msg_b = lax.optimization_barrier(
-        (other, mid, coef, done, msg_a, msg_b)
-    )
     ra = lax.ppermute(msg_a, "gx", inside_x)
     rb = lax.ppermute(msg_b, "gx", across_x)
+    far, mid, coef, done = lax.optimization_barrier((far, mid, coef, done))
+    face = join(face, far)
+    other = lax.ppermute(face, "gx", [(i, i + 1) for i in range(0, nx, 2)])
     own, *pairs = partial_sums(chosen, face, other)
     pairs = [
         lax.ppermute(pairs[k // 2 - 1], "gz", [(i, i ^ k) for i in range(nz)]) for k in (4, 2, 6)

time: 55.6 us -> 54.6 us (0.982)
  the two profiles are of different devices: /device:TPU:30 before, /device:TPU:24 now
where the time goes in v9:
time: 54.6 us; the launch traced here: 53.8 us
  starting transfers between devices  21 us (38%)
  Pallas kernels  16.9 us (31%)
  waiting for transfers between devices  15.1 us (28%)
  between operations  0.85 us (2%)
    ppermute x2, starting transfers between devices, shards(): rb = lax.ppermute(msg_b, 'gx', across_x)  7.35 us
    ppermute x3, waiting for transfers between devices, shards(): lax.ppermute(pairs[k // 2 - 1], 'gz', [(i, i ^ k) for i in range(nz)])  4.78 us
    ppermute x3, starting transfers between devices, shards(): lax.ppermute(pairs[k // 2 - 1], 'gz', [(i, i ^ k) for i in range(nz)])  4.68 us
    pallas_call x1, Pallas kernels, pack(): pl.pallas_call(pack_kernel, in_specs=[ANY, ANY, ANY], out_specs=[VM] * 7,...  4.1 us
    ppermute x3, waiting for transfers between devices, shards(): got = [lax.ppermute(face, 'gx', [(0, k)]) for k in (8, 2, 6)]  4.07 us
    pallas_call x1, Pallas kernels, middle_call(): pl.pallas_call(middle_kernel, in_specs=[VM] * 8 + [ANY], out_specs=[VM] *...  3.42 us
    ppermute x1, waiting for transfers between devices, shards(): hb = lax.ppermute(zb, 'gz', across_z)  3.38 us
    pallas_call x1, Pallas kernels, inner(): pl.pallas_call(inner_kernel, in_specs=[VM] * 9, out_specs=[VM] * 4, out_s...  2.67 us
  transfers between devices with their start and end apart: 15, of which 7 were waited for; matrix products, arithmetic and copies ran while one was open for 0% of the time, Pallas kernels for 19%

profile of v9, /device:TPU:24, one launch (start us, length us, event | category | flops | bytes accessed | tf_op | source)
XLA Modules:
  0.0 53.8 jit_solution(476887916994111247)
XLA Ops:
  0.6 4.1 %pack.1 = (f32[3,20,144,128]{3,2,1,0:T(8,128)S(1)}, f32[20,144,128]{2,1,0:T(8,128)S(1)}, f32[3,18,128,128]{3,2,1,0:T(8,128)S(1)}, f32[192,128]{1,0:T(8,128)S(1)}...) custom-call(f32[3,16,128,128]{3,2,1,0:T(8,128)} %adj.1, f32[3,16,128,128]{3,2,1,0:T(8,128)} %vel.1, ...), custom_call_target="tpu_custom_call" | custom-call | tf_op jit(solution)/shard_map/pack/pallas_call | solution.py:144
  4.7 0.8 %collective-permute-start = (f32[192,128]{1,0:T(8,128)S(1)}, f32[192,128]{1,0:T(8,128)S(1)}, u32[]{:S(2)}, u32[]{:S(2)}) collective-permute-start(f32[192,128]{1,0:T(8,128)S(1)} %get-tuple-element.54.za), channel_id=1, source_target_pairs={{0,1},{1,0},{2,3},{3,2},{4,5},{5,4},{6,7},{7,6},{8,9},{9,8},{10,11... | collective-permute-start | bytes 294920 | tf_op jit(solution)/shard_map/ppermute | solution.py:569
  5.6 2.6 %collective-permute-start.1 = (f32[192,128]{1,0:T(8,128)S(1)}, f32[192,128]{1,0:T(8,128)S(1)}, u32[]{:S(2)}, u32[]{:S(2)}) collective-permute-start(f32[192,128]{1,0:T(8,128)S(1)} %get-tuple-element.55.zb), channel_id=1, source_target_pairs={{0,7},{1,2},{2,1},{3,4},{4,3},{5,6},{6,5},{7,0},{8,15},{9,10},{10,... | collective-permute-start | bytes 294920 | tf_op jit(solution)/shard_map/ppermute | solution.py:570
  8.2 1.2 %collective-permute-done.ra.ha = f32[192,128]{1,0:T(8,128)S(1)} collective-permute-done((f32[192,128]{1,0:T(8,128)S(1)}, f32[192,128]{1,0:T(8,128)S(1)}, u32[]{:S(2)}, u32[]{:S(2)}) %collective-permute-start) | collective-permute-done | bytes 98336 | tf_op jit(solution)/shard_map/ppermute | solution.py:569
  9.4 3.4 %collective-permute-done.1.rb.hb = f32[192,128]{1,0:T(8,128)S(1)} collective-permute-done((f32[192,128]{1,0:T(8,128)S(1)}, f32[192,128]{1,0:T(8,128)S(1)}, u32[]{:S(2)}, u32[]{:S(2)}) %collective-permute-start.1) | collective-permute-done | bytes 98336 | tf_op jit(solution)/shard_map/ppermute | solution.py:570
  12.8 1.7 %face.1 = (f32[3,128,128]{2,1,0:T(8,128)S(1)}, f32[3,18,144,128]{3,2,1,0:T(8,128)S(1)}, f32[7,18,128,128]{3,2,1,0:T(8,128)S(1)}, f32[128,128]{1,0:T(8,128)S(1)}, f32[128,128]{1,0:T(8,128)S(1)}) custom-call(f32[3,20,144,128]{3,2,1,0:T(8,128)S(1)} %get-tuple-element.51.adj_s.adj_i, f32[20,144,128]{2,1,0:T(8,128)S(1)} %get-tuple-element.52.visc_s.visc_i, ...), custom_call_target="tpu_custom_call" | custom-call | flops 2949120 | bytes 4325376 | tf_op jit(solution)/shard_map/face/pallas_call | solution.py:297
  14.5 0.7 %collective-permute-start.4 = (f32[3,128,128]{2,1,0:T(8,128)S(1)}, f32[3,128,128]{2,1,0:T(8,128)S(1)}, u32[]{:S(2)}, u32[]{:S(2)}) collective-permute-start(f32[3,128,128]{2,1,0:T(8,128)S(1)} %get-tuple-element.64.refs_0_), channel_id=1, source_target_pairs={{0,48},{1,49},{2,50},{3,51},{4,52},{5,53},{6,54},{7,55}} | collective-permute-start | bytes 589832 | tf_op jit(solution)/shard_map/ppermute | solution.py:576
  15.2 0.7 %collective-permute-start.3 = (f32[3,128,128]{2,1,0:T(8,128)S(1)}, f32[3,128,128]{2,1,0:T(8,128)S(1)}, u32[]{:S(2)}, u32[]{:S(2)}) collective-permute-start(f32[3,128,128]{2,1,0:T(8,128)S(1)} %get-tuple-element.64.refs_0_), channel_id=1, source_target_pairs={{0,16},{1,17},{2,18},{3,19},{4,20},{5,21},{6,22},{7,23}} | collective-permute-start | bytes 589832 | tf_op jit(solution)/shard_map/ppermute | solution.py:576
  15.9 1.3 %collective-permute-start.2 = (f32[3,128,128]{2,1,0:T(8,128)S(1)}, f32[3,128,128]{2,1,0:T(8,128)S(1)}, u32[]{:S(2)}, u32[]{:S(2)}) collective-permute-start(f32[3,128,128]{2,1,0:T(8,128)S(1)} %get-tuple-element.64.refs_0_), channel_id=1, source_target_pairs={{0,64},{1,65},{2,66},{3,67},{4,68},{5,69},{6,70},{7,71}} | collective-permute-start | bytes 589832 | tf_op jit(solution)/shard_map/ppermute | solution.py:576
  17.2 5.4 %collective-permute-start.7 = (f32[4,128,128]{2,1,0:T(8,128)S(1)}, f32[4,128,128]{2,1,0:T(8,128)S(1)}, u32[]{:S(2)}, u32[]{:S(2)}) collective-permute-start(f32[4,128,128]{2,1,0:T(8,128)S(1)} %get-tuple-element.72), channel_id=1, source_target_pairs={{8,16},{16,8},{24,32},{32,24},{40,48},{48,40},{56,64},{64,56},{72,... | collective-permute-start | bytes 786440 | tf_op jit(solution)/shard_map/ppermute | solution.py:575
  22.7 2.7 %inner.1 = (f32[3,18,144,128]{3,2,1,0:T(8,128)S(1)}, f32[7,18,128,128]{3,2,1,0:T(8,128)S(1)}, f32[3,16,128,128]{3,2,1,0:T(8,128)S(1)}, f32[128,128]{1,0:T(8,128)S(1)}) custom-call(f32[3,20,144,128]{3,2,1,0:T(8,128)S(1)} %get-tuple-element.51.adj_s.adj_i, ...), custom_call_target="tpu_custom_call", output_to_operand_aliasing={{0}: (7, {}), {1}: (8, {})} | custom-call | flops 12779520 | bytes 18743296 | tf_op jit(solution)/shard_map/inner/pallas_call | solution.py:358
  25.4 4.1 %collective-permute-done.2.refs_1_ = f32[3,128,128]{2,1,0:T(8,128)S(1)} collective-permute-done((f32[3,128,128]{2,1,0:T(8,128)S(1)}, f32[3,128,128]{2,1,0:T(8,128)S(1)}, u32[]{:S(2)}, u32[]{:S(2)}) %collective-permute-start.2) | collective-permute-done | bytes 196640 | tf_op jit(solution)/shard_map/ppermute | solution.py:576
  29.5 1.3 %collective-permute-start.5 = (f32[3,128,128]{2,1,0:T(8,128)S(1)}, f32[3,128,128]{2,1,0:T(8,128)S(1)}, u32[]{:S(2)}, u32[]{:S(2)}) collective-permute-start(f32[3,128,128]{2,1,0:T(8,128)S(1)} %join.2.refs_0_), channel_id=1, source_target_pairs={{0,32},{16,80},{48,112},{64,96},{1,33},{17,81},{49,113},{65,97},{2... | collective-permute-start | bytes 589832 | tf_op jit(solution)/shard_map/ppermute | solution.py:582
  30.8 3.4 %middle.1 = (f32[3,18,144,128]{3,2,1,0:T(8,128)S(1)}, f32[7,18,128,128]{3,2,1,0:T(8,128)S(1)}, f32[3,16,128,128]{3,2,1,0:T(8,128)S(1)}, f32[3,16,128,128]{3,2,1,0:T(8,128)}, bf16[4,512,512]{2,1,0:T(8,128)(2,1)S(1)}) custom-call(f32[3,20,144,128]{3,2,1,0:T(8,128)S(1)} %get-tuple-element.51.adj_s.adj_i, ...), custom_call_target="tpu_custom_call", output_to_operand_aliasing={{0}: (5, {}), {1}: (6, {}), {2}: (7, {})} | custom-call | flops 11796480 | bytes 17301504 | tf_op jit(solution)/shard_map/middle/pallas_call | solution.py:420
  34.3 1.5 %ends.1 = (f32[3,20,144,128]{3,2,1,0:T(8,128)S(1)}, f32[20,144,128]{2,1,0:T(8,128)S(1)}, f32[3,18,144,128]{3,2,1,0:T(8,128)S(1)}, f32[7,18,128,128]{3,2,1,0:T(8,...) custom-call(f32[3,20,144,128]{3,2,1,0:T(8,128)S(1)} %get-tuple-eleme, ...), custom_call_target="tpu_custom_call", output_to_operand_aliasing={{0}: (0, {}), {1}: (1, {}), {2}: (7, {}), {3}: (8, {}), {4}... | custom-call | flops 3932160 | bytes 5767168 | tf_op jit(solution)/shard_map/ends/pallas_call | solution.py:393
  35.8 1.3 %collective-permute-start.8 = (f32[3,128,128]{2,1,0:T(8,128)S(1)}, f32[3,128,128]{2,1,0:T(8,128)S(1)}, u32[]{:S(2)}, u32[]{:S(2)}) collective-permute-start(f32[3,128,128]{2,1,0:T(8,128)S(1)} %join.3.face), channel_id=1, source_target_pairs={{0,8},{16,24},{32,40},{48,56},{64,72},{80,88},{96,104},{112,120},{... | collective-permute-start | bytes 589832 | tf_op jit(solution)/shard_map/ppermute | solution.py:591
  37.2 1.9 %collective-permute-start.14 = (f32[4,128,128]{2,1,0:T(8,128)S(1)}, f32[4,128,128]{2,1,0:T(8,128)S(1)}, u32[]{:S(2)}, u32[]{:S(2)}) collective-permute-start(f32[4,128,128]{2,1,0:T(8,128)S(1)} %get-tuple-element.90), channel_id=1, source_target_pairs={{8,16},{16,8},{24,32},{32,24},{40,48},{48,40},{56,64},{64,56},{72,... | collective-permute-start | bytes 786440 | tf_op jit(solution)/shard_map/ppermute | solution.py:588
  39.4 3.7 %collective-permute-start.9 = (f32[2,3,16,128]{3,2,1,0:T(8,128)S(1)}, f32[2,3,16,128]{3,2,1,0:T(8,128)S(1)}, u32[]{:S(2)}, u32[]{:S(2)}) collective-permute-start(f32[2,3,16,128]{3,2,1,0:T(8,128)S(1)} %get-tuple-element.85), channel_id=1, source_target_pairs={{0,4},{1,5},{2,6},{3,7},{4,0},{5,1},{6,2},{7,3},{8,12},{9,13},{10,... | collective-permute-start | bytes 147464 | tf_op jit(solution)/shard_map/ppermute | solution.py:594
  44.1 1.4 %collective-permute-done.9.b = f32[2,3,16,128]{3,2,1,0:T(8,128)S(1)} collective-permute-done((f32[2,3,16,128]{3,2,1,0:T(8,128)S(1)}, f32[2,3,16,128]{3,2,1,0:T(8,128)S(1)}, u32[]{:S(2)}, u32[]{:S(2)}) %collective-permute-start.9) | collective-permute-done | bytes 49184 | tf_op jit(solution)/shard_map/ppermute | solution.py:594
  45.4 1.7 %collective-permute-done.10.c = f32[2,3,16,128]{3,2,1,0:T(8,128)S(1)} collective-permute-done((f32[2,3,16,128]{3,2,1,0:T(8,128)S(1)}, f32[2,3,16,128]{3,2,1,0:T(8,128)S(1)}, u32[]{:S(2)}, u32[]{:S(2)}) %collective-permute-start.10) | collective-permute-done | bytes 49184 | tf_op jit(solution)/shard_map/ppermute | solution.py:594
  47.1 1.7 %collective-permute-done.11.d = f32[2,3,16,128]{3,2,1,0:T(8,128)S(1)} collective-permute-done((f32[2,3,16,128]{3,2,1,0:T(8,128)S(1)}, f32[2,3,16,128]{3,2,1,0:T(8,128)S(1)}, u32[]{:S(2)}, u32[]{:S(2)}) %collective-permute-start.11) | collective-permute-done | bytes 49184 | tf_op jit(solution)/shard_map/ppermute | solution.py:594
  49.0 2.2 %last.1 = (f32[3,18,144,128]{3,2,1,0:T(8,128)S(1)}, f32[3,16,128,128]{3,2,1,0:T(8,128)S(1)}, f32[3,16,128,128]{3,2,1,0:T(8,128)}) custom-call(f32[192,128]{1,0:T(8,128)S(1)} %collective-permute-done.ra.ha, f32[192,128]{1,0:T(8,128)S(1)} %collective-permute-done.1.rb.hb, ...), custom_call_target="tpu_custom_call", output_to_operand_aliasing={{0}: (6, {}), {1}: (8, {}), {2}: (9, {})} | custom-call | flops 3932160 | bytes 5767168 | tf_op jit(solution)/shard_map/last/pallas_call | solution.py:460
  51.2 1.6 %collective-permute-done.12.came = f32[3,16,128]{2,1,0:T(8,128)S(1)} collective-permute-done((f32[3,16,128]{2,1,0:T(8,128)S(1)}, f32[3,16,128]{2,1,0:T(8,128)S(1)}, u32[]{:S(2)}, u32[]{:S(2)}) %collective-permute-start.12) | collective-permute-done | bytes 24608 | tf_op jit(solution)/shard_map/ppermute | solution.py:597
  52.8 1.0 %product.1 = f32[3,4,512]{2,1,0:T(4,128)} custom-call(f32[3,16,128]{2,1,0:T(8,128)S(1)} %get-tuple-element.97.kept, f32[3,16,128]{2,1,0:T(8,128)S(1)} %collective-permute-done.12.came, bf16[4,512,512]{2,1,0:T(8,128)(2,1)S(1)} %get-tuple-element.99.filters), custom_call_target="tpu_custom_call" | custom-call | tf_op jit(solution)/shard_map/product/pallas_call | solution.py:549
  (21 shorter events, 1.6 us)
Async XLA Ops:
  4.7 4.7 %collective-permute-start = (f32[192,128]{1,0:T(8,128)S(1)}, f32[192,128]{1,0:T(8,128)S(1)}, u32[]{:S(2)}, u32[]{:S(2)}) collective-permute-start(f32[192,128]{1,0:T(8,128)S(1)} %get-tuple-element.54.za), channel_id=1, source_target_pairs={{0,1},{1,0},{2,3},{3,2},{4,5},{5,4},{6,7},{7,6},{8,9},{9,8},{10,11... | collective-permute-start | bytes 294920 | tf_op jit(solution)/shard_map/ppermute | solution.py:569
  5.6 7.3 %collective-permute-start.1 = (f32[192,128]{1,0:T(8,128)S(1)}, f32[192,128]{1,0:T(8,128)S(1)}, u32[]{:S(2)}, u32[]{:S(2)}) collective-permute-start(f32[192,128]{1,0:T(8,128)S(1)} %get-tuple-element.55.zb), channel_id=1, source_target_pairs={{0,7},{1,2},{2,1},{3,4},{4,3},{5,6},{6,5},{7,0},{8,15},{9,10},{10,... | collective-permute-start | bytes 294920 | tf_op jit(solution)/shard_map/ppermute | solution.py:570
  12.8 9.9 %copy-start = (s32[256,8]{0,1:T(8,128)S(1)}, s32[256,8]{0,1:T(8,128)}, u32[]{:S(2)}) copy-start(s32[256,8]{0,1:T(8,128)} %param.10) | copy-start | bytes 24580
  12.8 9.9 %copy-start.1 = (s32[512]{0:T(512)S(1)}, s32[512]{0:T(512)}, u32[]{:S(2)}) copy-start(s32[512]{0:T(512)} %param.11) | copy-start | bytes 6148
  14.5 10.9 %collective-permute-start.4 = (f32[3,128,128]{2,1,0:T(8,128)S(1)}, f32[3,128,128]{2,1,0:T(8,128)S(1)}, u32[]{:S(2)}, u32[]{:S(2)}) collective-permute-start(f32[3,128,128]{2,1,0:T(8,128)S(1)} %get-tuple-element.64.refs_0_), channel_id=1, source_target_pairs={{0,48},{1,49},{2,50},{3,51},{4,52},{5,53},{6,54},{7,55}} | collective-permute-start | bytes 589832 | tf_op jit(solution)/shard_map/ppermute | solution.py:576
  15.2 10.2 %collective-permute-start.3 = (f32[3,128,128]{2,1,0:T(8,128)S(1)}, f32[3,128,128]{2,1,0:T(8,128)S(1)}, u32[]{:S(2)}, u32[]{:S(2)}) collective-permute-start(f32[3,128,128]{2,1,0:T(8,128)S(1)} %get-tuple-element.64.refs_0_), channel_id=1, source_target_pairs={{0,16},{1,17},{2,18},{3,19},{4,20},{5,21},{6,22},{7,23}} | collective-permute-start | bytes 589832 | tf_op jit(solution)/shard_map/ppermute | solution.py:576
  15.9 13.6 %collective-permute-start.2 = (f32[3,128,128]{2,1,0:T(8,128)S(1)}, f32[3,128,128]{2,1,0:T(8,128)S(1)}, u32[]{:S(2)}, u32[]{:S(2)}) collective-permute-start(f32[3,128,128]{2,1,0:T(8,128)S(1)} %get-tuple-element.64.refs_0_), channel_id=1, source_target_pairs={{0,64},{1,65},{2,66},{3,67},{4,68},{5,69},{6,70},{7,71}} | collective-permute-start | bytes 589832 | tf_op jit(solution)/shard_map/ppermute | solution.py:576
  17.2 17.1 %collective-permute-start.6 = (f32[4,128,128]{2,1,0:T(8,128)S(1)}, f32[4,128,128]{2,1,0:T(8,128)S(1)}, u32[]{:S(2)}, u32[]{:S(2)}) collective-permute-start(f32[4,128,128]{2,1,0:T(8,128)S(1)} %get-tuple-element.71), channel_id=1, source_target_pairs={{0,8},{8,0},{16,24},{24,16},{32,40},{40,32},{48,56},{56,48},{64,72... | collective-permute-start | bytes 786440 | tf_op jit(solution)/shard_map/ppermute | solution.py:574
  17.2 17.0 %collective-permute-start.7 = (f32[4,128,128]{2,1,0:T(8,128)S(1)}, f32[4,128,128]{2,1,0:T(8,128)S(1)}, u32[]{:S(2)}, u32[]{:S(2)}) collective-permute-start(f32[4,128,128]{2,1,0:T(8,128)S(1)} %get-tuple-element.72), channel_id=1, source_target_pairs={{8,16},{16,8},{24,32},{32,24},{40,48},{48,40},{56,64},{64,56},{72,... | collective-permute-start | bytes 786440 | tf_op jit(solution)/shard_map/ppermute | solution.py:575
  29.5 6.3 %collective-permute-start.5 = (f32[3,128,128]{2,1,0:T(8,128)S(1)}, f32[3,128,128]{2,1,0:T(8,128)S(1)}, u32[]{:S(2)}, u32[]{:S(2)}) collective-permute-start(f32[3,128,128]{2,1,0:T(8,128)S(1)} %join.2.refs_0_), channel_id=1, source_target_pairs={{0,32},{16,80},{48,112},{64,96},{1,33},{17,81},{49,113},{65,97},{2... | collective-permute-start | bytes 589832 | tf_op jit(solution)/shard_map/ppermute | solution.py:582
  35.8 3.3 %collective-permute-start.8 = (f32[3,128,128]{2,1,0:T(8,128)S(1)}, f32[3,128,128]{2,1,0:T(8,128)S(1)}, u32[]{:S(2)}, u32[]{:S(2)}) collective-permute-start(f32[3,128,128]{2,1,0:T(8,128)S(1)} %join.3.face), channel_id=1, source_target_pairs={{0,8},{16,24},{32,40},{48,56},{64,72},{80,88},{96,104},{112,120},{... | collective-permute-start | bytes 589832 | tf_op jit(solution)/shard_map/ppermute | solution.py:591
  37.1 11.8 %collective-permute-start.13 = (f32[4,128,128]{2,1,0:T(8,128)S(1)}, f32[4,128,128]{2,1,0:T(8,128)S(1)}, u32[]{:S(2)}, u32[]{:S(2)}) collective-permute-start(f32[4,128,128]{2,1,0:T(8,128)S(1)} %get-tuple-element.89), channel_id=1, source_target_pairs={{0,8},{8,0},{16,24},{24,16},{32,40},{40,32},{48,56},{56,48},{64,72... | collective-permute-start | bytes 786440 | tf_op jit(solution)/shard_map/ppermute | solution.py:587
  37.2 11.8 %collective-permute-start.14 = (f32[4,128,128]{2,1,0:T(8,128)S(1)}, f32[4,128,128]{2,1,0:T(8,128)S(1)}, u32[]{:S(2)}, u32[]{:S(2)}) collective-permute-start(f32[4,128,128]{2,1,0:T(8,128)S(1)} %get-tuple-element.90), channel_id=1, source_target_pairs={{8,16},{16,8},{24,32},{32,24},{40,48},{48,40},{56,64},{64,56},{72,... | collective-permute-start | bytes 786440 | tf_op jit(solution)/shard_map/ppermute | solution.py:588
  39.4 6.1 %collective-permute-start.9 = (f32[2,3,16,128]{3,2,1,0:T(8,128)S(1)}, f32[2,3,16,128]{3,2,1,0:T(8,128)S(1)}, u32[]{:S(2)}, u32[]{:S(2)}) collective-permute-start(f32[2,3,16,128]{3,2,1,0:T(8,128)S(1)} %get-tuple-element.85), channel_id=1, source_target_pairs={{0,4},{1,5},{2,6},{3,7},{4,0},{5,1},{6,2},{7,3},{8,12},{9,13},{10,... | collective-permute-start | bytes 147464 | tf_op jit(solution)/shard_map/ppermute | solution.py:594
  43.0 4.1 %collective-permute-start.10 = (f32[2,3,16,128]{3,2,1,0:T(8,128)S(1)}, f32[2,3,16,128]{3,2,1,0:T(8,128)S(1)}, u32[]{:S(2)}, u32[]{:S(2)}) collective-permute-start(f32[2,3,16,128]{3,2,1,0:T(8,128)S(1)} %get-tuple-element.86), channel_id=1, source_target_pairs={{0,2},{1,3},{2,0},{3,1},{4,6},{5,7},{6,4},{7,5},{8,10},{9,11},{10,... | collective-permute-start | bytes 147464 | tf_op jit(solution)/shard_map/ppermute | solution.py:594
  43.5 5.3 %collective-permute-start.11 = (f32[2,3,16,128]{3,2,1,0:T(8,128)S(1)}, f32[2,3,16,128]{3,2,1,0:T(8,128)S(1)}, u32[]{:S(2)}, u32[]{:S(2)}) collective-permute-start(f32[2,3,16,128]{3,2,1,0:T(8,128)S(1)} %get-tuple-element.87), channel_id=1, source_target_pairs={{0,6},{1,7},{2,4},{3,5},{4,2},{5,3},{6,0},{7,1},{8,14},{9,15},{10,... | collective-permute-start | bytes 147464 | tf_op jit(solution)/shard_map/ppermute | solution.py:594
  48.9 3.9 %collective-permute-start.12 = (f32[3,16,128]{2,1,0:T(8,128)S(1)}, f32[3,16,128]{2,1,0:T(8,128)S(1)}, u32[]{:S(2)}, u32[]{:S(2)}) collective-permute-start(f32[3,16,128]{2,1,0:T(8,128)S(1)} %get-tuple-element.88), channel_id=1, source_target_pairs={{0,1},{1,0},{2,3},{3,2},{4,5},{5,4},{6,7},{7,6},{8,9},{9,8},{10,11... | collective-permute-start | bytes 73736 | tf_op jit(solution)/shard_map/ppermute | solution.py:597

commit v10 on v9

--- a/solution.py
+++ b/solution.py
@@ -593,10 +593,10 @@
     pairs = [
         lax.ppermute(pairs[k // 2 - 1], "gz", [(i, i ^ k) for i in range(nz)]) for k in (4, 2, 6)
     ]
+    out = last_call(ha, hb, za, zb, ra, rb, mid, coef, done, out)
+    *pairs, out = lax.optimization_barrier((*pairs, out))
     kept, given = gather((own, *pairs))
     came = lax.ppermute(given, "gz", inside_z)
-    out = last_call(ha, hb, za, zb, ra, rb, mid, coef, done, out)
-    came, out = lax.optimization_barrier((came, out))
     gradient = product((kept, came), near).transpose(1, 0, 2)
     return out, gradient
 

time: 54.6 us -> 58 us (1.062)
  the two profiles are of different devices: /device:TPU:24 before, /device:TPU:14 now
where the time goes in v10:
time: 58 us; the launch traced here: 57.7 us
  starting transfers between devices  27.2 us (47%)
  Pallas kernels  16.9 us (29%)
  waiting for transfers between devices  12.8 us (22%)
  between operations  0.82 us (1%)
    ppermute x1, starting transfers between devices, shards(): other = lax.ppermute(face, 'gx', [(i, i + 1) for i in range(0, nx, 2)])  8.59 us
    ppermute x3, starting transfers between devices, shards(): lax.ppermute(pairs[k // 2 - 1], 'gz', [(i, i ^ k) for i in range(nz)])  4.69 us
    ppermute x2, starting transfers between devices, shards(): rb = lax.ppermute(msg_b, 'gx', across_x)  4.13 us
    pallas_call x1, Pallas kernels, pack(): pl.pallas_call(pack_kernel, in_specs=[ANY, ANY, ANY], out_specs=[VM] * 7,...  4.1 us
    ppermute x1, waiting for transfers between devices, shards(): came = lax.ppermute(given, 'gz', inside_z)  3.46 us
    pallas_call x1, Pallas kernels, middle_call(): pl.pallas_call(middle_kernel, in_specs=[VM] * 8 + [ANY], out_specs=[VM] *...  3.42 us
    ppermute x1, waiting for transfers between devices, shards(): hb = lax.ppermute(zb, 'gz', across_z)  3.38 us
    ppermute x1, starting transfers between devices, shards(): far = lax.ppermute(face, 'gx', [(0, 4), (2, 10), (6, 14), (8, 12)])  3.12 us
  transfers between devices with their start and end apart: 15, of which 7 were waited for; matrix products, arithmetic and copies ran while one was open for 0% of the time, Pallas kernels for 17%

profile of v10, /device:TPU:14, one launch (start us, length us, event | category | flops | bytes accessed | tf_op | source)
XLA Modules:
  0.0 57.7 jit_solution(9981190097634482673)
XLA Ops:
  0.6 4.1 %pack.1 = (f32[3,20,144,128]{3,2,1,0:T(8,128)S(1)}, f32[20,144,128]{2,1,0:T(8,128)S(1)}, f32[3,18,128,128]{3,2,1,0:T(8,128)S(1)}, f32[192,128]{1,0:T(8,128)S(1)}...) custom-call(f32[3,16,128,128]{3,2,1,0:T(8,128)} %adj.1, f32[3,16,128,128]{3,2,1,0:T(8,128)} %vel.1, ...), custom_call_target="tpu_custom_call" | custom-call | tf_op jit(solution)/shard_map/pack/pallas_call | solution.py:144
  4.7 0.5 collective-permute-start
  5.3 2.9 %collective-permute-start.1 = (f32[192,128]{1,0:T(8,128)S(1)}, f32[192,128]{1,0:T(8,128)S(1)}, u32[]{:S(2)}, u32[]{:S(2)}) collective-permute-start(f32[192,128]{1,0:T(8,128)S(1)} %get-tuple-element.57.zb), channel_id=1, source_target_pairs={{0,7},{1,2},{2,1},{3,4},{4,3},{5,6},{6,5},{7,0},{8,15},{9,10},{10,... | collective-permute-start | bytes 294920 | tf_op jit(solution)/shard_map/ppermute | solution.py:570
  8.2 1.2 %collective-permute-done.ra.ha = f32[192,128]{1,0:T(8,128)S(1)} collective-permute-done((f32[192,128]{1,0:T(8,128)S(1)}, f32[192,128]{1,0:T(8,128)S(1)}, u32[]{:S(2)}, u32[]{:S(2)}) %collective-permute-start) | collective-permute-done | bytes 98336 | tf_op jit(solution)/shard_map/ppermute | solution.py:569
  9.4 3.4 %collective-permute-done.1.rb.hb = f32[192,128]{1,0:T(8,128)S(1)} collective-permute-done((f32[192,128]{1,0:T(8,128)S(1)}, f32[192,128]{1,0:T(8,128)S(1)}, u32[]{:S(2)}, u32[]{:S(2)}) %collective-permute-start.1) | collective-permute-done | bytes 98336 | tf_op jit(solution)/shard_map/ppermute | solution.py:570
  12.8 1.7 %face.1 = (f32[3,128,128]{2,1,0:T(8,128)S(1)}, f32[3,18,144,128]{3,2,1,0:T(8,128)S(1)}, f32[7,18,128,128]{3,2,1,0:T(8,128)S(1)}, f32[128,128]{1,0:T(8,128)S(1)}, f32[128,128]{1,0:T(8,128)S(1)}) custom-call(f32[3,20,144,128]{3,2,1,0:T(8,128)S(1)} %get-tuple-element.53.adj_s.adj_i, f32[20,144,128]{2,1,0:T(8,128)S(1)} %get-tuple-element.54.visc_s.visc_i, ...), custom_call_target="tpu_custom_call" | custom-call | flops 2949120 | bytes 4325376 | tf_op jit(solution)/shard_map/face/pallas_call | solution.py:297
  14.5 1.3 %collective-permute-start.4 = (f32[3,128,128]{2,1,0:T(8,128)S(1)}, f32[3,128,128]{2,1,0:T(8,128)S(1)}, u32[]{:S(2)}, u32[]{:S(2)}) collective-permute-start(f32[3,128,128]{2,1,0:T(8,128)S(1)} %get-tuple-element.66.refs_0_), channel_id=1, source_target_pairs={{0,48},{1,49},{2,50},{3,51},{4,52},{5,53},{6,54},{7,55}} | collective-permute-start | bytes 589832 | tf_op jit(solution)/shard_map/ppermute | solution.py:576
  15.8 0.7 %collective-permute-start.3 = (f32[3,128,128]{2,1,0:T(8,128)S(1)}, f32[3,128,128]{2,1,0:T(8,128)S(1)}, u32[]{:S(2)}, u32[]{:S(2)}) collective-permute-start(f32[3,128,128]{2,1,0:T(8,128)S(1)} %get-tuple-element.66.refs_0_), channel_id=1, source_target_pairs={{0,16},{1,17},{2,18},{3,19},{4,20},{5,21},{6,22},{7,23}} | collective-permute-start | bytes 589832 | tf_op jit(solution)/shard_map/ppermute | solution.py:576
  16.5 0.7 %collective-permute-start.2 = (f32[3,128,128]{2,1,0:T(8,128)S(1)}, f32[3,128,128]{2,1,0:T(8,128)S(1)}, u32[]{:S(2)}, u32[]{:S(2)}) collective-permute-start(f32[3,128,128]{2,1,0:T(8,128)S(1)} %get-tuple-element.66.refs_0_), channel_id=1, source_target_pairs={{0,64},{1,65},{2,66},{3,67},{4,68},{5,69},{6,70},{7,71}} | collective-permute-start | bytes 589832 | tf_op jit(solution)/shard_map/ppermute | solution.py:576
  17.2 2.2 %collective-permute-start.7 = (f32[4,128,128]{2,1,0:T(8,128)S(1)}, f32[4,128,128]{2,1,0:T(8,128)S(1)}, u32[]{:S(2)}, u32[]{:S(2)}) collective-permute-start(f32[4,128,128]{2,1,0:T(8,128)S(1)} %get-tuple-element.74), channel_id=1, source_target_pairs={{8,16},{16,8},{24,32},{32,24},{40,48},{48,40},{56,64},{64,56},{72,... | collective-permute-start | bytes 786440 | tf_op jit(solution)/shard_map/ppermute | solution.py:575
  19.5 2.7 %inner.1 = (f32[3,18,144,128]{3,2,1,0:T(8,128)S(1)}, f32[7,18,128,128]{3,2,1,0:T(8,128)S(1)}, f32[3,16,128,128]{3,2,1,0:T(8,128)S(1)}, f32[128,128]{1,0:T(8,128)S(1)}) custom-call(f32[3,20,144,128]{3,2,1,0:T(8,128)S(1)} %get-tuple-element.53.adj_s.adj_i, ...), custom_call_target="tpu_custom_call", output_to_operand_aliasing={{0}: (7, {}), {1}: (8, {})} | custom-call | flops 12779520 | bytes 18743296 | tf_op jit(solution)/shard_map/inner/pallas_call | solution.py:358
  22.1 1.1 %collective-permute-done.4.refs_3_ = f32[3,128,128]{2,1,0:T(8,128)S(1)} collective-permute-done((f32[3,128,128]{2,1,0:T(8,128)S(1)}, f32[3,128,128]{2,1,0:T(8,128)S(1)}, u32[]{:S(2)}, u32[]{:S(2)}) %collective-permute-start.4) | collective-permute-done | bytes 196640 | tf_op jit(solution)/shard_map/ppermute | solution.py:576
  23.3 3.1 %collective-permute-start.5 = (f32[3,128,128]{2,1,0:T(8,128)S(1)}, f32[3,128,128]{2,1,0:T(8,128)S(1)}, u32[]{:S(2)}, u32[]{:S(2)}) collective-permute-start(f32[3,128,128]{2,1,0:T(8,128)S(1)} %join.2.refs_0_), channel_id=1, source_target_pairs={{0,32},{16,80},{48,112},{64,96},{1,33},{17,81},{49,113},{65,97},{2... | collective-permute-start | bytes 589832 | tf_op jit(solution)/shard_map/ppermute | solution.py:582
  26.4 3.4 %middle.1 = (f32[3,18,144,128]{3,2,1,0:T(8,128)S(1)}, f32[7,18,128,128]{3,2,1,0:T(8,128)S(1)}, f32[3,16,128,128]{3,2,1,0:T(8,128)S(1)}, f32[3,16,128,128]{3,2,1,0:T(8,128)}, bf16[4,512,512]{2,1,0:T(8,128)(2,1)S(1)}) custom-call(f32[3,20,144,128]{3,2,1,0:T(8,128)S(1)} %get-tuple-element.53.adj_s.adj_i, ...), custom_call_target="tpu_custom_call", output_to_operand_aliasing={{0}: (5, {}), {1}: (6, {}), {2}: (7, {})} | custom-call | flops 11796480 | bytes 17301504 | tf_op jit(solution)/shard_map/middle/pallas_call | solution.py:420
  29.9 1.5 %ends.1 = (f32[3,20,144,128]{3,2,1,0:T(8,128)S(1)}, f32[20,144,128]{2,1,0:T(8,128)S(1)}, f32[3,18,144,128]{3,2,1,0:T(8,128)S(1)}, f32[7,18,128,128]{3,2,1,0:T(8,...) custom-call(f32[3,20,144,128]{3,2,1,0:T(8,128)S(1)} %get-tuple-eleme, ...), custom_call_target="tpu_custom_call", output_to_operand_aliasing={{0}: (0, {}), {1}: (1, {}), {2}: (7, {}), {3}: (8, {}), {4}... | custom-call | flops 3932160 | bytes 5767168 | tf_op jit(solution)/shard_map/ends/pallas_call | solution.py:393
  31.5 1.9 %collective-permute-start.13 = (f32[4,128,128]{2,1,0:T(8,128)S(1)}, f32[4,128,128]{2,1,0:T(8,128)S(1)}, u32[]{:S(2)}, u32[]{:S(2)}) collective-permute-start(f32[4,128,128]{2,1,0:T(8,128)S(1)} %get-tuple-element.90), channel_id=1, source_target_pairs={{8,16},{16,8},{24,32},{32,24},{40,48},{48,40},{56,64},{64,56},{72,... | collective-permute-start | bytes 786440 | tf_op jit(solution)/shard_map/ppermute | solution.py:588
  33.5 8.6 %collective-permute-start.8 = (f32[3,128,128]{2,1,0:T(8,128)S(1)}, f32[3,128,128]{2,1,0:T(8,128)S(1)}, u32[]{:S(2)}, u32[]{:S(2)}) collective-permute-start(f32[3,128,128]{2,1,0:T(8,128)S(1)} %join.3.face), channel_id=1, source_target_pairs={{0,8},{16,24},{32,40},{48,56},{64,72},{80,88},{96,104},{112,120},{... | collective-permute-start | bytes 589832 | tf_op jit(solution)/shard_map/ppermute | solution.py:591
  42.1 1.0 %collective-permute-done.8.more = f32[3,128,128]{2,1,0:T(8,128)S(1)} collective-permute-done((f32[3,128,128]{2,1,0:T(8,128)S(1)}, f32[3,128,128]{2,1,0:T(8,128)S(1)}, u32[]{:S(2)}, u32[]{:S(2)}) %collective-permute-start.8) | collective-permute-done | bytes 196640 | tf_op jit(solution)/shard_map/ppermute | solution.py:591
  43.3 3.7 %collective-permute-start.9 = (f32[2,3,16,128]{3,2,1,0:T(8,128)S(1)}, f32[2,3,16,128]{3,2,1,0:T(8,128)S(1)}, u32[]{:S(2)}, u32[]{:S(2)}) collective-permute-start(f32[2,3,16,128]{3,2,1,0:T(8,128)S(1)} %get-tuple-element.86), channel_id=1, source_target_pairs={{0,4},{1,5},{2,6},{3,7},{4,0},{5,1},{6,2},{7,3},{8,12},{9,13},{10,... | collective-permute-start | bytes 147464 | tf_op jit(solution)/shard_map/ppermute | solution.py:594
  48.0 2.2 %last.1 = (f32[3,18,144,128]{3,2,1,0:T(8,128)S(1)}, f32[3,16,128,128]{3,2,1,0:T(8,128)S(1)}, f32[3,16,128,128]{3,2,1,0:T(8,128)}) custom-call(f32[192,128]{1,0:T(8,128)S(1)} %collective-permute-done.ra.ha, f32[192,128]{1,0:T(8,128)S(1)} %collective-permute-done.1.rb.hb, ...), custom_call_target="tpu_custom_call", output_to_operand_aliasing={{0}: (6, {}), {1}: (8, {}), {2}: (9, {})} | custom-call | flops 3932160 | bytes 5767168 | tf_op jit(solution)/shard_map/last/pallas_call | solution.py:460
  50.3 0.8 %collective-permute-done.10.c = f32[2,3,16,128]{3,2,1,0:T(8,128)S(1)} collective-permute-done((f32[2,3,16,128]{3,2,1,0:T(8,128)S(1)}, f32[2,3,16,128]{3,2,1,0:T(8,128)S(1)}, u32[]{:S(2)}, u32[]{:S(2)}) %collective-permute-start.10) | collective-permute-done | bytes 49184 | tf_op jit(solution)/shard_map/ppermute | solution.py:594
  51.1 1.7 %collective-permute-done.11.d = f32[2,3,16,128]{3,2,1,0:T(8,128)S(1)} collective-permute-done((f32[2,3,16,128]{3,2,1,0:T(8,128)S(1)}, f32[2,3,16,128]{3,2,1,0:T(8,128)S(1)}, u32[]{:S(2)}, u32[]{:S(2)}) %collective-permute-start.11) | collective-permute-done | bytes 49184 | tf_op jit(solution)/shard_map/ppermute | solution.py:594
  53.3 3.5 %collective-permute-done.14.came = f32[3,16,128]{2,1,0:T(8,128)S(1)} collective-permute-done((f32[3,16,128]{2,1,0:T(8,128)S(1)}, f32[3,16,128]{2,1,0:T(8,128)S(1)}, u32[]{:S(2)}, u32[]{:S(2)}) %collective-permute-start.14) | collective-permute-done | bytes 24608 | tf_op jit(solution)/shard_map/ppermute | solution.py:599
  56.7 1.0 %product.1 = f32[3,4,512]{2,1,0:T(4,128)} custom-call(f32[3,16,128]{2,1,0:T(8,128)S(1)} %get-tuple-element.101.kept, f32[3,16,128]{2,1,0:T(8,128)S(1)} %collective-permute-done.14.came, bf16[4,512,512]{2,1,0:T(8,128)(2,1)S(1)} %get-tuple-element.103.filters), custom_call_target="tpu_custom_call" | custom-call | tf_op jit(solution)/shard_map/product/pallas_call | solution.py:549
  (21 shorter events, 2.0 us)
Async XLA Ops:
  4.7 4.7 %collective-permute-start = (f32[192,128]{1,0:T(8,128)S(1)}, f32[192,128]{1,0:T(8,128)S(1)}, u32[]{:S(2)}, u32[]{:S(2)}) collective-permute-start(f32[192,128]{1,0:T(8,128)S(1)} %get-tuple-element.56.za), channel_id=1, source_target_pairs={{0,1},{1,0},{2,3},{3,2},{4,5},{5,4},{6,7},{7,6},{8,9},{9,8},{10,11... | collective-permute-start | bytes 294920 | tf_op jit(solution)/shard_map/ppermute | solution.py:569
  5.3 7.5 %collective-permute-start.1 = (f32[192,128]{1,0:T(8,128)S(1)}, f32[192,128]{1,0:T(8,128)S(1)}, u32[]{:S(2)}, u32[]{:S(2)}) collective-permute-start(f32[192,128]{1,0:T(8,128)S(1)} %get-tuple-element.57.zb), channel_id=1, source_target_pairs={{0,7},{1,2},{2,1},{3,4},{4,3},{5,6},{6,5},{7,0},{8,15},{9,10},{10,... | collective-permute-start | bytes 294920 | tf_op jit(solution)/shard_map/ppermute | solution.py:570
  12.8 6.6 %copy-start = (s32[256,8]{0,1:T(8,128)S(1)}, s32[256,8]{0,1:T(8,128)}, u32[]{:S(2)}) copy-start(s32[256,8]{0,1:T(8,128)} %param.10) | copy-start | bytes 24580
  12.8 6.7 %copy-start.1 = (s32[512]{0:T(512)S(1)}, s32[512]{0:T(512)}, u32[]{:S(2)}) copy-start(s32[512]{0:T(512)} %param.11) | copy-start | bytes 6148
  14.5 8.8 %collective-permute-start.4 = (f32[3,128,128]{2,1,0:T(8,128)S(1)}, f32[3,128,128]{2,1,0:T(8,128)S(1)}, u32[]{:S(2)}, u32[]{:S(2)}) collective-permute-start(f32[3,128,128]{2,1,0:T(8,128)S(1)} %get-tuple-element.66.refs_0_), channel_id=1, source_target_pairs={{0,48},{1,49},{2,50},{3,51},{4,52},{5,53},{6,54},{7,55}} | collective-permute-start | bytes 589832 | tf_op jit(solution)/shard_map/ppermute | solution.py:576
  15.8 7.5 %collective-permute-start.3 = (f32[3,128,128]{2,1,0:T(8,128)S(1)}, f32[3,128,128]{2,1,0:T(8,128)S(1)}, u32[]{:S(2)}, u32[]{:S(2)}) collective-permute-start(f32[3,128,128]{2,1,0:T(8,128)S(1)} %get-tuple-element.66.refs_0_), channel_id=1, source_target_pairs={{0,16},{1,17},{2,18},{3,19},{4,20},{5,21},{6,22},{7,23}} | collective-permute-start | bytes 589832 | tf_op jit(solution)/shard_map/ppermute | solution.py:576
  16.5 6.8 %collective-permute-start.2 = (f32[3,128,128]{2,1,0:T(8,128)S(1)}, f32[3,128,128]{2,1,0:T(8,128)S(1)}, u32[]{:S(2)}, u32[]{:S(2)}) collective-permute-start(f32[3,128,128]{2,1,0:T(8,128)S(1)} %get-tuple-element.66.refs_0_), channel_id=1, source_target_pairs={{0,64},{1,65},{2,66},{3,67},{4,68},{5,69},{6,70},{7,71}} | collective-permute-start | bytes 589832 | tf_op jit(solution)/shard_map/ppermute | solution.py:576
  17.2 12.7 %collective-permute-start.6 = (f32[4,128,128]{2,1,0:T(8,128)S(1)}, f32[4,128,128]{2,1,0:T(8,128)S(1)}, u32[]{:S(2)}, u32[]{:S(2)}) collective-permute-start(f32[4,128,128]{2,1,0:T(8,128)S(1)} %get-tuple-element.73), channel_id=1, source_target_pairs={{0,8},{8,0},{16,24},{24,16},{32,40},{40,32},{48,56},{56,48},{64,72... | collective-permute-start | bytes 786440 | tf_op jit(solution)/shard_map/ppermute | solution.py:574
  17.2 12.6 %collective-permute-start.7 = (f32[4,128,128]{2,1,0:T(8,128)S(1)}, f32[4,128,128]{2,1,0:T(8,128)S(1)}, u32[]{:S(2)}, u32[]{:S(2)}) collective-permute-start(f32[4,128,128]{2,1,0:T(8,128)S(1)} %get-tuple-element.74), channel_id=1, source_target_pairs={{8,16},{16,8},{24,32},{32,24},{40,48},{48,40},{56,64},{64,56},{72,... | collective-permute-start | bytes 786440 | tf_op jit(solution)/shard_map/ppermute | solution.py:575
  23.3 10.1 %collective-permute-start.5 = (f32[3,128,128]{2,1,0:T(8,128)S(1)}, f32[3,128,128]{2,1,0:T(8,128)S(1)}, u32[]{:S(2)}, u32[]{:S(2)}) collective-permute-start(f32[3,128,128]{2,1,0:T(8,128)S(1)} %join.2.refs_0_), channel_id=1, source_target_pairs={{0,32},{16,80},{48,112},{64,96},{1,33},{17,81},{49,113},{65,97},{2... | collective-permute-start | bytes 589832 | tf_op jit(solution)/shard_map/ppermute | solution.py:582
  31.4 16.6 %collective-permute-start.12 = (f32[4,128,128]{2,1,0:T(8,128)S(1)}, f32[4,128,128]{2,1,0:T(8,128)S(1)}, u32[]{:S(2)}, u32[]{:S(2)}) collective-permute-start(f32[4,128,128]{2,1,0:T(8,128)S(1)} %get-tuple-element.89), channel_id=1, source_target_pairs={{0,8},{8,0},{16,24},{24,16},{32,40},{40,32},{48,56},{56,48},{64,72... | collective-permute-start | bytes 786440 | tf_op jit(solution)/shard_map/ppermute | solution.py:587
  31.5 16.5 %collective-permute-start.13 = (f32[4,128,128]{2,1,0:T(8,128)S(1)}, f32[4,128,128]{2,1,0:T(8,128)S(1)}, u32[]{:S(2)}, u32[]{:S(2)}) collective-permute-start(f32[4,128,128]{2,1,0:T(8,128)S(1)} %get-tuple-element.90), channel_id=1, source_target_pairs={{8,16},{16,8},{24,32},{32,24},{40,48},{48,40},{56,64},{64,56},{72,... | collective-permute-start | bytes 786440 | tf_op jit(solution)/shard_map/ppermute | solution.py:588
  33.5 9.6 %collective-permute-start.8 = (f32[3,128,128]{2,1,0:T(8,128)S(1)}, f32[3,128,128]{2,1,0:T(8,128)S(1)}, u32[]{:S(2)}, u32[]{:S(2)}) collective-permute-start(f32[3,128,128]{2,1,0:T(8,128)S(1)} %join.3.face), channel_id=1, source_target_pairs={{0,8},{16,24},{32,40},{48,56},{64,72},{80,88},{96,104},{112,120},{... | collective-permute-start | bytes 589832 | tf_op jit(solution)/shard_map/ppermute | solution.py:591
  43.3 6.9 %collective-permute-start.9 = (f32[2,3,16,128]{3,2,1,0:T(8,128)S(1)}, f32[2,3,16,128]{3,2,1,0:T(8,128)S(1)}, u32[]{:S(2)}, u32[]{:S(2)}) collective-permute-start(f32[2,3,16,128]{3,2,1,0:T(8,128)S(1)} %get-tuple-element.86), channel_id=1, source_target_pairs={{0,4},{1,5},{2,6},{3,7},{4,0},{5,1},{6,2},{7,3},{8,12},{9,13},{10,... | collective-permute-start | bytes 147464 | tf_op jit(solution)/shard_map/ppermute | solution.py:594
  47.0 4.1 %collective-permute-start.10 = (f32[2,3,16,128]{3,2,1,0:T(8,128)S(1)}, f32[2,3,16,128]{3,2,1,0:T(8,128)S(1)}, u32[]{:S(2)}, u32[]{:S(2)}) collective-permute-start(f32[2,3,16,128]{3,2,1,0:T(8,128)S(1)} %get-tuple-element.87), channel_id=1, source_target_pairs={{0,2},{1,3},{2,0},{3,1},{4,6},{5,7},{6,4},{7,5},{8,10},{9,11},{10,... | collective-permute-start | bytes 147464 | tf_op jit(solution)/shard_map/ppermute | solution.py:594
  47.5 5.3 %collective-permute-start.11 = (f32[2,3,16,128]{3,2,1,0:T(8,128)S(1)}, f32[2,3,16,128]{3,2,1,0:T(8,128)S(1)}, u32[]{:S(2)}, u32[]{:S(2)}) collective-permute-start(f32[2,3,16,128]{3,2,1,0:T(8,128)S(1)} %get-tuple-element.88), channel_id=1, source_target_pairs={{0,6},{1,7},{2,4},{3,5},{4,2},{5,3},{6,0},{7,1},{8,14},{9,15},{10,... | collective-permute-start | bytes 147464 | tf_op jit(solution)/shard_map/ppermute | solution.py:594
  52.8 3.9 %collective-permute-start.14 = (f32[3,16,128]{2,1,0:T(8,128)S(1)}, f32[3,16,128]{2,1,0:T(8,128)S(1)}, u32[]{:S(2)}, u32[]{:S(2)}) collective-permute-start(f32[3,16,128]{2,1,0:T(8,128)S(1)} %get-tuple-element.102), channel_id=1, source_target_pairs={{0,1},{1,0},{2,3},{3,2},{4,5},{5,4},{6,7},{7,6},{8,9},{9,8},{10,11... | collective-permute-start | bytes 73736 | tf_op jit(solution)/shard_map/ppermute | solution.py:599

commit v11 on v9

--- a/solution.py
+++ b/solution.py
@@ -573,7 +573,7 @@
     face, msg_a, msg_b = lax.optimization_barrier((face, msg_a, msg_b))
     ra = lax.ppermute(msg_a, "gx", inside_x)
     rb = lax.ppermute(msg_b, "gx", across_x)
-    got = [lax.ppermute(face, "gx", [(0, k)]) for k in (8, 2, 6)]
+    got = [lax.ppermute(face, "gx", [(0, k)]) for k in (6, 2, 8)]
     mid, coef, done, chosen = inner(
         state, centre, middle, block_tiles.T, tile_place.reshape(1, -1), mid, coef
     )

time: 54.6 us -> 53.8 us (0.985); the launches traced: 53.8 us -> 53.5 us
  waiting for transfers between devices: 15.1 us -> 11.2 us
  starting transfers between devices: 21 us -> 24.6 us
    ppermute x3, waiting for transfers between devices: 4.07 us -> 0.01 us  [shards(): got = [lax.ppermute(face, 'gx', [(0, k)]) for k in (6, 2, 8)]]
    ppermute x2, starting transfers between devices: 7.35 us -> 10.8 us  [shards(): rb = lax.ppermute(msg_b, 'gx', across_x)]
  transfers between devices with their start and end apart: 15 -> 15, of which waited for: 7 -> 6; matrix products, arithmetic and copies ran while one was open for 0% -> 0% of each run, Pallas kernels for 19% -> 19%
where the time goes in v11:
time: 53.8 us; the launch traced here: 53.5 us
  starting transfers between devices  24.6 us (46%)
  Pallas kernels  16.9 us (31%)
  waiting for transfers between devices  11.2 us (21%)
  between operations  0.84 us (2%)
    ppermute x2, starting transfers between devices, shards(): rb = lax.ppermute(msg_b, 'gx', across_x)  10.8 us
    ppermute x3, waiting for transfers between devices, shards(): lax.ppermute(pairs[k // 2 - 1], 'gz', [(i, i ^ k) for i in range(nz)])  5.07 us
    ppermute x3, starting transfers between devices, shards(): lax.ppermute(pairs[k // 2 - 1], 'gz', [(i, i ^ k) for i in range(nz)])  4.68 us
    pallas_call x1, Pallas kernels, pack(): pl.pallas_call(pack_kernel, in_specs=[ANY, ANY, ANY], out_specs=[VM] * 7,...  4.1 us
    pallas_call x1, Pallas kernels, middle_call(): pl.pallas_call(middle_kernel, in_specs=[VM] * 8 + [ANY], out_specs=[VM] *...  3.42 us
    ppermute x1, waiting for transfers between devices, shards(): hb = lax.ppermute(zb, 'gz', across_z)  3.38 us
    pallas_call x1, Pallas kernels, inner(): pl.pallas_call(inner_kernel, in_specs=[VM] * 9, out_specs=[VM] * 4, out_s...  2.67 us
    ppermute x3, starting transfers between devices, shards(): got = [lax.ppermute(face, 'gx', [(0, k)]) for k in (6, 2, 8)]  2.64 us
  transfers between devices with their start and end apart: 15, of which 6 were waited for; matrix products, arithmetic and copies ran while one was open for 0% of the time, Pallas kernels for 19%

profile of v11, /device:TPU:24, one launch (start us, length us, event | category | flops | bytes accessed | tf_op | source)
XLA Modules:
  0.0 53.5 jit_solution(18397911793348032264)
XLA Ops:
  0.6 4.1 %pack.1 = (f32[3,20,144,128]{3,2,1,0:T(8,128)S(1)}, f32[20,144,128]{2,1,0:T(8,128)S(1)}, f32[3,18,128,128]{3,2,1,0:T(8,128)S(1)}, f32[192,128]{1,0:T(8,128)S(1)}...) custom-call(f32[3,16,128,128]{3,2,1,0:T(8,128)} %adj.1, f32[3,16,128,128]{3,2,1,0:T(8,128)} %vel.1, ...), custom_call_target="tpu_custom_call" | custom-call | tf_op jit(solution)/shard_map/pack/pallas_call | solution.py:144
  4.7 0.8 %collective-permute-start = (f32[192,128]{1,0:T(8,128)S(1)}, f32[192,128]{1,0:T(8,128)S(1)}, u32[]{:S(2)}, u32[]{:S(2)}) collective-permute-start(f32[192,128]{1,0:T(8,128)S(1)} %get-tuple-element.54.za), channel_id=1, source_target_pairs={{0,1},{1,0},{2,3},{3,2},{4,5},{5,4},{6,7},{7,6},{8,9},{9,8},{10,11... | collective-permute-start | bytes 294920 | tf_op jit(solution)/shard_map/ppermute | solution.py:569
  5.6 2.6 %collective-permute-start.1 = (f32[192,128]{1,0:T(8,128)S(1)}, f32[192,128]{1,0:T(8,128)S(1)}, u32[]{:S(2)}, u32[]{:S(2)}) collective-permute-start(f32[192,128]{1,0:T(8,128)S(1)} %get-tuple-element.55.zb), channel_id=1, source_target_pairs={{0,7},{1,2},{2,1},{3,4},{4,3},{5,6},{6,5},{7,0},{8,15},{9,10},{10,... | collective-permute-start | bytes 294920 | tf_op jit(solution)/shard_map/ppermute | solution.py:570
  8.2 1.2 %collective-permute-done.ra.ha = f32[192,128]{1,0:T(8,128)S(1)} collective-permute-done((f32[192,128]{1,0:T(8,128)S(1)}, f32[192,128]{1,0:T(8,128)S(1)}, u32[]{:S(2)}, u32[]{:S(2)}) %collective-permute-start) | collective-permute-done | bytes 98336 | tf_op jit(solution)/shard_map/ppermute | solution.py:569
  9.4 3.4 %collective-permute-done.1.rb.hb = f32[192,128]{1,0:T(8,128)S(1)} collective-permute-done((f32[192,128]{1,0:T(8,128)S(1)}, f32[192,128]{1,0:T(8,128)S(1)}, u32[]{:S(2)}, u32[]{:S(2)}) %collective-permute-start.1) | collective-permute-done | bytes 98336 | tf_op jit(solution)/shard_map/ppermute | solution.py:570
  12.8 1.7 %face.1 = (f32[3,128,128]{2,1,0:T(8,128)S(1)}, f32[3,18,144,128]{3,2,1,0:T(8,128)S(1)}, f32[7,18,128,128]{3,2,1,0:T(8,128)S(1)}, f32[128,128]{1,0:T(8,128)S(1)}, f32[128,128]{1,0:T(8,128)S(1)}) custom-call(f32[3,20,144,128]{3,2,1,0:T(8,128)S(1)} %get-tuple-element.51.adj_s.adj_i, f32[20,144,128]{2,1,0:T(8,128)S(1)} %get-tuple-element.52.visc_s.visc_i, ...), custom_call_target="tpu_custom_call" | custom-call | flops 2949120 | bytes 4325376 | tf_op jit(solution)/shard_map/face/pallas_call | solution.py:297
  14.5 1.3 %collective-permute-start.4 = (f32[3,128,128]{2,1,0:T(8,128)S(1)}, f32[3,128,128]{2,1,0:T(8,128)S(1)}, u32[]{:S(2)}, u32[]{:S(2)}) collective-permute-start(f32[3,128,128]{2,1,0:T(8,128)S(1)} %get-tuple-element.64.refs_0_), channel_id=1, source_target_pairs={{0,64},{1,65},{2,66},{3,67},{4,68},{5,69},{6,70},{7,71}} | collective-permute-start | bytes 589832 | tf_op jit(solution)/shard_map/ppermute | solution.py:576
  15.8 0.7 %collective-permute-start.3 = (f32[3,128,128]{2,1,0:T(8,128)S(1)}, f32[3,128,128]{2,1,0:T(8,128)S(1)}, u32[]{:S(2)}, u32[]{:S(2)}) collective-permute-start(f32[3,128,128]{2,1,0:T(8,128)S(1)} %get-tuple-element.64.refs_0_), channel_id=1, source_target_pairs={{0,16},{1,17},{2,18},{3,19},{4,20},{5,21},{6,22},{7,23}} | collective-permute-start | bytes 589832 | tf_op jit(solution)/shard_map/ppermute | solution.py:576
  16.5 0.7 %collective-permute-start.2 = (f32[3,128,128]{2,1,0:T(8,128)S(1)}, f32[3,128,128]{2,1,0:T(8,128)S(1)}, u32[]{:S(2)}, u32[]{:S(2)}) collective-permute-start(f32[3,128,128]{2,1,0:T(8,128)S(1)} %get-tuple-element.64.refs_0_), channel_id=1, source_target_pairs={{0,48},{1,49},{2,50},{3,51},{4,52},{5,53},{6,54},{7,55}} | collective-permute-start | bytes 589832 | tf_op jit(solution)/shard_map/ppermute | solution.py:576
  17.2 5.4 %collective-permute-start.7 = (f32[4,128,128]{2,1,0:T(8,128)S(1)}, f32[4,128,128]{2,1,0:T(8,128)S(1)}, u32[]{:S(2)}, u32[]{:S(2)}) collective-permute-start(f32[4,128,128]{2,1,0:T(8,128)S(1)} %get-tuple-element.72), channel_id=1, source_target_pairs={{8,16},{16,8},{24,32},{32,24},{40,48},{48,40},{56,64},{64,56},{72,... | collective-permute-start | bytes 786440 | tf_op jit(solution)/shard_map/ppermute | solution.py:575
  22.7 2.7 %inner.1 = (f32[3,18,144,128]{3,2,1,0:T(8,128)S(1)}, f32[7,18,128,128]{3,2,1,0:T(8,128)S(1)}, f32[3,16,128,128]{3,2,1,0:T(8,128)S(1)}, f32[128,128]{1,0:T(8,128)S(1)}) custom-call(f32[3,20,144,128]{3,2,1,0:T(8,128)S(1)} %get-tuple-element.51.adj_s.adj_i, ...), custom_call_target="tpu_custom_call", output_to_operand_aliasing={{0}: (7, {}), {1}: (8, {})} | custom-call | flops 12779520 | bytes 18743296 | tf_op jit(solution)/shard_map/inner/pallas_call | solution.py:358
  25.4 1.4 %collective-permute-start.5 = (f32[3,128,128]{2,1,0:T(8,128)S(1)}, f32[3,128,128]{2,1,0:T(8,128)S(1)}, u32[]{:S(2)}, u32[]{:S(2)}) collective-permute-start(f32[3,128,128]{2,1,0:T(8,128)S(1)} %join.2.refs_0_), channel_id=1, source_target_pairs={{0,32},{16,80},{48,112},{64,96},{1,33},{17,81},{49,113},{65,97},{2... | collective-permute-start | bytes 589832 | tf_op jit(solution)/shard_map/ppermute | solution.py:582
  26.9 3.4 %middle.1 = (f32[3,18,144,128]{3,2,1,0:T(8,128)S(1)}, f32[7,18,128,128]{3,2,1,0:T(8,128)S(1)}, f32[3,16,128,128]{3,2,1,0:T(8,128)S(1)}, f32[3,16,128,128]{3,2,1,0:T(8,128)}, bf16[4,512,512]{2,1,0:T(8,128)(2,1)S(1)}) custom-call(f32[3,20,144,128]{3,2,1,0:T(8,128)S(1)} %get-tuple-element.51.adj_s.adj_i, ...), custom_call_target="tpu_custom_call", output_to_operand_aliasing={{0}: (5, {}), {1}: (6, {}), {2}: (7, {})} | custom-call | flops 11796480 | bytes 17301504 | tf_op jit(solution)/shard_map/middle/pallas_call | solution.py:420
  30.3 1.5 %ends.1 = (f32[3,20,144,128]{3,2,1,0:T(8,128)S(1)}, f32[20,144,128]{2,1,0:T(8,128)S(1)}, f32[3,18,144,128]{3,2,1,0:T(8,128)S(1)}, f32[7,18,128,128]{3,2,1,0:T(8,...) custom-call(f32[3,20,144,128]{3,2,1,0:T(8,128)S(1)} %get-tuple-eleme, ...), custom_call_target="tpu_custom_call", output_to_operand_aliasing={{0}: (0, {}), {1}: (1, {}), {2}: (7, {}), {3}: (8, {}), {4}... | custom-call | flops 3932160 | bytes 5767168 | tf_op jit(solution)/shard_map/ends/pallas_call | solution.py:393
  31.9 1.3 %collective-permute-start.8 = (f32[3,128,128]{2,1,0:T(8,128)S(1)}, f32[3,128,128]{2,1,0:T(8,128)S(1)}, u32[]{:S(2)}, u32[]{:S(2)}) collective-permute-start(f32[3,128,128]{2,1,0:T(8,128)S(1)} %join.3.face), channel_id=1, source_target_pairs={{0,8},{16,24},{32,40},{48,56},{64,72},{80,88},{96,104},{112,120},{... | collective-permute-start | bytes 589832 | tf_op jit(solution)/shard_map/ppermute | solution.py:591
  33.3 5.3 %collective-permute-start.14 = (f32[4,128,128]{2,1,0:T(8,128)S(1)}, f32[4,128,128]{2,1,0:T(8,128)S(1)}, u32[]{:S(2)}, u32[]{:S(2)}) collective-permute-start(f32[4,128,128]{2,1,0:T(8,128)S(1)} %get-tuple-element.90), channel_id=1, source_target_pairs={{8,16},{16,8},{24,32},{32,24},{40,48},{48,40},{56,64},{64,56},{72,... | collective-permute-start | bytes 786440 | tf_op jit(solution)/shard_map/ppermute | solution.py:588
  38.9 3.7 %collective-permute-start.9 = (f32[2,3,16,128]{3,2,1,0:T(8,128)S(1)}, f32[2,3,16,128]{3,2,1,0:T(8,128)S(1)}, u32[]{:S(2)}, u32[]{:S(2)}) collective-permute-start(f32[2,3,16,128]{3,2,1,0:T(8,128)S(1)} %get-tuple-element.85), channel_id=1, source_target_pairs={{0,4},{1,5},{2,6},{3,7},{4,0},{5,1},{6,2},{7,3},{8,12},{9,13},{10,... | collective-permute-start | bytes 147464 | tf_op jit(solution)/shard_map/ppermute | solution.py:594
  42.5 0.8 %collective-permute-start.10 = (f32[2,3,16,128]{3,2,1,0:T(8,128)S(1)}, f32[2,3,16,128]{3,2,1,0:T(8,128)S(1)}, u32[]{:S(2)}, u32[]{:S(2)}) collective-permute-start(f32[2,3,16,128]{3,2,1,0:T(8,128)S(1)} %get-tuple-element.86), channel_id=1, source_target_pairs={{0,2},{1,3},{2,0},{3,1},{4,6},{5,7},{6,4},{7,5},{8,10},{9,11},{10,... | collective-permute-start | bytes 147464 | tf_op jit(solution)/shard_map/ppermute | solution.py:594
  43.5 1.2 %collective-permute-done.9.b = f32[2,3,16,128]{3,2,1,0:T(8,128)S(1)} collective-permute-done((f32[2,3,16,128]{3,2,1,0:T(8,128)S(1)}, f32[2,3,16,128]{3,2,1,0:T(8,128)S(1)}, u32[]{:S(2)}, u32[]{:S(2)}) %collective-permute-start.9) | collective-permute-done | bytes 49184 | tf_op jit(solution)/shard_map/ppermute | solution.py:594
  44.8 1.8 %collective-permute-done.10.c = f32[2,3,16,128]{3,2,1,0:T(8,128)S(1)} collective-permute-done((f32[2,3,16,128]{3,2,1,0:T(8,128)S(1)}, f32[2,3,16,128]{3,2,1,0:T(8,128)S(1)}, u32[]{:S(2)}, u32[]{:S(2)}) %collective-permute-start.10) | collective-permute-done | bytes 49184 | tf_op jit(solution)/shard_map/ppermute | solution.py:594
  46.6 2.0 %collective-permute-done.11.d = f32[2,3,16,128]{3,2,1,0:T(8,128)S(1)} collective-permute-done((f32[2,3,16,128]{3,2,1,0:T(8,128)S(1)}, f32[2,3,16,128]{3,2,1,0:T(8,128)S(1)}, u32[]{:S(2)}, u32[]{:S(2)}) %collective-permute-start.11) | collective-permute-done | bytes 49184 | tf_op jit(solution)/shard_map/ppermute | solution.py:594
  48.8 2.2 %last.1 = (f32[3,18,144,128]{3,2,1,0:T(8,128)S(1)}, f32[3,16,128,128]{3,2,1,0:T(8,128)S(1)}, f32[3,16,128,128]{3,2,1,0:T(8,128)}) custom-call(f32[192,128]{1,0:T(8,128)S(1)} %collective-permute-done.ra.ha, f32[192,128]{1,0:T(8,128)S(1)} %collective-permute-done.1.rb.hb, ...), custom_call_target="tpu_custom_call", output_to_operand_aliasing={{0}: (6, {}), {1}: (8, {}), {2}: (9, {})} | custom-call | flops 3932160 | bytes 5767168 | tf_op jit(solution)/shard_map/last/pallas_call | solution.py:460
  51.0 1.5 %collective-permute-done.12.came = f32[3,16,128]{2,1,0:T(8,128)S(1)} collective-permute-done((f32[3,16,128]{2,1,0:T(8,128)S(1)}, f32[3,16,128]{2,1,0:T(8,128)S(1)}, u32[]{:S(2)}, u32[]{:S(2)}) %collective-permute-start.12) | collective-permute-done | bytes 24608 | tf_op jit(solution)/shard_map/ppermute | solution.py:597
  52.5 1.0 %product.1 = f32[3,4,512]{2,1,0:T(4,128)} custom-call(f32[3,16,128]{2,1,0:T(8,128)S(1)} %get-tuple-element.97.kept, f32[3,16,128]{2,1,0:T(8,128)S(1)} %collective-permute-done.12.came, bf16[4,512,512]{2,1,0:T(8,128)(2,1)S(1)} %get-tuple-element.99.filters), custom_call_target="tpu_custom_call" | custom-call | tf_op jit(solution)/shard_map/product/pallas_call | solution.py:549
  (21 shorter events, 0.9 us)
Async XLA Ops:
  4.7 4.7 %collective-permute-start = (f32[192,128]{1,0:T(8,128)S(1)}, f32[192,128]{1,0:T(8,128)S(1)}, u32[]{:S(2)}, u32[]{:S(2)}) collective-permute-start(f32[192,128]{1,0:T(8,128)S(1)} %get-tuple-element.54.za), channel_id=1, source_target_pairs={{0,1},{1,0},{2,3},{3,2},{4,5},{5,4},{6,7},{7,6},{8,9},{9,8},{10,11... | collective-permute-start | bytes 294920 | tf_op jit(solution)/shard_map/ppermute | solution.py:569
  5.6 7.3 %collective-permute-start.1 = (f32[192,128]{1,0:T(8,128)S(1)}, f32[192,128]{1,0:T(8,128)S(1)}, u32[]{:S(2)}, u32[]{:S(2)}) collective-permute-start(f32[192,128]{1,0:T(8,128)S(1)} %get-tuple-element.55.zb), channel_id=1, source_target_pairs={{0,7},{1,2},{2,1},{3,4},{4,3},{5,6},{6,5},{7,0},{8,15},{9,10},{10,... | collective-permute-start | bytes 294920 | tf_op jit(solution)/shard_map/ppermute | solution.py:570
  12.8 9.9 %copy-start = (s32[256,8]{0,1:T(8,128)S(1)}, s32[256,8]{0,1:T(8,128)}, u32[]{:S(2)}) copy-start(s32[256,8]{0,1:T(8,128)} %param.10) | copy-start | bytes 24580
  12.8 9.9 %copy-start.1 = (s32[512]{0:T(512)S(1)}, s32[512]{0:T(512)}, u32[]{:S(2)}) copy-start(s32[512]{0:T(512)} %param.11) | copy-start | bytes 6148
  14.5 10.9 %collective-permute-start.4 = (f32[3,128,128]{2,1,0:T(8,128)S(1)}, f32[3,128,128]{2,1,0:T(8,128)S(1)}, u32[]{:S(2)}, u32[]{:S(2)}) collective-permute-start(f32[3,128,128]{2,1,0:T(8,128)S(1)} %get-tuple-element.64.refs_0_), channel_id=1, source_target_pairs={{0,64},{1,65},{2,66},{3,67},{4,68},{5,69},{6,70},{7,71}} | collective-permute-start | bytes 589832 | tf_op jit(solution)/shard_map/ppermute | solution.py:576
  15.8 9.6 %collective-permute-start.3 = (f32[3,128,128]{2,1,0:T(8,128)S(1)}, f32[3,128,128]{2,1,0:T(8,128)S(1)}, u32[]{:S(2)}, u32[]{:S(2)}) collective-permute-start(f32[3,128,128]{2,1,0:T(8,128)S(1)} %get-tuple-element.64.refs_0_), channel_id=1, source_target_pairs={{0,16},{1,17},{2,18},{3,19},{4,20},{5,21},{6,22},{7,23}} | collective-permute-start | bytes 589832 | tf_op jit(solution)/shard_map/ppermute | solution.py:576
  16.5 8.9 %collective-permute-start.2 = (f32[3,128,128]{2,1,0:T(8,128)S(1)}, f32[3,128,128]{2,1,0:T(8,128)S(1)}, u32[]{:S(2)}, u32[]{:S(2)}) collective-permute-start(f32[3,128,128]{2,1,0:T(8,128)S(1)} %get-tuple-element.64.refs_0_), channel_id=1, source_target_pairs={{0,48},{1,49},{2,50},{3,51},{4,52},{5,53},{6,54},{7,55}} | collective-permute-start | bytes 589832 | tf_op jit(solution)/shard_map/ppermute | solution.py:576
  17.2 13.2 %collective-permute-start.6 = (f32[4,128,128]{2,1,0:T(8,128)S(1)}, f32[4,128,128]{2,1,0:T(8,128)S(1)}, u32[]{:S(2)}, u32[]{:S(2)}) collective-permute-start(f32[4,128,128]{2,1,0:T(8,128)S(1)} %get-tuple-element.71), channel_id=1, source_target_pairs={{0,8},{8,0},{16,24},{24,16},{32,40},{40,32},{48,56},{56,48},{64,72... | collective-permute-start | bytes 786440 | tf_op jit(solution)/shard_map/ppermute | solution.py:574
  17.2 13.1 %collective-permute-start.7 = (f32[4,128,128]{2,1,0:T(8,128)S(1)}, f32[4,128,128]{2,1,0:T(8,128)S(1)}, u32[]{:S(2)}, u32[]{:S(2)}) collective-permute-start(f32[4,128,128]{2,1,0:T(8,128)S(1)} %get-tuple-element.72), channel_id=1, source_target_pairs={{8,16},{16,8},{24,32},{32,24},{40,48},{48,40},{56,64},{64,56},{72,... | collective-permute-start | bytes 786440 | tf_op jit(solution)/shard_map/ppermute | solution.py:575
  25.4 6.4 %collective-permute-start.5 = (f32[3,128,128]{2,1,0:T(8,128)S(1)}, f32[3,128,128]{2,1,0:T(8,128)S(1)}, u32[]{:S(2)}, u32[]{:S(2)}) collective-permute-start(f32[3,128,128]{2,1,0:T(8,128)S(1)} %join.2.refs_0_), channel_id=1, source_target_pairs={{0,32},{16,80},{48,112},{64,96},{1,33},{17,81},{49,113},{65,97},{2... | collective-permute-start | bytes 589832 | tf_op jit(solution)/shard_map/ppermute | solution.py:582
  31.9 6.7 %collective-permute-start.8 = (f32[3,128,128]{2,1,0:T(8,128)S(1)}, f32[3,128,128]{2,1,0:T(8,128)S(1)}, u32[]{:S(2)}, u32[]{:S(2)}) collective-permute-start(f32[3,128,128]{2,1,0:T(8,128)S(1)} %join.3.face), channel_id=1, source_target_pairs={{0,8},{16,24},{32,40},{48,56},{64,72},{80,88},{96,104},{112,120},{... | collective-permute-start | bytes 589832 | tf_op jit(solution)/shard_map/ppermute | solution.py:591
  33.2 15.6 %collective-permute-start.13 = (f32[4,128,128]{2,1,0:T(8,128)S(1)}, f32[4,128,128]{2,1,0:T(8,128)S(1)}, u32[]{:S(2)}, u32[]{:S(2)}) collective-permute-start(f32[4,128,128]{2,1,0:T(8,128)S(1)} %get-tuple-element.89), channel_id=1, source_target_pairs={{0,8},{8,0},{16,24},{24,16},{32,40},{40,32},{48,56},{56,48},{64,72... | collective-permute-start | bytes 786440 | tf_op jit(solution)/shard_map/ppermute | solution.py:587
  33.3 15.5 %collective-permute-start.14 = (f32[4,128,128]{2,1,0:T(8,128)S(1)}, f32[4,128,128]{2,1,0:T(8,128)S(1)}, u32[]{:S(2)}, u32[]{:S(2)}) collective-permute-start(f32[4,128,128]{2,1,0:T(8,128)S(1)} %get-tuple-element.90), channel_id=1, source_target_pairs={{8,16},{16,8},{24,32},{32,24},{40,48},{48,40},{56,64},{64,56},{72,... | collective-permute-start | bytes 786440 | tf_op jit(solution)/shard_map/ppermute | solution.py:588
  38.9 5.9 %collective-permute-start.9 = (f32[2,3,16,128]{3,2,1,0:T(8,128)S(1)}, f32[2,3,16,128]{3,2,1,0:T(8,128)S(1)}, u32[]{:S(2)}, u32[]{:S(2)}) collective-permute-start(f32[2,3,16,128]{3,2,1,0:T(8,128)S(1)} %get-tuple-element.85), channel_id=1, source_target_pairs={{0,4},{1,5},{2,6},{3,7},{4,0},{5,1},{6,2},{7,3},{8,12},{9,13},{10,... | collective-permute-start | bytes 147464 | tf_op jit(solution)/shard_map/ppermute | solution.py:594
  42.5 4.1 %collective-permute-start.10 = (f32[2,3,16,128]{3,2,1,0:T(8,128)S(1)}, f32[2,3,16,128]{3,2,1,0:T(8,128)S(1)}, u32[]{:S(2)}, u32[]{:S(2)}) collective-permute-start(f32[2,3,16,128]{3,2,1,0:T(8,128)S(1)} %get-tuple-element.86), channel_id=1, source_target_pairs={{0,2},{1,3},{2,0},{3,1},{4,6},{5,7},{6,4},{7,5},{8,10},{9,11},{10,... | collective-permute-start | bytes 147464 | tf_op jit(solution)/shard_map/ppermute | solution.py:594
  43.3 5.3 %collective-permute-start.11 = (f32[2,3,16,128]{3,2,1,0:T(8,128)S(1)}, f32[2,3,16,128]{3,2,1,0:T(8,128)S(1)}, u32[]{:S(2)}, u32[]{:S(2)}) collective-permute-start(f32[2,3,16,128]{3,2,1,0:T(8,128)S(1)} %get-tuple-element.87), channel_id=1, source_target_pairs={{0,6},{1,7},{2,4},{3,5},{4,2},{5,3},{6,0},{7,1},{8,14},{9,15},{10,... | collective-permute-start | bytes 147464 | tf_op jit(solution)/shard_map/ppermute | solution.py:594
  48.6 3.9 %collective-permute-start.12 = (f32[3,16,128]{2,1,0:T(8,128)S(1)}, f32[3,16,128]{2,1,0:T(8,128)S(1)}, u32[]{:S(2)}, u32[]{:S(2)}) collective-permute-start(f32[3,16,128]{2,1,0:T(8,128)S(1)} %get-tuple-element.88), channel_id=1, source_target_pairs={{0,1},{1,0},{2,3},{3,2},{4,5},{5,4},{6,7},{7,6},{8,9},{9,8},{10,11... | collective-permute-start | bytes 73736 | tf_op jit(solution)/shard_map/ppermute | solution.py:597
